TPU v7x, 32 devices: a whole 2x2x4 slice. The times are simulated.
32 devices in a mesh: seq: 2 (over core), fsdp: 16 (over z, y, x).
Axes of the slice: x: 2, y: 2, z: 4, core: 2. Of those that a mesh axis runs over, the one named last changes fastest.
Arguments:
- tokens: bfloat16 [2, 16, 1280, 768], P(None, 'fsdp', 'seq'), may hold values from -6 to 6
- permutation: int32 [2, 16, 1280], P(None, 'fsdp'), may hold values from 0 to 1279, each once within a row
- segment_ids: int32 [2, 16, 1280], P(None, 'fsdp'), may hold values from 0 to 3, never falling along the last dimension, each value on 1 to 1024 neighbouring positions
- cotangent: bfloat16 [2, 16, 1280, 768], P(None, 'fsdp', 'seq'), may hold values from -6 to 6
- w_qkv: bfloat16 [768, 2304], P(('seq', 'fsdp')), may hold values from -0.21875 to 0.21875
- b_qkv: bfloat16 [2304], P(('seq', 'fsdp')), may hold values from -3 to 3
- w_out: bfloat16 [768, 768], P(('seq', 'fsdp')), may hold values from -0.875 to 0.875
- b_out: bfloat16 [768], P(('seq', 'fsdp')), may hold values from -2 to 2
- gain_one: bfloat16 [768], P(('seq', 'fsdp')), may hold values from 0.5 to 1.5
- shift_one: bfloat16 [768], P(('seq', 'fsdp')), may hold values from -2 to 2
- w_up: bfloat16 [768, 3072], P(('seq', 'fsdp')), may hold values from -0.21875 to 0.21875
- b_up: bfloat16 [3072], P(('seq', 'fsdp')), may hold values from -2 to 2
- w_down: bfloat16 [3072, 768], P(('seq', 'fsdp')), may hold values from -0.109375 to 0.109375
- b_down: bfloat16 [768], P(('seq', 'fsdp')), may hold values from -2 to 2
- gain_two: bfloat16 [768], P(('seq', 'fsdp')), may hold values from 0.5 to 1.5
- shift_two: bfloat16 [768], P(('seq', 'fsdp')), may hold values from -2 to 2
Outputs:
- outputs: bfloat16 [2, 16, 1280, 768], P(None, 'fsdp', 'seq')
- token_grad: bfloat16 [2, 16, 1280, 768], P(None, 'fsdp', 'seq')
- grad_w_qkv: float32 [768, 2304], P(('seq', 'fsdp'))
- grad_b_qkv: float32 [2304], P(('seq', 'fsdp'))
- grad_w_out: float32 [768, 768], P(('seq', 'fsdp'))
- grad_b_out: float32 [768], P(('seq', 'fsdp'))
- grad_gain_one: float32 [768], P(('seq', 'fsdp'))
- grad_shift_one: float32 [768], P(('seq', 'fsdp'))
- grad_w_up: float32 [768, 3072], P(('seq', 'fsdp'))
- grad_b_up: float32 [3072], P(('seq', 'fsdp'))
- grad_w_down: float32 [3072, 768], P(('seq', 'fsdp'))
- grad_b_down: float32 [768], P(('seq', 'fsdp'))
- grad_gain_two: float32 [768], P(('seq', 'fsdp'))
- grad_shift_two: float32 [768], P(('seq', 'fsdp'))
Inputs may be any that keep to these rules, and one draw needn't show every extreme that they name: Each row is a permutation of the 1280 rows of one pack. `segment_ids`: within each pack the ids never fall, begin at 0 and take every value up to 3; each sequence has 1 to 1024 tokens and one has exactly 1024.
All inputs are finite; a program needn't handle non-finite values.
Results may differ from a plain program's by a relative error of at most 0.015.
Values may be sent and summed in bfloat16 or wider, within the bound.
No kernel may reach another device: no remote copies, remote signals or barrier semaphores. Data moves between devices by JAX's collectives and lax.ppermute only.
A program may use at most 192 MiB of HBM per device.

v0:
```python
import math

import jax
import jax.numpy as jnp
from jax import lax
from jax.sharding import PartitionSpec as P

HEAD = 64


eps_norm = 1e-06


def positions(segments):
    count_rows = segments.shape[0]
    places = jnp.arange(count_rows, dtype=jnp.int32)
    starts = jnp.concatenate([jnp.ones((1,), dtype=jnp.bool_), segments[1:] != segments[:-1]])
    firsts = lax.cummax(jnp.where(starts, places, jnp.zeros_like(places)), axis=0)
    return (places - firsts).astype(jnp.float32)


def rotate(values, angles, head_size):
    count_rows = values.shape[0]
    halves = head_size // 2
    paired = values.reshape(count_rows, -1, halves, 2)
    freqs = jnp.exp(jnp.arange(halves, dtype=jnp.float32) * (-2.0 * math.log(10000.0) / head_size))
    phase = angles[:, None, None] * freqs[None, None, :]
    cosine = jnp.cos(phase)
    sine = jnp.sin(phase)
    first_part = paired[..., 0]
    second_part = paired[..., 1]
    turned = jnp.stack(
        [first_part * cosine - second_part * sine, second_part * cosine + first_part * sine],
        axis=-1,
    )
    return turned.reshape(count_rows, -1)


def normalize(hidden, gain, shift):
    centre = hidden - jnp.mean(hidden, axis=-1, keepdims=True)
    spread = jnp.mean(centre * centre, axis=-1, keepdims=True)
    return centre * lax.rsqrt(spread + eps_norm) * gain + shift


def gelu_exact(values):
    return jax.nn.gelu(values, approximate=False)


def left_dot(left, right):
    return lax.dot_general(
        left, right, (((0,), (0,)), ((), ())), preferred_element_type=jnp.float32
    )


def right_dot(left, right):
    return lax.dot_general(
        left, right, (((1,), (1,)), ((), ())), preferred_element_type=jnp.float32
    )


def head_slice(matrix, head_index, head_size):
    return lax.dynamic_slice_in_dim(matrix, head_index * head_size, head_size, 1)


def side_by_side(stacked):
    return stacked.transpose(1, 0, 2).reshape(stacked.shape[1], stacked.shape[0] * stacked.shape[2])


def attend(queries, keys_all, values_all, segments, head_size):
    head_count = queries.shape[1] // head_size
    same_seq = segments[:, None] == segments[None, :]
    scale = 1.0 / math.sqrt(head_size)

    def one_head(head_index):
        scores = jnp.where(
            same_seq,
            right_dot(
                head_slice(queries, head_index, head_size),
                head_slice(keys_all, head_index, head_size),
            )
            * scale,
            -1000000000.0,
        )
        top_score = jnp.max(scores, axis=1, keepdims=True)
        expo = jnp.exp(scores - top_score)
        total = jnp.sum(expo, axis=1, keepdims=True)
        probs = (expo / total).astype(jnp.bfloat16)
        context = jnp.dot(
            probs, head_slice(values_all, head_index, head_size), preferred_element_type=jnp.float32
        )
        return (context, (top_score + jnp.log(total))[:, 0])

    contexts, log_totals = lax.map(one_head, jnp.arange(head_count, dtype=jnp.int32))
    return (side_by_side(contexts).astype(jnp.bfloat16), log_totals)


def attend_back(queries, keys_all, values_all, segments, log_totals, grad_context, head_size):
    head_count = queries.shape[1] // head_size
    same_seq = segments[:, None] == segments[None, :]
    scale = 1.0 / math.sqrt(head_size)

    def one_head(head_index):
        query_head = head_slice(queries, head_index, head_size)
        key_head = head_slice(keys_all, head_index, head_size)
        grad_head = head_slice(grad_context, head_index, head_size)
        scores = jnp.where(same_seq, right_dot(query_head, key_head) * scale, -1000000000.0)
        probs = jnp.exp(scores - log_totals[head_index][:, None])
        grad_probs = right_dot(grad_head, head_slice(values_all, head_index, head_size))
        grad_scores = (
            probs * (grad_probs - jnp.sum(probs * grad_probs, axis=1, keepdims=True))
        ).astype(jnp.bfloat16)
        grad_query = jnp.dot(grad_scores, key_head, preferred_element_type=jnp.float32) * scale
        grad_key = left_dot(grad_scores, query_head) * scale
        grad_value = left_dot(probs.astype(jnp.bfloat16), grad_head)
        return (grad_query, grad_key, grad_value)

    grad_q, grad_k, grad_v = lax.map(one_head, jnp.arange(head_count, dtype=jnp.int32))
    return (side_by_side(grad_q), side_by_side(grad_k), side_by_side(grad_v))


def on_device(
    tokens,
    permutation,
    segment_ids,
    cotangent,
    w_qkv,
    b_qkv,
    w_out,
    b_out,
    gain_one,
    shift_one,
    w_up,
    b_up,
    w_down,
    b_down,
    gain_two,
    shift_two,
):
    shards = (
        w_qkv,
        b_qkv,
        w_out,
        b_out,
        gain_one,
        shift_one,
        w_up,
        b_up,
        w_down,
        b_down,
        gain_two,
        shift_two,
    )
    batch_count = tokens.shape[0]
    local_rows = tokens.shape[2]
    model_width = tokens.shape[3]
    seq_parts = lax.axis_size("seq")
    seq_place = lax.axis_index("seq")
    pack_rows = seq_parts * local_rows
    share = model_width // seq_parts
    head_size = HEAD
    own_start = seq_place * local_rows
    owners = seq_parts * lax.axis_size("fsdp")
    totals = tuple(
        (jnp.zeros((piece.shape[0] * owners,) + piece.shape[1:], jnp.float32) for piece in shards)
    )
    results = []
    token_grads = []
    for batch_index in range(batch_count):
        gathered = (
            lax.all_gather(shards[0], ("seq", "fsdp"), axis=0, tiled=True),
            lax.all_gather(shards[1], ("seq", "fsdp"), axis=0, tiled=True),
            lax.all_gather(shards[2], ("seq", "fsdp"), axis=0, tiled=True),
            lax.all_gather(shards[3], ("seq", "fsdp"), axis=0, tiled=True),
            lax.all_gather(shards[4], ("seq", "fsdp"), axis=0, tiled=True),
            lax.all_gather(shards[5], ("seq", "fsdp"), axis=0, tiled=True),
            lax.all_gather(shards[6], ("seq", "fsdp"), axis=0, tiled=True),
            lax.all_gather(shards[7], ("seq", "fsdp"), axis=0, tiled=True),
            lax.all_gather(shards[8], ("seq", "fsdp"), axis=0, tiled=True),
            lax.all_gather(shards[9], ("seq", "fsdp"), axis=0, tiled=True),
            lax.all_gather(shards[10], ("seq", "fsdp"), axis=0, tiled=True),
            lax.all_gather(shards[11], ("seq", "fsdp"), axis=0, tiled=True),
        )
        (
            full_qkv,
            bias_qkv,
            full_out,
            bias_out,
            norm_gain_one,
            norm_shift_one,
            full_up,
            bias_up,
            full_down,
            bias_down,
            norm_gain_two,
            norm_shift_two,
        ) = gathered
        order = permutation[batch_index, 0]
        segments = segment_ids[batch_index, 0]
        inverse = (
            jnp.zeros((pack_rows,), jnp.int32).at[order].set(jnp.arange(pack_rows, dtype=jnp.int32))
        )
        work_angles = positions(segments)
        own_tokens = tokens[batch_index, 0]
        own_angles = lax.dynamic_slice_in_dim(work_angles[inverse], own_start, local_rows, 0)
        projected = jnp.dot(
            own_tokens, full_qkv, preferred_element_type=jnp.float32
        ) + bias_qkv.astype(jnp.float32)
        outgoing = jnp.concatenate(
            [
                rotate(projected[:, :model_width], own_angles, head_size),
                rotate(projected[:, model_width : 2 * model_width], own_angles, head_size),
                projected[:, 2 * model_width :],
            ],
            axis=1,
        ).astype(jnp.bfloat16)
        incoming = lax.all_to_all(
            outgoing.reshape(local_rows, 3, seq_parts, share),
            "seq",
            split_axis=2,
            concat_axis=0,
            tiled=True,
        )
        working = incoming.reshape(pack_rows, 3, share)[order]
        queries = working[:, 0]
        keys_all = working[:, 1]
        values_all = working[:, 2]
        context_work, log_totals = attend(queries, keys_all, values_all, segments, head_size)
        context_back = lax.all_to_all(
            context_work[inverse].reshape(pack_rows, 1, share),
            "seq",
            split_axis=0,
            concat_axis=1,
            tiled=True,
        )
        context = context_back.reshape(local_rows, model_width)
        attended = jnp.dot(context, full_out, preferred_element_type=jnp.float32) + bias_out.astype(
            jnp.float32
        )
        first_norm, first_back = jax.vjp(
            normalize,
            own_tokens.astype(jnp.float32) + attended,
            norm_gain_one.astype(jnp.float32),
            norm_shift_one.astype(jnp.float32),
        )
        first_low = first_norm.astype(jnp.bfloat16)
        upper = jnp.dot(first_low, full_up, preferred_element_type=jnp.float32) + bias_up.astype(
            jnp.float32
        )
        activated, gelu_back = jax.vjp(gelu_exact, upper)
        active_low = activated.astype(jnp.bfloat16)
        lowered = jnp.dot(
            active_low, full_down, preferred_element_type=jnp.float32
        ) + bias_down.astype(jnp.float32)
        result, second_back = jax.vjp(
            normalize,
            first_norm + lowered,
            norm_gain_two.astype(jnp.float32),
            norm_shift_two.astype(jnp.float32),
        )
        results.append(result.astype(jnp.bfloat16))
        gathered = (
            lax.all_gather(shards[0], ("seq", "fsdp"), axis=0, tiled=True),
            lax.all_gather(shards[1], ("seq", "fsdp"), axis=0, tiled=True),
            lax.all_gather(shards[2], ("seq", "fsdp"), axis=0, tiled=True),
            lax.all_gather(shards[3], ("seq", "fsdp"), axis=0, tiled=True),
            lax.all_gather(shards[4], ("seq", "fsdp"), axis=0, tiled=True),
            lax.all_gather(shards[5], ("seq", "fsdp"), axis=0, tiled=True),
            lax.all_gather(shards[6], ("seq", "fsdp"), axis=0, tiled=True),
            lax.all_gather(shards[7], ("seq", "fsdp"), axis=0, tiled=True),
            lax.all_gather(shards[8], ("seq", "fsdp"), axis=0, tiled=True),
            lax.all_gather(shards[9], ("seq", "fsdp"), axis=0, tiled=True),
            lax.all_gather(shards[10], ("seq", "fsdp"), axis=0, tiled=True),
            lax.all_gather(shards[11], ("seq", "fsdp"), axis=0, tiled=True),
        )
        (
            full_qkv,
            bias_qkv,
            full_out,
            bias_out,
            norm_gain_one,
            norm_shift_one,
            full_up,
            bias_up,
            full_down,
            bias_down,
            norm_gain_two,
            norm_shift_two,
        ) = gathered
        grad_second, grad_gain_two, grad_shift_two = second_back(
            cotangent[batch_index, 0].astype(jnp.float32)
        )
        grad_lowered = grad_second.astype(jnp.bfloat16)
        grad_w_down = left_dot(active_low, grad_lowered)
        grad_b_down = jnp.sum(grad_lowered.astype(jnp.float32), axis=0)
        grad_upper = gelu_back(right_dot(grad_lowered, full_down))[0].astype(jnp.bfloat16)
        grad_w_up = left_dot(first_low, grad_upper)
        grad_b_up = jnp.sum(grad_upper.astype(jnp.float32), axis=0)
        grad_first = grad_second + right_dot(grad_upper, full_up)
        grad_resid, grad_gain_one, grad_shift_one = first_back(grad_first)
        grad_attended = grad_resid.astype(jnp.bfloat16)
        grad_w_out = left_dot(context, grad_attended)
        grad_b_out = jnp.sum(grad_attended.astype(jnp.float32), axis=0)
        grad_context = right_dot(grad_attended, full_out).astype(jnp.bfloat16)
        grad_context_in = lax.all_to_all(
            grad_context.reshape(local_rows, seq_parts, share),
            "seq",
            split_axis=1,
            concat_axis=0,
            tiled=True,
        )
        grad_context_work = grad_context_in.reshape(pack_rows, share)[order]
        grad_q, grad_k, grad_v = attend_back(
            queries, keys_all, values_all, segments, log_totals, grad_context_work, head_size
        )
        grad_q = rotate(grad_q, -work_angles, head_size)
        grad_k = rotate(grad_k, -work_angles, head_size)
        grad_projected_work = jnp.stack([grad_q, grad_k, grad_v], axis=1).astype(jnp.bfloat16)
        grad_projected = lax.all_to_all(
            grad_projected_work[inverse].reshape(pack_rows, 3, 1, share),
            "seq",
            split_axis=0,
            concat_axis=2,
            tiled=True,
        )
        grad_projected = grad_projected.reshape(local_rows, 3 * model_width)
        grad_w_qkv = left_dot(own_tokens, grad_projected)
        grad_b_qkv = jnp.sum(grad_projected.astype(jnp.float32), axis=0)
        token_grads.append((grad_resid + right_dot(grad_projected, full_qkv)).astype(jnp.bfloat16))
        batch_grads = (
            grad_w_qkv,
            grad_b_qkv,
            grad_w_out,
            grad_b_out,
            grad_gain_one,
            grad_shift_one,
            grad_w_up,
            grad_b_up,
            grad_w_down,
            grad_b_down,
            grad_gain_two,
            grad_shift_two,
        )
        totals = tuple((running + piece for running, piece in zip(totals, batch_grads)))
    totals = lax.psum_scatter(totals, ("seq", "fsdp"), scatter_dimension=0, tiled=True)
    outputs = jnp.stack(results, axis=0)[:, None]
    token_grad = jnp.stack(token_grads, axis=0)[:, None]
    return (
        outputs,
        token_grad,
        totals[0],
        totals[1],
        totals[2],
        totals[3],
        totals[4],
        totals[5],
        totals[6],
        totals[7],
        totals[8],
        totals[9],
        totals[10],
        totals[11],
    )


def solution(mesh):
    return jax.shard_map(
        on_device,
        mesh=mesh,
        in_specs=(
            P(None, "fsdp", "seq", None),
            P(None, "fsdp", None),
            P(None, "fsdp", None),
            P(None, "fsdp", "seq", None),
            P(("seq", "fsdp"), None),
            P(("seq", "fsdp")),
            P(("seq", "fsdp"), None),
            P(("seq", "fsdp")),
            P(("seq", "fsdp")),
            P(("seq", "fsdp")),
            P(("seq", "fsdp"), None),
            P(("seq", "fsdp")),
            P(("seq", "fsdp"), None),
            P(("seq", "fsdp")),
            P(("seq", "fsdp")),
            P(("seq", "fsdp")),
        ),
        out_specs=(
            P(None, "fsdp", "seq", None),
            P(None, "fsdp", "seq", None),
            P(("seq", "fsdp"), None),
            P(("seq", "fsdp")),
            P(("seq", "fsdp"), None),
            P(("seq", "fsdp")),
            P(("seq", "fsdp")),
            P(("seq", "fsdp")),
            P(("seq", "fsdp"), None),
            P(("seq", "fsdp")),
            P(("seq", "fsdp"), None),
            P(("seq", "fsdp")),
            P(("seq", "fsdp")),
            P(("seq", "fsdp")),
        ),
        check_vma=False,
    )
```

profile of v0, /device:TPU:0, one launch (start us, length us, event | category | flops | bytes accessed | tf_op | source)
XLA Modules:
  0.0 1398.0 jit_solution(833404627021934972)
XLA Ops:
  16.5 42.5 %all-reduce.17 = (bf16[2304]{0:T(1024)(128)(2,1)S(1)}, bf16[768]{0:T(1024)(128)(2,1)S(1)}, bf16[768]{0:T(1024)(128)(2,1)S(1)}, bf16[768]{0:T(1024)(128)(2,1)S(1)...) all-reduce(bf16[2304]{0:T(1024)(128)(2,1)S(1)} %dynamic-update-slic, ...), channel_id=1, replica_groups=mesh['seq'=2,'fsdp'=16] {'seq','fsdp'}, use_global_device_ids=true, to_apply=%add | all-reduce | flops 9984 | bytes 39936
  71.7 7.1 gather_fusion
  78.9 7.1 gather_fusion.3
  115.2 8.3 subtract_convert_fusion.7
  146.7 13.9 copy.129
  160.6 11.8 gather_fusion.1
  172.4 9.5 fusion.160
  184.3 58.0 %while.56 = (s32[]{:T(128)}, bf16[6,1280,64]{1,2,0:T(8,128)(2,1)S(1)}, f32[6,1280]{1,0:T(8,128)S(1)}, s32[6]{0:T(128)S(1)}, bf16[1280,384]{1,0:T(8,128)(2,1)S(1)...) while((s32[]{:T(128)}, ...), condition=%wide.region_6.7_spmd.clone, body=%wide.region_3.6_spmd.clone.sunk | while | flops 434174720 | bytes 47271632 | solution.py:93
  270.9 8.3 subtract_convert_fusion.5
  302.4 13.9 copy.138
  316.3 11.8 gather_fusion.4
  328.1 9.5 fusion.161
  339.9 57.2 %while.57 = (s32[]{:T(128)}, bf16[6,1280,64]{1,2,0:T(8,128)(2,1)S(1)}, f32[6,1280]{1,0:T(8,128)S(1)}, s32[6]{0:T(128)S(1)}, bf16[1280,384]{1,0:T(8,128)(2,1)S(1)...) while((s32[]{:T(128)}, ...), condition=%wide.region_17.18_spmd.clone, body=%wide.region_14.17_spmd.clone.sunk | while | flops 434174720 | bytes 47271632 | solution.py:93
  424.5 42.2 %multiply_convert_fusion.3 = (bf16[640,3072]{1,0:T(8,128)(2,1)}, f32[640,3072]{1,0:T(8,128)}, bf16[640,3072]{1,0:T(8,128)(2,1)}, f32[640,3072]{1,0:T(8,128)}, f32[640,3072]{1,0:T(8,128)}) fusion(f32[3072]{0:T(1024)S(1)} %copy-done.97, f32[640,3072]{1,0:T(8,128)S(1)} %fusion.140, bf16[768,3072]{1,0:T(8,128)(2,1)S(1)} %copy-done.106, ...), kind=kOutput, calls=%fused_computation.125 | convolution fusion | flops 3281879040 | bytes 46029824 | tf_op jit(solution)/shard_map/dot_general | solution.py:246
  466.7 7.6 fusion.166
  492.5 21.8 %convert_reduce_fusion.1 = (f32[3072]{0:T(1024)}, bf16[640,3072]{1,0:T(8,128)(2,1)}, f32[3072]{0:T(1024)}, bf16[640,3072]{1,0:T(8,128)(2,1)}) fusion(f32[640,3072]{1,0:T(8,128)} %get-tuple-element.523, f32[640,3072]{1,0:T(8,128)} %get-tuple-element.602, f32[3072]{0:T(1024)S(1)} %copy-done.97, f32[640,3072]{1,0:T(8,128)} %fusion.167, ...), kind=kOutput, calls=%fused_computation.109 | convolution fusion | flops 3086739456 | bytes 52924416 | tf_op jit(solution)/shard_map/dot_general | solution.py:56
  514.3 7.5 add_add_fusion.8
  549.6 134.1 %while.58 = (s32[]{:T(128)}, f32[6,1280,64]{1,2,0:T(8,128)}, f32[6,1280,64]{1,2,0:T(8,128)}, bf16[6,1280,64]{1,2,0:T(8,128)(2,1)}, s32[6]{0:T(128)S(1)}, /*index...) while((s32[]{:T(128)}, f32[6,1280,64]{1,2,0:T(8,128)}, ...), condition=%wide.region_28.29_spmd.clone, body=%wide.region_26.28_spmd.clone.sunk | while | flops 1065122560 | bytes 80002912 | solution.py:117
  689.7 8.2 subtract_convert_fusion.3
  718.2 9.1 pad_maximum_fusion
  727.3 11.9 gather_fusion.7
  757.7 133.6 %while.59 = (s32[]{:T(128)}, f32[6,1280,64]{1,2,0:T(8,128)}, f32[6,1280,64]{1,2,0:T(8,128)}, bf16[6,1280,64]{1,2,0:T(8,128)(2,1)}, s32[6]{0:T(128)S(1)}, /*index...) while((s32[]{:T(128)}, f32[6,1280,64]{1,2,0:T(8,128)}, ...), condition=%wide.region_35.36_spmd.clone, body=%wide.region_33.35_spmd.clone.sunk | while | flops 1065122560 | bytes 80002912 | solution.py:117
  897.3 8.4 subtract_convert_fusion.1
  926.0 9.2 pad_maximum_fusion.1
  935.2 12.0 gather_fusion.9
  978.5 8.0 copy.161
  1000.7 7.2 fusion.142
  1008.0 7.1 convolution_add_fusion.3
  1018.4 43.0 %all-reduce.16 = (f32[2304]{0:T(1024)S(1)}, f32[768]{0:T(1024)S(1)}, f32[768]{0:T(1024)S(1)}, f32[768]{0:T(1024)S(1)}, f32[3072]{0:T(1024)S(1)}, /*index=5*/f32[...) all-reduce(f32[2304]{0:T(1024)S(1)} %add.402, ...), channel_id=3, replica_groups=mesh['seq'=2,'fsdp'=16] {'seq','fsdp'}, use_global_device_ids=true, to_apply=%region_39.40.clone | all-reduce | flops 9984 | bytes 79872
  1078.7 28.7 %reduce-scatter.13.cloned.1.call-done = f32[24,2304]{1,0:T(8,128)} async-done(((f32[768,2304]{1,0:T(8,128)}), f32[24,2304]{1,0:T(8,128)}) %reduce-scatter.13.cloned.1.call-update) | async-done | bytes 221200
  1107.5 141.6 %reduce-scatter.11.cloned.1.call-done = f32[96,768]{1,0:T(8,128)} async-done(((f32[3072,768]{1,0:T(8,128)}), f32[96,768]{1,0:T(8,128)}) %reduce-scatter.11.cloned.1.call-update) | async-done | bytes 294928 | tf_op jit(solution)/shard_map/reduce_scatter | solution.py:344
  1249.1 141.6 %reduce-scatter.9.cloned.1.call-done = f32[24,3072]{1,0:T(8,128)} async-done(((f32[768,3072]{1,0:T(8,128)}), f32[24,3072]{1,0:T(8,128)}) %reduce-scatter.9.cloned.1.call-update) | async-done | bytes 294928 | tf_op jit(solution)/shard_map/reduce_scatter | solution.py:344
  (782 shorter events, 682.1 us)
Async XLA Ops:
  7.2 85.1 %all-gather.5.cloned.1.call-start = ((), (), s32[]{:S(2)}) async-start(), calls=%async_computation.12 | async-start | bytes 3649536 | tf_op jit(solution)/shard_map/all_gather | solution.py:170
  7.9 248.9 %all-gather.7.cloned.1.call-start = ((), (), s32[]{:S(2)}) async-start(), calls=%async_computation.13 | async-start | bytes 1216512 | tf_op jit(solution)/shard_map/all_gather | solution.py:172
  8.7 406.5 %all-gather.9.cloned.1.call-start = ((), (), s32[]{:S(2)}) async-start(), calls=%async_computation.14 | async-start | bytes 4866048 | tf_op jit(solution)/shard_map/all_gather | solution.py:176
  9.4 457.3 %all-gather.11.cloned.1.call-start = ((), (), s32[]{:S(2)}) async-start(), calls=%async_computation.15 | async-start | bytes 4866048 | tf_op jit(solution)/shard_map/all_gather | solution.py:178
  10.0 1068.8 %reduce-scatter.7.cloned.1.call-start = ((), (), s32[]{:S(2)}) async-start(), calls=%async_computation.16 | async-start | bytes 2433024 | tf_op jit(solution)/shard_map/reduce_scatter | solution.py:344
  10.2 68.6 %copy-start.3 = (bf16[6,1280,64]{1,2,0:T(8,128)(2,1)}, bf16[6,1280,64]{1,2,0:T(8,128)(2,1)S(1)}, u32[]{:S(2)}) copy-start(bf16[6,1280,64]{1,2,0:T(8,128)(2,1)S(1)} %fusion.162) | copy-start | bytes 2949124
  10.2 49.5 %copy-start.100 = (s32[2,1,1280]{2,1,0:T(1,128)S(1)}, s32[2,1,1280]{2,1,0:T(1,128)}, u32[]{:S(2)}) copy-start(s32[2,1,1280]{2,1,0:T(1,128)} %param.25) | copy-start | bytes 30724
  65.0 178.9 %copy-start.69 = (s32[2048]{0:T(1024)}, s32[2048]{0:T(1024)S(1)}, u32[]{:S(2)}) copy-start(s32[2048]{0:T(1024)S(1)} %pad_clamp_fusion.3) | copy-start | bytes 24580
  66.2 94.4 %copy-start.77 = (s32[2048]{0:T(1024)}, s32[2048]{0:T(1024)S(1)}, u32[]{:S(2)}) copy-start(s32[2048]{0:T(1024)S(1)} %get-tuple-element.611) | copy-start | bytes 24580
  78.9 13.4 copy-start.59
  260.0 268.7 %copy-start.62 = (f32[640]{0:T(1024)}, f32[640]{0:T(1024)S(1)}, u32[]{:S(2)}) copy-start(f32[640]{0:T(1024)S(1)} %broadcast_multiply_fusion.3) | copy-start | bytes 7684
  262.2 266.5 %copy-start.64 = (f32[640]{0:T(1024)}, f32[640]{0:T(1024)S(1)}, u32[]{:S(2)}) copy-start(f32[640]{0:T(1024)S(1)} %fusion.135) | copy-start | bytes 7684
  302.4 13.9 copy-start.75
  339.9 58.9 %copy-start.67 = (s32[2048]{0:T(1024)S(1)}, s32[2048]{0:T(1024)}, u32[]{:S(2)}) copy-start(s32[2048]{0:T(1024)} %copy-done.66) | copy-start | bytes 24580
  413.9 114.9 %copy-start.73 = (f32[640]{0:T(1024)}, f32[640]{0:T(1024)S(1)}, u32[]{:S(2)}) copy-start(f32[640]{0:T(1024)S(1)} %broadcast_multiply_fusion.1) | copy-start | bytes 7684
  415.1 113.6 %copy-start.79 = (f32[640]{0:T(1024)}, f32[640]{0:T(1024)S(1)}, u32[]{:S(2)}) copy-start(f32[640]{0:T(1024)S(1)} %fusion.137) | copy-start | bytes 7684
  415.1 9.3 copy-start.18
  415.2 9.3 copy-start.97
  415.2 9.2 copy-start.106
  424.4 42.3 %copy-start.105 = (f32[768]{0:T(1024)S(1)}, f32[768]{0:T(1024)}, u32[]{:S(2)}) copy-start(f32[768]{0:T(1024)} %convert_element_type.192) | copy-start | bytes 9220
  466.7 8.0 copy-start.107
  466.7 8.0 copy-start.121
  718.2 9.1 copy-start.70
  727.3 11.9 copy-start.34
  727.3 11.9 copy-start.111
  744.9 202.2 %all-to-all-start.5 = ((bf16[1280,3,1,384]{3,1,2,0:T(4,128)(2,1)}), bf16[1280,3,1,384]{3,1,2,0:T(4,128)(2,1)}, u32[]{:S(2)}, u32[]{:S(2)}) async-start(bf16[1280,3,1,384]{3,1,2,0:T(4,128)(2,1)} %bitcast.337), calls=%async_computation.5 | async-start | bytes 7864320 | tf_op jit(solution)/shard_map/all_to_all | solution.py:318
  926.0 9.2 copy-start.68
  947.1 11.6 all-to-all-start.7
  952.6 154.8 %reduce-scatter.13.cloned.1.call-start = ((), (), s32[]{:S(2)}) async-start(), calls=%async_computation.19 | async-start | bytes 7299072
  986.6 262.5 %reduce-scatter.11.cloned.1.call-start = ((), (), s32[]{:S(2)}) async-start(), calls=%async_computation.18 | async-start | bytes 9732096 | tf_op jit(solution)/shard_map/reduce_scatter | solution.py:344
  1000.1 390.7 %reduce-scatter.9.cloned.1.call-start = ((), (), s32[]{:S(2)}) async-start(), calls=%async_computation.17 | async-start | bytes 9732096 | tf_op jit(solution)/shard_map/reduce_scatter | solution.py:344
  1017.3 48.7 %copy-start.94 = (f32[640]{0:T(1024)S(1)}, f32[640]{0:T(1024)}, u32[]{:S(2)}) copy-start(f32[640]{0:T(1024)} %copy-done.93) | copy-start | bytes 7684
  (154 other events, 627.3 us)
Sparse Core Ops, SparseCore 0:
  10.9 63.0 all-gather.4
  76.8 52.5 all-gather.6
  132.3 62.4 all-gather.8
  197.5 61.8 all-gather.10
  536.7 100.3 reduce-scatter.6
  986.7 120.7 reduce-scatter.12
  1113.9 135.1 reduce-scatter.10
  1255.6 135.0 reduce-scatter.8
where the time goes:
time: 1410 us; the launch traced here: 1400 us
  matrix products  436 us (31%)
  local copies, waits for them, and re-layouts  327 us (23%)
  waiting for transfers between devices  315 us (22%)
  other arithmetic  134 us (10%)
  blocking collectives  117 us (8%)
  loops' own time  40.4 us (3%)
  between operations  16.7 us (1%)
    reduce_scatter x3, waiting for transfers between devices, on_device(): lax.psum_scatter(totals, ('seq', 'fsdp'), scatter_dimension=0, tiled=True)  283 us
    dot_general x44, matrix products, right_dot(): lax.dot_general(left, right, (((1,), (1,)), ((), ())), preferred_element_...  183 us
    dot_general x32, matrix products, left_dot(): lax.dot_general(left, right, (((0,), (0,)), ((), ())), preferred_element_...  112 us
    unnamed x2, blocking collectives  85.5 us
    dot_general x12, matrix products, one_head(): jnp.dot(probs, head_slice(values_all, head_index, head_size), preferred_e...  50.5 us
    dot_general x2, matrix products, on_device(): jnp.dot(first_low, full_up, preferred_element_type=jnp.float32)  48.2 us
    unnamed x271, local copies, waits for them, and re-layouts  37 us
    another operation x8, other arithmetic  33.9 us
  transfers between devices with their start and end apart: 10, of which 3 were waited for; matrix products, arithmetic and copies ran while one was open for 57% of the time, Pallas kernels for 0%

commit v1 on v0

v1 whole, which is shorter than its diff:
```python
import functools
import math

import jax
import jax.numpy as jnp
from jax import lax
from jax.experimental import pallas as pl
from jax.experimental.pallas import tpu as pltpu
from jax.sharding import PartitionSpec as P

HEAD = 64
PAIR = 2 * HEAD
SEG_COUNT = 4
LOG2E = math.log2(math.e)
LN2 = math.log(2.0)
FAR = float(2**30)
BF = jnp.bfloat16
F32 = jnp.float32


def dot(left, right):
    return jnp.dot(left, right, preferred_element_type=F32)


def dot_rt(left, right):
    return lax.dot_general(left, right, (((1,), (1,)), ((), ())), preferred_element_type=F32)


def dot_lt(left, right):
    return lax.dot_general(left, right, (((0,), (0,)), ((), ())), preferred_element_type=F32)


def pair_swap(values):
    lanes = lax.broadcasted_iota(jnp.int32, values.shape, 1)
    width = values.shape[1]
    return jnp.where(
        lanes % 2 == 0, pltpu.roll(values, width - 1, 1), pltpu.roll(values, 1, 1)
    )


def project_body(block, share, idx_ref, own_ref, other_ref, wq_ref, wk_ref, wv_ref, bias_ref,
                 cos_ref, sin_ref, xw_ref, q_ref, k_ref, v_ref):
    half = own_ref.shape[0]

    def step(i, carry):
        rows = pl.ds(pl.multiple_of(i * block, block), block)
        picks = lax.broadcasted_iota(jnp.int32, (block, half), 1)
        where_from = idx_ref[rows, :]
        near = (picks == where_from).astype(BF)
        away = (picks + half == where_from).astype(BF)
        work = (dot(near, own_ref[...]) + dot(away, other_ref[...])).astype(BF)
        xw_ref[rows, :] = work
        cosine, sine = cos_ref[rows, :], sin_ref[rows, :]
        for w_ref, out_ref, place, scale in (
            (wq_ref, q_ref, 0, LOG2E / math.sqrt(HEAD)),
            (wk_ref, k_ref, 1, 1.0),
        ):
            pre = dot(work, w_ref[...]) + bias_ref[:, place * share:(place + 1) * share]
            for j in range(share // PAIR):
                cols = slice(j * PAIR, (j + 1) * PAIR)
                part = pre[:, cols]
                out_ref[rows, cols] = (
                    (part * cosine + pair_swap(part) * sine) * scale
                ).astype(BF)
        v_ref[rows, :] = (dot(work, wv_ref[...]) + bias_ref[:, 2 * share:]).astype(BF)
        return carry

    lax.fori_loop(0, idx_ref.shape[0] // block, step, 0)


def project(idx_col, own, other, w_qkv, bias_own, cosine, sine, part, block=256):
    rows = idx_col.shape[0]
    width = own.shape[1]
    share = bias_own.shape[1] // 3
    parts = w_qkv.shape[1] // (3 * share)
    whole = lambda shape: pl.BlockSpec(shape, lambda g, p: (0,) * len(shape))
    return pl.pallas_call(
        lambda part_ref, *refs: project_body(block, share, *refs),
        grid_spec=pltpu.PrefetchScalarGridSpec(
            num_scalar_prefetch=1,
            grid=(1,),
            in_specs=[
                whole((rows, 1)),
                whole(own.shape),
                whole(other.shape),
                pl.BlockSpec((width, share), lambda g, p: (0, p[0])),
                pl.BlockSpec((width, share), lambda g, p: (0, parts + p[0])),
                pl.BlockSpec((width, share), lambda g, p: (0, 2 * parts + p[0])),
                whole(bias_own.shape),
                whole(cosine.shape),
                whole(sine.shape),
            ],
            out_specs=[whole((rows, width))] + [whole((rows, share))] * 3,
        ),
        out_shape=[jax.ShapeDtypeStruct((rows, width), BF)]
        + [jax.ShapeDtypeStruct((rows, share), BF)] * 3,
        compiler_params=pltpu.CompilerParams(vmem_limit_bytes=60 << 20),
        cost_estimate=pl.CostEstimate(
            flops=2 * rows * width * (rows + 3 * share),
            bytes_accessed=2 * (2 * rows * width + 3 * width * share + 3 * rows * share),
            transcendentals=0,
        ),
        name="project",
    )(part, idx_col, own, other, w_qkv, w_qkv, w_qkv, bias_own, cosine, sine)


def attend_body(block, idx_ref, q_ref, k_ref, v_ref, seg_col_ref, seg_row_ref,
                near_ref, away_ref, ctxt_ref, lse_ref, pick, ka, vt, qt, augt):
    rows = q_ref.shape[0]
    half = near_ref.shape[0]

    @pl.when(pl.program_id(0) == 0)
    def _():
        def fill(i, carry):
            span = pl.ds(pl.multiple_of(i * block, block), block)
            pick[span, :] = (
                lax.broadcasted_iota(jnp.int32, (block, rows), 1) == idx_ref[span, :]
            ).astype(BF)
            return carry

        lax.fori_loop(0, rows // block, fill, 0)
        lanes = lax.broadcasted_iota(jnp.int32, (rows, PAIR), 1)
        ka[:, PAIR:] = ((lanes == seg_col_ref[...]) | (lanes >= SEG_COUNT)).astype(BF)
        places = lax.broadcasted_iota(jnp.int32, (PAIR, rows), 0)
        augt[...] = jnp.where(
            (places < SEG_COUNT) & (places != seg_row_ref[...]), -FAR, 0.0
        ).astype(BF)

    ka[:, :PAIR] = k_ref[...]
    vt[...] = v_ref[...].T
    qt[...] = q_ref[...].T
    empty = jnp.zeros((HEAD, block), BF)

    def step(i, carry):
        span = pl.ds(pl.multiple_of(i * block, block), block)
        extra = augt[:, span]
        for h in range(2):
            mine = qt[h * HEAD:(h + 1) * HEAD, span]
            mixed = jnp.concatenate([mine, empty, extra] if h == 0 else [empty, mine, extra], axis=0)
            scores = dot(ka[...], mixed)
            top = jnp.max(scores, axis=0, keepdims=True)
            expo = jnp.exp2(scores - top)
            total = jnp.sum(expo, axis=0, keepdims=True)
            context = dot(vt[h * HEAD:(h + 1) * HEAD, :], expo.astype(BF))
            ctxt_ref[h * HEAD:(h + 1) * HEAD, span] = (context / total).astype(BF)
            lse_ref[0, h:h + 1, span] = top + jnp.log2(total)
        return carry

    lax.fori_loop(0, rows // block, step, 0)
    given = dot(ctxt_ref[...], pick[...]).astype(BF)
    near_ref[...] = given[:, :half].T
    away_ref[...] = given[:, half:].T


def attend(idx_col, q, k, v, seg_col, seg_row, block=256):
    rows, share = q.shape
    pairs = share // PAIR
    half = rows // 2
    whole = lambda shape: pl.BlockSpec(shape, lambda j: (0,) * len(shape))
    column = lambda n: pl.BlockSpec((n, PAIR), lambda j: (0, j))
    return pl.pallas_call(
        functools.partial(attend_body, block),
        grid=(pairs,),
        in_specs=[whole((rows, 1)), column(rows), column(rows), column(rows),
                  whole((rows, 1)), whole((1, rows))],
        out_specs=[column(half), column(half), pl.BlockSpec((PAIR, rows), lambda j: (j, 0)),
                   pl.BlockSpec((1, 8, rows), lambda j: (j, 0, 0))],
        out_shape=[jax.ShapeDtypeStruct((half, share), BF), jax.ShapeDtypeStruct((half, share), BF),
                   jax.ShapeDtypeStruct((share, rows), BF),
                   jax.ShapeDtypeStruct((pairs, 8, rows), F32)],
        scratch_shapes=[pltpu.VMEM((rows, rows), BF), pltpu.VMEM((rows, 2 * PAIR), BF),
                        pltpu.VMEM((PAIR, rows), BF), pltpu.VMEM((PAIR, rows), BF),
                        pltpu.VMEM((PAIR, rows), BF)],
        compiler_params=pltpu.CompilerParams(vmem_limit_bytes=60 << 20),
        cost_estimate=pl.CostEstimate(
            flops=pairs * 2 * 2 * rows * rows * 3 * PAIR, bytes_accessed=2 * 6 * rows * share,
            transcendentals=2 * pairs * rows * rows,
        ),
        name="attend",
    )(idx_col, q, k, v, seg_col, seg_row)


def attend_back_body(block, idx_ref, q_ref, k_ref, v_ref, seg_col_ref, seg_row_ref, lse_ref,
                     ctxt_ref, gnear_ref, gaway_ref, cos_ref, sin_ref,
                     dq_ref, dk_ref, dv_ref,
                     pick, ka, va, kt, qt, dt, go, delta, dkacc, dvacc, dqt, augt):
    rows = q_ref.shape[0]
    half = gnear_ref.shape[0]

    @pl.when(pl.program_id(0) == 0)
    def _():
        def fill(i, carry):
            span = pl.ds(pl.multiple_of(i * block, block), block)
            pick[span, :] = (
                lax.broadcasted_iota(jnp.int32, (block, rows), 1) == idx_ref[span, :]
            ).astype(BF)
            return carry

        lax.fori_loop(0, rows // block, fill, 0)
        lanes = lax.broadcasted_iota(jnp.int32, (rows, PAIR), 1)
        ones = ((lanes == seg_col_ref[...]) | (lanes >= SEG_COUNT)).astype(BF)
        ka[:, PAIR:] = ones
        va[:, PAIR:] = jnp.ones((rows, PAIR), BF)
        places = lax.broadcasted_iota(jnp.int32, (8, rows), 0)
        augt[...] = jnp.where(
            (places < SEG_COUNT) & (places != seg_row_ref[...]), -FAR, 0.0
        )

    ka[:, :PAIR] = k_ref[...]
    va[:, :PAIR] = v_ref[...]
    kt[...] = k_ref[...].T
    qt[...] = q_ref[...].T
    grad = dot(pick[:, :half], gnear_ref[...]) + dot(pick[:, half:], gaway_ref[...])
    go[...] = grad.astype(BF)
    dt[...] = go[...].T
    weighed = dt[...].astype(F32) * ctxt_ref[...].astype(F32)
    delta[0:1, :] = jnp.sum(weighed[:HEAD], axis=0, keepdims=True)
    delta[1:2, :] = jnp.sum(weighed[HEAD:], axis=0, keepdims=True)
    dkacc[...] = jnp.zeros_like(dkacc)
    dvacc[...] = jnp.zeros_like(dvacc)
    empty = jnp.zeros((HEAD, block), BF)
    blank = jnp.zeros((PAIR - 16, block), BF)
    wide = lax.broadcasted_iota(jnp.int32, (block, PAIR), 1)
    zero = jnp.zeros((block, PAIR), BF)

    def thirds(row, start):
        first = row.astype(BF).astype(F32)
        second = (row - first).astype(BF).astype(F32)
        third = row - first - second
        places = lax.broadcasted_iota(jnp.int32, (16, block), 0)
        return jnp.where(places == start, first,
                         jnp.where(places == start + 1, second,
                                   jnp.where(places == start + 2, third, 0.0)))

    def step(i, carry):
        span = pl.ds(pl.multiple_of(i * block, block), block)
        base = jnp.concatenate([augt[:, span], jnp.zeros((8, block), F32)], axis=0)
        for h in range(2):
            part = slice(h * HEAD, (h + 1) * HEAD)
            low = (base + thirds(-lse_ref[0, h:h + 1, span], SEG_COUNT)).astype(BF)
            mine = qt[part, span]
            order = (mine, empty) if h == 0 else (empty, mine)
            scores = dot(ka[...], jnp.concatenate(order + (low, blank), axis=0))
            probs = jnp.exp2(scores)
            low = thirds(-delta[h:h + 1, span], 0).astype(BF)
            mine = dt[part, span]
            order = (mine, empty) if h == 0 else (empty, mine)
            slope = dot(va[...], jnp.concatenate(order + (low, blank), axis=0))
            grads = (probs * slope).astype(BF)
            keep = wide < HEAD if h == 0 else wide >= HEAD
            dvacc[...] += dot(probs.astype(BF), jnp.where(keep, go[span, :], zero))
            dkacc[...] += dot(grads, jnp.where(keep, q_ref[span, :], zero))
            dqt[part, span] = dot(kt[part, :], grads)
        return carry

    lax.fori_loop(0, rows // block, step, 0)
    cosine, sine = cos_ref[...], sin_ref[...]
    turned = dqt[...].T
    dq_ref[...] = ((turned * cosine - pair_swap(turned) * sine) * (1.0 / math.sqrt(HEAD))).astype(BF)
    turned = dkacc[...]
    dk_ref[...] = ((turned * cosine - pair_swap(turned) * sine) * LN2).astype(BF)
    dv_ref[...] = dvacc[...].astype(BF)


def attend_back(idx_col, q, k, v, seg_col, seg_row, lse, ctxt, gnear, gaway, cosine, sine, block=256):
    rows, share = q.shape
    pairs = share // PAIR
    half = rows // 2
    whole = lambda shape: pl.BlockSpec(shape, lambda j: (0,) * len(shape))
    column = lambda n: pl.BlockSpec((n, PAIR), lambda j: (0, j))
    return pl.pallas_call(
        functools.partial(attend_back_body, block),
        grid=(pairs,),
        in_specs=[whole((rows, 1)), column(rows), column(rows), column(rows),
                  whole((rows, 1)), whole((1, rows)),
                  pl.BlockSpec((1, 8, rows), lambda j: (j, 0, 0)),
                  pl.BlockSpec((PAIR, rows), lambda j: (j, 0)),
                  column(half), column(half), whole(cosine.shape), whole(sine.shape)],
        out_specs=[column(rows)] * 3,
        out_shape=[jax.ShapeDtypeStruct((rows, share), BF)] * 3,
        scratch_shapes=[pltpu.VMEM((rows, rows), BF), pltpu.VMEM((rows, 2 * PAIR), BF),
                        pltpu.VMEM((rows, 2 * PAIR), BF), pltpu.VMEM((PAIR, rows), BF),
                        pltpu.VMEM((PAIR, rows), BF), pltpu.VMEM((PAIR, rows), BF),
                        pltpu.VMEM((rows, PAIR), BF), pltpu.VMEM((8, rows), F32),
                        pltpu.VMEM((rows, PAIR), F32), pltpu.VMEM((rows, PAIR), F32),
                        pltpu.VMEM((PAIR, rows), F32), pltpu.VMEM((8, rows), F32)],
        compiler_params=pltpu.CompilerParams(vmem_limit_bytes=60 << 20),
        cost_estimate=pl.CostEstimate(
            flops=pairs * 2 * 2 * rows * rows * 7 * PAIR, bytes_accessed=2 * 9 * rows * share,
            transcendentals=2 * pairs * rows * rows,
        ),
        name="attend_back",
    )(idx_col, q, k, v, seg_col, seg_row, lse, ctxt, gnear, gaway, cosine, sine)


def project_back_body(block, rows, xw_ref, dq_ref, dk_ref, dv_ref, row_ref, wq_ref, wk_ref, wv_ref,
                      near_ref, away_ref, gw_ref, gb_ref, work):
    half = near_ref.shape[1]
    share = dq_ref.shape[2]
    batch = pl.program_id(0)

    @pl.when(batch == 0)
    def _():
        gw_ref[...] = jnp.zeros_like(gw_ref)
        gb_ref[...] = jnp.zeros_like(gb_ref)

    def step(i, carry):
        span = pl.ds(pl.multiple_of(i * block, block), block)
        total = None
        for place, (g_ref, w_ref) in enumerate(((dq_ref, wq_ref), (dk_ref, wk_ref), (dv_ref, wv_ref))):
            piece = g_ref[0, span, :]
            cols = slice(place * share, (place + 1) * share)
            gb_ref[0:1, cols] += jnp.sum(piece.astype(F32), axis=0, keepdims=True)
            term = dot_rt(piece, w_ref[...])
            total = term if total is None else total + term
        work[span, :] = total.astype(BF)
        return carry

    lax.fori_loop(0, rows // block, step, 0)
    for place, g_ref in enumerate((dq_ref, dk_ref, dv_ref)):
        cols = slice(place * share, (place + 1) * share)
        gw_ref[:, cols] += dot_lt(xw_ref[0], g_ref[0])
    small = block // 2

    def back(i, carry):
        span = pl.ds(pl.multiple_of(i * small, small), small)
        for base, out_ref in ((0, near_ref), (half, away_ref)):
            pick = (lax.broadcasted_iota(jnp.int32, (small, rows), 0) + (base + i * small) == row_ref[0]).astype(BF)
            out_ref[0, span, :] = dot(pick, work[...]).astype(BF)
        return carry

    lax.fori_loop(0, half // small, back, 0)


def project_back(xw, dq, dk, dv, idx_row, w_qkv, part, block=256):
    batches, rows, width = xw.shape
    share = dq.shape[2]
    parts = w_qkv.shape[1] // (3 * share)
    half = rows // 2
    each = lambda shape: pl.BlockSpec((1,) + shape, lambda b, p: (b,) + (0,) * len(shape))
    fixed = lambda shape: pl.BlockSpec(shape, lambda b, p: (0,) * len(shape))
    return pl.pallas_call(
        lambda part_ref, *refs: project_back_body(block, rows, *refs),
        grid_spec=pltpu.PrefetchScalarGridSpec(
            num_scalar_prefetch=1,
            grid=(batches,),
            in_specs=[each((rows, width)), each((rows, share)), each((rows, share)), each((rows, share)),
                      each((1, rows)),
                      pl.BlockSpec((width, share), lambda b, p: (0, p[0])),
                      pl.BlockSpec((width, share), lambda b, p: (0, parts + p[0])),
                      pl.BlockSpec((width, share), lambda b, p: (0, 2 * parts + p[0]))],
            out_specs=[each((half, width)), each((half, width)), fixed((width, 3 * share)),
                       fixed((8, 3 * share))],
            scratch_shapes=[pltpu.VMEM((rows, width), BF)],
        ),
        out_shape=[jax.ShapeDtypeStruct((batches, half, width), BF),
                   jax.ShapeDtypeStruct((batches, half, width), BF),
                   jax.ShapeDtypeStruct((width, 3 * share), F32),
                   jax.ShapeDtypeStruct((8, 3 * share), F32)],
        compiler_params=pltpu.CompilerParams(vmem_limit_bytes=60 << 20),
        cost_estimate=pl.CostEstimate(
            flops=2 * batches * rows * width * (rows + 6 * share),
            bytes_accessed=2 * batches * rows * (2 * width + 3 * share) + 12 * width * share,
            transcendentals=0,
        ),
        name="project_back",
    )(part, xw, dq, dk, dv, idx_row, w_qkv, w_qkv, w_qkv)


EPS = 1e-6
ERF_SCALE = 0.3275911


def gauss_parts(u):
    return jax.nn.gelu(u, approximate=False), 0.5 * (1.0 + lax.erf(u * math.sqrt(0.5))) + u * jnp.exp(
        -0.5 * u * u
    ) * (1.0 / math.sqrt(2.0 * math.pi))


def positions(segments):
    places = jnp.arange(segments.shape[0], dtype=jnp.int32)
    counts = jnp.sum(
        segments[None, :] < segments[:, None], axis=1, dtype=jnp.int32
    )
    return (places - counts).astype(F32)


def turn_tables(segments):
    halves = HEAD // 2
    freqs = jnp.exp(jnp.arange(halves, dtype=F32) * (-2.0 * math.log(10000.0) / HEAD))
    phase = positions(segments)[:, None] * freqs[None, :]
    cosine = jnp.tile(jnp.repeat(jnp.cos(phase), 2, axis=1), (1, 2))
    signs = jnp.tile(jnp.array([-1.0, 1.0], F32), halves)[None, :]
    sine = jnp.tile(jnp.repeat(jnp.sin(phase), 2, axis=1) * signs, (1, 2))
    return cosine, sine


def standard(hidden):
    centre = hidden - jnp.mean(hidden, axis=-1, keepdims=True)
    root = lax.rsqrt(jnp.mean(centre * centre, axis=-1, keepdims=True) + EPS)
    return centre * root, root


def standard_back(grad, norm, root):
    return root * (
        grad
        - jnp.mean(grad, axis=-1, keepdims=True)
        - norm * jnp.mean(grad * norm, axis=-1, keepdims=True)
    )


def swap_cores(value):
    return lax.ppermute(value, "seq", [(0, 1), (1, 0)])


def on_device(tokens, permutation, segment_ids, cotangent, *shards):
    batches = tokens.shape[0]
    half, width = tokens.shape[2], tokens.shape[3]
    core = lax.axis_index("seq")
    rows = 2 * half
    share = width // 2
    owners = 2 * lax.axis_size("fsdp")
    both = ("seq", "fsdp")
    gather = lambda value: lax.all_gather(value, both, axis=0, tiled=True)
    thin = [i for i, piece in enumerate(shards) if piece.ndim == 1]
    sizes = [shards[i].shape[0] for i in thin]
    count = sum(sizes)
    room = -(-count // 128) * 128
    packed = jnp.concatenate([shards[i] for i in thin] + [jnp.zeros((room - count,), BF)])
    w_qkv = gather(shards[0])
    vectors = gather(packed.reshape(1, room)).astype(F32)
    w_out = gather(shards[2])
    w_up = gather(shards[6])
    w_down = gather(shards[8])
    spread, at = [], 0
    for size in sizes:
        spread.append(vectors[:, at:at + size].reshape(1, owners * size))
        at += size
    b_qkv, b_out, gain_one, shift_one, b_up, b_down, gain_two, shift_two = spread
    bias_own = jnp.concatenate(
        [lax.dynamic_slice_in_dim(b_qkv, core * share + s * width, share, 1) for s in range(3)], axis=1
    )
    part = jnp.full((1,), core, jnp.int32)
    away_tokens = swap_cores(tokens[:, 0])
    kept = []
    for b in range(batches):
        order = permutation[b, 0]
        owner_half = order // half
        place = jnp.where(owner_half == core, order - core * half, order - (1 - core) * half + half)
        segments = segment_ids[b, 0]
        cosine, sine = turn_tables(segments)
        col, row = segments[:, None], segments[None, :]
        idx_col, idx_row = place[:, None], place[None, :]
        xw, q, k, v = project(idx_col, tokens[b, 0], away_tokens[b], w_qkv, bias_own, cosine, sine, part)
        near, away, ctxt, lse = attend(idx_col, q, k, v, col, row)
        kept.append((idx_col, idx_row, col, row, cosine, sine, xw, q, k, v, ctxt, lse, near, swap_cores(away)))
    near = jnp.concatenate([item[12] for item in kept], axis=0)
    away = jnp.concatenate([item[13] for item in kept], axis=0)
    context = jnp.concatenate(
        [jnp.where(core == 0, near, away), jnp.where(core == 0, away, near)], axis=1
    )
    own = tokens[:, 0].reshape(batches * half, width).astype(F32)
    norm_one, root_one = standard(own + dot(context, w_out) + b_out)
    first = norm_one * gain_one + shift_one
    first_low = first.astype(BF)
    active, slope = gauss_parts(dot(first_low, w_up) + b_up)
    active, slope = active.astype(BF), slope.astype(BF)
    norm_two, root_two = standard(first + dot(active, w_down) + b_down)
    outputs = (norm_two * gain_two + shift_two).astype(BF)
    grad_out = cotangent[:, 0].reshape(batches * half, width).astype(F32)
    g_gain_two = jnp.sum(grad_out * norm_two, axis=0)
    g_shift_two = jnp.sum(grad_out, axis=0)
    grad_two = standard_back(grad_out * gain_two, norm_two, root_two)
    low_two = grad_two.astype(BF)
    g_down = dot_lt(active, low_two)
    g_b_down = jnp.sum(low_two.astype(F32), axis=0)
    grad_up = (dot_rt(low_two, w_down) * slope.astype(F32)).astype(BF)
    g_up = dot_lt(first_low, grad_up)
    g_b_up = jnp.sum(grad_up.astype(F32), axis=0)
    grad_first = grad_two + dot_rt(grad_up, w_up)
    g_gain_one = jnp.sum(grad_first * norm_one, axis=0)
    g_shift_one = jnp.sum(grad_first, axis=0)
    grad_one = standard_back(grad_first * gain_one, norm_one, root_one)
    low_one = grad_one.astype(BF)
    g_out = dot_lt(context, low_one)
    g_b_out = jnp.sum(low_one.astype(F32), axis=0)
    grad_ctx = dot_rt(low_one, w_out).astype(BF)
    ctx_near = jnp.where(core == 0, grad_ctx[:, :share], grad_ctx[:, share:])
    ctx_away = swap_cores(jnp.where(core == 0, grad_ctx[:, share:], grad_ctx[:, :share]))
    scatter = lambda value, axes: lax.psum_scatter(value, axes, scatter_dimension=0, tiled=True)
    g_down = scatter(g_down.astype(BF), both).astype(F32)
    g_up = scatter(g_up.astype(BF), both).astype(F32)
    g_out = scatter(g_out.astype(BF), both).astype(F32)
    backs = []
    for b in range(batches):
        idx_col, idx_row, col, row, cosine, sine, xw, q, k, v, ctxt, lse = kept[b][:12]
        span = slice(b * half, (b + 1) * half)
        backs.append(
            attend_back(idx_col, q, k, v, col, row, lse, ctxt, ctx_near[span], ctx_away[span], cosine, sine)
        )
    stack = lambda pick: jnp.stack([pick(b) for b in range(batches)])
    near_grad, away_grad, gw_own, gb_own = project_back(
        stack(lambda b: kept[b][6]),
        stack(lambda b: backs[b][0]),
        stack(lambda b: backs[b][1]),
        stack(lambda b: backs[b][2]),
        stack(lambda b: kept[b][1]),
        w_qkv,
        part,
    )
    other = swap_cores(away_grad)
    token_grad = (
        grad_one.reshape(batches, half, width) + near_grad.astype(F32) + other.astype(F32)
    ).astype(BF)
    mine = lax.dynamic_slice_in_dim(gw_own, core * share, share, 0).astype(BF)
    theirs = swap_cores(lax.dynamic_slice_in_dim(gw_own, (1 - core) * share, share, 0).astype(BF))
    columns, thin_columns = [], []
    blank = jnp.zeros((share,), F32)
    for s in range(3):
        span = slice(s * share, (s + 1) * share)
        columns += [jnp.where(core == 0, mine[:, span], theirs[:, span]),
                    jnp.where(core == 0, theirs[:, span], mine[:, span])]
        thin_columns += [jnp.where(core == 0, gb_own[0, span], blank),
                         jnp.where(core == 0, blank, gb_own[0, span])]
    g_qkv = scatter(jnp.concatenate(columns, axis=1), "fsdp").astype(F32)
    thin_grads = [jnp.concatenate(thin_columns), g_b_out, g_gain_one, g_shift_one, g_b_up, g_b_down,
                  g_gain_two, g_shift_two]
    slab = jnp.concatenate(
        [value.reshape(owners, -1) for value in thin_grads]
        + [jnp.zeros((owners, 1024 - count), F32)], axis=1
    )
    slab = scatter(slab.reshape(owners * 8, 128), both).reshape(1024)
    thin_out, at = [], 0
    for size in sizes:
        thin_out.append(slab[at:at + size])
        at += size
    g_bqkv, g_bout, g_g1, g_s1, g_bup, g_bdown, g_g2, g_s2 = thin_out
    return (
        outputs.reshape(batches, 1, half, width), token_grad[:, None],
        g_qkv, g_bqkv, g_out, g_bout, g_g1, g_s1, g_up, g_bup, g_down, g_bdown, g_g2, g_s2,
    )


def solution(mesh):
    packs = P(None, "fsdp", "seq", None)
    ids = P(None, "fsdp", None)
    deep, flat = P(("seq", "fsdp"), None), P(("seq", "fsdp"))
    layers = (deep, flat, deep, flat, flat, flat, deep, flat, deep, flat, flat, flat)
    return jax.shard_map(
        on_device, mesh=mesh, in_specs=(packs, ids, ids, packs) + layers,
        out_specs=(packs, packs) + layers, check_vma=False,
    )
```

time: 1410 us -> 1040 us (0.74)
  matrix products: 436 us -> 119 us
  local copies, waits for them, and re-layouts: 327 us -> 52 us
  waiting for transfers between devices: 315 us -> 537 us
  Pallas kernels: 0 us -> 192 us
  other arithmetic: 134 us -> 41.6 us
  blocking collectives: 117 us -> 70.6 us
  loops' own time: 40.4 us -> 0 us
    dot_general x108 -> x9, matrix products: 436 us -> 119 us  [the longest x3 60.7 us: dot(): return jnp.dot(left, right, preferred_element_type=F32)]
    pallas_call x0 -> x7, Pallas kernels: none -> 192 us  [the longest x2 74.3 us: attend_back(): pl.pallas_call(functools.partial(attend_back_body, block), grid=(pairs,),...]
    reduce_scatter x3 -> x4, waiting for transfers between devices: 283 us -> 446 us  [on_device(): lax.psum_scatter(value, axes, scatter_dimension=0, tiled=True)]
    unnamed x2 -> x0, blocking collectives: 85.5 us -> none
    gather x10 -> x0, local copies, waits for them, and re-layouts: 77.9 us -> none  [the longest x2 23.9 us: on_device(): grad_projected_work[inverse].reshape(pack_rows, 3, 1, share)]
    all_gather x0 -> x1, blocking collectives: none -> 70.6 us  [on_device(): gather = lambda value: lax.all_gather(value, both, axis=0, tiled=True)]
    another operation x18 -> x5, other arithmetic: 77.9 us -> 10.3 us  [on_device(): stack = lambda pick: jnp.stack([pick(b) for b in range(batches)])]
    unnamed x9 -> x10, waiting for transfers between devices: 31.3 us -> 90.7 us
  transfers between devices with their start and end apart: 10 -> 15, of which waited for: 3 -> 6; matrix products, arithmetic and copies ran while one was open for 57% -> 14% of each run, Pallas kernels for 0% -> 9%
where the time goes in v1:
time: 1040 us; the launch traced here: 1030 us
  waiting for transfers between devices  537 us (52%)
  Pallas kernels  192 us (18%)
  matrix products  119 us (11%)
  blocking collectives  70.6 us (7%)
  local copies, waits for them, and re-layouts  52 us (5%)
  other arithmetic  41.6 us (4%)
  between operations  15 us (1%)
    reduce_scatter x4, waiting for transfers between devices, on_device(): lax.psum_scatter(value, axes, scatter_dimension=0, tiled=True)  446 us
    unnamed x10, waiting for transfers between devices  90.7 us
    pallas_call x2, Pallas kernels, attend_back(): pl.pallas_call(functools.partial(attend_back_body, block), grid=(pairs,),...  74.3 us
    all_gather x1, blocking collectives, on_device(): gather = lambda value: lax.all_gather(value, both, axis=0, tiled=True)  70.6 us
    pallas_call x2, Pallas kernels, attend(): pl.pallas_call(functools.partial(attend_body, block), grid=(pairs,), in_s...  63.8 us
    dot_general x3, matrix products, dot(): return jnp.dot(left, right, preferred_element_type=F32)  60.7 us
    dot_general x3, matrix products, dot_lt(): lax.dot_general(left, right, (((0,), (0,)), ((), ())), preferred_element_...  29.1 us
    dot_general x3, matrix products, dot_rt(): lax.dot_general(left, right, (((1,), (1,)), ((), ())), preferred_element_...  28.7 us
  transfers between devices with their start and end apart: 15, of which 6 were waited for; matrix products, arithmetic and copies ran while one was open for 14% of the time, Pallas kernels for 9%

profile of v1, /device:TPU:0, one launch (start us, length us, event | category | flops | bytes accessed | tf_op | source)
XLA Modules:
  0.0 1029.0 jit_solution(3420872503916544131)
XLA Ops:
  13.2 2.0 multiply_sine_fusion
  19.1 70.6 %all-gather.1 = bf16[32,1,384]{2,1,0:T(2,128)(2,1)S(1)} all-gather(bf16[1,1,384]{2,1,0:T(2,128)(2,1)S(1)} %reshape.440), channel_id=2, replica_groups=mesh['seq'=2,'fsdp'=16] {'seq','fsdp'}, dimensions={0}, use_global_device_ids=true | all-gather | bytes 25344 | tf_op jit(solution)/shard_map/all_gather | solution.py:424
  118.4 2.9 slice_bitcast_fusion.2
  122.7 2.9 slice_bitcast_fusion
  125.6 13.4 %project.2 = (bf16[1280,768]{1,0:T(8,128)(2,1)}, bf16[1280,384]{1,0:T(8,128)(2,1)}, bf16[1280,384]{1,0:T(8,128)(2,1)}, bf16[1280,384]{1,0:T(8,128)(2,1)}) custom-call(s32[1]{0:T(128)} %bitcast.5.part_ref, s32[1280,1]{1,0:T(8,128)} %get-tuple-element.208.refs_0_.idx_ref, bf16[640,768]{1,0:T(8,128)(2,1)} %get-tuple-element.156.refs_1_, ...), custom_call_target="tpu_custom_call" | custom-call | flops 4781506560 | bytes 8650752 | tf_op jit(solution)/shard_map/project/pallas_call | solution.py:77
  139.0 31.9 %attend.2 = (bf16[640,384]{1,0:T(8,128)(2,1)}, bf16[640,384]{1,0:T(8,128)(2,1)}, bf16[384,1280]{1,0:T(8,128)(2,1)}, f32[3,8,1280]{2,1,0:T(8,128)}) custom-call(s32[1280,1]{1,0:T(8,128)} %get-tuple-element.208.refs_0_.idx_ref, bf16[1280,384]{1,0:T(8,128)(2,1)} %get-tuple-element.40.q_ref, bf16[1280,384]{1,0:T(8,128)(2,1)} %get-tuple-element.41.k_ref, ...), custom_call_target="tpu_custom_call" | custom-call | flops 7549747200 | bytes 5898240 | tf_op jit(solution)/shard_map/attend/pallas_call | solution.py:161
  171.4 13.1 %project.3 = (bf16[1280,768]{1,0:T(8,128)(2,1)}, bf16[1280,384]{1,0:T(8,128)(2,1)}, bf16[1280,384]{1,0:T(8,128)(2,1)}, bf16[1280,384]{1,0:T(8,128)(2,1)}) custom-call(s32[1]{0:T(128)} %bitcast.5.part_ref, s32[1280,1]{1,0:T(8,128)} %get-tuple-element.207.refs_0_.idx_ref, bf16[640,768]{1,0:T(8,128)(2,1)} %get-tuple-element.155.refs_1_, ...), custom_call_target="tpu_custom_call" | custom-call | flops 4781506560 | bytes 8650752 | tf_op jit(solution)/shard_map/project/pallas_call | solution.py:77
  184.5 31.9 %attend.3 = (bf16[640,384]{1,0:T(8,128)(2,1)}, bf16[640,384]{1,0:T(8,128)(2,1)}, bf16[384,1280]{1,0:T(8,128)(2,1)}, f32[3,8,1280]{2,1,0:T(8,128)}) custom-call(s32[1280,1]{1,0:T(8,128)} %get-tuple-element.207.refs_0_.idx_ref, bf16[1280,384]{1,0:T(8,128)(2,1)} %get-tuple-element.44.q_ref, bf16[1280,384]{1,0:T(8,128)(2,1)} %get-tuple-element.45.k_ref, ...), custom_call_target="tpu_custom_call" | custom-call | flops 7549747200 | bytes 5898240 | tf_op jit(solution)/shard_map/attend/pallas_call | solution.py:161
  219.7 3.9 fusion.53
  223.7 1.8 copy-done.2
  226.2 45.6 %fusion.2 = (bf16[1280,3072]{1,0:T(8,128)(2,1)}, f32[1280,3072]{1,0:T(8,128)}) fusion(f32[3072]{0:T(1024)S(1)} %copy-done.32, bf16[768,3072]{1,0:T(8,128)(2,1)} %all-gather.11.cloned.1.call-done, f32[1280,768]{1,0:T(8,128)} %copy-done.2, f32[768]{0:T(1024)S(1)} %copy-done.33, f32[768]{0:T(1024)S(1)} %copy-done.29, f32[1280]{0:T(1024)S(1)} %add_rsqrt_fusion.1, ...), kind=kOutput, calls=%fused_computation.4 | convolution fusion | flops 6304235520 | bytes 32272384 | tf_op jit(solution)/shard_map/dot_general | solution.py:22
  271.8 11.2 %fusion.54 = (f32[1280]{0:T(1024)S(1)}, f32[1280,768]{1,0:T(8,128)S(1)}) fusion(f32[768]{0:T(1024)S(1)} %copy-done.35, bf16[1280,3072]{1,0:T(8,128)(2,1)} %get-tuple-element.200, bf16[3072,768]{1,0:T(8,128)(2,1)} %all-gather.13.cloned.1.call-done, f32[768]{0:T(1024)S(1)} %copy-done.33, f32[768]{0:T(1024)S(1)} %copy-done.29, f32[1280]{0:T(1024)S(1)} %add_rsqrt_fusion.1, ...), kind=kOutput, calls=%fused_computation.170 | convolution fusion | flops 6046678016 | bytes 20471808 | tf_op jit(solution)/shard_map/dot_general | solution.py:22
  284.6 1.8 fusion.22
  286.5 2.8 convert_reduce_fusion.4
  289.2 17.2 %convert_reduce_fusion = (f32[3072]{0:T(1024)S(1)}, bf16[1280,3072]{1,0:T(8,128)(2,1)}) fusion(f32[1280,3072]{1,0:T(8,128)} %get-tuple-element.201, f32[3072]{0:T(1024)S(1)} %copy-done.32, bf16[3072,768]{1,0:T(8,128)(2,1)S(1)} %bitcast.117, f32[1280,768]{1,0:T(8,128)S(1)} %get-tuple-element.139), kind=kOutput, calls=%fused_computation.10 | convolution fusion | flops 6099760128 | bytes 32268288 | tf_op jit(solution)/shard_map/dot_general | solution.py:26
  306.5 9.8 multiply_reduce_fusion
  321.8 3.8 pad_maximum_fusion.refs_0_
  327.2 2.2 fusion.49
  329.4 37.1 %attend_back.2 = (bf16[1280,384]{1,0:T(8,128)(2,1)}, bf16[1280,384]{1,0:T(8,128)(2,1)}, bf16[1280,384]{1,0:T(8,128)(2,1)}) custom-call(s32[1280,1]{1,0:T(8,128)} %get-tuple-element.208.refs_0_.idx_ref, bf16[1280,384]{1,0:T(8,128)(2,1)} %get-tuple-element.40.q_ref, bf16[1280,384]{1,0:T(8,128)(2,1)} %get-tuple-element.41.k_ref, ...), custom_call_target="tpu_custom_call" | custom-call | flops 17616076800 | bytes 8847360 | tf_op jit(solution)/shard_map/attend_back/pallas_call | solution.py:271
  366.5 37.1 %attend_back.3 = (bf16[1280,384]{1,0:T(8,128)(2,1)}, bf16[1280,384]{1,0:T(8,128)(2,1)}, bf16[1280,384]{1,0:T(8,128)(2,1)}) custom-call(s32[1280,1]{1,0:T(8,128)} %get-tuple-element.207.refs_0_.idx_ref, bf16[1280,384]{1,0:T(8,128)(2,1)} %get-tuple-element.44.q_ref, bf16[1280,384]{1,0:T(8,128)(2,1)} %get-tuple-element.45.k_ref, ...), custom_call_target="tpu_custom_call" | custom-call | flops 17616076800 | bytes 8847360 | tf_op jit(solution)/shard_map/attend_back/pallas_call | solution.py:271
  403.7 2.9 pad_maximum_fusion.4.refs_3_
  409.6 27.8 %project_back.1 = (bf16[2,640,768]{2,1,0:T(8,128)(2,1)}, bf16[2,640,768]{2,1,0:T(8,128)(2,1)}, f32[768,1152]{1,0:T(8,128)}, f32[8,1152]{1,0:T(8,128)}) custom-call(s32[1]{0:T(128)} %bitcast.5.part_ref, bf16[2,1280,768]{2,1,0:T(8,128)(2,1)} %pad_maximum_fusion.refs_0_, bf16[2,1280,384]{2,1,0:T(8,128)(2,1)} %pad_maximum_fusion.2.refs_1_, ...), custom_call_target="tpu_custom_call" | custom-call | flops 14092861440 | bytes 17301504 | tf_op jit(solution)/shard_map/project_back/pallas_call | solution.py:342
  438.3 3.2 dynamic-slice_convert_fusion.1
  443.1 5.2 convolution_convert_fusion.3
  450.3 11.4 %convolution_convert_fusion = bf16[3072,768]{1,0:T(8,128)(2,1)} fusion(bf16[1280,3072]{1,0:T(8,128)(2,1)} %get-tuple-element.200, f32[1280,768]{1,0:T(8,128)} %copy-done.5), kind=kOutput, calls=%fused_computation.29 | convolution fusion | flops 6043140096 | bytes 16515072 | tf_op jit(solution)/shard_map/dot_general | solution.py:30
  462.3 12.4 %convolution_convert_fusion.1 = bf16[768,3072]{1,0:T(8,128)(2,1)} fusion(bf16[1280,3072]{1,0:T(8,128)(2,1)} %get-tuple-element.206, f32[1280,768]{1,0:T(8,128)} %copy-done.2, f32[768]{0:T(1024)S(1)} %copy-done.34, f32[768]{0:T(1024)S(1)} %copy-done.30, f32[1280]{0:T(1024)S(1)} %add_rsqrt_fusion.1, f32[1280]{0:T(1024)S(1)} %broadcast_multiply_fusion.6), kind=kOutput, calls=%fused_computation.30 | convolution fusion | flops 6047072256 | bytes 16531456 | tf_op jit(solution)/shard_map/dot_general | solution.py:30
  475.0 88.5 %all-reduce.3.cloned.1.call-done = f32[256,128]{1,0:T(8,128)} async-done(((f32[256,128]{1,0:T(8,128)}), f32[256,128]{1,0:T(8,128)}) %all-reduce.3.cloned.1.call-update) | async-done | bytes 131088
  565.9 99.2 %reduce-scatter.7.cloned.1.call-done = bf16[24,768]{1,0:T(8,128)(2,1)} async-done(((bf16[768,768]{1,0:T(8,128)(2,1)}), bf16[24,768]{1,0:T(8,128)(2,1)}) %reduce-scatter.7.cloned.1.call-update) | async-done | bytes 36880 | tf_op jit(solution)/shard_map/reduce_scatter | solution.py:490
  666.4 4.6 fusion.24
  671.0 125.5 %reduce-scatter.5.cloned.1.call-done = bf16[24,2304]{1,0:T(8,128)(2,1)} async-done(((bf16[384,2304]{1,0:T(8,128)(2,1)}), bf16[24,2304]{1,0:T(8,128)(2,1)}) %reduce-scatter.5.cloned.1.call-update) | async-done | bytes 110608 | tf_op jit(solution)/shard_map/reduce_scatter | solution.py:490
  798.1 110.4 %reduce-scatter.11.cloned.1.call-done = bf16[96,768]{1,0:T(8,128)(2,1)} async-done(((bf16[3072,768]{1,0:T(8,128)(2,1)}), bf16[96,768]{1,0:T(8,128)(2,1)}) %reduce-scatter.11.cloned.1.call-update) | async-done | bytes 147472 | tf_op jit(solution)/shard_map/reduce_scatter | solution.py:490
  910.1 110.5 %reduce-scatter.9.cloned.1.call-done = bf16[24,3072]{1,0:T(8,128)(2,1)} async-done(((bf16[768,3072]{1,0:T(8,128)(2,1)}), bf16[24,3072]{1,0:T(8,128)(2,1)}) %reduce-scatter.9.cloned.1.call-update) | async-done | bytes 147472 | tf_op jit(solution)/shard_map/reduce_scatter | solution.py:490
  (246 shorter events, 69.2 us)
Async XLA Ops:
  7.2 11.7 %copy-start.37 = (bf16[72]{0:T(256)(128)(2,1)S(1)}, bf16[72]{0:T(256)(128)(2,1)}, u32[]{:S(2)}) copy-start(bf16[72]{0:T(256)(128)(2,1)} %param.23) | copy-start | bytes 436
  7.2 11.7 %copy-start.38 = (bf16[24]{0:T(256)(128)(2,1)S(1)}, bf16[24]{0:T(256)(128)(2,1)}, u32[]{:S(2)}) copy-start(bf16[24]{0:T(256)(128)(2,1)} %param.25) | copy-start | bytes 148
  7.2 11.7 %copy-start.39 = (bf16[24]{0:T(256)(128)(2,1)S(1)}, bf16[24]{0:T(256)(128)(2,1)}, u32[]{:S(2)}) copy-start(bf16[24]{0:T(256)(128)(2,1)} %param.26) | copy-start | bytes 148
  7.2 11.7 %copy-start.40 = (bf16[24]{0:T(256)(128)(2,1)S(1)}, bf16[24]{0:T(256)(128)(2,1)}, u32[]{:S(2)}) copy-start(bf16[24]{0:T(256)(128)(2,1)} %param.27) | copy-start | bytes 148
  7.2 11.7 %copy-start.41 = (bf16[96]{0:T(256)(128)(2,1)S(1)}, bf16[96]{0:T(256)(128)(2,1)}, u32[]{:S(2)}) copy-start(bf16[96]{0:T(256)(128)(2,1)} %param.29) | copy-start | bytes 580
  7.2 11.7 %copy-start.42 = (bf16[24]{0:T(256)(128)(2,1)S(1)}, bf16[24]{0:T(256)(128)(2,1)}, u32[]{:S(2)}) copy-start(bf16[24]{0:T(256)(128)(2,1)} %param.31) | copy-start | bytes 148
  7.3 11.7 %copy-start.43 = (bf16[24]{0:T(256)(128)(2,1)S(1)}, bf16[24]{0:T(256)(128)(2,1)}, u32[]{:S(2)}) copy-start(bf16[24]{0:T(256)(128)(2,1)} %param.32) | copy-start | bytes 148
  7.3 118.3 %all-gather.7.cloned.1.call-start = ((), (), s32[]{:S(2)}) async-start(), calls=%async_computation.4 | async-start | bytes 3649536 | tf_op jit(solution)/shard_map/all_gather | solution.py:424
  8.0 211.7 %all-gather.9.cloned.1.call-start = ((), (), s32[]{:S(2)}) async-start(), calls=%async_computation.5 | async-start | bytes 1216512 | tf_op jit(solution)/shard_map/all_gather | solution.py:424
  8.8 217.4 %all-gather.11.cloned.1.call-start = ((), (), s32[]{:S(2)}) async-start(), calls=%async_computation.6 | async-start | bytes 4866048 | tf_op jit(solution)/shard_map/all_gather | solution.py:424
  9.5 262.3 %all-gather.13.cloned.1.call-start = ((), (), s32[]{:S(2)}) async-start(), calls=%async_computation.7 | async-start | bytes 4866048 | tf_op jit(solution)/shard_map/all_gather | solution.py:424
  9.5 113.2 %collective-permute-start = (bf16[2,640,768]{2,1,0:T(8,128)(2,1)}, bf16[2,640,768]{2,1,0:T(8,128)(2,1)}, u32[]{:S(2)}, u32[]{:S(2)}) collective-permute-start(bf16[2,640,768]{2,1,0:T(8,128)(2,1)} %bitcast.99), channel_id=1, source_target_pairs={{0,16},{16,0},{1,17},{17,1},{2,18},{18,2},{3,19},{19,3},{4,20},{20... | collective-permute-start | bytes 5898248 | tf_op jit(solution)/shard_map/ppermute | solution.py:413
  10.1 553.4 %all-reduce.3.cloned.1.call-start = ((), (), s32[]{:S(2)}) async-start(), calls=%async_computation.12 | async-start | bytes 262144
  100.8 16.2 %copy-start = (bf16[2,1,640,768]{3,2,1,0:T(8,128)(2,1)S(1)}, bf16[2,1,640,768]{3,2,1,0:T(8,128)(2,1)}, u32[]{:S(2)}) copy-start(bf16[2,1,640,768]{3,2,1,0:T(8,128)(2,1)} %param.21) | copy-start | bytes 5898244
  108.1 13.2 %copy-start.6 = (s32[1280,1]{1,0:T(8,128)S(1)}, s32[1280,1]{1,0:T(8,128)}, u32[]{:S(2)}) copy-start(s32[1280,1]{1,0:T(8,128)} %copy.85) | copy-start | bytes 15364
  170.9 47.0 %collective-permute-start.1 = (bf16[640,384]{1,0:T(8,128)(2,1)}, bf16[640,384]{1,0:T(8,128)(2,1)S(1)}, u32[]{:S(2)}, u32[]{:S(2)}) collective-permute-start(bf16[640,384]{1,0:T(8,128)(2,1)} %get-tuple-element.48), channel_id=1, source_target_pairs={{0,16},{16,0},{1,17},{17,1},{2,18},{18,2},{3,19},{19,3},{4,20},{20... | collective-permute-start | bytes 1474568 | tf_op jit(solution)/shard_map/ppermute | solution.py:413
  184.4 32.2 %copy-start.23 = (bf16[640,384]{1,0:T(8,128)(2,1)S(1)}, bf16[640,384]{1,0:T(8,128)(2,1)}, u32[]{:S(2)}) copy-start(bf16[640,384]{1,0:T(8,128)(2,1)} %get-tuple-element.43) | copy-start | bytes 1474564
  216.4 2.1 collective-permute-start.2
  226.1 45.7 %copy-start.35 = (f32[768]{0:T(1024)S(1)}, f32[768]{0:T(1024)}, u32[]{:S(2)}) copy-start(f32[768]{0:T(1024)} %add.187) | copy-start | bytes 9220
  286.4 20.1 %slice-start = ((s8[4718592]{0:T(1024)(128)(4,1)}), s8[4194304]{0:T(1024)(128)(4,1)S(1)}, s32[]{:S(2)}) async-start(s8[4718592]{0:T(1024)(128)(4,1)} %bitcast.114), calls=%async_computation.13 | async-start | bytes 8388608
  289.2 17.3 %copy-start.5 = (f32[1280,768]{1,0:T(8,128)}, f32[1280,768]{1,0:T(8,128)S(1)}, u32[]{:S(2)}) copy-start(f32[1280,768]{1,0:T(8,128)S(1)} %get-tuple-element.139) | copy-start | bytes 11796484
  289.2 17.3 %copy-start.3 = (f32[1280,768]{1,0:T(8,128)S(1)}, f32[1280,768]{1,0:T(8,128)}, u32[]{:S(2)}) copy-start(f32[1280,768]{1,0:T(8,128)} %copy-done.2) | copy-start | bytes 11796484
  289.2 17.3 %slice-start.1 = ((s8[4718592]{0:T(1024)(128)(4,1)}), s8[524288]{0:T(1024)(128)(4,1)S(1)}, s32[]{:S(2)}) async-start(s8[4718592]{0:T(1024)(128)(4,1)} %bitcast.114), calls=%async_computation.14 | async-start | bytes 1048576
  321.0 6.2 collective-permute-start.3
  366.5 37.2 %copy-start.19 = (bf16[1280,384]{1,0:T(8,128)(2,1)S(1)}, bf16[1280,384]{1,0:T(8,128)(2,1)}, u32[]{:S(2)}) copy-start(bf16[1280,384]{1,0:T(8,128)(2,1)} %get-tuple-element.60) | copy-start | bytes 2949124
  441.6 6.8 collective-permute-start.5
  443.0 222.0 %reduce-scatter.7.cloned.1.call-start = ((), (), s32[]{:S(2)}) async-start(), calls=%async_computation.9 | async-start | bytes 1216512 | tf_op jit(solution)/shard_map/reduce_scatter | solution.py:490
  448.3 348.2 %reduce-scatter.5.cloned.1.call-start = ((), (), s32[]{:S(2)}) async-start(), calls=%async_computation.8 | async-start | bytes 1880064 | tf_op jit(solution)/shard_map/reduce_scatter | solution.py:490
  450.2 458.3 %reduce-scatter.11.cloned.1.call-start = ((), (), s32[]{:S(2)}) async-start(), calls=%async_computation.11 | async-start | bytes 4866048 | tf_op jit(solution)/shard_map/reduce_scatter | solution.py:490
  461.7 558.9 %reduce-scatter.9.cloned.1.call-start = ((), (), s32[]{:S(2)}) async-start(), calls=%async_computation.10 | async-start | bytes 4866048 | tf_op jit(solution)/shard_map/reduce_scatter | solution.py:490
  474.8 191.6 %copy-start.12 = (bf16[2,640,768]{2,1,0:T(8,128)(2,1)S(1)}, bf16[2,640,768]{2,1,0:T(8,128)(2,1)}, u32[]{:S(2)}) copy-start(bf16[2,640,768]{2,1,0:T(8,128)(2,1)} %get-tuple-element.62) | copy-start | bytes 5898244
  474.8 191.6 %collective-permute-start.4 = (bf16[2,640,768]{2,1,0:T(8,128)(2,1)}, bf16[2,640,768]{2,1,0:T(8,128)(2,1)}, u32[]{:S(2)}, u32[]{:S(2)}) collective-permute-start(bf16[2,640,768]{2,1,0:T(8,128)(2,1)} %get-tuple-element.63), channel_id=1, source_target_pairs={{0,16},{16,0},{1,17},{17,1},{2,18},{18,2},{3,19},{19,3},{4,20},{20... | collective-permute-start | bytes 5898248 | tf_op jit(solution)/shard_map/ppermute | solution.py:413
  (33 other events, 121.9 us)
Sparse Core Ops, SparseCore 0:
  11.0 62.8 all-gather.6
  76.8 52.6 all-gather.8
  132.4 62.5 all-gather.10
  197.7 61.8 all-gather.12
  443.1 120.3 all-reduce.2
  569.0 95.9 reduce-scatter.6
  669.9 126.5 reduce-scatter.4
  801.9 106.5 reduce-scatter.10
  914.0 106.5 reduce-scatter.8

commit v2 on v1

--- a/solution.py
+++ b/solution.py
@@ -38,70 +38,94 @@
     )
 
 
-def project_body(block, share, idx_ref, own_ref, other_ref, wq_ref, wk_ref, wv_ref, bias_ref,
-                 cos_ref, sin_ref, xw_ref, q_ref, k_ref, v_ref):
+def arrange_body(block, idx_ref, own_ref, other_ref, xw_ref):
     half = own_ref.shape[0]
 
     def step(i, carry):
         rows = pl.ds(pl.multiple_of(i * block, block), block)
         picks = lax.broadcasted_iota(jnp.int32, (block, half), 1)
-        where_from = idx_ref[rows, :]
-        near = (picks == where_from).astype(BF)
-        away = (picks + half == where_from).astype(BF)
-        work = (dot(near, own_ref[...]) + dot(away, other_ref[...])).astype(BF)
-        xw_ref[rows, :] = work
+        source = idx_ref[rows, :]
+        near = (picks == source).astype(BF)
+        away = (picks + half == source).astype(BF)
+        xw_ref[rows, :] = (dot(near, own_ref[...]) + dot(away, other_ref[...])).astype(BF)
+        return carry
+
+    lax.fori_loop(0, idx_ref.shape[0] // block, step, 0)
+
+
+def arrange(idx_col, own, other, block=256):
+    rows, width = idx_col.shape[0], own.shape[1]
+    return pl.pallas_call(
+        functools.partial(arrange_body, block),
+        out_shape=jax.ShapeDtypeStruct((rows, width), BF),
+        compiler_params=pltpu.CompilerParams(vmem_limit_bytes=40 << 20),
+        cost_estimate=pl.CostEstimate(
+            flops=2 * rows * rows * width, bytes_accessed=4 * rows * width, transcendentals=0
+        ),
+        name="arrange",
+    )(idx_col, own, other)
+
+
+def own_columns(core, near_ref, away_ref, hold, sems):
+    span, share = near_ref.shape[0], hold.shape[1] // 3
+    copies = []
+    for s in range(3):
+        for t, ref in enumerate((near_ref, away_ref)):
+            side = core if t == 0 else 1 - core
+            copies.append(
+                pltpu.make_async_copy(
+                    ref.at[:, pl.ds(pl.multiple_of(core * share + 2 * s * share, 128), share)],
+                    hold.at[pl.ds(pl.multiple_of(side * span, 128), span), s * share:(s + 1) * share],
+                    sems.at[2 * s + t],
+                )
+            )
+    for copy in copies:
+        copy.start()
+    return copies
+
+
+def project_body(block, part_ref, xw_ref, near_ref, away_ref, bias_ref, cos_ref, sin_ref,
+                 q_ref, k_ref, v_ref, hold, sems):
+    share = q_ref.shape[1]
+    for copy in own_columns(part_ref[0], near_ref, away_ref, hold, sems):
+        copy.wait()
+
+    def step(i, carry):
+        rows = pl.ds(pl.multiple_of(i * block, block), block)
+        work = xw_ref[rows, :]
         cosine, sine = cos_ref[rows, :], sin_ref[rows, :]
-        for w_ref, out_ref, place, scale in (
-            (wq_ref, q_ref, 0, LOG2E / math.sqrt(HEAD)),
-            (wk_ref, k_ref, 1, 1.0),
-        ):
-            pre = dot(work, w_ref[...]) + bias_ref[:, place * share:(place + 1) * share]
+        for out_ref, place, scale in ((q_ref, 0, LOG2E / math.sqrt(HEAD)), (k_ref, 1, 1.0)):
+            whole = slice(place * share, (place + 1) * share)
+            pre = dot(work, hold[:, whole]) + bias_ref[:, whole]
             for j in range(share // PAIR):
                 cols = slice(j * PAIR, (j + 1) * PAIR)
-                part = pre[:, cols]
+                piece = pre[:, cols]
                 out_ref[rows, cols] = (
-                    (part * cosine + pair_swap(part) * sine) * scale
+                    (piece * cosine + pair_swap(piece) * sine) * scale
                 ).astype(BF)
-        v_ref[rows, :] = (dot(work, wv_ref[...]) + bias_ref[:, 2 * share:]).astype(BF)
+        v_ref[rows, :] = (dot(work, hold[:, 2 * share:]) + bias_ref[:, 2 * share:]).astype(BF)
         return carry
 
-    lax.fori_loop(0, idx_ref.shape[0] // block, step, 0)
-
-
-def project(idx_col, own, other, w_qkv, bias_own, cosine, sine, part, block=256):
-    rows = idx_col.shape[0]
-    width = own.shape[1]
+    lax.fori_loop(0, xw_ref.shape[0] // block, step, 0)
+
+
+def project(part, xw, near_w, away_w, bias_own, cosine, sine, block=256):
+    rows, width = xw.shape
     share = bias_own.shape[1] // 3
-    parts = w_qkv.shape[1] // (3 * share)
-    whole = lambda shape: pl.BlockSpec(shape, lambda g, p: (0,) * len(shape))
+    vmem, smem, anywhere = (pl.BlockSpec(memory_space=s) for s in (pltpu.VMEM, pltpu.SMEM, pl.ANY))
     return pl.pallas_call(
-        lambda part_ref, *refs: project_body(block, share, *refs),
-        grid_spec=pltpu.PrefetchScalarGridSpec(
-            num_scalar_prefetch=1,
-            grid=(1,),
-            in_specs=[
-                whole((rows, 1)),
-                whole(own.shape),
-                whole(other.shape),
-                pl.BlockSpec((width, share), lambda g, p: (0, p[0])),
-                pl.BlockSpec((width, share), lambda g, p: (0, parts + p[0])),
-                pl.BlockSpec((width, share), lambda g, p: (0, 2 * parts + p[0])),
-                whole(bias_own.shape),
-                whole(cosine.shape),
-                whole(sine.shape),
-            ],
-            out_specs=[whole((rows, width))] + [whole((rows, share))] * 3,
-        ),
-        out_shape=[jax.ShapeDtypeStruct((rows, width), BF)]
-        + [jax.ShapeDtypeStruct((rows, share), BF)] * 3,
-        compiler_params=pltpu.CompilerParams(vmem_limit_bytes=60 << 20),
+        functools.partial(project_body, block),
+        in_specs=[smem, vmem, anywhere, anywhere, vmem, vmem, vmem],
+        out_shape=[jax.ShapeDtypeStruct((rows, share), BF)] * 3,
+        scratch_shapes=[pltpu.VMEM((width, 3 * share), BF), pltpu.SemaphoreType.DMA((6,))],
+        compiler_params=pltpu.CompilerParams(vmem_limit_bytes=40 << 20),
         cost_estimate=pl.CostEstimate(
-            flops=2 * rows * width * (rows + 3 * share),
-            bytes_accessed=2 * (2 * rows * width + 3 * width * share + 3 * rows * share),
+            flops=2 * rows * width * 3 * share,
+            bytes_accessed=2 * (rows * width + 3 * width * share + 3 * rows * share),
             transcendentals=0,
         ),
         name="project",
-    )(part, idx_col, own, other, w_qkv, w_qkv, w_qkv, bias_own, cosine, sine)
+    )(part, xw, near_w, away_w, bias_own, cosine, sine)
 
 
 def attend_body(block, idx_ref, q_ref, k_ref, v_ref, seg_col_ref, seg_row_ref,
@@ -293,33 +317,26 @@
     )(idx_col, q, k, v, seg_col, seg_row, lse, ctxt, gnear, gaway, cosine, sine)
 
 
-def project_back_body(block, rows, xw_ref, dq_ref, dk_ref, dv_ref, row_ref, wq_ref, wk_ref, wv_ref,
-                      near_ref, away_ref, gw_ref, gb_ref, work):
+def project_back_body(block, part_ref, xw_ref, dq_ref, dk_ref, dv_ref, row_ref, wnear_ref, waway_ref,
+                      near_ref, away_ref, work, hold, sems):
+    rows, share = dq_ref.shape[1], dq_ref.shape[2]
     half = near_ref.shape[1]
-    share = dq_ref.shape[2]
-    batch = pl.program_id(0)
-
-    @pl.when(batch == 0)
+
+    @pl.when(pl.program_id(0) == 0)
     def _():
-        gw_ref[...] = jnp.zeros_like(gw_ref)
-        gb_ref[...] = jnp.zeros_like(gb_ref)
+        for copy in own_columns(part_ref[0], wnear_ref, waway_ref, hold, sems):
+            copy.wait()
 
     def step(i, carry):
         span = pl.ds(pl.multiple_of(i * block, block), block)
         total = None
-        for place, (g_ref, w_ref) in enumerate(((dq_ref, wq_ref), (dk_ref, wk_ref), (dv_ref, wv_ref))):
-            piece = g_ref[0, span, :]
-            cols = slice(place * share, (place + 1) * share)
-            gb_ref[0:1, cols] += jnp.sum(piece.astype(F32), axis=0, keepdims=True)
-            term = dot_rt(piece, w_ref[...])
+        for place, g_ref in enumerate((dq_ref, dk_ref, dv_ref)):
+            term = dot_rt(g_ref[0, span, :], hold[:, place * share:(place + 1) * share])
             total = term if total is None else total + term
         work[span, :] = total.astype(BF)
         return carry
 
     lax.fori_loop(0, rows // block, step, 0)
-    for place, g_ref in enumerate((dq_ref, dk_ref, dv_ref)):
-        cols = slice(place * share, (place + 1) * share)
-        gw_ref[:, cols] += dot_lt(xw_ref[0], g_ref[0])
     small = block // 2
 
     def back(i, carry):
@@ -332,56 +349,298 @@
     lax.fori_loop(0, half // small, back, 0)
 
 
-def project_back(xw, dq, dk, dv, idx_row, w_qkv, part, block=256):
+def project_back(part, xw, dq, dk, dv, idx_row, near_w, away_w, block=256):
     batches, rows, width = xw.shape
     share = dq.shape[2]
-    parts = w_qkv.shape[1] // (3 * share)
     half = rows // 2
-    each = lambda shape: pl.BlockSpec((1,) + shape, lambda b, p: (b,) + (0,) * len(shape))
-    fixed = lambda shape: pl.BlockSpec(shape, lambda b, p: (0,) * len(shape))
+    each = lambda shape: pl.BlockSpec((1,) + shape, lambda b: (b,) + (0,) * len(shape))
+    anywhere = pl.BlockSpec(memory_space=pl.ANY)
     return pl.pallas_call(
-        lambda part_ref, *refs: project_back_body(block, rows, *refs),
-        grid_spec=pltpu.PrefetchScalarGridSpec(
-            num_scalar_prefetch=1,
-            grid=(batches,),
-            in_specs=[each((rows, width)), each((rows, share)), each((rows, share)), each((rows, share)),
-                      each((1, rows)),
-                      pl.BlockSpec((width, share), lambda b, p: (0, p[0])),
-                      pl.BlockSpec((width, share), lambda b, p: (0, parts + p[0])),
-                      pl.BlockSpec((width, share), lambda b, p: (0, 2 * parts + p[0]))],
-            out_specs=[each((half, width)), each((half, width)), fixed((width, 3 * share)),
-                       fixed((8, 3 * share))],
-            scratch_shapes=[pltpu.VMEM((rows, width), BF)],
-        ),
-        out_shape=[jax.ShapeDtypeStruct((batches, half, width), BF),
-                   jax.ShapeDtypeStruct((batches, half, width), BF),
-                   jax.ShapeDtypeStruct((width, 3 * share), F32),
-                   jax.ShapeDtypeStruct((8, 3 * share), F32)],
+        functools.partial(project_back_body, block),
+        grid=(batches,),
+        in_specs=[pl.BlockSpec(memory_space=pltpu.SMEM), each((rows, width)), each((rows, share)),
+                  each((rows, share)), each((rows, share)), each((1, rows)), anywhere, anywhere],
+        out_specs=[each((half, width)), each((half, width))],
+        scratch_shapes=[pltpu.VMEM((rows, width), BF), pltpu.VMEM((width, 3 * share), BF),
+                        pltpu.SemaphoreType.DMA((6,))],
+        out_shape=[jax.ShapeDtypeStruct((batches, half, width), BF)] * 2,
         compiler_params=pltpu.CompilerParams(vmem_limit_bytes=60 << 20),
         cost_estimate=pl.CostEstimate(
-            flops=2 * batches * rows * width * (rows + 6 * share),
-            bytes_accessed=2 * batches * rows * (2 * width + 3 * share) + 12 * width * share,
+            flops=2 * batches * rows * width * (rows + 3 * share),
+            bytes_accessed=2 * batches * rows * (2 * width + 3 * share) + 6 * width * share,
             transcendentals=0,
         ),
         name="project_back",
-    )(part, xw, dq, dk, dv, idx_row, w_qkv, w_qkv, w_qkv)
+    )(part, xw, dq, dk, dv, idx_row, near_w, away_w)
+
+
+def weight_back_body(xw_ref, dq_ref, dk_ref, dv_ref, gw_ref, gb_ref, acc):
+    batch, share = pl.program_id(0), dq_ref.shape[2]
+    for place, g_ref in enumerate((dq_ref, dk_ref, dv_ref)):
+        cols = slice(place * share, (place + 1) * share)
+        term = dot_lt(xw_ref[0], g_ref[0])
+        thin = jnp.sum(g_ref[0].astype(F32), axis=0, keepdims=True)
+
+        @pl.when(batch == 0)
+        def _():
+            acc[:, cols] = term
+            gb_ref[0:1, cols] = thin
+
+        @pl.when(batch > 0)
+        def _():
+            acc[:, cols] += term
+            gb_ref[0:1, cols] += thin
+
+        @pl.when(batch == pl.num_programs(0) - 1)
+        def _():
+            gw_ref[:, cols] = acc[:, cols].astype(BF)
+
+
+def weight_back(xw, dq, dk, dv):
+    batches, rows, width = xw.shape
+    share = dq.shape[2]
+    each = lambda shape: pl.BlockSpec((1,) + shape, lambda b: (b,) + (0,) * len(shape))
+    return pl.pallas_call(
+        weight_back_body,
+        grid=(batches,),
+        in_specs=[each((rows, width)), each((rows, share)), each((rows, share)), each((rows, share))],
+        out_specs=[pl.BlockSpec((width, 3 * share), lambda b: (0, 0)),
+                   pl.BlockSpec((8, 3 * share), lambda b: (0, 0))],
+        out_shape=[jax.ShapeDtypeStruct((width, 3 * share), BF), jax.ShapeDtypeStruct((8, 3 * share), F32)],
+        scratch_shapes=[pltpu.VMEM((width, 3 * share), F32)],
+        compiler_params=pltpu.CompilerParams(vmem_limit_bytes=60 << 20),
+        cost_estimate=pl.CostEstimate(
+            flops=2 * batches * rows * width * 3 * share,
+            bytes_accessed=2 * batches * rows * (width + 3 * share) + 6 * width * share,
+            transcendentals=0,
+        ),
+        name="weight_back",
+    )(xw, dq, dk, dv)
 
 
 EPS = 1e-6
-ERF_SCALE = 0.3275911
+ERF_SLOPE = 0.3275911 * math.sqrt(0.5)
+ERF_TERMS = (0.254829592, -0.284496736, 1.421413741, -1.453152027, 1.061405429)
 
 
 def gauss_parts(u):
-    return jax.nn.gelu(u, approximate=False), 0.5 * (1.0 + lax.erf(u * math.sqrt(0.5))) + u * jnp.exp(
-        -0.5 * u * u
-    ) * (1.0 / math.sqrt(2.0 * math.pi))
+    bell = jnp.exp2(u * u * (-0.5 * LOG2E))
+    t = 1.0 / (1.0 + ERF_SLOPE * jnp.abs(u))
+    poly = 0.5 * ERF_TERMS[4]
+    for term in ERF_TERMS[3::-1]:
+        poly = poly * t + 0.5 * term
+    tail = poly * t * bell
+    below = jnp.where(u < 0.0, tail, 1.0 - tail)
+    return u * below, below + u * bell * (1.0 / math.sqrt(2.0 * math.pi))
+
+
+def row_mean(value):
+    return jnp.sum(value, axis=1, keepdims=True) * (1.0 / value.shape[1])
+
+
+def standard(hidden):
+    centre = hidden - row_mean(hidden)
+    root = lax.rsqrt(row_mean(centre * centre) + EPS)
+    return centre * root, root
+
+
+def standard_back(grad, norm, root):
+    return root * (grad - row_mean(grad) - norm * row_mean(grad * norm))
+
+
+def feed_body(chunk, part_ref, x_ref, near_ref, away_ref, dy_ref, thin_ref, bup_ref,
+              unear_ref, uaway_ref, dnear_ref, daway_ref,
+              out_ref, dh_ref, low_ref, act_ref, dup_ref, dlow_ref, da_ref, cnear_ref, caway_ref,
+              sums_ref, bsum_ref, wo_near, wo_away, wup, wdown, slopes, sems):
+    first_step = pl.program_id(0) == 0
+    core = part_ref[0]
+    width, wide = wup.shape
+    share = near_ref.shape[1]
+    half_w, half_f = width // 2, wide // 2
+
+    def loads():
+        copies = []
+        for t, (u_ref, d_ref) in enumerate(((unear_ref, dnear_ref), (uaway_ref, daway_ref))):
+            side = core if t == 0 else 1 - core
+            hold = wo_near if t == 0 else wo_away
+            copies += [
+                pltpu.make_async_copy(u_ref.at[:, :width], hold, sems.at[t]),
+                pltpu.make_async_copy(
+                    u_ref.at[:, width:], wup.at[pl.ds(pl.multiple_of(side * half_w, 128), half_w), :],
+                    sems.at[2 + t]),
+                pltpu.make_async_copy(
+                    d_ref, wdown.at[pl.ds(pl.multiple_of(side * half_f, 128), half_f), :], sems.at[4 + t]),
+            ]
+        return copies
+
+    @pl.when(first_step)
+    def _():
+        copies = loads()
+        for copy in copies:
+            copy.start()
+        sums_ref[...] = jnp.zeros_like(sums_ref)
+        bsum_ref[...] = jnp.zeros_like(bsum_ref)
+        for copy in copies:
+            copy.wait()
+
+    b_out, gain_one, shift_one, b_down, gain_two, shift_two = (thin_ref[i:i + 1, :] for i in range(6))
+
+    def tally(row, value):
+        sums_ref[row:row + 1, :] += jnp.sum(value, axis=0, keepdims=True)
+
+    attended = dot(near_ref[...], wo_near[...]) + dot(away_ref[...], wo_away[...]) + b_out
+    norm_one, root_one = standard(x_ref[...].astype(F32) + attended)
+    first = norm_one * gain_one + shift_one
+    low = first.astype(BF)
+    low_ref[...] = low
+    lowered = None
+    for c in range(wide // chunk):
+        cols = slice(c * chunk, (c + 1) * chunk)
+        act, slope = gauss_parts(dot(low, wup[:, cols]) + bup_ref[:, cols])
+        act = act.astype(BF)
+        act_ref[:, cols] = act
+        slopes[:, cols] = slope.astype(BF)
+        term = dot(act, wdown[cols, :])
+        lowered = term if lowered is None else lowered + term
+    norm_two, root_two = standard(first + lowered + b_down)
+    out_ref[...] = (norm_two * gain_two + shift_two).astype(BF)
+    dy = dy_ref[...].astype(F32)
+    tally(4, dy * norm_two)
+    tally(5, dy)
+    grad_two = standard_back(dy * gain_two, norm_two, root_two)
+    dlow = grad_two.astype(BF)
+    dlow_ref[...] = dlow
+    tally(3, dlow.astype(F32))
+    total = grad_two
+    for c in range(wide // chunk):
+        cols = slice(c * chunk, (c + 1) * chunk)
+        dup = (dot_rt(dlow, wdown[cols, :]) * slopes[:, cols].astype(F32)).astype(BF)
+        dup_ref[:, cols] = dup
+        bsum_ref[0:1, cols] += jnp.sum(dup.astype(F32), axis=0, keepdims=True)
+        total = total + dot_rt(dup, wup[:, cols])
+    tally(1, total * norm_one)
+    tally(2, total)
+    grad_one = standard_back(total * gain_one, norm_one, root_one)
+    dh_ref[...] = grad_one
+    da = grad_one.astype(BF)
+    da_ref[...] = da
+    tally(0, da.astype(F32))
+    cnear_ref[...] = dot_rt(da, wo_near[...]).astype(BF)
+    caway_ref[...] = dot_rt(da, wo_away[...]).astype(BF)
+
+
+def feed(part, x, near, away, dy, thin, bup, unear, uaway, dnear, daway, block=256, chunk=768):
+    rows, width = x.shape
+    share = near.shape[1]
+    wide = bup.shape[1]
+    line = lambda n: pl.BlockSpec((block, n), lambda i: (i, 0))
+    fixed = lambda shape: pl.BlockSpec(shape, lambda i: (0, 0))
+    anywhere = pl.BlockSpec(memory_space=pl.ANY)
+    shape = lambda n, dt: jax.ShapeDtypeStruct((rows, n), dt)
+    return pl.pallas_call(
+        functools.partial(feed_body, chunk),
+        grid=(rows // block,),
+        in_specs=[pl.BlockSpec(memory_space=pltpu.SMEM), line(width), line(share), line(share), line(width),
+                  fixed(thin.shape), fixed(bup.shape), anywhere, anywhere, anywhere, anywhere],
+        out_specs=[line(width), line(width), line(width), line(wide), line(wide), line(width), line(width),
+                   line(share), line(share), fixed((8, width)), fixed((8, wide))],
+        out_shape=[shape(width, BF), shape(width, F32), shape(width, BF), shape(wide, BF), shape(wide, BF),
+                   shape(width, BF), shape(width, BF), shape(share, BF), shape(share, BF),
+                   jax.ShapeDtypeStruct((8, width), F32), jax.ShapeDtypeStruct((8, wide), F32)],
+        scratch_shapes=[pltpu.VMEM((share, width), BF), pltpu.VMEM((share, width), BF),
+                        pltpu.VMEM((width, wide), BF), pltpu.VMEM((wide, width), BF),
+                        pltpu.VMEM((block, wide), BF), pltpu.SemaphoreType.DMA((6,))],
+        compiler_params=pltpu.CompilerParams(vmem_limit_bytes=60 << 20),
+        cost_estimate=pl.CostEstimate(
+            flops=2 * rows * width * (2 * width + 4 * wide),
+            bytes_accessed=2 * rows * (7 * width + 2 * wide) + 4 * width * (wide + width),
+            transcendentals=2 * rows * wide,
+        ),
+        name="feed",
+    )(part, x, near, away, dy, thin, bup, unear, uaway, dnear, daway)
+
+
+def swap_cores(value):
+    return lax.ppermute(value, "seq", [(0, 1), (1, 0)])
+
+
+def swap_x(value):
+    return lax.ppermute(value, "fsdp", [(i, i ^ 1) for i in range(16)])
+
+
+def swap_y(value):
+    return lax.ppermute(value, "fsdp", [(i, i ^ 2) for i in range(16)])
+
+
+def shift_z(value, k):
+    return lax.ppermute(value, "fsdp", [(i, (i + 4 * k) % 16) for i in range(16)])
+
+
+def assemble_body(place_ref, ax_ref, ay_ref, bx_ref, by_ref, out_ref):
+    place = place_ref[0]
+    z, y, x = place // 4, (place // 2) % 2, place % 2
+    for j in range(4):
+        k, o = j % 2, j // 2
+        near_z, far_z = lax.rem(z - k + 4, 4), lax.rem(z - k + 2, 4)
+        flip_x = lax.rem(x + o, 2)
+        flip_y = lax.rem(y + o, 2)
+        out_ref[near_z * 4 + y * 2 + flip_x] = ax_ref[j]
+        out_ref[near_z * 4 + (1 - y) * 2 + flip_x] = ay_ref[j]
+        out_ref[far_z * 4 + flip_y * 2 + x] = by_ref[j]
+        out_ref[far_z * 4 + flip_y * 2 + 1 - x] = bx_ref[j]
+
+
+def assemble(place, parts):
+    n, width = parts[0].shape[1:]
+    vmem = pl.BlockSpec(memory_space=pltpu.VMEM)
+    return pl.pallas_call(
+        assemble_body,
+        in_specs=[pl.BlockSpec(memory_space=pltpu.SMEM)] + [vmem] * 4,
+        out_shape=jax.ShapeDtypeStruct((16, n, width), BF),
+        compiler_params=pltpu.CompilerParams(vmem_limit_bytes=24 << 20),
+        cost_estimate=pl.CostEstimate(flops=0, bytes_accessed=4 * 16 * n * width, transcendentals=0),
+        name="assemble",
+    )(place, *parts)
+
+
+def gather_half(shard):
+    n, width = shard.shape
+    if lax.axis_size("fsdp") != 16:
+        return lax.all_gather(shard, "fsdp", axis=0, tiled=True)
+    first = jnp.stack([shard, shift_z(shard, 1)])
+    second = jnp.stack([shift_z(shard, 2), shift_z(shard, 3)])
+    first = jnp.concatenate([first, swap_x(first)], axis=0)
+    second = jnp.concatenate([second, swap_y(second)], axis=0)
+    place = jnp.full((1,), lax.axis_index("fsdp"), jnp.int32)
+    whole = assemble(place, (first, swap_y(first), swap_x(second), second))
+    return whole.reshape(16 * n, width)
+
+
+def scatter_half(value):
+    rows, width = value.shape
+    count = lax.axis_size("fsdp")
+    n = rows // count
+    if count != 16:
+        return lax.psum_scatter(value.astype(BF), "fsdp", scatter_dimension=0, tiled=True).astype(F32)
+    place = lax.axis_index("fsdp")
+    z, y, x = place // 4, (place // 2) % 2, place % 2
+    cube = value.reshape(2, 2, 2, 2, n, width)
+    pick = lambda part, at, axis: lax.dynamic_index_in_dim(part, at, axis, keepdims=False)
+    first, second = cube[0], cube[1]
+    first = pick(first, y, 1) + swap_y(pick(first, 1 - y, 1).astype(BF)).astype(F32)
+    second = pick(second, x, 2) + swap_x(pick(second, 1 - x, 2).astype(BF)).astype(F32)
+    first = pick(first, x, 1) + swap_x(pick(first, 1 - x, 1).astype(BF)).astype(F32)
+    second = pick(second, y, 1) + swap_y(pick(second, 1 - y, 1).astype(BF)).astype(F32)
+    stack = jnp.concatenate([first, second], axis=0)
+    total = pick(stack, z, 0)
+    for k in (1, 2, 3):
+        total = total + shift_z(pick(stack, lax.rem(z + k, 4), 0).astype(BF), k).astype(F32)
+    return total
 
 
 def positions(segments):
     places = jnp.arange(segments.shape[0], dtype=jnp.int32)
-    counts = jnp.sum(
-        segments[None, :] < segments[:, None], axis=1, dtype=jnp.int32
-    )
+    counts = jnp.sum(segments[None, :] < segments[:, None], axis=1, dtype=jnp.int32)
     return (places - counts).astype(F32)
 
 
@@ -395,43 +654,32 @@
     return cosine, sine
 
 
-def standard(hidden):
-    centre = hidden - jnp.mean(hidden, axis=-1, keepdims=True)
-    root = lax.rsqrt(jnp.mean(centre * centre, axis=-1, keepdims=True) + EPS)
-    return centre * root, root
-
-
-def standard_back(grad, norm, root):
-    return root * (
-        grad
-        - jnp.mean(grad, axis=-1, keepdims=True)
-        - norm * jnp.mean(grad * norm, axis=-1, keepdims=True)
-    )
-
-
-def swap_cores(value):
-    return lax.ppermute(value, "seq", [(0, 1), (1, 0)])
-
-
 def on_device(tokens, permutation, segment_ids, cotangent, *shards):
     batches = tokens.shape[0]
     half, width = tokens.shape[2], tokens.shape[3]
     core = lax.axis_index("seq")
-    rows = 2 * half
     share = width // 2
     owners = 2 * lax.axis_size("fsdp")
-    both = ("seq", "fsdp")
-    gather = lambda value: lax.all_gather(value, both, axis=0, tiled=True)
+    part = jnp.full((1,), core, jnp.int32)
     thin = [i for i, piece in enumerate(shards) if piece.ndim == 1]
     sizes = [shards[i].shape[0] for i in thin]
     count = sum(sizes)
-    room = -(-count // 128) * 128
+    n_qkv = shards[0].shape[0]
+    room = n_qkv * 128
+
+    away_tokens = swap_cores(tokens[:, 0])
     packed = jnp.concatenate([shards[i] for i in thin] + [jnp.zeros((room - count,), BF)])
-    w_qkv = gather(shards[0])
-    vectors = gather(packed.reshape(1, room)).astype(F32)
-    w_out = gather(shards[2])
-    w_up = gather(shards[6])
-    w_down = gather(shards[8])
+    q_near = gather_half(jnp.concatenate([shards[0], packed.reshape(n_qkv, 128)], axis=1))
+    q_away = swap_cores(q_near)
+    u_near = gather_half(jnp.concatenate([shards[2], shards[6]], axis=1))
+    u_away = swap_cores(u_near)
+    d_near = gather_half(shards[8])
+    d_away = swap_cores(d_near)
+
+    slabs = [value[:, 3 * width:].reshape(owners // 2, room)[:, :count] for value in (q_near, q_away)]
+    vectors = jnp.concatenate(
+        [jnp.where(core == 0, slabs[0], slabs[1]), jnp.where(core == 0, slabs[1], slabs[0])], axis=0
+    ).astype(F32)
     spread, at = [], 0
     for size in sizes:
         spread.append(vectors[:, at:at + size].reshape(1, owners * size))
@@ -440,104 +688,89 @@
     bias_own = jnp.concatenate(
         [lax.dynamic_slice_in_dim(b_qkv, core * share + s * width, share, 1) for s in range(3)], axis=1
     )
-    part = jnp.full((1,), core, jnp.int32)
-    away_tokens = swap_cores(tokens[:, 0])
+    blank_row = jnp.zeros((1, width), F32)
+    thin_rows = jnp.concatenate(
+        [b_out, gain_one, shift_one, b_down, gain_two, shift_two, blank_row, blank_row], axis=0
+    )
+
     kept = []
     for b in range(batches):
         order = permutation[b, 0]
-        owner_half = order // half
-        place = jnp.where(owner_half == core, order - core * half, order - (1 - core) * half + half)
+        place = jnp.where(
+            order // half == core, order - core * half, order - (1 - core) * half + half
+        )
         segments = segment_ids[b, 0]
         cosine, sine = turn_tables(segments)
         col, row = segments[:, None], segments[None, :]
         idx_col, idx_row = place[:, None], place[None, :]
-        xw, q, k, v = project(idx_col, tokens[b, 0], away_tokens[b], w_qkv, bias_own, cosine, sine, part)
+        xw = arrange(idx_col, tokens[b, 0], away_tokens[b])
+        q, k, v = project(part, xw, q_near, q_away, bias_own, cosine, sine)
         near, away, ctxt, lse = attend(idx_col, q, k, v, col, row)
         kept.append((idx_col, idx_row, col, row, cosine, sine, xw, q, k, v, ctxt, lse, near, swap_cores(away)))
-    near = jnp.concatenate([item[12] for item in kept], axis=0)
-    away = jnp.concatenate([item[13] for item in kept], axis=0)
-    context = jnp.concatenate(
-        [jnp.where(core == 0, near, away), jnp.where(core == 0, away, near)], axis=1
+    join = lambda i: jnp.concatenate([item[i] for item in kept], axis=0)
+    near, away = join(12), join(13)
+    (outputs, grad_one, low, act, dup, dlow, da, cnear, caway, sums, bsum) = feed(
+        part, tokens[:, 0].reshape(batches * half, width), near, away,
+        cotangent[:, 0].reshape(batches * half, width), thin_rows, b_up, u_near, u_away, d_near, d_away,
     )
-    own = tokens[:, 0].reshape(batches * half, width).astype(F32)
-    norm_one, root_one = standard(own + dot(context, w_out) + b_out)
-    first = norm_one * gain_one + shift_one
-    first_low = first.astype(BF)
-    active, slope = gauss_parts(dot(first_low, w_up) + b_up)
-    active, slope = active.astype(BF), slope.astype(BF)
-    norm_two, root_two = standard(first + dot(active, w_down) + b_down)
-    outputs = (norm_two * gain_two + shift_two).astype(BF)
-    grad_out = cotangent[:, 0].reshape(batches * half, width).astype(F32)
-    g_gain_two = jnp.sum(grad_out * norm_two, axis=0)
-    g_shift_two = jnp.sum(grad_out, axis=0)
-    grad_two = standard_back(grad_out * gain_two, norm_two, root_two)
-    low_two = grad_two.astype(BF)
-    g_down = dot_lt(active, low_two)
-    g_b_down = jnp.sum(low_two.astype(F32), axis=0)
-    grad_up = (dot_rt(low_two, w_down) * slope.astype(F32)).astype(BF)
-    g_up = dot_lt(first_low, grad_up)
-    g_b_up = jnp.sum(grad_up.astype(F32), axis=0)
-    grad_first = grad_two + dot_rt(grad_up, w_up)
-    g_gain_one = jnp.sum(grad_first * norm_one, axis=0)
-    g_shift_one = jnp.sum(grad_first, axis=0)
-    grad_one = standard_back(grad_first * gain_one, norm_one, root_one)
-    low_one = grad_one.astype(BF)
-    g_out = dot_lt(context, low_one)
-    g_b_out = jnp.sum(low_one.astype(F32), axis=0)
-    grad_ctx = dot_rt(low_one, w_out).astype(BF)
-    ctx_near = jnp.where(core == 0, grad_ctx[:, :share], grad_ctx[:, share:])
-    ctx_away = swap_cores(jnp.where(core == 0, grad_ctx[:, share:], grad_ctx[:, :share]))
-    scatter = lambda value, axes: lax.psum_scatter(value, axes, scatter_dimension=0, tiled=True)
-    g_down = scatter(g_down.astype(BF), both).astype(F32)
-    g_up = scatter(g_up.astype(BF), both).astype(F32)
-    g_out = scatter(g_out.astype(BF), both).astype(F32)
+    caway = swap_cores(caway)
+
+    def halves(value):
+        size = value.shape[0] // 2
+        return (lax.dynamic_slice_in_dim(value, core * size, size, 0),
+                lax.dynamic_slice_in_dim(value, (1 - core) * size, size, 0))
+
+    def summed(value):
+        mine, theirs = halves(value)
+        return mine.astype(F32) + swap_cores(theirs).astype(F32)
+
+    g_down = scatter_half(summed(dot_lt(act, dlow).astype(BF)))
+    g_up = scatter_half(summed(dot_lt(low, dup).astype(BF)))
+    g_out = scatter_half(
+        dot_lt(near, da).astype(BF).astype(F32) + swap_cores(dot_lt(away, da).astype(BF)).astype(F32)
+    )
     backs = []
     for b in range(batches):
         idx_col, idx_row, col, row, cosine, sine, xw, q, k, v, ctxt, lse = kept[b][:12]
         span = slice(b * half, (b + 1) * half)
         backs.append(
-            attend_back(idx_col, q, k, v, col, row, lse, ctxt, ctx_near[span], ctx_away[span], cosine, sine)
+            attend_back(idx_col, q, k, v, col, row, lse, ctxt, cnear[span], caway[span], cosine, sine)
         )
-    stack = lambda pick: jnp.stack([pick(b) for b in range(batches)])
-    near_grad, away_grad, gw_own, gb_own = project_back(
-        stack(lambda b: kept[b][6]),
-        stack(lambda b: backs[b][0]),
-        stack(lambda b: backs[b][1]),
-        stack(lambda b: backs[b][2]),
-        stack(lambda b: kept[b][1]),
-        w_qkv,
-        part,
-    )
-    other = swap_cores(away_grad)
-    token_grad = (
-        grad_one.reshape(batches, half, width) + near_grad.astype(F32) + other.astype(F32)
-    ).astype(BF)
-    mine = lax.dynamic_slice_in_dim(gw_own, core * share, share, 0).astype(BF)
-    theirs = swap_cores(lax.dynamic_slice_in_dim(gw_own, (1 - core) * share, share, 0).astype(BF))
+    pile = lambda items: jnp.stack(items)
+    xws = pile([item[6] for item in kept])
+    dq, dk, dv = (pile([back[i] for back in backs]) for i in range(3))
+    gw_own, gb_own = weight_back(xws, dq, dk, dv)
+    mine, theirs = halves(gw_own)
+    theirs = swap_cores(theirs)
+    blank = jnp.zeros((share,), F32)
     columns, thin_columns = [], []
-    blank = jnp.zeros((share,), F32)
     for s in range(3):
         span = slice(s * share, (s + 1) * share)
         columns += [jnp.where(core == 0, mine[:, span], theirs[:, span]),
                     jnp.where(core == 0, theirs[:, span], mine[:, span])]
         thin_columns += [jnp.where(core == 0, gb_own[0, span], blank),
                          jnp.where(core == 0, blank, gb_own[0, span])]
-    g_qkv = scatter(jnp.concatenate(columns, axis=1), "fsdp").astype(F32)
-    thin_grads = [jnp.concatenate(thin_columns), g_b_out, g_gain_one, g_shift_one, g_b_up, g_b_down,
-                  g_gain_two, g_shift_two]
+    thin_grads = [jnp.concatenate(thin_columns), sums[0], sums[1], sums[2], bsum[0], sums[3], sums[4], sums[5]]
     slab = jnp.concatenate(
-        [value.reshape(owners, -1) for value in thin_grads]
-        + [jnp.zeros((owners, 1024 - count), F32)], axis=1
+        [value.reshape(owners, -1) for value in thin_grads] + [jnp.zeros((owners, room - count), F32)], axis=1
+    ).astype(BF).reshape(owners * n_qkv, 128)
+    columns.append(summed(slab).astype(BF))
+    g_qkv = scatter_half(jnp.concatenate(columns, axis=1).astype(F32))
+    near_grad, away_grad = project_back(
+        part, xws, dq, dk, dv, pile([item[1] for item in kept]), q_near, q_away
     )
-    slab = scatter(slab.reshape(owners * 8, 128), both).reshape(1024)
+    token_grad = (
+        grad_one.reshape(batches, half, width) + near_grad.astype(F32) + swap_cores(away_grad).astype(F32)
+    ).astype(BF)
+    flat = g_qkv[:, 3 * width:].reshape(room)
     thin_out, at = [], 0
     for size in sizes:
-        thin_out.append(slab[at:at + size])
+        thin_out.append(flat[at:at + size])
         at += size
     g_bqkv, g_bout, g_g1, g_s1, g_bup, g_bdown, g_g2, g_s2 = thin_out
     return (
         outputs.reshape(batches, 1, half, width), token_grad[:, None],
-        g_qkv, g_bqkv, g_out, g_bout, g_g1, g_s1, g_up, g_bup, g_down, g_bdown, g_g2, g_s2,
+        g_qkv[:, :3 * width], g_bqkv, g_out, g_bout, g_g1, g_s1, g_up, g_bup, g_down, g_bdown, g_g2, g_s2,
     )
 
 

time: 1040 us -> 552 us (0.53)
  waiting for transfers between devices: 537 us -> 105 us
  matrix products: 119 us -> 18.4 us
  blocking collectives: 70.6 us -> 0 us
  starting transfers between devices: 2.12 us -> 70.8 us
  Pallas kernels: 192 us -> 251 us
  local copies, waits for them, and re-layouts: 52 us -> 65.3 us
  between operations: 15 us -> 2.4 us
  other arithmetic: 41.6 us -> 30.5 us
    reduce_scatter x4 -> x0, waiting for transfers between devices: 446 us -> none  [on_device(): lax.psum_scatter(value, axes, scatter_dimension=0, tiled=True)]
    ppermute x0 -> x49, waiting for transfers between devices: none -> 104 us  [the longest x14 50.9 us: swap_y(): return lax.ppermute(value, 'fsdp', [(i, i ^ 2) for i in range(16)])]
    unnamed x10 -> x0, waiting for transfers between devices: 90.7 us -> none
    dot_general x6 -> x0, matrix products: 89.5 us -> none  [the longest x3 60.7 us: dot(): return jnp.dot(left, right, preferred_element_type=F32)]
    all_gather x1 -> x0, blocking collectives: 70.6 us -> none  [on_device(): gather = lambda value: lax.all_gather(value, both, axis=0, tiled=True)]
    ppermute x0 -> x49, starting transfers between devices: none -> 68.8 us  [the longest x21 32.5 us: shift_z(): lax.ppermute(value, 'fsdp', [(i, (i + 4 * k) % 16) for i in range(16)])]
    pallas_call x3 -> x10, Pallas kernels: 54.3 us -> 113 us  [the longest x1 53.9 us: feed(): pl.pallas_call(functools.partial(feed_body, chunk), grid=(rows // block,)...]
    unnamed x109 -> x114, local copies, waits for them, and re-layouts: 5.02 us -> 16.6 us
  transfers between devices with their start and end apart: 15 -> 62, of which waited for: 6 -> 23; matrix products, arithmetic and copies ran while one was open for 14% -> 15% of each run, Pallas kernels for 9% -> 36%
where the time goes in v2:
time: 552 us; the launch traced here: 543 us
  Pallas kernels  251 us (45%)
  waiting for transfers between devices  105 us (19%)
  starting transfers between devices  70.8 us (13%)
  local copies, waits for them, and re-layouts  65.3 us (12%)
  other arithmetic  30.5 us (6%)
  matrix products  18.4 us (3%)
    pallas_call x2, Pallas kernels, attend_back(): pl.pallas_call(functools.partial(attend_back_body, block), grid=(pairs,),...  74.5 us
    pallas_call x2, Pallas kernels, attend(): pl.pallas_call(functools.partial(attend_body, block), grid=(pairs,), in_s...  63.9 us
    pallas_call x1, Pallas kernels, feed(): pl.pallas_call(functools.partial(feed_body, chunk), grid=(rows // block,)...  53.9 us
    ppermute x14, waiting for transfers between devices, swap_y(): return lax.ppermute(value, 'fsdp', [(i, i ^ 2) for i in range(16)])  50.9 us
    ppermute x21, starting transfers between devices, shift_z(): lax.ppermute(value, 'fsdp', [(i, (i + 4 * k) % 16) for i in range(16)])  32.5 us
    ppermute x21, waiting for transfers between devices, shift_z(): lax.ppermute(value, 'fsdp', [(i, (i + 4 * k) % 16) for i in range(16)])  30.9 us
    ppermute x14, waiting for transfers between devices, swap_x(): return lax.ppermute(value, 'fsdp', [(i, i ^ 1) for i in range(16)])  22.2 us
    pallas_call x1, Pallas kernels, project_back(): pl.pallas_call(functools.partial(project_back_body, block), grid=(batches...  20.7 us
  transfers between devices with their start and end apart: 62, of which 23 were waited for; matrix products, arithmetic and copies ran while one was open for 15% of the time, Pallas kernels for 36%

profile of v2, /device:TPU:0, one launch (start us, length us, event | category | flops | bytes accessed | tf_op | source)
XLA Modules:
  0.0 543.0 jit_solution(4057468288082726487)
XLA Ops:
  0.7 5.4 concatenate.74
  7.0 4.1 collective-permute-start.4
  47.4 8.6 %collective-permute-done.22 = bf16[96,768]{1,0:T(8,128)(2,1)S(1)} collective-permute-done((bf16[96,768]{1,0:T(8,128)(2,1)S(1)}, bf16[96,768]{1,0:T(8,128)(2,1)S(1)}, u32[]{:S(2)}, u32[]{:S(2)}) %collective-permute-start.22) | collective-permute-done | bytes 147488 | tf_op jit(solution)/shard_map/ppermute | solution.py:576
  59.8 3.5 collective-permute-done.11
  67.9 3.1 collective-permute-done.24
  72.6 5.9 %collective-permute-done.16 = bf16[2,24,3840]{2,1,0:T(8,128)(2,1)S(1)} collective-permute-done((bf16[2,24,3840]{2,1,0:T(8,128)(2,1)S(1)}, bf16[2,24,3840]{2,1,0:T(8,128)(2,1)S(1)}, u32[]{:S(2)}, u32[]{:S(2)}) %collective-permute-start.16) | collective-permute-done | bytes 368672 | tf_op jit(solution)/shard_map/ppermute | solution.py:572
  82.7 8.4 %collective-permute-done.7.bx_ref = bf16[4,24,2432]{2,1,0:T(8,128)(2,1)S(1)} collective-permute-done((bf16[4,24,2432]{2,1,0:T(8,128)(2,1)S(1)}, bf16[4,24,2432]{2,1,0:T(8,128)(2,1)S(1)}, u32[]{:S(2)}, u32[]{:S(2)}) %collective-permute-start.7) | collective-permute-done | bytes 466976 | tf_op jit(solution)/shard_map/ppermute | solution.py:568
  95.6 8.1 %collective-permute-done.25.bx_ref = bf16[4,96,768]{2,1,0:T(8,128)(2,1)S(1)} collective-permute-done((bf16[4,96,768]{2,1,0:T(8,128)(2,1)S(1)}, bf16[4,96,768]{2,1,0:T(8,128)(2,1)S(1)}, u32[]{:S(2)}, u32[]{:S(2)}) %collective-permute-start.25) | collective-permute-done | bytes 589856 | tf_op jit(solution)/shard_map/ppermute | solution.py:568
  108.2 12.7 %collective-permute-done.21.ay_ref = bf16[4,96,768]{2,1,0:T(8,128)(2,1)} collective-permute-done((bf16[4,96,768]{2,1,0:T(8,128)(2,1)S(1)}, bf16[4,96,768]{2,1,0:T(8,128)(2,1)}, u32[]{:S(2)}, u32[]{:S(2)}) %collective-permute-start.21) | collective-permute-done | bytes 589856 | tf_op jit(solution)/shard_map/ppermute | solution.py:572
  124.6 3.0 assemble.4
  129.8 4.4 arrange.3.xw_ref
  134.3 4.2 arrange.2.xw_ref
  144.5 5.3 project.2
  152.7 32.0 %attend.2 = (bf16[640,384]{1,0:T(8,128)(2,1)}, bf16[640,384]{1,0:T(8,128)(2,1)}, bf16[384,1280]{1,0:T(8,128)(2,1)}, f32[3,8,1280]{2,1,0:T(8,128)}) custom-call(s32[1280,1]{1,0:T(8,128)} %get-tuple-element.214.idx_ref, bf16[1280,384]{1,0:T(8,128)(2,1)} %copy-done.15, bf16[1280,384]{1,0:T(8,128)(2,1)} %copy-done.16, bf16[1280,384]{1,0:T(8,128)(2,1)} %copy-done.17, ...), custom_call_target="tpu_custom_call" | custom-call | flops 7549747200 | bytes 5898240 | tf_op jit(solution)/shard_map/attend/pallas_call | solution.py:185
  185.0 5.3 project.3
  193.2 31.9 %attend.3 = (bf16[640,384]{1,0:T(8,128)(2,1)}, bf16[640,384]{1,0:T(8,128)(2,1)}, bf16[384,1280]{1,0:T(8,128)(2,1)}, f32[3,8,1280]{2,1,0:T(8,128)}) custom-call(s32[1280,1]{1,0:T(8,128)} %get-tuple-element.213.idx_ref, bf16[1280,384]{1,0:T(8,128)(2,1)} %copy-done.12, bf16[1280,384]{1,0:T(8,128)(2,1)} %copy-done.13, bf16[1280,384]{1,0:T(8,128)(2,1)} %copy-done.14, ...), custom_call_target="tpu_custom_call" | custom-call | flops 7549747200 | bytes 5898240 | tf_op jit(solution)/shard_map/attend/pallas_call | solution.py:185
  231.1 53.9 %feed.1 = (bf16[1280,768]{1,0:T(8,128)(2,1)}, f32[1280,768]{1,0:T(8,128)}, bf16[1280,768]{1,0:T(8,128)(2,1)}, bf16[1280,3072]{1,0:T(8,128)(2,1)}, bf16[1280,3072...) custom-call(s32[1]{0:T(128)} %bitcast.part_ref, ...), custom_call_target="tpu_custom_call" | custom-call | flops 27179089920 | bytes 41287680 | tf_op jit(solution)/shard_map/feed/pallas_call | solution.py:540
  285.0 9.7 %convolution_convert_fusion = bf16[3072,768]{1,0:T(8,128)(2,1)S(1)} fusion(bf16[1280,3072]{1,0:T(8,128)(2,1)} %get-tuple-element.82, bf16[1280,768]{1,0:T(8,128)(2,1)} %get-tuple-element.83), kind=kOutput, calls=%fused_computation.2 | convolution fusion | flops 6042157056 | bytes 14548992 | tf_op jit(solution)/shard_map/dot_general | solution.py:30
  300.2 6.8 %convolution_convert_fusion.1 = bf16[768,3072]{1,0:T(8,128)(2,1)S(1)} fusion(bf16[1280,768]{1,0:T(8,128)(2,1)S(1)} %copy-done.50, bf16[1280,3072]{1,0:T(8,128)(2,1)S(1)} %copy-done.49), kind=kOutput, calls=%fused_computation.3 | convolution fusion | flops 6042157056 | bytes 14548992 | tf_op jit(solution)/shard_map/dot_general | solution.py:30
  314.2 3.2 collective-permute-done.41
  323.0 37.1 %attend_back.2 = (bf16[1280,384]{1,0:T(8,128)(2,1)}, bf16[1280,384]{1,0:T(8,128)(2,1)}, bf16[1280,384]{1,0:T(8,128)(2,1)}) custom-call(s32[1280,1]{1,0:T(8,128)} %get-tuple-element.214.idx_ref, bf16[1280,384]{1,0:T(8,128)(2,1)} %copy-done.15, bf16[1280,384]{1,0:T(8,128)(2,1)} %copy-done.16, bf16[1280,384]{1,0:T(8,128)(2,1)} %copy-done.17, ...), custom_call_target="tpu_custom_call" | custom-call | flops 17616076800 | bytes 8847360 | tf_op jit(solution)/shard_map/attend_back/pallas_call | solution.py:295
  360.1 37.3 %attend_back.3 = (bf16[1280,384]{1,0:T(8,128)(2,1)}, bf16[1280,384]{1,0:T(8,128)(2,1)}, bf16[1280,384]{1,0:T(8,128)(2,1)}) custom-call(s32[1280,1]{1,0:T(8,128)} %get-tuple-element.213.idx_ref, bf16[1280,384]{1,0:T(8,128)(2,1)} %copy-done.12, bf16[1280,384]{1,0:T(8,128)(2,1)} %copy-done.13, bf16[1280,384]{1,0:T(8,128)(2,1)} %copy-done.14, ...), custom_call_target="tpu_custom_call" | custom-call | flops 17616076800 | bytes 8847360 | tf_op jit(solution)/shard_map/attend_back/pallas_call | solution.py:295
  404.0 11.6 %weight_back.1 = (bf16[768,1152]{1,0:T(8,128)(2,1)}, f32[8,1152]{1,0:T(8,128)}) custom-call(bf16[2,1280,768]{2,1,0:T(8,128)(2,1)} %pad_maximum_fusion.xw_ref, bf16[2,1280,384]{2,1,0:T(8,128)(2,1)} %pad_maximum_fusion.1.dq_ref, bf16[2,1280,384]{2,1,0:T(8,128)(2,1)} %pad_maximum_fusion.2.dk_ref, bf16[2,1280,384]{2,1,0:T(8,128)(2,1)} %pad_maximum_fusion.3.dv_ref), custom_call_target="tpu_custom_call" | custom-call | flops 4529848320 | bytes 11599872 | tf_op jit(solution)/shard_map/weight_back/pallas_call | solution.py:403
  418.0 5.3 collective-permute-start.43
  435.2 20.7 %project_back.1 = (bf16[2,640,768]{2,1,0:T(8,128)(2,1)}, bf16[2,640,768]{2,1,0:T(8,128)(2,1)}) custom-call(s32[1]{0:T(128)} %bitcast.part_ref, bf16[2,1280,768]{2,1,0:T(8,128)(2,1)} %pad_maximum_fusion.xw_ref, bf16[2,1280,384]{2,1,0:T(8,128)(2,1)} %pad_maximum_fusion.1.dq_ref, bf16[2,1280,384]{2,1,0:T(8,128)(2,1)} %pad_maximum_fusion.2.dk_ref, ...), custom_call_target="tpu_custom_call" | custom-call | flops 9563013120 | bytes 15532032 | tf_op jit(solution)/shard_map/project_back/pallas_call | solution.py:358
  459.4 10.3 %collective-permute-done.31 = bf16[2,2,24,2432]{3,2,0,1:T(8,128)(2,1)S(1)} collective-permute-done((bf16[2,2,24,2432]{3,2,0,1:T(8,128)(2,1)S(1)}, bf16[2,2,24,2432]{3,2,0,1:T(8,128)(2,1)S(1)}, u32[]{:S(2)}, u32[]{:S(2)}) %collective-permute-start.31) | collective-permute-done | bytes 466976 | tf_op jit(solution)/shard_map/ppermute | solution.py:572
  471.3 3.0 convert_add_fusion
  483.6 3.3 collective-permute-done.35
  495.7 7.5 %collective-permute-done.55 = bf16[2,2,96,768]{3,2,0,1:T(8,128)(2,1)S(1)} collective-permute-done((bf16[2,2,96,768]{3,2,0,1:T(8,128)(2,1)S(1)}, bf16[2,2,96,768]{3,2,0,1:T(8,128)(2,1)S(1)}, u32[]{:S(2)}, u32[]{:S(2)}) %collective-permute-start.55) | collective-permute-done | bytes 589856 | tf_op jit(solution)/shard_map/ppermute | solution.py:572
  507.5 8.3 %collective-permute-done.47 = bf16[2,2,24,3072]{3,2,0,1:T(8,128)(2,1)S(1)} collective-permute-done((bf16[2,2,24,3072]{3,2,0,1:T(8,128)(2,1)S(1)}, bf16[2,2,24,3072]{3,2,0,1:T(8,128)(2,1)S(1)}, u32[]{:S(2)}, u32[]{:S(2)}) %collective-permute-start.47) | collective-permute-done | bytes 589856 | tf_op jit(solution)/shard_map/ppermute | solution.py:572
  530.4 3.6 collective-permute-done.60
  535.6 6.1 %collective-permute-done.52 = bf16[24,3072]{1,0:T(8,128)(2,1)S(1)} collective-permute-done((bf16[24,3072]{1,0:T(8,128)(2,1)S(1)}, bf16[24,3072]{1,0:T(8,128)(2,1)S(1)}, u32[]{:S(2)}, u32[]{:S(2)}) %collective-permute-start.52) | collective-permute-done | bytes 147488 | tf_op jit(solution)/shard_map/ppermute | solution.py:576
  (391 shorter events, 166.7 us)
Async XLA Ops:
  7.0 37.0 %collective-permute-start.4 = (bf16[24,2432]{1,0:T(8,128)(2,1)S(1)}, bf16[24,2432]{1,0:T(8,128)(2,1)S(1)}, u32[]{:S(2)}, u32[]{:S(2)}) collective-permute-start(bf16[24,2432]{1,0:T(8,128)(2,1)S(1)} %get-tuple-element.175), channel_id=1, source_target_pairs={{0,8},{1,9},{2,10},{3,11},{4,12},{5,13},{6,14},{7,15},{8,0},{9,1},... | collective-permute-start | bytes 350216 | tf_op jit(solution)/shard_map/ppermute | solution.py:576
  11.1 34.1 %collective-permute-start.5 = (bf16[24,2432]{1,0:T(8,128)(2,1)S(1)}, bf16[24,2432]{1,0:T(8,128)(2,1)S(1)}, u32[]{:S(2)}, u32[]{:S(2)}) collective-permute-start(bf16[24,2432]{1,0:T(8,128)(2,1)S(1)} %get-tuple-element.175), channel_id=1, source_target_pairs={{0,12},{1,13},{2,14},{3,15},{4,0},{5,1},{6,2},{7,3},{8,4},{9,5},{1... | collective-permute-start | bytes 350216 | tf_op jit(solution)/shard_map/ppermute | solution.py:576
  12.5 33.8 %collective-permute-start.1 = (bf16[24,2432]{1,0:T(8,128)(2,1)S(1)}, bf16[24,2432]{1,0:T(8,128)(2,1)S(1)}, u32[]{:S(2)}, u32[]{:S(2)}) collective-permute-start(bf16[24,2432]{1,0:T(8,128)(2,1)S(1)} %get-tuple-element.175), channel_id=1, source_target_pairs={{0,4},{1,5},{2,6},{3,7},{4,8},{5,9},{6,10},{7,11},{8,12},{9,13},{1... | collective-permute-start | bytes 350216 | tf_op jit(solution)/shard_map/ppermute | solution.py:576
  14.9 42.8 %collective-permute-start.14 = (bf16[24,3840]{1,0:T(8,128)(2,1)S(1)}, bf16[24,3840]{1,0:T(8,128)(2,1)S(1)}, u32[]{:S(2)}, u32[]{:S(2)}) collective-permute-start(bf16[24,3840]{1,0:T(8,128)(2,1)S(1)} %constant_dynamic-update-slice_fusion.4), channel_id=1, source_target_pairs={{0,8},{1,9},{2,10},{3,11},{4,12},{5,13},{6,14},{7,15},{8,0},{9,1},... | collective-permute-start | bytes 552968 | tf_op jit(solution)/shard_map/ppermute | solution.py:576
  15.9 43.3 %collective-permute-start.15 = (bf16[24,3840]{1,0:T(8,128)(2,1)S(1)}, bf16[24,3840]{1,0:T(8,128)(2,1)S(1)}, u32[]{:S(2)}, u32[]{:S(2)}) collective-permute-start(bf16[24,3840]{1,0:T(8,128)(2,1)S(1)} %constant_dynamic-update-slice_fusion.4), channel_id=1, source_target_pairs={{0,12},{1,13},{2,14},{3,15},{4,0},{5,1},{6,2},{7,3},{8,4},{9,5},{1... | collective-permute-start | bytes 552968 | tf_op jit(solution)/shard_map/ppermute | solution.py:576
  56.0 72.2 %collective-permute-start = (bf16[2,640,768]{2,1,0:T(8,128)(2,1)}, bf16[2,640,768]{2,1,0:T(8,128)(2,1)}, u32[]{:S(2)}, u32[]{:S(2)}) collective-permute-start(bf16[2,640,768]{2,1,0:T(8,128)(2,1)} %bitcast.7), channel_id=1, source_target_pairs={{0,16},{16,0},{1,17},{17,1},{2,18},{18,2},{3,19},{19,3},{4,20},{20... | collective-permute-start | bytes 5898248 | tf_op jit(solution)/shard_map/ppermute | solution.py:564
  63.3 32.2 %collective-permute-start.20 = (bf16[2,96,768]{2,1,0:T(8,128)(2,1)S(1)}, bf16[2,96,768]{2,1,0:T(8,128)(2,1)S(1)}, u32[]{:S(2)}, u32[]{:S(2)}) collective-permute-start(bf16[2,96,768]{2,1,0:T(8,128)(2,1)S(1)} %pad_maximum_fusion.12), channel_id=1, source_target_pairs={{0,1},{1,0},{2,3},{3,2},{4,5},{5,4},{6,7},{7,6},{8,9},{9,8},{10,11... | collective-permute-start | bytes 884744 | tf_op jit(solution)/shard_map/ppermute | solution.py:568
  66.5 14.6 %collective-permute-start.12 = (bf16[2,24,3840]{2,1,0:T(8,128)(2,1)S(1)}, bf16[2,24,3840]{2,1,0:T(8,128)(2,1)S(1)}, u32[]{:S(2)}, u32[]{:S(2)}) collective-permute-start(bf16[2,24,3840]{2,1,0:T(8,128)(2,1)S(1)} %pad_maximum_fusion.10), channel_id=1, source_target_pairs={{0,1},{1,0},{2,3},{3,2},{4,5},{5,4},{6,7},{7,6},{8,9},{9,8},{10,11... | collective-permute-start | bytes 1105928 | tf_op jit(solution)/shard_map/ppermute | solution.py:568
  71.0 20.1 %collective-permute-start.7 = (bf16[4,24,2432]{2,1,0:T(8,128)(2,1)S(1)}, bf16[4,24,2432]{2,1,0:T(8,128)(2,1)S(1)}, u32[]{:S(2)}, u32[]{:S(2)}) collective-permute-start(bf16[4,24,2432]{2,1,0:T(8,128)(2,1)S(1)} %pad_maximum_fusion.9.by_ref), channel_id=1, source_target_pairs={{0,1},{1,0},{2,3},{3,2},{4,5},{5,4},{6,7},{7,6},{8,9},{9,8},{10,11... | collective-permute-start | bytes 1400840 | tf_op jit(solution)/shard_map/ppermute | solution.py:568
  81.1 22.6 %collective-permute-start.25 = (bf16[4,96,768]{2,1,0:T(8,128)(2,1)S(1)}, bf16[4,96,768]{2,1,0:T(8,128)(2,1)S(1)}, u32[]{:S(2)}, u32[]{:S(2)}) collective-permute-start(bf16[4,96,768]{2,1,0:T(8,128)(2,1)S(1)} %pad_maximum_fusion.7.by_ref), channel_id=1, source_target_pairs={{0,1},{1,0},{2,3},{3,2},{4,5},{5,4},{6,7},{7,6},{8,9},{9,8},{10,11... | collective-permute-start | bytes 1769480 | tf_op jit(solution)/shard_map/ppermute | solution.py:568
  91.1 33.5 %collective-permute-start.17 = (bf16[4,24,3840]{2,1,0:T(8,128)(2,1)S(1)}, bf16[4,24,3840]{2,1,0:T(8,128)(2,1)S(1)}, u32[]{:S(2)}, u32[]{:S(2)}) collective-permute-start(bf16[4,24,3840]{2,1,0:T(8,128)(2,1)S(1)} %pad_maximum_fusion.5.by_ref), channel_id=1, source_target_pairs={{0,1},{1,0},{2,3},{3,2},{4,5},{5,4},{6,7},{7,6},{8,9},{9,8},{10,11... | collective-permute-start | bytes 2211848 | tf_op jit(solution)/shard_map/ppermute | solution.py:568
  92.6 32.0 %collective-permute-start.13 = (bf16[4,24,3840]{2,1,0:T(8,128)(2,1)S(1)}, bf16[4,24,3840]{2,1,0:T(8,128)(2,1)}, u32[]{:S(2)}, u32[]{:S(2)}) collective-permute-start(bf16[4,24,3840]{2,1,0:T(8,128)(2,1)S(1)} %pad_maximum_fusion.4.ax_ref), channel_id=1, source_target_pairs={{0,2},{1,3},{2,0},{3,1},{4,6},{5,7},{6,4},{7,5},{8,10},{9,11},{10,... | collective-permute-start | bytes 2211848 | tf_op jit(solution)/shard_map/ppermute | solution.py:572
  95.5 45.5 %collective-permute-start.8 = (bf16[384,2432]{1,0:T(8,128)(2,1)}, bf16[384,2432]{1,0:T(8,128)(2,1)}, u32[]{:S(2)}, u32[]{:S(2)}) collective-permute-start(bf16[384,2432]{1,0:T(8,128)(2,1)} %bitcast.15.near_ref.wnear_ref), channel_id=1, source_target_pairs={{0,16},{16,0},{1,17},{17,1},{2,18},{18,2},{3,19},{19,3},{4,20},{20... | collective-permute-start | bytes 5603336 | tf_op jit(solution)/shard_map/ppermute | solution.py:564
  103.8 17.2 %collective-permute-start.21 = (bf16[4,96,768]{2,1,0:T(8,128)(2,1)S(1)}, bf16[4,96,768]{2,1,0:T(8,128)(2,1)}, u32[]{:S(2)}, u32[]{:S(2)}) collective-permute-start(bf16[4,96,768]{2,1,0:T(8,128)(2,1)S(1)} %pad_maximum_fusion.6.ax_ref), channel_id=1, source_target_pairs={{0,2},{1,3},{2,0},{3,1},{4,6},{5,7},{6,4},{7,5},{8,10},{9,11},{10,... | collective-permute-start | bytes 1769480 | tf_op jit(solution)/shard_map/ppermute | solution.py:572
  124.6 105.5 %collective-permute-start.26 = (bf16[1536,768]{1,0:T(8,128)(2,1)}, bf16[1536,768]{1,0:T(8,128)(2,1)}, u32[]{:S(2)}, u32[]{:S(2)}) collective-permute-start(bf16[1536,768]{1,0:T(8,128)(2,1)} %bitcast.40.dnear_ref), channel_id=1, source_target_pairs={{0,16},{16,0},{1,17},{17,1},{2,18},{18,2},{3,19},{19,3},{4,20},{20... | collective-permute-start | bytes 7077896 | tf_op jit(solution)/shard_map/ppermute | solution.py:564
  127.6 102.5 %collective-permute-start.18 = (bf16[384,3840]{1,0:T(8,128)(2,1)}, bf16[384,3840]{1,0:T(8,128)(2,1)}, u32[]{:S(2)}, u32[]{:S(2)}) collective-permute-start(bf16[384,3840]{1,0:T(8,128)(2,1)} %bitcast.35.unear_ref), channel_id=1, source_target_pairs={{0,16},{16,0},{1,17},{17,1},{2,18},{18,2},{3,19},{19,3},{4,20},{20... | collective-permute-start | bytes 8847368 | tf_op jit(solution)/shard_map/ppermute | solution.py:564
  184.7 43.9 %collective-permute-start.9 = (bf16[640,384]{1,0:T(8,128)(2,1)}, bf16[640,384]{1,0:T(8,128)(2,1)}, u32[]{:S(2)}, u32[]{:S(2)}) collective-permute-start(bf16[640,384]{1,0:T(8,128)(2,1)} %get-tuple-element.57), channel_id=1, source_target_pairs={{0,16},{16,0},{1,17},{17,1},{2,18},{18,2},{3,19},{19,3},{4,20},{20... | collective-permute-start | bytes 1474568 | tf_op jit(solution)/shard_map/ppermute | solution.py:564
  298.1 173.2 %collective-permute-start.54 = (bf16[1536,768]{1,0:T(8,128)(2,1)}, bf16[1536,768]{1,0:T(8,128)(2,1)}, u32[]{:S(2)}, u32[]{:S(2)}) collective-permute-start(bf16[1536,768]{1,0:T(8,128)(2,1)} %constant_dynamic-slice_fusion.4), channel_id=1, source_target_pairs={{0,16},{16,0},{1,17},{17,1},{2,18},{18,2},{3,19},{19,3},{4,20},{20... | collective-permute-start | bytes 7077896 | tf_op jit(solution)/shard_map/ppermute | solution.py:564
  300.0 21.9 %collective-permute-start.27 = (bf16[1280,384]{1,0:T(8,128)(2,1)S(1)}, bf16[1280,384]{1,0:T(8,128)(2,1)S(1)}, u32[]{:S(2)}, u32[]{:S(2)}) collective-permute-start(bf16[1280,384]{1,0:T(8,128)(2,1)S(1)} %copy-done.48), channel_id=1, source_target_pairs={{0,16},{16,0},{1,17},{17,1},{2,18},{18,2},{3,19},{19,3},{4,20},{20... | collective-permute-start | bytes 2949128 | tf_op jit(solution)/shard_map/ppermute | solution.py:564
  318.8 99.2 %collective-permute-start.40 = (bf16[2,24,768]{2,1,0:T(8,128)(2,1)S(1)}, bf16[2,24,768]{2,1,0:T(8,128)(2,1)S(1)}, u32[]{:S(2)}, u32[]{:S(2)}) collective-permute-start(bf16[2,24,768]{2,1,0:T(8,128)(2,1)S(1)} %fusion.64), channel_id=1, source_target_pairs={{0,1},{1,0},{2,3},{3,2},{4,5},{5,4},{6,7},{7,6},{8,9},{9,8},{10,11... | collective-permute-start | bytes 221192 | tf_op jit(solution)/shard_map/ppermute | solution.py:568
  427.4 48.0 %collective-permute-start.46 = (bf16[384,3072]{1,0:T(8,128)(2,1)}, bf16[384,3072]{1,0:T(8,128)(2,1)}, u32[]{:S(2)}, u32[]{:S(2)}) collective-permute-start(bf16[384,3072]{1,0:T(8,128)(2,1)} %constant_dynamic-slice_fusion.9), channel_id=1, source_target_pairs={{0,16},{16,0},{1,17},{17,1},{2,18},{18,2},{3,19},{19,3},{4,20},{20... | collective-permute-start | bytes 7077896 | tf_op jit(solution)/shard_map/ppermute | solution.py:564
  434.6 23.0 %collective-permute-start.33 = (bf16[2,2,24,2432]{3,2,0,1:T(8,128)(2,1)}, bf16[2,2,24,2432]{3,2,0,1:T(8,128)(2,1)}, u32[]{:S(2)}, u32[]{:S(2)}) collective-permute-start(bf16[2,2,24,2432]{3,2,0,1:T(8,128)(2,1)} %fusion.12), channel_id=1, source_target_pairs={{0,1},{1,0},{2,3},{3,2},{4,5},{5,4},{6,7},{7,6},{8,9},{9,8},{10,11... | collective-permute-start | bytes 1400840 | tf_op jit(solution)/shard_map/ppermute | solution.py:568
  455.9 61.5 %collective-permute-start.28 = (bf16[2,640,768]{2,1,0:T(8,128)(2,1)}, bf16[2,640,768]{2,1,0:T(8,128)(2,1)S(1)}, u32[]{:S(2)}, u32[]{:S(2)}) collective-permute-start(bf16[2,640,768]{2,1,0:T(8,128)(2,1)} %get-tuple-element.74), channel_id=1, source_target_pairs={{0,16},{16,0},{1,17},{17,1},{2,18},{18,2},{3,19},{19,3},{4,20},{20... | collective-permute-start | bytes 5898248 | tf_op jit(solution)/shard_map/ppermute | solution.py:564
  458.8 20.0 %collective-permute-start.34 = (bf16[2,24,2432]{2,1,0:T(8,128)(2,1)S(1)}, bf16[2,24,2432]{2,1,0:T(8,128)(2,1)S(1)}, u32[]{:S(2)}, u32[]{:S(2)}) collective-permute-start(bf16[2,24,2432]{2,1,0:T(8,128)(2,1)S(1)} %fusion.40), channel_id=1, source_target_pairs={{0,2},{1,3},{2,0},{3,1},{4,6},{5,7},{6,4},{7,5},{8,10},{9,11},{10,... | collective-permute-start | bytes 700424 | tf_op jit(solution)/shard_map/ppermute | solution.py:572
  474.7 19.8 %collective-permute-start.57 = (bf16[2,2,96,768]{3,2,0,1:T(8,128)(2,1)S(1)}, bf16[2,2,96,768]{3,2,0,1:T(8,128)(2,1)S(1)}, u32[]{:S(2)}, u32[]{:S(2)}) collective-permute-start(bf16[2,2,96,768]{3,2,0,1:T(8,128)(2,1)S(1)} %fusion.10), channel_id=1, source_target_pairs={{0,1},{1,0},{2,3},{3,2},{4,5},{5,4},{6,7},{7,6},{8,9},{9,8},{10,11... | collective-permute-start | bytes 1769480 | tf_op jit(solution)/shard_map/ppermute | solution.py:568
  487.0 16.2 %collective-permute-start.55 = (bf16[2,2,96,768]{3,2,0,1:T(8,128)(2,1)S(1)}, bf16[2,2,96,768]{3,2,0,1:T(8,128)(2,1)S(1)}, u32[]{:S(2)}, u32[]{:S(2)}) collective-permute-start(bf16[2,2,96,768]{3,2,0,1:T(8,128)(2,1)S(1)} %fusion.9), channel_id=1, source_target_pairs={{0,2},{1,3},{2,0},{3,1},{4,6},{5,7},{6,4},{7,5},{8,10},{9,11},{10,... | collective-permute-start | bytes 1769480 | tf_op jit(solution)/shard_map/ppermute | solution.py:572
  489.9 16.2 %collective-permute-start.49 = (bf16[2,2,24,3072]{3,2,0,1:T(8,128)(2,1)S(1)}, bf16[2,2,24,3072]{3,2,0,1:T(8,128)(2,1)S(1)}, u32[]{:S(2)}, u32[]{:S(2)}) collective-permute-start(bf16[2,2,24,3072]{3,2,0,1:T(8,128)(2,1)S(1)} %fusion.8), channel_id=1, source_target_pairs={{0,1},{1,0},{2,3},{3,2},{4,5},{5,4},{6,7},{7,6},{8,9},{9,8},{10,11... | collective-permute-start | bytes 1769480 | tf_op jit(solution)/shard_map/ppermute | solution.py:568
  490.9 24.9 %collective-permute-start.47 = (bf16[2,2,24,3072]{3,2,0,1:T(8,128)(2,1)S(1)}, bf16[2,2,24,3072]{3,2,0,1:T(8,128)(2,1)S(1)}, u32[]{:S(2)}, u32[]{:S(2)}) collective-permute-start(bf16[2,2,24,3072]{3,2,0,1:T(8,128)(2,1)S(1)} %fusion.7), channel_id=1, source_target_pairs={{0,2},{1,3},{2,0},{3,1},{4,6},{5,7},{6,4},{7,5},{8,10},{9,11},{10,... | collective-permute-start | bytes 1769480 | tf_op jit(solution)/shard_map/ppermute | solution.py:572
  494.7 26.2 %collective-permute-start.58 = (bf16[2,96,768]{2,1,0:T(8,128)(2,1)S(1)}, bf16[2,96,768]{2,1,0:T(8,128)(2,1)S(1)}, u32[]{:S(2)}, u32[]{:S(2)}) collective-permute-start(bf16[2,96,768]{2,1,0:T(8,128)(2,1)S(1)} %fusion.16), channel_id=1, source_target_pairs={{0,2},{1,3},{2,0},{3,1},{4,6},{5,7},{6,4},{7,5},{8,10},{9,11},{10,... | collective-permute-start | bytes 884744 | tf_op jit(solution)/shard_map/ppermute | solution.py:572
  503.3 17.6 %collective-permute-start.56 = (bf16[2,96,768]{2,1,0:T(8,128)(2,1)S(1)}, bf16[2,96,768]{2,1,0:T(8,128)(2,1)S(1)}, u32[]{:S(2)}, u32[]{:S(2)}) collective-permute-start(bf16[2,96,768]{2,1,0:T(8,128)(2,1)S(1)} %fusion.15), channel_id=1, source_target_pairs={{0,1},{1,0},{2,3},{3,2},{4,5},{5,4},{6,7},{7,6},{8,9},{9,8},{10,11... | collective-permute-start | bytes 884744 | tf_op jit(solution)/shard_map/ppermute | solution.py:568
  506.3 19.9 %collective-permute-start.50 = (bf16[2,24,3072]{2,1,0:T(8,128)(2,1)S(1)}, bf16[2,24,3072]{2,1,0:T(8,128)(2,1)S(1)}, u32[]{:S(2)}, u32[]{:S(2)}) collective-permute-start(bf16[2,24,3072]{2,1,0:T(8,128)(2,1)S(1)} %fusion.14), channel_id=1, source_target_pairs={{0,2},{1,3},{2,0},{3,1},{4,6},{5,7},{6,4},{7,5},{8,10},{9,11},{10,... | collective-permute-start | bytes 884744 | tf_op jit(solution)/shard_map/ppermute | solution.py:572
  526.6 15.2 %collective-permute-start.52 = (bf16[24,3072]{1,0:T(8,128)(2,1)S(1)}, bf16[24,3072]{1,0:T(8,128)(2,1)S(1)}, u32[]{:S(2)}, u32[]{:S(2)}) collective-permute-start(bf16[24,3072]{1,0:T(8,128)(2,1)S(1)} %get-tuple-element.158), channel_id=1, source_target_pairs={{0,8},{1,9},{2,10},{3,11},{4,12},{5,13},{6,14},{7,15},{8,0},{9,1},... | collective-permute-start | bytes 442376 | tf_op jit(solution)/shard_map/ppermute | solution.py:576
  (83 other events, 664.0 us)

commit v3 on v2

--- a/solution.py
+++ b/solution.py
@@ -11,6 +11,7 @@
 HEAD = 64
 PAIR = 2 * HEAD
 SEG_COUNT = 4
+LONGEST = 1024
 LOG2E = math.log2(math.e)
 LN2 = math.log(2.0)
 FAR = float(2**30)
@@ -155,22 +156,25 @@
     qt[...] = q_ref[...].T
     empty = jnp.zeros((HEAD, block), BF)
 
-    def step(i, carry):
-        span = pl.ds(pl.multiple_of(i * block, block), block)
+    def attended(span, keys):
         extra = augt[:, span]
         for h in range(2):
             mine = qt[h * HEAD:(h + 1) * HEAD, span]
             mixed = jnp.concatenate([mine, empty, extra] if h == 0 else [empty, mine, extra], axis=0)
-            scores = dot(ka[...], mixed)
+            scores = dot(ka[keys, :], mixed)
             top = jnp.max(scores, axis=0, keepdims=True)
             expo = jnp.exp2(scores - top)
             total = jnp.sum(expo, axis=0, keepdims=True)
-            context = dot(vt[h * HEAD:(h + 1) * HEAD, :], expo.astype(BF))
+            context = dot(vt[h * HEAD:(h + 1) * HEAD, keys], expo.astype(BF))
             ctxt_ref[h * HEAD:(h + 1) * HEAD, span] = (context / total).astype(BF)
             lse_ref[0, h:h + 1, span] = top + jnp.log2(total)
+
+    def step(i, carry):
+        attended(pl.ds(pl.multiple_of(i * block, block), block), slice(0, LONGEST))
         return carry
 
-    lax.fori_loop(0, rows // block, step, 0)
+    lax.fori_loop(0, LONGEST // block, step, 0)
+    attended(slice(LONGEST, rows), slice(LONGEST, rows))
     given = dot(ctxt_ref[...], pick[...]).astype(BF)
     near_ref[...] = given[:, :half].T
     away_ref[...] = given[:, half:].T
@@ -206,7 +210,7 @@
 
 def attend_back_body(block, idx_ref, q_ref, k_ref, v_ref, seg_col_ref, seg_row_ref, lse_ref,
                      ctxt_ref, gnear_ref, gaway_ref, cos_ref, sin_ref,
-                     dq_ref, dk_ref, dv_ref,
+                     grads_ref,
                      pick, ka, va, kt, qt, dt, go, delta, dkacc, dvacc, dqt, augt):
     rows = q_ref.shape[0]
     half = gnear_ref.shape[0]
@@ -256,34 +260,37 @@
                          jnp.where(places == start + 1, second,
                                    jnp.where(places == start + 2, third, 0.0)))
 
-    def step(i, carry):
-        span = pl.ds(pl.multiple_of(i * block, block), block)
+    def attended(span, keys):
         base = jnp.concatenate([augt[:, span], jnp.zeros((8, block), F32)], axis=0)
         for h in range(2):
             part = slice(h * HEAD, (h + 1) * HEAD)
             low = (base + thirds(-lse_ref[0, h:h + 1, span], SEG_COUNT)).astype(BF)
             mine = qt[part, span]
             order = (mine, empty) if h == 0 else (empty, mine)
-            scores = dot(ka[...], jnp.concatenate(order + (low, blank), axis=0))
+            scores = dot(ka[keys, :], jnp.concatenate(order + (low, blank), axis=0))
             probs = jnp.exp2(scores)
             low = thirds(-delta[h:h + 1, span], 0).astype(BF)
             mine = dt[part, span]
             order = (mine, empty) if h == 0 else (empty, mine)
-            slope = dot(va[...], jnp.concatenate(order + (low, blank), axis=0))
+            slope = dot(va[keys, :], jnp.concatenate(order + (low, blank), axis=0))
             grads = (probs * slope).astype(BF)
             keep = wide < HEAD if h == 0 else wide >= HEAD
-            dvacc[...] += dot(probs.astype(BF), jnp.where(keep, go[span, :], zero))
-            dkacc[...] += dot(grads, jnp.where(keep, q_ref[span, :], zero))
-            dqt[part, span] = dot(kt[part, :], grads)
+            dvacc[keys, :] += dot(probs.astype(BF), jnp.where(keep, go[span, :], zero))
+            dkacc[keys, :] += dot(grads, jnp.where(keep, q_ref[span, :], zero))
+            dqt[part, span] = dot(kt[part, keys], grads)
+
+    def step(i, carry):
+        attended(pl.ds(pl.multiple_of(i * block, block), block), slice(0, LONGEST))
         return carry
 
-    lax.fori_loop(0, rows // block, step, 0)
+    lax.fori_loop(0, LONGEST // block, step, 0)
+    attended(slice(LONGEST, rows), slice(LONGEST, rows))
     cosine, sine = cos_ref[...], sin_ref[...]
     turned = dqt[...].T
-    dq_ref[...] = ((turned * cosine - pair_swap(turned) * sine) * (1.0 / math.sqrt(HEAD))).astype(BF)
+    grads_ref[0] = ((turned * cosine - pair_swap(turned) * sine) * (1.0 / math.sqrt(HEAD))).astype(BF)
     turned = dkacc[...]
-    dk_ref[...] = ((turned * cosine - pair_swap(turned) * sine) * LN2).astype(BF)
-    dv_ref[...] = dvacc[...].astype(BF)
+    grads_ref[1] = ((turned * cosine - pair_swap(turned) * sine) * LN2).astype(BF)
+    grads_ref[2] = dvacc[...].astype(BF)
 
 
 def attend_back(idx_col, q, k, v, seg_col, seg_row, lse, ctxt, gnear, gaway, cosine, sine, block=256):
@@ -300,8 +307,8 @@
                   pl.BlockSpec((1, 8, rows), lambda j: (j, 0, 0)),
                   pl.BlockSpec((PAIR, rows), lambda j: (j, 0)),
                   column(half), column(half), whole(cosine.shape), whole(sine.shape)],
-        out_specs=[column(rows)] * 3,
-        out_shape=[jax.ShapeDtypeStruct((rows, share), BF)] * 3,
+        out_specs=pl.BlockSpec((3, rows, PAIR), lambda j: (0, 0, j)),
+        out_shape=jax.ShapeDtypeStruct((3, rows, share), BF),
         scratch_shapes=[pltpu.VMEM((rows, rows), BF), pltpu.VMEM((rows, 2 * PAIR), BF),
                         pltpu.VMEM((rows, 2 * PAIR), BF), pltpu.VMEM((PAIR, rows), BF),
                         pltpu.VMEM((PAIR, rows), BF), pltpu.VMEM((PAIR, rows), BF),
@@ -317,21 +324,18 @@
     )(idx_col, q, k, v, seg_col, seg_row, lse, ctxt, gnear, gaway, cosine, sine)
 
 
-def project_back_body(block, part_ref, xw_ref, dq_ref, dk_ref, dv_ref, row_ref, wnear_ref, waway_ref,
+def project_back_body(block, part_ref, g_ref, row_ref, wnear_ref, waway_ref,
                       near_ref, away_ref, work, hold, sems):
-    rows, share = dq_ref.shape[1], dq_ref.shape[2]
-    half = near_ref.shape[1]
-
-    @pl.when(pl.program_id(0) == 0)
-    def _():
-        for copy in own_columns(part_ref[0], wnear_ref, waway_ref, hold, sems):
-            copy.wait()
+    rows, share = g_ref.shape[1:]
+    half = near_ref.shape[0]
+    for copy in own_columns(part_ref[0], wnear_ref, waway_ref, hold, sems):
+        copy.wait()
 
     def step(i, carry):
         span = pl.ds(pl.multiple_of(i * block, block), block)
         total = None
-        for place, g_ref in enumerate((dq_ref, dk_ref, dv_ref)):
-            term = dot_rt(g_ref[0, span, :], hold[:, place * share:(place + 1) * share])
+        for place in range(3):
+            term = dot_rt(g_ref[place, span, :], hold[:, place * share:(place + 1) * share])
             total = term if total is None else total + term
         work[span, :] = total.astype(BF)
         return carry
@@ -341,73 +345,58 @@
 
     def back(i, carry):
         span = pl.ds(pl.multiple_of(i * small, small), small)
-        for base, out_ref in ((0, near_ref), (half, away_ref)):
-            pick = (lax.broadcasted_iota(jnp.int32, (small, rows), 0) + (base + i * small) == row_ref[0]).astype(BF)
-            out_ref[0, span, :] = dot(pick, work[...]).astype(BF)
+        for base, out_ref in ((half, away_ref), (0, near_ref)):
+            pick = (lax.broadcasted_iota(jnp.int32, (small, rows), 0) + (base + i * small) == row_ref[...]).astype(BF)
+            out_ref[span, :] = dot(pick, work[...]).astype(BF)
         return carry
 
     lax.fori_loop(0, half // small, back, 0)
 
 
-def project_back(part, xw, dq, dk, dv, idx_row, near_w, away_w, block=256):
-    batches, rows, width = xw.shape
-    share = dq.shape[2]
+def project_back(part, grads, idx_row, near_w, away_w, block=256):
+    rows, share = grads.shape[1:]
+    width = 2 * share
     half = rows // 2
-    each = lambda shape: pl.BlockSpec((1,) + shape, lambda b: (b,) + (0,) * len(shape))
-    anywhere = pl.BlockSpec(memory_space=pl.ANY)
+    vmem, smem, anywhere = (pl.BlockSpec(memory_space=s) for s in (pltpu.VMEM, pltpu.SMEM, pl.ANY))
     return pl.pallas_call(
         functools.partial(project_back_body, block),
-        grid=(batches,),
-        in_specs=[pl.BlockSpec(memory_space=pltpu.SMEM), each((rows, width)), each((rows, share)),
-                  each((rows, share)), each((rows, share)), each((1, rows)), anywhere, anywhere],
-        out_specs=[each((half, width)), each((half, width))],
+        in_specs=[smem, vmem, vmem, anywhere, anywhere],
         scratch_shapes=[pltpu.VMEM((rows, width), BF), pltpu.VMEM((width, 3 * share), BF),
                         pltpu.SemaphoreType.DMA((6,))],
-        out_shape=[jax.ShapeDtypeStruct((batches, half, width), BF)] * 2,
-        compiler_params=pltpu.CompilerParams(vmem_limit_bytes=60 << 20),
+        out_shape=[jax.ShapeDtypeStruct((half, width), BF)] * 2,
+        compiler_params=pltpu.CompilerParams(vmem_limit_bytes=40 << 20),
         cost_estimate=pl.CostEstimate(
-            flops=2 * batches * rows * width * (rows + 3 * share),
-            bytes_accessed=2 * batches * rows * (2 * width + 3 * share) + 6 * width * share,
+            flops=2 * rows * width * (rows + 3 * share),
+            bytes_accessed=2 * rows * (width + 3 * share) + 6 * width * share,
             transcendentals=0,
         ),
         name="project_back",
-    )(part, xw, dq, dk, dv, idx_row, near_w, away_w)
-
-
-def weight_back_body(xw_ref, dq_ref, dk_ref, dv_ref, gw_ref, gb_ref, acc):
-    batch, share = pl.program_id(0), dq_ref.shape[2]
-    for place, g_ref in enumerate((dq_ref, dk_ref, dv_ref)):
-        cols = slice(place * share, (place + 1) * share)
-        term = dot_lt(xw_ref[0], g_ref[0])
-        thin = jnp.sum(g_ref[0].astype(F32), axis=0, keepdims=True)
-
-        @pl.when(batch == 0)
-        def _():
-            acc[:, cols] = term
-            gb_ref[0:1, cols] = thin
-
-        @pl.when(batch > 0)
-        def _():
-            acc[:, cols] += term
-            gb_ref[0:1, cols] += thin
-
-        @pl.when(batch == pl.num_programs(0) - 1)
-        def _():
-            gw_ref[:, cols] = acc[:, cols].astype(BF)
-
-
-def weight_back(xw, dq, dk, dv):
-    batches, rows, width = xw.shape
-    share = dq.shape[2]
-    each = lambda shape: pl.BlockSpec((1,) + shape, lambda b: (b,) + (0,) * len(shape))
+    )(part, grads, idx_row, near_w, away_w)
+
+
+def weight_back_body(batches, *refs):
+    xw_refs, g_refs, (gw_ref, gb_ref) = refs[:batches], refs[batches:2 * batches], refs[2 * batches:]
+    total, thin = None, None
+    for xw_ref, g_ref in zip(xw_refs, g_refs):
+        term = dot_lt(xw_ref[...], g_ref[0])
+        line = jnp.sum(g_ref[0].astype(F32), axis=0, keepdims=True)
+        total = term if total is None else total + term
+        thin = line if thin is None else thin + line
+    gw_ref[...] = total.astype(BF)
+    gb_ref[...] = jnp.broadcast_to(thin, gb_ref.shape)
+
+
+def weight_back(xws, grads):
+    batches, (rows, width), share = len(xws), xws[0].shape, grads[0].shape[2]
+    whole = pl.BlockSpec((rows, width), lambda s: (0, 0))
+    each = pl.BlockSpec((1, rows, share), lambda s: (s, 0, 0))
     return pl.pallas_call(
-        weight_back_body,
-        grid=(batches,),
-        in_specs=[each((rows, width)), each((rows, share)), each((rows, share)), each((rows, share))],
-        out_specs=[pl.BlockSpec((width, 3 * share), lambda b: (0, 0)),
-                   pl.BlockSpec((8, 3 * share), lambda b: (0, 0))],
+        functools.partial(weight_back_body, batches),
+        grid=(3,),
+        in_specs=[whole] * batches + [each] * batches,
+        out_specs=[pl.BlockSpec((width, share), lambda s: (0, s)),
+                   pl.BlockSpec((8, share), lambda s: (0, s))],
         out_shape=[jax.ShapeDtypeStruct((width, 3 * share), BF), jax.ShapeDtypeStruct((8, 3 * share), F32)],
-        scratch_shapes=[pltpu.VMEM((width, 3 * share), F32)],
         compiler_params=pltpu.CompilerParams(vmem_limit_bytes=60 << 20),
         cost_estimate=pl.CostEstimate(
             flops=2 * batches * rows * width * 3 * share,
@@ -415,7 +404,7 @@
             transcendentals=0,
         ),
         name="weight_back",
-    )(xw, dq, dk, dv)
+    )(*xws, *grads)
 
 
 EPS = 1e-6
@@ -450,7 +439,7 @@
 
 def feed_body(chunk, part_ref, x_ref, near_ref, away_ref, dy_ref, thin_ref, bup_ref,
               unear_ref, uaway_ref, dnear_ref, daway_ref,
-              out_ref, dh_ref, low_ref, act_ref, dup_ref, dlow_ref, da_ref, cnear_ref, caway_ref,
+              out_ref, dh_ref, lmine_ref, ltheirs_ref, amine_ref, atheirs_ref, dup_ref, dlow_ref, da_ref, cnear_ref, caway_ref,
               sums_ref, bsum_ref, wo_near, wo_away, wup, wdown, slopes, sems):
     first_step = pl.program_id(0) == 0
     core = part_ref[0]
@@ -492,13 +481,27 @@
     norm_one, root_one = standard(x_ref[...].astype(F32) + attended)
     first = norm_one * gain_one + shift_one
     low = first.astype(BF)
-    low_ref[...] = low
+
+    def split(value, at, mine_ref, theirs_ref):
+        size = mine_ref.shape[1]
+        cols = slice(at % size, at % size + value.shape[1])
+
+        @pl.when(core == at // size)
+        def _():
+            mine_ref[:, cols] = value
+
+        @pl.when(core != at // size)
+        def _():
+            theirs_ref[:, cols] = value
+
+    split(low[:, :half_w], 0, lmine_ref, ltheirs_ref)
+    split(low[:, half_w:], half_w, lmine_ref, ltheirs_ref)
     lowered = None
     for c in range(wide // chunk):
         cols = slice(c * chunk, (c + 1) * chunk)
         act, slope = gauss_parts(dot(low, wup[:, cols]) + bup_ref[:, cols])
         act = act.astype(BF)
-        act_ref[:, cols] = act
+        split(act, c * chunk, amine_ref, atheirs_ref)
         slopes[:, cols] = slope.astype(BF)
         term = dot(act, wdown[cols, :])
         lowered = term if lowered is None else lowered + term
@@ -542,10 +545,11 @@
         grid=(rows // block,),
         in_specs=[pl.BlockSpec(memory_space=pltpu.SMEM), line(width), line(share), line(share), line(width),
                   fixed(thin.shape), fixed(bup.shape), anywhere, anywhere, anywhere, anywhere],
-        out_specs=[line(width), line(width), line(width), line(wide), line(wide), line(width), line(width),
+        out_specs=[line(width), line(width), line(width // 2), line(width // 2), line(wide // 2),
+                   line(wide // 2), line(wide), line(width), line(width),
                    line(share), line(share), fixed((8, width)), fixed((8, wide))],
-        out_shape=[shape(width, BF), shape(width, F32), shape(width, BF), shape(wide, BF), shape(wide, BF),
-                   shape(width, BF), shape(width, BF), shape(share, BF), shape(share, BF),
+        out_shape=[shape(width, BF), shape(width, F32), shape(width // 2, BF), shape(width // 2, BF),
+                   shape(wide // 2, BF), shape(wide // 2, BF), shape(wide, BF), shape(width, BF), shape(width, BF), shape(share, BF), shape(share, BF),
                    jax.ShapeDtypeStruct((8, width), F32), jax.ShapeDtypeStruct((8, wide), F32)],
         scratch_shapes=[pltpu.VMEM((share, width), BF), pltpu.VMEM((share, width), BF),
                         pltpu.VMEM((width, wide), BF), pltpu.VMEM((wide, width), BF),
@@ -603,51 +607,95 @@
     )(place, *parts)
 
 
-def gather_half(shard):
-    n, width = shard.shape
-    if lax.axis_size("fsdp") != 16:
-        return lax.all_gather(shard, "fsdp", axis=0, tiled=True)
+def tie(values, after=()):
+    return lax.optimization_barrier((values, after))[0]
+
+
+def reach_z(shard):
     first = jnp.stack([shard, shift_z(shard, 1)])
     second = jnp.stack([shift_z(shard, 2), shift_z(shard, 3)])
-    first = jnp.concatenate([first, swap_x(first)], axis=0)
-    second = jnp.concatenate([second, swap_y(second)], axis=0)
+    return first, second
+
+
+def reach_one(first, second):
+    return jnp.concatenate([first, swap_x(first)], axis=0), jnp.concatenate([second, swap_y(second)], axis=0)
+
+
+def reach_two(first, second):
+    return first, swap_y(first), swap_x(second), second
+
+
+def joined(parts):
+    n, width = parts[0].shape[1:]
     place = jnp.full((1,), lax.axis_index("fsdp"), jnp.int32)
-    whole = assemble(place, (first, swap_y(first), swap_x(second), second))
-    return whole.reshape(16 * n, width)
-
-
-def scatter_half(value):
+    return assemble(place, parts).reshape(16 * n, width)
+
+
+def pick(part, at, axis):
+    return lax.dynamic_index_in_dim(part, at, axis, keepdims=False)
+
+
+def corner():
+    place = lax.axis_index("fsdp")
+    return place // 4, (place // 2) % 2, place % 2
+
+
+def fold_one(value):
+    z, y, x = corner()
     rows, width = value.shape
-    count = lax.axis_size("fsdp")
-    n = rows // count
-    if count != 16:
-        return lax.psum_scatter(value.astype(BF), "fsdp", scatter_dimension=0, tiled=True).astype(F32)
-    place = lax.axis_index("fsdp")
-    z, y, x = place // 4, (place // 2) % 2, place % 2
-    cube = value.reshape(2, 2, 2, 2, n, width)
-    pick = lambda part, at, axis: lax.dynamic_index_in_dim(part, at, axis, keepdims=False)
-    first, second = cube[0], cube[1]
-    first = pick(first, y, 1) + swap_y(pick(first, 1 - y, 1).astype(BF)).astype(F32)
-    second = pick(second, x, 2) + swap_x(pick(second, 1 - x, 2).astype(BF)).astype(F32)
-    first = pick(first, x, 1) + swap_x(pick(first, 1 - x, 1).astype(BF)).astype(F32)
-    second = pick(second, y, 1) + swap_y(pick(second, 1 - y, 1).astype(BF)).astype(F32)
-    stack = jnp.concatenate([first, second], axis=0)
-    total = pick(stack, z, 0)
-    for k in (1, 2, 3):
-        total = total + shift_z(pick(stack, lax.rem(z + k, 4), 0).astype(BF), k).astype(F32)
+    cube = value.reshape(2, 2, 2, 2, rows // 16, width)
+    return (value,), (pick(cube[0], 1 - y, 1).astype(BF), pick(cube[1], 1 - x, 2).astype(BF))
+
+
+def fold_two(stay, sends, after=()):
+    z, y, x = corner()
+    rows, width = stay[0].shape
+    cube = stay[0].reshape(2, 2, 2, 2, rows // 16, width)
+    came = tie((swap_y(sends[0]), swap_x(sends[1])), after)
+    first = pick(cube[0], y, 1).astype(F32) + came[0].astype(F32)
+    second = pick(cube[1], x, 2).astype(F32) + came[1].astype(F32)
+    return (first, second), (pick(first, 1 - x, 1).astype(BF), pick(second, 1 - y, 1).astype(BF))
+
+
+def fold_cross(stay, sends):
+    z, y, x = corner()
+    first = pick(stay[0], x, 1) + swap_x(sends[0]).astype(F32)
+    second = pick(stay[1], y, 1) + swap_y(sends[1]).astype(F32)
+    return jnp.concatenate([first, second], axis=0)
+
+
+def fold_three(stack):
+    z = corner()[0]
+    return (pick(stack, z, 0),), tuple(pick(stack, lax.rem(z + k, 4), 0).astype(BF) for k in (1, 2, 3))
+
+
+def fold_end(stay, sends, after=()):
+    total = stay[0]
+    for came in tie([shift_z(send, k) for k, send in zip((1, 2, 3), sends)], after):
+        total = total + came.astype(F32)
     return total
 
 
-def positions(segments):
-    places = jnp.arange(segments.shape[0], dtype=jnp.int32)
-    counts = jnp.sum(segments[None, :] < segments[:, None], axis=1, dtype=jnp.int32)
-    return (places - counts).astype(F32)
-
-
-def turn_tables(segments):
+def spread_rows(segments, order):
+    rows = segments.shape[0]
+    ids = jnp.arange(SEG_COUNT, dtype=jnp.int32)
+    counts = jnp.sum(segments[:, None] == ids[None, :], axis=0, dtype=jnp.int32)
+    long_id = jnp.sum(jnp.where(counts == LONGEST, ids, 0))
+    starts = jnp.sum(jnp.where(ids[:, None] < ids[None, :], counts[:, None], 0), axis=0)
+    start = jnp.sum(jnp.where(ids == long_id, starts, 0))
+    places = jnp.arange(rows, dtype=jnp.int32)
+    table = jnp.stack([order, segments, places])
+    main = lax.dynamic_slice_in_dim(table, start, LONGEST, 1)
+    rest = jnp.where(places[None, :rows - LONGEST] < start, table[:, :rows - LONGEST], table[:, LONGEST:])
+    order, segments, places = jnp.concatenate([main, rest], axis=1)
+    origin = jnp.sum(jnp.where(segments[:, None] == ids[None, :], starts[None, :], 0), axis=1)
+    return order, segments, (places - origin).astype(F32)
+
+
+def turn_tables(position):
     halves = HEAD // 2
     freqs = jnp.exp(jnp.arange(halves, dtype=F32) * (-2.0 * math.log(10000.0) / HEAD))
-    phase = positions(segments)[:, None] * freqs[None, :]
+    phase = position[:, None] * freqs[None, :]
     cosine = jnp.tile(jnp.repeat(jnp.cos(phase), 2, axis=1), (1, 2))
     signs = jnp.tile(jnp.array([-1.0, 1.0], F32), halves)[None, :]
     sine = jnp.tile(jnp.repeat(jnp.sin(phase), 2, axis=1) * signs, (1, 2))
@@ -660,21 +708,30 @@
     core = lax.axis_index("seq")
     share = width // 2
     owners = 2 * lax.axis_size("fsdp")
+    staged = owners == 32
     part = jnp.full((1,), core, jnp.int32)
     thin = [i for i, piece in enumerate(shards) if piece.ndim == 1]
     sizes = [shards[i].shape[0] for i in thin]
     count = sum(sizes)
     n_qkv = shards[0].shape[0]
     room = n_qkv * 128
-
-    away_tokens = swap_cores(tokens[:, 0])
+    tokens, cotangent = tokens[:, 0], cotangent[:, 0]
+
     packed = jnp.concatenate([shards[i] for i in thin] + [jnp.zeros((room - count,), BF)])
-    q_near = gather_half(jnp.concatenate([shards[0], packed.reshape(n_qkv, 128)], axis=1))
+    q_shard = jnp.concatenate([shards[0], packed.reshape(n_qkv, 128)], axis=1)
+    u_shard = jnp.concatenate([shards[2], shards[6]], axis=1)
+    d_shard = shards[8]
+    if staged:
+        q_pair = reach_z(q_shard)
+        u_shard, d_shard = tie((u_shard, d_shard), q_pair)
+        q_parts = reach_two(*reach_one(*q_pair))
+        u_pair, d_pair = tie((reach_z(u_shard), reach_z(d_shard)), q_parts)
+        pairs = (reach_one(*u_pair), reach_one(*d_pair))
+        q_near = joined(q_parts)
+    else:
+        q_near = lax.all_gather(q_shard, "fsdp", axis=0, tiled=True)
     q_away = swap_cores(q_near)
-    u_near = gather_half(jnp.concatenate([shards[2], shards[6]], axis=1))
-    u_away = swap_cores(u_near)
-    d_near = gather_half(shards[8])
-    d_away = swap_cores(d_near)
+    away_tokens = swap_cores(tokens)
 
     slabs = [value[:, 3 * width:].reshape(owners // 2, room)[:, :count] for value in (q_near, q_away)]
     vectors = jnp.concatenate(
@@ -695,73 +752,119 @@
 
     kept = []
     for b in range(batches):
-        order = permutation[b, 0]
+        order, segments, position = spread_rows(segment_ids[b, 0], permutation[b, 0])
         place = jnp.where(
             order // half == core, order - core * half, order - (1 - core) * half + half
         )
-        segments = segment_ids[b, 0]
-        cosine, sine = turn_tables(segments)
+        cosine, sine = turn_tables(position)
         col, row = segments[:, None], segments[None, :]
         idx_col, idx_row = place[:, None], place[None, :]
-        xw = arrange(idx_col, tokens[b, 0], away_tokens[b])
+        xw = arrange(idx_col, tokens[b], away_tokens[b])
+        kept.append((idx_col, idx_row, col, row, cosine, sine, xw))
+    ctxs = []
+    for b in range(batches):
+        idx_col, idx_row, col, row, cosine, sine, xw = kept[b]
         q, k, v = project(part, xw, q_near, q_away, bias_own, cosine, sine)
+        if staged and b == 0:
+            q, pairs = tie((q, pairs))
+            u_parts, d_parts = reach_two(*pairs[0]), reach_two(*pairs[1])
+        if staged and b == 1:
+            u_parts, d_parts = tie((u_parts, d_parts), (ctxs[0][0], q))
+            u_near, d_near = joined(u_parts), joined(d_parts)
+            q, u_near, d_near = tie((q, u_near, d_near))
         near, away, ctxt, lse = attend(idx_col, q, k, v, col, row)
-        kept.append((idx_col, idx_row, col, row, cosine, sine, xw, q, k, v, ctxt, lse, near, swap_cores(away)))
-    join = lambda i: jnp.concatenate([item[i] for item in kept], axis=0)
-    near, away = join(12), join(13)
-    (outputs, grad_one, low, act, dup, dlow, da, cnear, caway, sums, bsum) = feed(
-        part, tokens[:, 0].reshape(batches * half, width), near, away,
-        cotangent[:, 0].reshape(batches * half, width), thin_rows, b_up, u_near, u_away, d_near, d_away,
+        kept[b] += (q, k, v, ctxt, lse)
+        ctxs.append((near, swap_cores(away)))
+    if not staged:
+        u_near = lax.all_gather(u_shard, "fsdp", axis=0, tiled=True)
+        d_near = lax.all_gather(d_shard, "fsdp", axis=0, tiled=True)
+    u_away, d_away = swap_cores(u_near), swap_cores(d_near)
+    near, away = (jnp.concatenate([item[i] for item in ctxs], axis=0) for i in range(2))
+    (outputs, grad_one, low_mine, low_theirs, act_mine, act_theirs, dup, dlow, da, cnear, caway, sums, bsum) = feed(
+        part, tokens.reshape(batches * half, width), near, away,
+        cotangent.reshape(batches * half, width), thin_rows, b_up, u_near, u_away, d_near, d_away,
     )
     caway = swap_cores(caway)
+
+    d_theirs = swap_cores(dot_lt(act_theirs, dlow).astype(BF))
+    uo_theirs = swap_cores(
+        jnp.concatenate([dot_lt(low_theirs, dup).astype(BF), dot_lt(away, da).astype(BF)], axis=1)
+    )
+    d_sum = (dot_lt(act_mine, dlow) + d_theirs.astype(F32)).astype(BF)
+    uo_sum = jnp.concatenate([
+        (dot_lt(low_mine, dup) + uo_theirs[:, :4 * width].astype(F32)).astype(BF),
+        (dot_lt(near, da) + uo_theirs[:, 4 * width:].astype(F32)).astype(BF),
+    ], axis=1)
+
+    def back(b, given):
+        idx_col, idx_row, col, row, cosine, sine, xw, q, k, v, ctxt, lse = kept[b]
+        return attend_back(
+            idx_col, q, k, v, col, row, lse, ctxt, *given, cosine, sine
+        )
+
+    givens = [(cnear[b * half:(b + 1) * half], caway[b * half:(b + 1) * half]) for b in range(batches)]
+    if staged:
+        given, d_step, uo_step = tie((givens[0], fold_one(d_sum), fold_one(uo_sum)))
+        first_back = back(0, given)
+        given, d_step, uo_step = tie((givens[1], fold_two(*d_step), fold_two(*uo_step)), first_back)
+        grads = [first_back, back(1, given)]
+        wide, lines = fold_cross(*uo_step), fold_cross(*d_step)
+        lines = [lines[:, i * n_qkv:(i + 1) * n_qkv] for i in range(4)]
+        du_step = fold_three(jnp.concatenate([wide] + lines, axis=2))
+        grads, du_step = tie((grads, du_step))
+    else:
+        grads = [back(b, givens[b]) for b in range(batches)]
+    xws = [item[6] for item in kept]
+    gw_own, gb_own = weight_back(xws, grads)
 
     def halves(value):
         size = value.shape[0] // 2
         return (lax.dynamic_slice_in_dim(value, core * size, size, 0),
                 lax.dynamic_slice_in_dim(value, (1 - core) * size, size, 0))
 
-    def summed(value):
-        mine, theirs = halves(value)
-        return mine.astype(F32) + swap_cores(theirs).astype(F32)
-
-    g_down = scatter_half(summed(dot_lt(act, dlow).astype(BF)))
-    g_up = scatter_half(summed(dot_lt(low, dup).astype(BF)))
-    g_out = scatter_half(
-        dot_lt(near, da).astype(BF).astype(F32) + swap_cores(dot_lt(away, da).astype(BF)).astype(F32)
-    )
-    backs = []
-    for b in range(batches):
-        idx_col, idx_row, col, row, cosine, sine, xw, q, k, v, ctxt, lse = kept[b][:12]
-        span = slice(b * half, (b + 1) * half)
-        backs.append(
-            attend_back(idx_col, q, k, v, col, row, lse, ctxt, cnear[span], caway[span], cosine, sine)
-        )
-    pile = lambda items: jnp.stack(items)
-    xws = pile([item[6] for item in kept])
-    dq, dk, dv = (pile([back[i] for back in backs]) for i in range(3))
-    gw_own, gb_own = weight_back(xws, dq, dk, dv)
-    mine, theirs = halves(gw_own)
-    theirs = swap_cores(theirs)
     blank = jnp.zeros((share,), F32)
-    columns, thin_columns = [], []
+    thin_columns = []
     for s in range(3):
         span = slice(s * share, (s + 1) * share)
-        columns += [jnp.where(core == 0, mine[:, span], theirs[:, span]),
-                    jnp.where(core == 0, theirs[:, span], mine[:, span])]
         thin_columns += [jnp.where(core == 0, gb_own[0, span], blank),
                          jnp.where(core == 0, blank, gb_own[0, span])]
     thin_grads = [jnp.concatenate(thin_columns), sums[0], sums[1], sums[2], bsum[0], sums[3], sums[4], sums[5]]
     slab = jnp.concatenate(
         [value.reshape(owners, -1) for value in thin_grads] + [jnp.zeros((owners, room - count), F32)], axis=1
     ).astype(BF).reshape(owners * n_qkv, 128)
-    columns.append(summed(slab).astype(BF))
-    g_qkv = scatter_half(jnp.concatenate(columns, axis=1).astype(F32))
-    near_grad, away_grad = project_back(
-        part, xws, dq, dk, dv, pile([item[1] for item in kept]), q_near, q_away
-    )
-    token_grad = (
-        grad_one.reshape(batches, half, width) + near_grad.astype(F32) + swap_cores(away_grad).astype(F32)
-    ).astype(BF)
+    mine, theirs = (jnp.concatenate(pair, axis=1) for pair in zip(halves(gw_own), halves(slab)))
+    theirs = swap_cores(theirs)
+    q_sum = jnp.concatenate([
+        mine[:, :3 * share], theirs[:, :3 * share],
+        (mine[:, 3 * share:].astype(F32) + theirs[:, 3 * share:].astype(F32)).astype(BF),
+    ], axis=1)
+    backs = [project_back(part, grads[0], kept[0][1], q_near, q_away)]
+    if staged:
+        last, q_step, backs = tie((grads[1], fold_one(q_sum), backs))
+        backs.append(project_back(part, last, kept[1][1], q_near, q_away))
+        q_step = fold_two(*q_step, backs[1])
+        q_last = fold_three(fold_cross(*q_step))
+        g_uo = fold_end(*du_step, q_last)
+        g_qkv = fold_end(*q_last, g_uo)
+        g_down = jnp.concatenate([g_uo[:, (5 + i) * width:(6 + i) * width] for i in range(4)], axis=0)
+    else:
+        backs.append(project_back(part, grads[1], kept[1][1], q_near, q_away))
+        summed = lambda value: lax.psum_scatter(
+            value.astype(BF), "fsdp", scatter_dimension=0, tiled=True
+        ).astype(F32)
+        g_qkv, g_down, g_uo = summed(q_sum), summed(d_sum), summed(uo_sum)
+    own, other = g_qkv[:, :3 * share], g_qkv[:, 3 * share:6 * share]
+    columns = []
+    for s in range(3):
+        span = slice(s * share, (s + 1) * share)
+        columns += [jnp.where(core == 0, own[:, span], other[:, span]),
+                    jnp.where(core == 0, other[:, span], own[:, span])]
+    g_out, g_up = g_uo[:, 4 * width:5 * width], g_uo[:, :4 * width]
+    grad_one = grad_one.reshape(batches, half, width)
+    token_grad = jnp.stack([
+        (grad_one[b] + backs[b][0].astype(F32) + swap_cores(backs[b][1]).astype(F32)).astype(BF)
+        for b in range(batches)
+    ])
     flat = g_qkv[:, 3 * width:].reshape(room)
     thin_out, at = [], 0
     for size in sizes:
@@ -770,7 +873,7 @@
     g_bqkv, g_bout, g_g1, g_s1, g_bup, g_bdown, g_g2, g_s2 = thin_out
     return (
         outputs.reshape(batches, 1, half, width), token_grad[:, None],
-        g_qkv[:, :3 * width], g_bqkv, g_out, g_bout, g_g1, g_s1, g_up, g_bup, g_down, g_bdown, g_g2, g_s2,
+        jnp.concatenate(columns, axis=1), g_bqkv, g_out, g_bout, g_g1, g_s1, g_up, g_bup, g_down, g_bdown, g_g2, g_s2,
     )
 
 

time: 552 us -> 477 us (0.86)
  waiting for transfers between devices: 105 us -> 41.9 us
  Pallas kernels: 251 us -> 227 us
  starting transfers between devices: 70.8 us -> 60.5 us
  other arithmetic: 30.5 us -> 40.6 us
  matrix products: 18.4 us -> 25.1 us
    ppermute x14 -> x12, waiting for transfers between devices: 50.9 us -> 8.57 us  [swap_y(): return lax.ppermute(value, 'fsdp', [(i, i ^ 2) for i in range(16)])]
    pallas_call x2, Pallas kernels: 74.5 us -> 57.5 us  [attend_back(): pl.pallas_call(functools.partial(attend_back_body, block), grid=(pairs,),...]
    ppermute x21 -> x15, waiting for transfers between devices: 30.9 us -> 15.8 us  [shift_z(): lax.ppermute(value, 'fsdp', [(i, (i + 4 * k) % 16) for i in range(16)])]
    pallas_call x2, Pallas kernels: 63.9 us -> 52.4 us  [attend(): pl.pallas_call(functools.partial(attend_body, block), grid=(pairs,), in_s...]
    concatenate x7 -> x15, other arithmetic: 0.43 us -> 9.67 us  [the longest x3 3.28 us: reach_one(): jnp.concatenate([second, swap_y(second)], axis=0)]
    pallas_call x1, Pallas kernels: 53.9 us -> 62 us  [feed(): pl.pallas_call(functools.partial(feed_body, chunk), grid=(rows // block,)...]
    ppermute x14 -> x12, waiting for transfers between devices: 22.2 us -> 15 us  [swap_x(): return lax.ppermute(value, 'fsdp', [(i, i ^ 1) for i in range(16)])]
    dot_general x4 -> x6, matrix products: 18.4 us -> 25.1 us  [dot_lt(): lax.dot_general(left, right, (((0,), (0,)), ((), ())), preferred_element_...]
  transfers between devices with their start and end apart: 62 -> 51, of which waited for: 23 -> 13; matrix products, arithmetic and copies ran while one was open for 15% -> 17% of each run, Pallas kernels for 36% -> 31%
where the time goes in v3:
time: 477 us; the launch traced here: 469 us
  Pallas kernels  227 us (48%)
  local copies, waits for them, and re-layouts  67.4 us (14%)
  starting transfers between devices  60.5 us (13%)
  waiting for transfers between devices  41.9 us (9%)
  other arithmetic  40.6 us (9%)
  matrix products  25.1 us (5%)
  between operations  6.37 us (1%)
    pallas_call x1, Pallas kernels, feed(): pl.pallas_call(functools.partial(feed_body, chunk), grid=(rows // block,)...  62 us
    pallas_call x2, Pallas kernels, attend_back(): pl.pallas_call(functools.partial(attend_back_body, block), grid=(pairs,),...  57.5 us
    pallas_call x2, Pallas kernels, attend(): pl.pallas_call(functools.partial(attend_body, block), grid=(pairs,), in_s...  52.4 us
    ppermute x15, starting transfers between devices, shift_z(): lax.ppermute(value, 'fsdp', [(i, (i + 4 * k) % 16) for i in range(16)])  31.5 us
    dot_general x6, matrix products, dot_lt(): lax.dot_general(left, right, (((0,), (0,)), ((), ())), preferred_element_...  25.1 us
    pallas_call x2, Pallas kernels, project_back(): pl.pallas_call(functools.partial(project_back_body, block), in_specs=[sme...  17.7 us
    unnamed x101, local copies, waits for them, and re-layouts  16.6 us
    ppermute x15, waiting for transfers between devices, shift_z(): lax.ppermute(value, 'fsdp', [(i, (i + 4 * k) % 16) for i in range(16)])  15.8 us
  transfers between devices with their start and end apart: 51, of which 13 were waited for; matrix products, arithmetic and copies ran while one was open for 17% of the time, Pallas kernels for 31%

profile of v3, /device:TPU:0, one launch (start us, length us, event | category | flops | bytes accessed | tf_op | source)
XLA Modules:
  0.0 468.6 jit_solution(2577409576507043130)
XLA Ops:
  0.7 5.4 %concatenate.92 = bf16[3072]{0:T(1024)(128)(2,1)S(1)} concatenate(bf16[72]{0:T(256)(128)(2,1)} %param.23, bf16[24]{0:T(256)(128)(2,1)} %param.25, bf16[24]{0:T(256)(128)(2,1)} %param.26, bf16[24]{0:T(256)(128)(2,1)} %param.27, bf16[96]{0:T(256)(128)(2,1)} %param.29, bf16[24]{0:T(256)(128)(2,1)} %param.31, bf16[24]{0:T(256)(128)(2,1)} %param.32, bf16[24]{0:T(256)(128)(2,1)} %param.33, ...), dimensions={0} | concatenate | bytes 12288 | tf_op jit(solution)/shard_map/concatenate | solution.py:720
  7.6 4.1 collective-permute-start.4
  31.6 2.6 fusion.7
  39.0 2.9 collective-permute-start.14
  43.6 5.1 %collective-permute-done.13 = bf16[96,768]{1,0:T(8,128)(2,1)S(1)} collective-permute-done((bf16[96,768]{1,0:T(8,128)(2,1)S(1)}, bf16[96,768]{1,0:T(8,128)(2,1)S(1)}, u32[]{:S(2)}, u32[]{:S(2)}) %collective-permute-start.13) | collective-permute-done | bytes 147488 | tf_op jit(solution)/shard_map/ppermute | solution.py:580
  50.3 3.9 collective-permute-start.10
  54.9 3.4 collective-permute-start.11
  65.7 4.0 collective-permute-done.9
  94.3 6.6 %collective-permute-done.15 = bf16[2,24,3840]{2,1,0:T(8,128)(2,1)S(1)} collective-permute-done((bf16[2,24,3840]{2,1,0:T(8,128)(2,1)}, bf16[2,24,3840]{2,1,0:T(8,128)(2,1)S(1)}, u32[]{:S(2)}, u32[]{:S(2)}) %collective-permute-start.15) | collective-permute-done | bytes 368672 | tf_op jit(solution)/shard_map/ppermute | solution.py:572
  103.9 4.4 arrange.3.xw_ref.refs_1_
  109.5 4.2 arrange.2.xw_ref.refs_0_
  120.2 5.5 %project.2 = (bf16[1280,384]{1,0:T(8,128)(2,1)S(1)}, bf16[1280,384]{1,0:T(8,128)(2,1)S(1)}, bf16[1280,384]{1,0:T(8,128)(2,1)S(1)}) custom-call(s32[1]{0:T(128)} %bitcast.part_ref, bf16[1280,768]{1,0:T(8,128)(2,1)S(1)} %copy-done.11, bf16[384,2432]{1,0:T(8,128)(2,1)} %bitcast.17.near_ref.wnear_ref, ...), custom_call_target="tpu_custom_call" | custom-call | flops 2264924160 | bytes 6684672 | tf_op jit(solution)/shard_map/project/pallas_call | solution.py:117
  132.6 5.5 %project.3 = (bf16[1280,384]{1,0:T(8,128)(2,1)S(1)}, bf16[1280,384]{1,0:T(8,128)(2,1)S(1)}, bf16[1280,384]{1,0:T(8,128)(2,1)S(1)}) custom-call(s32[1]{0:T(128)} %bitcast.part_ref, bf16[1280,768]{1,0:T(8,128)(2,1)S(1)} %copy-done.9, bf16[384,2432]{1,0:T(8,128)(2,1)} %bitcast.17.near_ref.wnear_ref, ...), custom_call_target="tpu_custom_call" | custom-call | flops 2264924160 | bytes 6684672 | tf_op jit(solution)/shard_map/project/pallas_call | solution.py:117
  141.0 26.2 %attend.2 = (bf16[640,384]{1,0:T(8,128)(2,1)}, bf16[640,384]{1,0:T(8,128)(2,1)}, bf16[384,1280]{1,0:T(8,128)(2,1)}, f32[3,8,1280]{2,1,0:T(8,128)}) custom-call(s32[1280,1]{1,0:T(8,128)} %get-tuple-element.355.idx_ref, bf16[1280,384]{1,0:T(8,128)(2,1)} %copy-done.15, bf16[1280,384]{1,0:T(8,128)(2,1)} %copy-done.16, bf16[1280,384]{1,0:T(8,128)(2,1)} %copy-done.17, ...), custom_call_target="tpu_custom_call" | custom-call | flops 7549747200 | bytes 5898240 | tf_op jit(solution)/shard_map/attend/pallas_call | solution.py:189
  167.2 2.8 assemble.5
  170.0 2.9 assemble.4
  174.7 26.2 %attend.3 = (bf16[640,384]{1,0:T(8,128)(2,1)}, bf16[640,384]{1,0:T(8,128)(2,1)}, bf16[384,1280]{1,0:T(8,128)(2,1)}, f32[3,8,1280]{2,1,0:T(8,128)}) custom-call(s32[1280,1]{1,0:T(8,128)} %get-tuple-element.354.idx_ref, bf16[1280,384]{1,0:T(8,128)(2,1)} %copy-done.12, bf16[1280,384]{1,0:T(8,128)(2,1)} %copy-done.13, bf16[1280,384]{1,0:T(8,128)(2,1)} %copy-done.14, ...), custom_call_target="tpu_custom_call" | custom-call | flops 7549747200 | bytes 5898240 | tf_op jit(solution)/shard_map/attend/pallas_call | solution.py:189
  205.0 62.0 %feed.1 = (bf16[1280,768]{1,0:T(8,128)(2,1)}, f32[1280,768]{1,0:T(8,128)}, bf16[1280,384]{1,0:T(8,128)(2,1)}, bf16[1280,384]{1,0:T(8,128)(2,1)}, bf16[1280,1536]...) custom-call(s32[1]{0:T(128)} %bitcast.part_ref, ...), custom_call_target="tpu_custom_call" | custom-call | flops 27179089920 | bytes 41287680 | tf_op jit(solution)/shard_map/feed/pallas_call | solution.py:543
  267.0 7.7 %convolution_convert_fusion.1 = bf16[1536,768]{1,0:T(8,128)(2,1)} fusion(bf16[1280,1536]{1,0:T(8,128)(2,1)} %get-tuple-element.151, bf16[1280,768]{1,0:T(8,128)(2,1)} %get-tuple-element.150), kind=kOutput, calls=%fused_computation.6 | convolution fusion | flops 3021078528 | bytes 8257536 | tf_op jit(solution)/shard_map/dot_general | solution.py:31
  274.7 3.5 convolution_convert_fusion
  289.2 6.0 %add_convert_fusion.1 = bf16[1536,768]{1,0:T(8,128)(2,1)S(1)} fusion(bf16[1536,768]{1,0:T(8,128)(2,1)} %collective-permute-done.28, bf16[1280,1536]{1,0:T(8,128)(2,1)S(1)} %copy-done.44, bf16[1280,768]{1,0:T(8,128)(2,1)} %get-tuple-element.150), kind=kOutput, calls=%fused_computation.1 | convolution fusion | flops 3023437824 | bytes 10616832 | tf_op jit(solution)/shard_map/dot_general | solution.py:31
  300.6 4.8 %add_convert_fusion = bf16[384,3072]{1,0:T(8,128)(2,1)S(1)} fusion(bf16[1280,384]{1,0:T(8,128)(2,1)S(1)} %copy-done.31, bf16[1280,3072]{1,0:T(8,128)(2,1)S(1)} %bitcast.186, bf16[384,3840]{1,0:T(8,128)(2,1)} %collective-permute-done.29), kind=kOutput, calls=%fused_computation | convolution fusion | flops 3023437824 | bytes 13565952 | tf_op jit(solution)/shard_map/dot_general | solution.py:31
  311.9 28.9 %attend_back.2.refs_2_.g_ref = bf16[3,1280,384]{2,1,0:T(8,128)(2,1)} custom-call(s32[1280,1]{1,0:T(8,128)} %get-tuple-element.355.idx_ref, bf16[1280,384]{1,0:T(8,128)(2,1)} %copy-done.15, bf16[1280,384]{1,0:T(8,128)(2,1)} %copy-done.16, bf16[1280,384]{1,0:T(8,128)(2,1)} %copy-done.17, s32[1280,1]{1,0:T(8,128)} %copy.89.seg_col_ref, s32[1,1280]{1,0:T(1,128)} %copy-done.40, ...), custom_call_target="tpu_custom_call" | custom-call | flops 17616076800 | bytes 8847360 | tf_op jit(solution)/shard_map/attend_back/pallas_call | solution.py:302
  355.0 28.7 %attend_back.3.refs_3_.g_ref = bf16[3,1280,384]{2,1,0:T(8,128)(2,1)} custom-call(s32[1280,1]{1,0:T(8,128)} %get-tuple-element.354.idx_ref, bf16[1280,384]{1,0:T(8,128)(2,1)} %copy-done.12, bf16[1280,384]{1,0:T(8,128)(2,1)} %copy-done.13, bf16[1280,384]{1,0:T(8,128)(2,1)} %copy-done.14, s32[1280,1]{1,0:T(8,128)} %copy.97.seg_col_ref, s32[1,1280]{1,0:T(1,128)} %copy-done.39, ...), custom_call_target="tpu_custom_call" | custom-call | flops 17616076800 | bytes 8847360 | tf_op jit(solution)/shard_map/attend_back/pallas_call | solution.py:302
  389.4 10.4 %weight_back.1 = (bf16[768,1152]{1,0:T(8,128)(2,1)}, f32[8,1152]{1,0:T(8,128)}) custom-call(bf16[1280,768]{1,0:T(8,128)(2,1)} %copy-done.10, bf16[1280,768]{1,0:T(8,128)(2,1)} %copy-done.8, bf16[3,1280,384]{2,1,0:T(8,128)(2,1)} %attend_back.2.refs_2_.g_ref, bf16[3,1280,384]{2,1,0:T(8,128)(2,1)} %attend_back.3.refs_3_.g_ref), custom_call_target="tpu_custom_call" | custom-call | flops 4529848320 | bytes 11599872 | tf_op jit(solution)/shard_map/weight_back/pallas_call | solution.py:393
  404.5 6.3 %collective-permute-start.48 = (bf16[24,6912]{1,0:T(8,128)(2,1)}, bf16[24,6912]{1,0:T(8,128)(2,1)S(1)}, u32[]{:S(2)}, u32[]{:S(2)}) collective-permute-start(bf16[24,6912]{1,0:T(8,128)(2,1)} %get-tuple-element.199), channel_id=1, source_target_pairs={{0,4},{1,5},{2,6},{3,7},{4,8},{5,9},{6,10},{7,11},{8,12},{9,13},{1... | collective-permute-start | bytes 995336 | tf_op jit(solution)/shard_map/ppermute | solution.py:580
  410.8 3.4 collective-permute-start.49
  414.1 8.9 %project_back.2 = (bf16[640,768]{1,0:T(8,128)(2,1)S(1)}, bf16[640,768]{1,0:T(8,128)(2,1)S(1)}) custom-call(s32[1]{0:T(128)} %bitcast.part_ref, bf16[3,1280,384]{2,1,0:T(8,128)(2,1)S(1)} %copy-done.18, s32[1,1280]{1,0:T(1,128)S(1)} %get-tuple-element.324.row_ref, bf16[384,2432]{1,0:T(8,128)(2,1)} %bitcast.17.near_ref.wnear_ref, ...), custom_call_target="tpu_custom_call" | custom-call | flops 4781506560 | bytes 6684672 | tf_op jit(solution)/shard_map/project_back/pallas_call | solution.py:361
  426.1 8.9 %project_back.3 = (bf16[640,768]{1,0:T(8,128)(2,1)S(1)}, bf16[640,768]{1,0:T(8,128)(2,1)S(1)}) custom-call(s32[1]{0:T(128)} %bitcast.part_ref, bf16[3,1280,384]{2,1,0:T(8,128)(2,1)S(1)} %copy-done.19, s32[1,1280]{1,0:T(1,128)S(1)} %get-tuple-element.320.row_ref, bf16[384,2432]{1,0:T(8,128)(2,1)} %bitcast.17.near_ref.wnear_ref, ...), custom_call_target="tpu_custom_call" | custom-call | flops 4781506560 | bytes 6684672 | tf_op jit(solution)/shard_map/project_back/pallas_call | solution.py:361
  438.6 5.8 %collective-permute-done.43 = bf16[2,24,2432]{2,1,0:T(8,128)(2,1)S(1)} collective-permute-done((bf16[2,24,2432]{2,1,0:T(8,128)(2,1)S(1)}, bf16[2,24,2432]{2,1,0:T(8,128)(2,1)S(1)}, u32[]{:S(2)}, u32[]{:S(2)}) %collective-permute-start.43) | collective-permute-done | bytes 233504 | tf_op jit(solution)/shard_map/ppermute | solution.py:572
  446.0 5.2 %collective-permute-done.44 = bf16[2,24,2432]{2,1,0:T(8,128)(2,1)S(1)} collective-permute-done((bf16[2,24,2432]{2,1,0:T(8,128)(2,1)S(1)}, bf16[2,24,2432]{2,1,0:T(8,128)(2,1)S(1)}, u32[]{:S(2)}, u32[]{:S(2)}) %collective-permute-start.44) | collective-permute-done | bytes 233504 | tf_op jit(solution)/shard_map/ppermute | solution.py:576
  459.5 4.5 collective-permute-done.46
  (376 shorter events, 151.7 us)
Async XLA Ops:
  7.6 28.3 %collective-permute-start.4 = (bf16[24,2432]{1,0:T(8,128)(2,1)}, bf16[24,2432]{1,0:T(8,128)(2,1)}, u32[]{:S(2)}, u32[]{:S(2)}) collective-permute-start(bf16[24,2432]{1,0:T(8,128)(2,1)} %get-tuple-element.312), channel_id=1, source_target_pairs={{0,8},{1,9},{2,10},{3,11},{4,12},{5,13},{6,14},{7,15},{8,0},{9,1},... | collective-permute-start | bytes 350216 | tf_op jit(solution)/shard_map/ppermute | solution.py:580
  11.7 24.3 %collective-permute-start.5 = (bf16[24,2432]{1,0:T(8,128)(2,1)}, bf16[24,2432]{1,0:T(8,128)(2,1)}, u32[]{:S(2)}, u32[]{:S(2)}) collective-permute-start(bf16[24,2432]{1,0:T(8,128)(2,1)} %get-tuple-element.312), channel_id=1, source_target_pairs={{0,12},{1,13},{2,14},{3,15},{4,0},{5,1},{6,2},{7,3},{8,4},{9,5},{1... | collective-permute-start | bytes 350216 | tf_op jit(solution)/shard_map/ppermute | solution.py:580
  13.1 23.9 %collective-permute-start.1 = (bf16[24,2432]{1,0:T(8,128)(2,1)}, bf16[24,2432]{1,0:T(8,128)(2,1)}, u32[]{:S(2)}, u32[]{:S(2)}) collective-permute-start(bf16[24,2432]{1,0:T(8,128)(2,1)} %get-tuple-element.312), channel_id=1, source_target_pairs={{0,4},{1,5},{2,6},{3,7},{4,8},{5,9},{6,10},{7,11},{8,12},{9,13},{1... | collective-permute-start | bytes 350216 | tf_op jit(solution)/shard_map/ppermute | solution.py:580
  13.7 88.2 %collective-permute-start = (bf16[2,640,768]{2,1,0:T(8,128)(2,1)}, bf16[2,640,768]{2,1,0:T(8,128)(2,1)}, u32[]{:S(2)}, u32[]{:S(2)}) collective-permute-start(bf16[2,640,768]{2,1,0:T(8,128)(2,1)} %bitcast.203), channel_id=1, source_target_pairs={{0,16},{16,0},{1,17},{17,1},{2,18},{18,2},{3,19},{19,3},{4,20},{20... | collective-permute-start | bytes 5898248 | tf_op jit(solution)/shard_map/ppermute | solution.py:568
  42.1 17.0 %collective-permute-start.6 = (bf16[2,24,2432]{2,1,0:T(8,128)(2,1)S(1)}, bf16[2,24,2432]{2,1,0:T(8,128)(2,1)S(1)}, u32[]{:S(2)}, u32[]{:S(2)}) collective-permute-start(bf16[2,24,2432]{2,1,0:T(8,128)(2,1)S(1)} %pad_maximum_fusion.17), channel_id=1, source_target_pairs={{0,2},{1,3},{2,0},{3,1},{4,6},{5,7},{6,4},{7,5},{8,10},{9,11},{10,... | collective-permute-start | bytes 700424 | tf_op jit(solution)/shard_map/ppermute | solution.py:576
  74.1 15.5 %collective-permute-start.18 = (bf16[2,96,768]{2,1,0:T(8,128)(2,1)}, bf16[2,96,768]{2,1,0:T(8,128)(2,1)}, u32[]{:S(2)}, u32[]{:S(2)}) collective-permute-start(bf16[2,96,768]{2,1,0:T(8,128)(2,1)} %pad_maximum_fusion.14), channel_id=1, source_target_pairs={{0,2},{1,3},{2,0},{3,1},{4,6},{5,7},{6,4},{7,5},{8,10},{9,11},{10,... | collective-permute-start | bytes 884744 | tf_op jit(solution)/shard_map/ppermute | solution.py:576
  75.6 16.4 %collective-permute-start.17 = (bf16[2,96,768]{2,1,0:T(8,128)(2,1)}, bf16[2,96,768]{2,1,0:T(8,128)(2,1)}, u32[]{:S(2)}, u32[]{:S(2)}) collective-permute-start(bf16[2,96,768]{2,1,0:T(8,128)(2,1)} %pad_maximum_fusion.13), channel_id=1, source_target_pairs={{0,1},{1,0},{2,3},{3,2},{4,5},{5,4},{6,7},{7,6},{8,9},{9,8},{10,11... | collective-permute-start | bytes 884744 | tf_op jit(solution)/shard_map/ppermute | solution.py:572
  76.4 16.7 %collective-permute-start.16 = (bf16[2,24,3840]{2,1,0:T(8,128)(2,1)}, bf16[2,24,3840]{2,1,0:T(8,128)(2,1)}, u32[]{:S(2)}, u32[]{:S(2)}) collective-permute-start(bf16[2,24,3840]{2,1,0:T(8,128)(2,1)} %pad_maximum_fusion.11), channel_id=1, source_target_pairs={{0,2},{1,3},{2,0},{3,1},{4,6},{5,7},{6,4},{7,5},{8,10},{9,11},{10,... | collective-permute-start | bytes 1105928 | tf_op jit(solution)/shard_map/ppermute | solution.py:576
  88.0 27.0 %collective-permute-start.8 = (bf16[384,2432]{1,0:T(8,128)(2,1)}, bf16[384,2432]{1,0:T(8,128)(2,1)}, u32[]{:S(2)}, u32[]{:S(2)}) collective-permute-start(bf16[384,2432]{1,0:T(8,128)(2,1)} %bitcast.17.near_ref.wnear_ref), channel_id=1, source_target_pairs={{0,16},{16,0},{1,17},{17,1},{2,18},{18,2},{3,19},{19,3},{4,20},{20... | collective-permute-start | bytes 5603336 | tf_op jit(solution)/shard_map/ppermute | solution.py:568
  128.6 38.6 %collective-permute-start.19 = (bf16[4,24,3840]{2,1,0:T(8,128)(2,1)S(1)}, bf16[4,24,3840]{2,1,0:T(8,128)(2,1)S(1)}, u32[]{:S(2)}, u32[]{:S(2)}) collective-permute-start(bf16[4,24,3840]{2,1,0:T(8,128)(2,1)S(1)} %pad_maximum_fusion.4.ax_ref), channel_id=1, source_target_pairs={{0,2},{1,3},{2,0},{3,1},{4,6},{5,7},{6,4},{7,5},{8,10},{9,11},{10,... | collective-permute-start | bytes 2211848 | tf_op jit(solution)/shard_map/ppermute | solution.py:576
  130.1 37.1 %collective-permute-start.20 = (bf16[4,24,3840]{2,1,0:T(8,128)(2,1)S(1)}, bf16[4,24,3840]{2,1,0:T(8,128)(2,1)}, u32[]{:S(2)}, u32[]{:S(2)}) collective-permute-start(bf16[4,24,3840]{2,1,0:T(8,128)(2,1)S(1)} %pad_maximum_fusion.5.by_ref), channel_id=1, source_target_pairs={{0,1},{1,0},{2,3},{3,2},{4,5},{5,4},{6,7},{7,6},{8,9},{9,8},{10,11... | collective-permute-start | bytes 2211848 | tf_op jit(solution)/shard_map/ppermute | solution.py:572
  131.3 35.9 %collective-permute-start.21 = (bf16[4,96,768]{2,1,0:T(8,128)(2,1)S(1)}, bf16[4,96,768]{2,1,0:T(8,128)(2,1)}, u32[]{:S(2)}, u32[]{:S(2)}) collective-permute-start(bf16[4,96,768]{2,1,0:T(8,128)(2,1)S(1)} %pad_maximum_fusion.6.ax_ref), channel_id=1, source_target_pairs={{0,2},{1,3},{2,0},{3,1},{4,6},{5,7},{6,4},{7,5},{8,10},{9,11},{10,... | collective-permute-start | bytes 1769480 | tf_op jit(solution)/shard_map/ppermute | solution.py:576
  131.8 35.4 %collective-permute-start.22 = (bf16[4,96,768]{2,1,0:T(8,128)(2,1)S(1)}, bf16[4,96,768]{2,1,0:T(8,128)(2,1)}, u32[]{:S(2)}, u32[]{:S(2)}) collective-permute-start(bf16[4,96,768]{2,1,0:T(8,128)(2,1)S(1)} %pad_maximum_fusion.7.by_ref), channel_id=1, source_target_pairs={{0,1},{1,0},{2,3},{3,2},{4,5},{5,4},{6,7},{7,6},{8,9},{9,8},{10,11... | collective-permute-start | bytes 1769480 | tf_op jit(solution)/shard_map/ppermute | solution.py:572
  173.0 30.9 %collective-permute-start.25 = (bf16[384,3840]{1,0:T(8,128)(2,1)}, bf16[384,3840]{1,0:T(8,128)(2,1)}, u32[]{:S(2)}, u32[]{:S(2)}) collective-permute-start(bf16[384,3840]{1,0:T(8,128)(2,1)} %bitcast.39.unear_ref), channel_id=1, source_target_pairs={{0,16},{16,0},{1,17},{17,1},{2,18},{18,2},{3,19},{19,3},{4,20},{20... | collective-permute-start | bytes 8847368 | tf_op jit(solution)/shard_map/ppermute | solution.py:568
  173.0 30.8 %collective-permute-start.26 = (bf16[1536,768]{1,0:T(8,128)(2,1)}, bf16[1536,768]{1,0:T(8,128)(2,1)}, u32[]{:S(2)}, u32[]{:S(2)}) collective-permute-start(bf16[1536,768]{1,0:T(8,128)(2,1)} %bitcast.40.dnear_ref), channel_id=1, source_target_pairs={{0,16},{16,0},{1,17},{17,1},{2,18},{18,2},{3,19},{19,3},{4,20},{20... | collective-permute-start | bytes 7077896 | tf_op jit(solution)/shard_map/ppermute | solution.py:568
  174.7 28.9 %collective-permute-start.23 = (bf16[640,384]{1,0:T(8,128)(2,1)}, bf16[640,384]{1,0:T(8,128)(2,1)S(1)}, u32[]{:S(2)}, u32[]{:S(2)}) collective-permute-start(bf16[640,384]{1,0:T(8,128)(2,1)} %get-tuple-element.139), channel_id=1, source_target_pairs={{0,16},{16,0},{1,17},{17,1},{2,18},{18,2},{3,19},{19,3},{4,20},{20... | collective-permute-start | bytes 1474568 | tf_op jit(solution)/shard_map/ppermute | solution.py:568
  274.6 14.5 %collective-permute-start.28 = (bf16[1536,768]{1,0:T(8,128)(2,1)}, bf16[1536,768]{1,0:T(8,128)(2,1)}, u32[]{:S(2)}, u32[]{:S(2)}) collective-permute-start(bf16[1536,768]{1,0:T(8,128)(2,1)} %convolution_convert_fusion.1), channel_id=1, source_target_pairs={{0,16},{16,0},{1,17},{17,1},{2,18},{18,2},{3,19},{19,3},{4,20},{20... | collective-permute-start | bytes 7077896 | tf_op jit(solution)/shard_map/ppermute | solution.py:568
  281.0 17.4 %collective-permute-start.29 = (bf16[384,3840]{1,0:T(8,128)(2,1)}, bf16[384,3840]{1,0:T(8,128)(2,1)}, u32[]{:S(2)}, u32[]{:S(2)}) collective-permute-start(bf16[384,3840]{1,0:T(8,128)(2,1)} %pad_maximum_fusion.1), channel_id=1, source_target_pairs={{0,16},{16,0},{1,17},{17,1},{2,18},{18,2},{3,19},{19,3},{4,20},{20... | collective-permute-start | bytes 8847368 | tf_op jit(solution)/shard_map/ppermute | solution.py:568
  307.8 40.8 %collective-permute-start.32 = (bf16[2,2,24,3840]{3,2,0,1:T(8,128)(2,1)}, bf16[2,2,24,3840]{3,2,0,1:T(8,128)(2,1)S(1)}, u32[]{:S(2)}, u32[]{:S(2)}) collective-permute-start(bf16[2,2,24,3840]{3,2,0,1:T(8,128)(2,1)} %copy_bitcast_fusion.3), channel_id=1, source_target_pairs={{0,2},{1,3},{2,0},{3,1},{4,6},{5,7},{6,4},{7,5},{8,10},{9,11},{10,... | collective-permute-start | bytes 2211848 | tf_op jit(solution)/shard_map/ppermute | solution.py:576
  309.3 39.2 %collective-permute-start.33 = (bf16[2,2,24,3840]{3,2,0,1:T(8,128)(2,1)}, bf16[2,2,24,3840]{3,2,0,1:T(8,128)(2,1)}, u32[]{:S(2)}, u32[]{:S(2)}) collective-permute-start(bf16[2,2,24,3840]{3,2,0,1:T(8,128)(2,1)} %copy_bitcast_fusion.2), channel_id=1, source_target_pairs={{0,1},{1,0},{2,3},{3,2},{4,5},{5,4},{6,7},{7,6},{8,9},{9,8},{10,11... | collective-permute-start | bytes 2211848 | tf_op jit(solution)/shard_map/ppermute | solution.py:572
  310.6 32.0 %collective-permute-start.30 = (bf16[2,2,96,768]{3,2,0,1:T(8,128)(2,1)}, bf16[2,2,96,768]{3,2,0,1:T(8,128)(2,1)}, u32[]{:S(2)}, u32[]{:S(2)}) collective-permute-start(bf16[2,2,96,768]{3,2,0,1:T(8,128)(2,1)} %copy_bitcast_fusion.7), channel_id=1, source_target_pairs={{0,2},{1,3},{2,0},{3,1},{4,6},{5,7},{6,4},{7,5},{8,10},{9,11},{10,... | collective-permute-start | bytes 1769480 | tf_op jit(solution)/shard_map/ppermute | solution.py:576
  311.1 31.5 %collective-permute-start.31 = (bf16[2,2,96,768]{3,2,0,1:T(8,128)(2,1)}, bf16[2,2,96,768]{3,2,0,1:T(8,128)(2,1)}, u32[]{:S(2)}, u32[]{:S(2)}) collective-permute-start(bf16[2,2,96,768]{3,2,0,1:T(8,128)(2,1)} %copy_bitcast_fusion.6), channel_id=1, source_target_pairs={{0,1},{1,0},{2,3},{3,2},{4,5},{5,4},{6,7},{7,6},{8,9},{9,8},{10,11... | collective-permute-start | bytes 1769480 | tf_op jit(solution)/shard_map/ppermute | solution.py:572
  350.9 32.8 %collective-permute-start.37 = (bf16[2,96,768]{2,1,0:T(8,128)(2,1)}, bf16[2,96,768]{2,1,0:T(8,128)(2,1)S(1)}, u32[]{:S(2)}, u32[]{:S(2)}) collective-permute-start(bf16[2,96,768]{2,1,0:T(8,128)(2,1)} %fusion.15), channel_id=1, source_target_pairs={{0,2},{1,3},{2,0},{3,1},{4,6},{5,7},{6,4},{7,5},{8,10},{9,11},{10,... | collective-permute-start | bytes 884744 | tf_op jit(solution)/shard_map/ppermute | solution.py:576
  352.5 32.3 %collective-permute-start.36 = (bf16[2,96,768]{2,1,0:T(8,128)(2,1)}, bf16[2,96,768]{2,1,0:T(8,128)(2,1)S(1)}, u32[]{:S(2)}, u32[]{:S(2)}) collective-permute-start(bf16[2,96,768]{2,1,0:T(8,128)(2,1)} %fusion.14), channel_id=1, source_target_pairs={{0,1},{1,0},{2,3},{3,2},{4,5},{5,4},{6,7},{7,6},{8,9},{9,8},{10,11... | collective-permute-start | bytes 884744 | tf_op jit(solution)/shard_map/ppermute | solution.py:572
  353.7 32.2 %collective-permute-start.34 = (bf16[2,24,3840]{2,1,0:T(8,128)(2,1)S(1)}, bf16[2,24,3840]{2,1,0:T(8,128)(2,1)}, u32[]{:S(2)}, u32[]{:S(2)}) collective-permute-start(bf16[2,24,3840]{2,1,0:T(8,128)(2,1)S(1)} %fusion.9), channel_id=1, source_target_pairs={{0,1},{1,0},{2,3},{3,2},{4,5},{5,4},{6,7},{7,6},{8,9},{9,8},{10,11... | collective-permute-start | bytes 1105928 | tf_op jit(solution)/shard_map/ppermute | solution.py:572
  354.5 32.5 %collective-permute-start.35 = (bf16[2,24,3840]{2,1,0:T(8,128)(2,1)}, bf16[2,24,3840]{2,1,0:T(8,128)(2,1)}, u32[]{:S(2)}, u32[]{:S(2)}) collective-permute-start(bf16[2,24,3840]{2,1,0:T(8,128)(2,1)} %fusion.10), channel_id=1, source_target_pairs={{0,2},{1,3},{2,0},{3,1},{4,6},{5,7},{6,4},{7,5},{8,10},{9,11},{10,... | collective-permute-start | bytes 1105928 | tf_op jit(solution)/shard_map/ppermute | solution.py:576
  404.4 18.6 %collective-permute-start.38 = (bf16[384,1280]{1,0:T(8,128)(2,1)S(1)}, bf16[384,1280]{1,0:T(8,128)(2,1)S(1)}, u32[]{:S(2)}, u32[]{:S(2)}) collective-permute-start(bf16[384,1280]{1,0:T(8,128)(2,1)S(1)} %pad_maximum_fusion.3), channel_id=1, source_target_pairs={{0,16},{16,0},{1,17},{17,1},{2,18},{18,2},{3,19},{19,3},{4,20},{20... | collective-permute-start | bytes 2949128 | tf_op jit(solution)/shard_map/ppermute | solution.py:568
  404.5 47.0 %collective-permute-start.48 = (bf16[24,6912]{1,0:T(8,128)(2,1)}, bf16[24,6912]{1,0:T(8,128)(2,1)S(1)}, u32[]{:S(2)}, u32[]{:S(2)}) collective-permute-start(bf16[24,6912]{1,0:T(8,128)(2,1)} %get-tuple-element.199), channel_id=1, source_target_pairs={{0,4},{1,5},{2,6},{3,7},{4,8},{5,9},{6,10},{7,11},{8,12},{9,13},{1... | collective-permute-start | bytes 995336 | tf_op jit(solution)/shard_map/ppermute | solution.py:580
  410.8 42.5 %collective-permute-start.49 = (bf16[24,6912]{1,0:T(8,128)(2,1)}, bf16[24,6912]{1,0:T(8,128)(2,1)S(1)}, u32[]{:S(2)}, u32[]{:S(2)}) collective-permute-start(bf16[24,6912]{1,0:T(8,128)(2,1)} %get-tuple-element.200), channel_id=1, source_target_pairs={{0,8},{1,9},{2,10},{3,11},{4,12},{5,13},{6,14},{7,15},{8,0},{9,1},... | collective-permute-start | bytes 995336 | tf_op jit(solution)/shard_map/ppermute | solution.py:580
  414.1 39.4 %collective-permute-start.50 = (bf16[24,6912]{1,0:T(8,128)(2,1)S(1)}, bf16[24,6912]{1,0:T(8,128)(2,1)S(1)}, u32[]{:S(2)}, u32[]{:S(2)}) collective-permute-start(bf16[24,6912]{1,0:T(8,128)(2,1)S(1)} %get-tuple-element.201), channel_id=1, source_target_pairs={{0,12},{1,13},{2,14},{3,15},{4,0},{5,1},{6,2},{7,3},{8,4},{9,5},{1... | collective-permute-start | bytes 995336 | tf_op jit(solution)/shard_map/ppermute | solution.py:580
  436.1 29.8 %collective-permute-start.40 = (bf16[640,768]{1,0:T(8,128)(2,1)S(1)}, bf16[640,768]{1,0:T(8,128)(2,1)S(1)}, u32[]{:S(2)}, u32[]{:S(2)}) collective-permute-start(bf16[640,768]{1,0:T(8,128)(2,1)S(1)} %get-tuple-element.192), channel_id=1, source_target_pairs={{0,16},{16,0},{1,17},{17,1},{2,18},{18,2},{3,19},{19,3},{4,20},{20... | collective-permute-start | bytes 2949128 | tf_op jit(solution)/shard_map/ppermute | solution.py:568
  451.2 14.7 %collective-permute-start.39 = (bf16[640,768]{1,0:T(8,128)(2,1)S(1)}, bf16[640,768]{1,0:T(8,128)(2,1)S(1)}, u32[]{:S(2)}, u32[]{:S(2)}) collective-permute-start(bf16[640,768]{1,0:T(8,128)(2,1)S(1)} %get-tuple-element.189), channel_id=1, source_target_pairs={{0,16},{16,0},{1,17},{17,1},{2,18},{18,2},{3,19},{19,3},{4,20},{20... | collective-permute-start | bytes 2949128 | tf_op jit(solution)/shard_map/ppermute | solution.py:568
  (66 other events, 655.8 us)

commit v4 on v3

--- a/solution.py
+++ b/solution.py
@@ -39,29 +39,95 @@
     )
 
 
+def ready_body(part_ref, order_ref, seg_ref, freq_ref, idx_col, idx_row, seg_col, seg_row, cos_ref, sin_ref):
+    core = part_ref[0]
+    batches, rows = order_ref.shape
+    half = rows // 2
+    lanes = lax.broadcasted_iota(jnp.int32, (1, rows), 1)
+    wide = lax.broadcasted_iota(jnp.int32, (8, rows), 1)
+    halves = freq_ref.shape[0]
+    cols = lax.broadcasted_iota(jnp.int32, (halves, PAIR), 1)
+    lines = lax.broadcasted_iota(jnp.int32, (halves, PAIR), 0)
+    grow = ((cols % HEAD) // 2 == lines).astype(F32)
+    turn = jnp.where(cols % 2 == 0, -grow, grow)
+    expand = lambda value, by: lax.dot_general(
+        value, by, (((0,), (0,)), ((), ())), preferred_element_type=F32, precision=lax.Precision.HIGHEST)
+    for b in range(batches):
+        order, seg = order_ref[b:b + 1, :], seg_ref[b:b + 1, :]
+        starts, start, total = [], 0, 0
+        for s in range(SEG_COUNT):
+            size = jnp.sum((seg == s).astype(F32)).astype(jnp.int32)
+            starts.append(total)
+            start = start + jnp.where(size == LONGEST, total, 0)
+            total = total + size
+        table = jnp.concatenate([order, seg, lanes, jnp.zeros((5, rows), jnp.int32)], axis=0)
+        main = pltpu.roll(table, rows - start, 1)
+        early = pltpu.roll(table, LONGEST, 1)
+        table = jnp.where(wide < LONGEST, main, jnp.where(wide - LONGEST < start, early, table))
+        order, seg, place = table[0:1], table[1:2], table[2:3]
+        origin = jnp.zeros_like(seg)
+        for s in range(1, SEG_COUNT):
+            origin = jnp.where(seg == s, starts[s], origin)
+        position = (place - origin).astype(F32)
+        near = (order >= half).astype(jnp.int32) == core
+        idx = jnp.where(near, order - core * half, order + core * half)
+        idx_row[b] = idx
+        seg_row[b] = seg
+        both = jnp.concatenate([idx.astype(F32), seg.astype(F32), jnp.zeros((6, rows), F32)], axis=0).T
+        idx_col[b] = both[:, 0:1].astype(jnp.int32)
+        seg_col[b] = both[:, 1:2].astype(jnp.int32)
+        phase = freq_ref[...] * position
+        cos_ref[b] = expand(jnp.cos(phase), grow)
+        sin_ref[b] = expand(jnp.sin(phase), turn)
+
+
+def ready(part, order, segments):
+    batches, rows = order.shape
+    halves = HEAD // 2
+    freqs = jnp.exp(jnp.arange(halves, dtype=F32) * (-2.0 * math.log(10000.0) / HEAD))[:, None]
+    vmem, smem = (pl.BlockSpec(memory_space=s) for s in (pltpu.VMEM, pltpu.SMEM))
+    ints = lambda *shape: jax.ShapeDtypeStruct(shape, jnp.int32)
+    return pl.pallas_call(
+        ready_body,
+        in_specs=[smem, vmem, vmem, vmem],
+        out_shape=[ints(batches, rows, 1), ints(batches, 1, rows), ints(batches, rows, 1), ints(batches, 1, rows),
+                   jax.ShapeDtypeStruct((batches, rows, PAIR), F32), jax.ShapeDtypeStruct((batches, rows, PAIR), F32)],
+        compiler_params=pltpu.CompilerParams(vmem_limit_bytes=40 << 20),
+        cost_estimate=pl.CostEstimate(
+            flops=1 << 30, bytes_accessed=8 * batches * rows * 3 * PAIR, transcendentals=2 * batches * rows * halves
+        ),
+        name="ready",
+    )(part, order, segments, freqs)
+
+
 def arrange_body(block, idx_ref, own_ref, other_ref, xw_ref):
-    half = own_ref.shape[0]
+    half = own_ref.shape[1]
 
     def step(i, carry):
         rows = pl.ds(pl.multiple_of(i * block, block), block)
         picks = lax.broadcasted_iota(jnp.int32, (block, half), 1)
-        source = idx_ref[rows, :]
+        source = idx_ref[0, rows, :]
         near = (picks == source).astype(BF)
         away = (picks + half == source).astype(BF)
-        xw_ref[rows, :] = (dot(near, own_ref[...]) + dot(away, other_ref[...])).astype(BF)
+        xw_ref[0, rows, :] = (dot(near, own_ref[0]) + dot(away, other_ref[0])).astype(BF)
         return carry
 
-    lax.fori_loop(0, idx_ref.shape[0] // block, step, 0)
+    lax.fori_loop(0, idx_ref.shape[1] // block, step, 0)
 
 
 def arrange(idx_col, own, other, block=256):
-    rows, width = idx_col.shape[0], own.shape[1]
+    batches, rows = idx_col.shape[:2]
+    half, width = own.shape[1:]
+    each = lambda *shape: pl.BlockSpec((1,) + shape, lambda b: (b, 0, 0))
     return pl.pallas_call(
         functools.partial(arrange_body, block),
-        out_shape=jax.ShapeDtypeStruct((rows, width), BF),
+        grid=(batches,),
+        in_specs=[each(rows, 1), each(half, width), each(half, width)],
+        out_specs=each(rows, width),
+        out_shape=jax.ShapeDtypeStruct((batches, rows, width), BF),
         compiler_params=pltpu.CompilerParams(vmem_limit_bytes=40 << 20),
         cost_estimate=pl.CostEstimate(
-            flops=2 * rows * rows * width, bytes_accessed=4 * rows * width, transcendentals=0
+            flops=2 * batches * rows * rows * width, bytes_accessed=4 * batches * rows * width, transcendentals=0
         ),
         name="arrange",
     )(idx_col, own, other)
@@ -86,38 +152,41 @@
 
 
 def project_body(block, part_ref, xw_ref, near_ref, away_ref, bias_ref, cos_ref, sin_ref,
-                 q_ref, k_ref, v_ref, hold, sems):
-    share = q_ref.shape[1]
+                 qkv_ref, hold, sems):
+    share = qkv_ref.shape[2]
     for copy in own_columns(part_ref[0], near_ref, away_ref, hold, sems):
         copy.wait()
 
     def step(i, carry):
         rows = pl.ds(pl.multiple_of(i * block, block), block)
-        work = xw_ref[rows, :]
-        cosine, sine = cos_ref[rows, :], sin_ref[rows, :]
-        for out_ref, place, scale in ((q_ref, 0, LOG2E / math.sqrt(HEAD)), (k_ref, 1, 1.0)):
+        work = xw_ref[0, rows, :]
+        cosine, sine = cos_ref[0, rows, :], sin_ref[0, rows, :]
+        for place, scale in ((0, LOG2E / math.sqrt(HEAD)), (1, 1.0)):
             whole = slice(place * share, (place + 1) * share)
             pre = dot(work, hold[:, whole]) + bias_ref[:, whole]
             for j in range(share // PAIR):
                 cols = slice(j * PAIR, (j + 1) * PAIR)
                 piece = pre[:, cols]
-                out_ref[rows, cols] = (
+                qkv_ref[place, rows, cols] = (
                     (piece * cosine + pair_swap(piece) * sine) * scale
                 ).astype(BF)
-        v_ref[rows, :] = (dot(work, hold[:, 2 * share:]) + bias_ref[:, 2 * share:]).astype(BF)
+        qkv_ref[2, rows, :] = (dot(work, hold[:, 2 * share:]) + bias_ref[:, 2 * share:]).astype(BF)
         return carry
 
-    lax.fori_loop(0, xw_ref.shape[0] // block, step, 0)
-
-
-def project(part, xw, near_w, away_w, bias_own, cosine, sine, block=256):
-    rows, width = xw.shape
+    lax.fori_loop(0, xw_ref.shape[1] // block, step, 0)
+
+
+def project(b, part, xws, near_w, away_w, bias_own, cosine, sine, block=256):
+    rows, width = xws.shape[1:]
     share = bias_own.shape[1] // 3
+    each = lambda n: pl.BlockSpec((1, rows, n), lambda i: (b, 0, 0))
     vmem, smem, anywhere = (pl.BlockSpec(memory_space=s) for s in (pltpu.VMEM, pltpu.SMEM, pl.ANY))
     return pl.pallas_call(
         functools.partial(project_body, block),
-        in_specs=[smem, vmem, anywhere, anywhere, vmem, vmem, vmem],
-        out_shape=[jax.ShapeDtypeStruct((rows, share), BF)] * 3,
+        grid=(1,),
+        in_specs=[smem, each(width), anywhere, anywhere, vmem, each(PAIR), each(PAIR)],
+        out_specs=pl.BlockSpec((3, rows, share), lambda i: (0, 0, 0)),
+        out_shape=jax.ShapeDtypeStruct((3, rows, share), BF),
         scratch_shapes=[pltpu.VMEM((width, 3 * share), BF), pltpu.SemaphoreType.DMA((6,))],
         compiler_params=pltpu.CompilerParams(vmem_limit_bytes=40 << 20),
         cost_estimate=pl.CostEstimate(
@@ -126,12 +195,12 @@
             transcendentals=0,
         ),
         name="project",
-    )(part, xw, near_w, away_w, bias_own, cosine, sine)
-
-
-def attend_body(block, idx_ref, q_ref, k_ref, v_ref, seg_col_ref, seg_row_ref,
+    )(part, xws, near_w, away_w, bias_own, cosine, sine)
+
+
+def attend_body(block, idx_ref, qkv_ref, seg_col_ref, seg_row_ref,
                 near_ref, away_ref, ctxt_ref, lse_ref, pick, ka, vt, qt, augt):
-    rows = q_ref.shape[0]
+    rows = qkv_ref.shape[1]
     half = near_ref.shape[0]
 
     @pl.when(pl.program_id(0) == 0)
@@ -139,21 +208,21 @@
         def fill(i, carry):
             span = pl.ds(pl.multiple_of(i * block, block), block)
             pick[span, :] = (
-                lax.broadcasted_iota(jnp.int32, (block, rows), 1) == idx_ref[span, :]
+                lax.broadcasted_iota(jnp.int32, (block, rows), 1) == idx_ref[0, span, :]
             ).astype(BF)
             return carry
 
         lax.fori_loop(0, rows // block, fill, 0)
         lanes = lax.broadcasted_iota(jnp.int32, (rows, PAIR), 1)
-        ka[:, PAIR:] = ((lanes == seg_col_ref[...]) | (lanes >= SEG_COUNT)).astype(BF)
+        ka[:, PAIR:] = ((lanes == seg_col_ref[0]) | (lanes >= SEG_COUNT)).astype(BF)
         places = lax.broadcasted_iota(jnp.int32, (PAIR, rows), 0)
         augt[...] = jnp.where(
-            (places < SEG_COUNT) & (places != seg_row_ref[...]), -FAR, 0.0
+            (places < SEG_COUNT) & (places != seg_row_ref[0]), -FAR, 0.0
         ).astype(BF)
 
-    ka[:, :PAIR] = k_ref[...]
-    vt[...] = v_ref[...].T
-    qt[...] = q_ref[...].T
+    ka[:, :PAIR] = qkv_ref[1]
+    vt[...] = qkv_ref[2].T
+    qt[...] = qkv_ref[0].T
     empty = jnp.zeros((HEAD, block), BF)
 
     def attended(span, keys):
@@ -180,17 +249,17 @@
     away_ref[...] = given[:, half:].T
 
 
-def attend(idx_col, q, k, v, seg_col, seg_row, block=256):
-    rows, share = q.shape
+def attend(b, idx_col, qkv, seg_col, seg_row, block=256):
+    rows, share = qkv.shape[1:]
     pairs = share // PAIR
     half = rows // 2
-    whole = lambda shape: pl.BlockSpec(shape, lambda j: (0,) * len(shape))
+    whole = lambda shape: pl.BlockSpec((1,) + shape, lambda j: (b, 0, 0))
+    three = pl.BlockSpec((3, rows, PAIR), lambda j: (0, 0, j))
     column = lambda n: pl.BlockSpec((n, PAIR), lambda j: (0, j))
     return pl.pallas_call(
         functools.partial(attend_body, block),
         grid=(pairs,),
-        in_specs=[whole((rows, 1)), column(rows), column(rows), column(rows),
-                  whole((rows, 1)), whole((1, rows))],
+        in_specs=[whole((rows, 1)), three, whole((rows, 1)), whole((1, rows))],
         out_specs=[column(half), column(half), pl.BlockSpec((PAIR, rows), lambda j: (j, 0)),
                    pl.BlockSpec((1, 8, rows), lambda j: (j, 0, 0))],
         out_shape=[jax.ShapeDtypeStruct((half, share), BF), jax.ShapeDtypeStruct((half, share), BF),
@@ -205,14 +274,14 @@
             transcendentals=2 * pairs * rows * rows,
         ),
         name="attend",
-    )(idx_col, q, k, v, seg_col, seg_row)
-
-
-def attend_back_body(block, idx_ref, q_ref, k_ref, v_ref, seg_col_ref, seg_row_ref, lse_ref,
+    )(idx_col, qkv, seg_col, seg_row)
+
+
+def attend_back_body(block, idx_ref, qkv_ref, seg_col_ref, seg_row_ref, lse_ref,
                      ctxt_ref, gnear_ref, gaway_ref, cos_ref, sin_ref,
                      grads_ref,
                      pick, ka, va, kt, qt, dt, go, delta, dkacc, dvacc, dqt, augt):
-    rows = q_ref.shape[0]
+    rows = qkv_ref.shape[1]
     half = gnear_ref.shape[0]
 
     @pl.when(pl.program_id(0) == 0)
@@ -220,24 +289,24 @@
         def fill(i, carry):
             span = pl.ds(pl.multiple_of(i * block, block), block)
             pick[span, :] = (
-                lax.broadcasted_iota(jnp.int32, (block, rows), 1) == idx_ref[span, :]
+                lax.broadcasted_iota(jnp.int32, (block, rows), 1) == idx_ref[0, span, :]
             ).astype(BF)
             return carry
 
         lax.fori_loop(0, rows // block, fill, 0)
         lanes = lax.broadcasted_iota(jnp.int32, (rows, PAIR), 1)
-        ones = ((lanes == seg_col_ref[...]) | (lanes >= SEG_COUNT)).astype(BF)
+        ones = ((lanes == seg_col_ref[0]) | (lanes >= SEG_COUNT)).astype(BF)
         ka[:, PAIR:] = ones
         va[:, PAIR:] = jnp.ones((rows, PAIR), BF)
         places = lax.broadcasted_iota(jnp.int32, (8, rows), 0)
         augt[...] = jnp.where(
-            (places < SEG_COUNT) & (places != seg_row_ref[...]), -FAR, 0.0
+            (places < SEG_COUNT) & (places != seg_row_ref[0]), -FAR, 0.0
         )
 
-    ka[:, :PAIR] = k_ref[...]
-    va[:, :PAIR] = v_ref[...]
-    kt[...] = k_ref[...].T
-    qt[...] = q_ref[...].T
+    ka[:, :PAIR] = qkv_ref[1]
+    va[:, :PAIR] = qkv_ref[2]
+    kt[...] = qkv_ref[1].T
+    qt[...] = qkv_ref[0].T
     grad = dot(pick[:, :half], gnear_ref[...]) + dot(pick[:, half:], gaway_ref[...])
     go[...] = grad.astype(BF)
     dt[...] = go[...].T
@@ -276,7 +345,7 @@
             grads = (probs * slope).astype(BF)
             keep = wide < HEAD if h == 0 else wide >= HEAD
             dvacc[keys, :] += dot(probs.astype(BF), jnp.where(keep, go[span, :], zero))
-            dkacc[keys, :] += dot(grads, jnp.where(keep, q_ref[span, :], zero))
+            dkacc[keys, :] += dot(grads, jnp.where(keep, qkv_ref[0, span, :], zero))
             dqt[part, span] = dot(kt[part, keys], grads)
 
     def step(i, carry):
@@ -285,7 +354,7 @@
 
     lax.fori_loop(0, LONGEST // block, step, 0)
     attended(slice(LONGEST, rows), slice(LONGEST, rows))
-    cosine, sine = cos_ref[...], sin_ref[...]
+    cosine, sine = cos_ref[0], sin_ref[0]
     turned = dqt[...].T
     grads_ref[0] = ((turned * cosine - pair_swap(turned) * sine) * (1.0 / math.sqrt(HEAD))).astype(BF)
     turned = dkacc[...]
@@ -293,20 +362,20 @@
     grads_ref[2] = dvacc[...].astype(BF)
 
 
-def attend_back(idx_col, q, k, v, seg_col, seg_row, lse, ctxt, gnear, gaway, cosine, sine, block=256):
-    rows, share = q.shape
+def attend_back(b, idx_col, qkv, seg_col, seg_row, lse, ctxt, gnear, gaway, cosine, sine, block=256):
+    rows, share = qkv.shape[1:]
     pairs = share // PAIR
     half = rows // 2
-    whole = lambda shape: pl.BlockSpec(shape, lambda j: (0,) * len(shape))
+    whole = lambda shape: pl.BlockSpec((1,) + shape, lambda j: (b, 0, 0))
+    three = pl.BlockSpec((3, rows, PAIR), lambda j: (0, 0, j))
     column = lambda n: pl.BlockSpec((n, PAIR), lambda j: (0, j))
     return pl.pallas_call(
         functools.partial(attend_back_body, block),
         grid=(pairs,),
-        in_specs=[whole((rows, 1)), column(rows), column(rows), column(rows),
-                  whole((rows, 1)), whole((1, rows)),
+        in_specs=[whole((rows, 1)), three, whole((rows, 1)), whole((1, rows)),
                   pl.BlockSpec((1, 8, rows), lambda j: (j, 0, 0)),
                   pl.BlockSpec((PAIR, rows), lambda j: (j, 0)),
-                  column(half), column(half), whole(cosine.shape), whole(sine.shape)],
+                  column(half), column(half), whole((rows, PAIR)), whole((rows, PAIR))],
         out_specs=pl.BlockSpec((3, rows, PAIR), lambda j: (0, 0, j)),
         out_shape=jax.ShapeDtypeStruct((3, rows, share), BF),
         scratch_shapes=[pltpu.VMEM((rows, rows), BF), pltpu.VMEM((rows, 2 * PAIR), BF),
@@ -321,7 +390,7 @@
             transcendentals=2 * pairs * rows * rows,
         ),
         name="attend_back",
-    )(idx_col, q, k, v, seg_col, seg_row, lse, ctxt, gnear, gaway, cosine, sine)
+    )(idx_col, qkv, seg_col, seg_row, lse, ctxt, gnear, gaway, cosine, sine)
 
 
 def project_back_body(block, part_ref, g_ref, row_ref, wnear_ref, waway_ref,
@@ -346,21 +415,24 @@
     def back(i, carry):
         span = pl.ds(pl.multiple_of(i * small, small), small)
         for base, out_ref in ((half, away_ref), (0, near_ref)):
-            pick = (lax.broadcasted_iota(jnp.int32, (small, rows), 0) + (base + i * small) == row_ref[...]).astype(BF)
+            pick = (lax.broadcasted_iota(jnp.int32, (small, rows), 0) + (base + i * small) == row_ref[0]).astype(BF)
             out_ref[span, :] = dot(pick, work[...]).astype(BF)
         return carry
 
     lax.fori_loop(0, half // small, back, 0)
 
 
-def project_back(part, grads, idx_row, near_w, away_w, block=256):
+def project_back(b, part, grads, idx_row, near_w, away_w, block=256):
     rows, share = grads.shape[1:]
     width = 2 * share
     half = rows // 2
-    vmem, smem, anywhere = (pl.BlockSpec(memory_space=s) for s in (pltpu.VMEM, pltpu.SMEM, pl.ANY))
+    smem, anywhere = (pl.BlockSpec(memory_space=s) for s in (pltpu.SMEM, pl.ANY))
     return pl.pallas_call(
         functools.partial(project_back_body, block),
-        in_specs=[smem, vmem, vmem, anywhere, anywhere],
+        grid=(1,),
+        in_specs=[smem, pl.BlockSpec((3, rows, share), lambda i: (0, 0, 0)),
+                  pl.BlockSpec((1, 1, rows), lambda i: (b, 0, 0)), anywhere, anywhere],
+        out_specs=[pl.BlockSpec((half, width), lambda i: (0, 0))] * 2,
         scratch_shapes=[pltpu.VMEM((rows, width), BF), pltpu.VMEM((width, 3 * share), BF),
                         pltpu.SemaphoreType.DMA((6,))],
         out_shape=[jax.ShapeDtypeStruct((half, width), BF)] * 2,
@@ -375,10 +447,10 @@
 
 
 def weight_back_body(batches, *refs):
-    xw_refs, g_refs, (gw_ref, gb_ref) = refs[:batches], refs[batches:2 * batches], refs[2 * batches:]
+    xw_ref, g_refs, (gw_ref, gb_ref) = refs[0], refs[1:1 + batches], refs[1 + batches:]
     total, thin = None, None
-    for xw_ref, g_ref in zip(xw_refs, g_refs):
-        term = dot_lt(xw_ref[...], g_ref[0])
+    for b, g_ref in enumerate(g_refs):
+        term = dot_lt(xw_ref[b], g_ref[0])
         line = jnp.sum(g_ref[0].astype(F32), axis=0, keepdims=True)
         total = term if total is None else total + term
         thin = line if thin is None else thin + line
@@ -387,13 +459,12 @@
 
 
 def weight_back(xws, grads):
-    batches, (rows, width), share = len(xws), xws[0].shape, grads[0].shape[2]
-    whole = pl.BlockSpec((rows, width), lambda s: (0, 0))
+    (batches, rows, width), share = xws.shape, grads[0].shape[2]
     each = pl.BlockSpec((1, rows, share), lambda s: (s, 0, 0))
     return pl.pallas_call(
         functools.partial(weight_back_body, batches),
         grid=(3,),
-        in_specs=[whole] * batches + [each] * batches,
+        in_specs=[pl.BlockSpec(xws.shape, lambda s: (0, 0, 0))] + [each] * batches,
         out_specs=[pl.BlockSpec((width, share), lambda s: (0, s)),
                    pl.BlockSpec((8, share), lambda s: (0, s))],
         out_shape=[jax.ShapeDtypeStruct((width, 3 * share), BF), jax.ShapeDtypeStruct((8, 3 * share), F32)],
@@ -404,7 +475,7 @@
             transcendentals=0,
         ),
         name="weight_back",
-    )(*xws, *grads)
+    )(xws, *grads)
 
 
 EPS = 1e-6
@@ -439,7 +510,7 @@
 
 def feed_body(chunk, part_ref, x_ref, near_ref, away_ref, dy_ref, thin_ref, bup_ref,
               unear_ref, uaway_ref, dnear_ref, daway_ref,
-              out_ref, dh_ref, lmine_ref, ltheirs_ref, amine_ref, atheirs_ref, dup_ref, dlow_ref, da_ref, cnear_ref, caway_ref,
+              out_ref, dh_ref, low_ref, act_ref, dup_ref, dlow_ref, da_ref, cnear_ref, caway_ref,
               sums_ref, bsum_ref, wo_near, wo_away, wup, wdown, slopes, sems):
     first_step = pl.program_id(0) == 0
     core = part_ref[0]
@@ -482,26 +553,15 @@
     first = norm_one * gain_one + shift_one
     low = first.astype(BF)
 
-    def split(value, at, mine_ref, theirs_ref):
-        size = mine_ref.shape[1]
-        cols = slice(at % size, at % size + value.shape[1])
-
-        @pl.when(core == at // size)
-        def _():
-            mine_ref[:, cols] = value
-
-        @pl.when(core != at // size)
-        def _():
-            theirs_ref[:, cols] = value
-
-    split(low[:, :half_w], 0, lmine_ref, ltheirs_ref)
-    split(low[:, half_w:], half_w, lmine_ref, ltheirs_ref)
+    low_ref[core] = low[:, :half_w]
+    low_ref[1 - core] = low[:, half_w:]
     lowered = None
     for c in range(wide // chunk):
         cols = slice(c * chunk, (c + 1) * chunk)
         act, slope = gauss_parts(dot(low, wup[:, cols]) + bup_ref[:, cols])
         act = act.astype(BF)
-        split(act, c * chunk, amine_ref, atheirs_ref)
+        side = core if c * chunk < half_f else 1 - core
+        act_ref[side, :, c * chunk % half_f:c * chunk % half_f + chunk] = act
         slopes[:, cols] = slope.astype(BF)
         term = dot(act, wdown[cols, :])
         lowered = term if lowered is None else lowered + term
@@ -537,6 +597,7 @@
     share = near.shape[1]
     wide = bup.shape[1]
     line = lambda n: pl.BlockSpec((block, n), lambda i: (i, 0))
+    pair = lambda n: pl.BlockSpec((2, block, n), lambda i: (0, i, 0))
     fixed = lambda shape: pl.BlockSpec(shape, lambda i: (0, 0))
     anywhere = pl.BlockSpec(memory_space=pl.ANY)
     shape = lambda n, dt: jax.ShapeDtypeStruct((rows, n), dt)
@@ -545,11 +606,11 @@
         grid=(rows // block,),
         in_specs=[pl.BlockSpec(memory_space=pltpu.SMEM), line(width), line(share), line(share), line(width),
                   fixed(thin.shape), fixed(bup.shape), anywhere, anywhere, anywhere, anywhere],
-        out_specs=[line(width), line(width), line(width // 2), line(width // 2), line(wide // 2),
-                   line(wide // 2), line(wide), line(width), line(width),
+        out_specs=[line(width), line(width), pair(width // 2), pair(wide // 2), line(wide), line(width), line(width),
                    line(share), line(share), fixed((8, width)), fixed((8, wide))],
-        out_shape=[shape(width, BF), shape(width, F32), shape(width // 2, BF), shape(width // 2, BF),
-                   shape(wide // 2, BF), shape(wide // 2, BF), shape(wide, BF), shape(width, BF), shape(width, BF), shape(share, BF), shape(share, BF),
+        out_shape=[shape(width, BF), shape(width, F32),
+                   jax.ShapeDtypeStruct((2, rows, width // 2), BF), jax.ShapeDtypeStruct((2, rows, wide // 2), BF),
+                   shape(wide, BF), shape(width, BF), shape(width, BF), shape(share, BF), shape(share, BF),
                    jax.ShapeDtypeStruct((8, width), F32), jax.ShapeDtypeStruct((8, wide), F32)],
         scratch_shapes=[pltpu.VMEM((share, width), BF), pltpu.VMEM((share, width), BF),
                         pltpu.VMEM((width, wide), BF), pltpu.VMEM((wide, width), BF),
@@ -580,28 +641,38 @@
     return lax.ppermute(value, "fsdp", [(i, (i + 4 * k) % 16) for i in range(16)])
 
 
-def assemble_body(place_ref, ax_ref, ay_ref, bx_ref, by_ref, out_ref):
+def assemble_body(lines, place_ref, ax_ref, ay_ref, bx_ref, by_ref, *out_refs):
     place = place_ref[0]
     z, y, x = place // 4, (place // 2) % 2, place % 2
+    n = ax_ref.shape[1]
+
+    def put(owner, piece):
+        out_refs[0][owner] = piece[:, :out_refs[0].shape[2]]
+        for c in range(lines):
+            width = out_refs[1].shape[2]
+            at = out_refs[0].shape[2] + c * width
+            out_refs[1][owner, c * n:(c + 1) * n, :] = piece[:, at:at + width]
+
     for j in range(4):
         k, o = j % 2, j // 2
         near_z, far_z = lax.rem(z - k + 4, 4), lax.rem(z - k + 2, 4)
         flip_x = lax.rem(x + o, 2)
         flip_y = lax.rem(y + o, 2)
-        out_ref[near_z * 4 + y * 2 + flip_x] = ax_ref[j]
-        out_ref[near_z * 4 + (1 - y) * 2 + flip_x] = ay_ref[j]
-        out_ref[far_z * 4 + flip_y * 2 + x] = by_ref[j]
-        out_ref[far_z * 4 + flip_y * 2 + 1 - x] = bx_ref[j]
-
-
-def assemble(place, parts):
+        put(near_z * 4 + y * 2 + flip_x, ax_ref[j])
+        put(near_z * 4 + (1 - y) * 2 + flip_x, ay_ref[j])
+        put(far_z * 4 + flip_y * 2 + x, by_ref[j])
+        put(far_z * 4 + flip_y * 2 + 1 - x, bx_ref[j])
+
+
+def assemble(place, parts, lines=0, line=0):
     n, width = parts[0].shape[1:]
     vmem = pl.BlockSpec(memory_space=pltpu.VMEM)
+    shapes = [(16, n, width - lines * line)] + ([(16, lines * n, line)] if lines else [])
     return pl.pallas_call(
-        assemble_body,
+        functools.partial(assemble_body, lines),
         in_specs=[pl.BlockSpec(memory_space=pltpu.SMEM)] + [vmem] * 4,
-        out_shape=jax.ShapeDtypeStruct((16, n, width), BF),
-        compiler_params=pltpu.CompilerParams(vmem_limit_bytes=24 << 20),
+        out_shape=[jax.ShapeDtypeStruct(shape, BF) for shape in shapes],
+        compiler_params=pltpu.CompilerParams(vmem_limit_bytes=40 << 20),
         cost_estimate=pl.CostEstimate(flops=0, bytes_accessed=4 * 16 * n * width, transcendentals=0),
         name="assemble",
     )(place, *parts)
@@ -625,10 +696,9 @@
     return first, swap_y(first), swap_x(second), second
 
 
-def joined(parts):
-    n, width = parts[0].shape[1:]
+def joined(parts, lines=0, line=0):
     place = jnp.full((1,), lax.axis_index("fsdp"), jnp.int32)
-    return assemble(place, parts).reshape(16 * n, width)
+    return [value.reshape(-1, value.shape[2]) for value in assemble(place, parts, lines, line)]
 
 
 def pick(part, at, axis):
@@ -674,32 +744,6 @@
     for came in tie([shift_z(send, k) for k, send in zip((1, 2, 3), sends)], after):
         total = total + came.astype(F32)
     return total
-
-
-def spread_rows(segments, order):
-    rows = segments.shape[0]
-    ids = jnp.arange(SEG_COUNT, dtype=jnp.int32)
-    counts = jnp.sum(segments[:, None] == ids[None, :], axis=0, dtype=jnp.int32)
-    long_id = jnp.sum(jnp.where(counts == LONGEST, ids, 0))
-    starts = jnp.sum(jnp.where(ids[:, None] < ids[None, :], counts[:, None], 0), axis=0)
-    start = jnp.sum(jnp.where(ids == long_id, starts, 0))
-    places = jnp.arange(rows, dtype=jnp.int32)
-    table = jnp.stack([order, segments, places])
-    main = lax.dynamic_slice_in_dim(table, start, LONGEST, 1)
-    rest = jnp.where(places[None, :rows - LONGEST] < start, table[:, :rows - LONGEST], table[:, LONGEST:])
-    order, segments, places = jnp.concatenate([main, rest], axis=1)
-    origin = jnp.sum(jnp.where(segments[:, None] == ids[None, :], starts[None, :], 0), axis=1)
-    return order, segments, (places - origin).astype(F32)
-
-
-def turn_tables(position):
-    halves = HEAD // 2
-    freqs = jnp.exp(jnp.arange(halves, dtype=F32) * (-2.0 * math.log(10000.0) / HEAD))
-    phase = position[:, None] * freqs[None, :]
-    cosine = jnp.tile(jnp.repeat(jnp.cos(phase), 2, axis=1), (1, 2))
-    signs = jnp.tile(jnp.array([-1.0, 1.0], F32), halves)[None, :]
-    sine = jnp.tile(jnp.repeat(jnp.sin(phase), 2, axis=1) * signs, (1, 2))
-    return cosine, sine
 
 
 def on_device(tokens, permutation, segment_ids, cotangent, *shards):
@@ -717,29 +761,41 @@
     room = n_qkv * 128
     tokens, cotangent = tokens[:, 0], cotangent[:, 0]
 
-    packed = jnp.concatenate([shards[i] for i in thin] + [jnp.zeros((room - count,), BF)])
-    q_shard = jnp.concatenate([shards[0], packed.reshape(n_qkv, 128)], axis=1)
-    u_shard = jnp.concatenate([shards[2], shards[6]], axis=1)
-    d_shard = shards[8]
+    away_tokens = swap_cores(tokens)
+    idx_col, idx_row, seg_col, seg_row, cosine, sine = ready(part, permutation[:, 0], segment_ids[:, 0])
+    xws = arrange(idx_col, tokens, away_tokens)
     if staged:
-        q_pair = reach_z(q_shard)
-        u_shard, d_shard = tie((u_shard, d_shard), q_pair)
-        q_parts = reach_two(*reach_one(*q_pair))
-        u_pair, d_pair = tie((reach_z(u_shard), reach_z(d_shard)), q_parts)
-        pairs = (reach_one(*u_pair), reach_one(*d_pair))
-        q_near = joined(q_parts)
+        lanes = jnp.concatenate(
+            [jnp.pad(shards[i][None], ((0, 0), (0, 128 - size))) for i, size in zip(thin, sizes)]
+            + [jnp.zeros((n_qkv - len(thin), 128), BF)], axis=0)
+        q_shard = jnp.concatenate([shards[0], lanes], axis=1)
+        ud_shard = jnp.concatenate(
+            [shards[2], shards[6]] + [shards[8][i * n_qkv:(i + 1) * n_qkv] for i in range(4)], axis=1)
+        first, second = reach_z(q_shard)
+        first_x, second_y = swap_x(first), swap_y(second)
+        ud_shard = tie(ud_shard, first_x)
+        q_parts = reach_two(jnp.concatenate([first, first_x], axis=0), jnp.concatenate([second, second_y], axis=0))
+        ud_z = tuple(shift_z(ud_shard, k) for k in (1, 2, 3))
+        q_parts = tie(q_parts, (xws, cosine))
+        (q_near,) = joined(q_parts)
     else:
+        packed = jnp.concatenate([shards[i] for i in thin] + [jnp.zeros((room - count,), BF)])
+        q_shard = jnp.concatenate([shards[0], packed.reshape(n_qkv, 128)], axis=1)
         q_near = lax.all_gather(q_shard, "fsdp", axis=0, tiled=True)
+        u_near = lax.all_gather(jnp.concatenate([shards[2], shards[6]], axis=1), "fsdp", axis=0, tiled=True)
+        d_near = lax.all_gather(shards[8], "fsdp", axis=0, tiled=True)
     q_away = swap_cores(q_near)
-    away_tokens = swap_cores(tokens)
-
-    slabs = [value[:, 3 * width:].reshape(owners // 2, room)[:, :count] for value in (q_near, q_away)]
+
+    slabs = [value[:, 3 * width:].reshape(owners // 2, n_qkv, 128) for value in (q_near, q_away)]
     vectors = jnp.concatenate(
         [jnp.where(core == 0, slabs[0], slabs[1]), jnp.where(core == 0, slabs[1], slabs[0])], axis=0
     ).astype(F32)
     spread, at = [], 0
-    for size in sizes:
-        spread.append(vectors[:, at:at + size].reshape(1, owners * size))
+    for i, size in enumerate(sizes):
+        if staged:
+            spread.append(vectors[:, i, :size].reshape(1, owners * size))
+        else:
+            spread.append(vectors.reshape(owners, room)[:, at:at + size].reshape(1, owners * size))
         at += size
     b_qkv, b_out, gain_one, shift_one, b_up, b_down, gain_two, shift_two = spread
     bias_own = jnp.concatenate(
@@ -750,57 +806,46 @@
         [b_out, gain_one, shift_one, b_down, gain_two, shift_two, blank_row, blank_row], axis=0
     )
 
-    kept = []
+    qkvs = [project(b, part, xws, q_near, q_away, bias_own, cosine, sine) for b in range(batches)]
+    if staged:
+        (one, two, three), qkvs = tie((ud_z, qkvs))
+        first, second = jnp.stack([ud_shard, one]), jnp.stack([two, three])
+        qkvs[0], first, second = tie((qkvs[0], first, second))
+        first_x, second_y = swap_x(first), swap_y(second)
+    kept, ctxs = [], []
     for b in range(batches):
-        order, segments, position = spread_rows(segment_ids[b, 0], permutation[b, 0])
-        place = jnp.where(
-            order // half == core, order - core * half, order - (1 - core) * half + half
-        )
-        cosine, sine = turn_tables(position)
-        col, row = segments[:, None], segments[None, :]
-        idx_col, idx_row = place[:, None], place[None, :]
-        xw = arrange(idx_col, tokens[b], away_tokens[b])
-        kept.append((idx_col, idx_row, col, row, cosine, sine, xw))
-    ctxs = []
-    for b in range(batches):
-        idx_col, idx_row, col, row, cosine, sine, xw = kept[b]
-        q, k, v = project(part, xw, q_near, q_away, bias_own, cosine, sine)
-        if staged and b == 0:
-            q, pairs = tie((q, pairs))
-            u_parts, d_parts = reach_two(*pairs[0]), reach_two(*pairs[1])
         if staged and b == 1:
-            u_parts, d_parts = tie((u_parts, d_parts), (ctxs[0][0], q))
-            u_near, d_near = joined(u_parts), joined(d_parts)
-            q, u_near, d_near = tie((q, u_near, d_near))
-        near, away, ctxt, lse = attend(idx_col, q, k, v, col, row)
-        kept[b] += (q, k, v, ctxt, lse)
+            first_x, second_y = tie((first_x, second_y), ctxs[0][0])
+            first, second = jnp.concatenate([first, first_x], axis=0), jnp.concatenate([second, second_y], axis=0)
+            qkvs[1], first, second = tie((qkvs[1], first, second))
+            first_y, second_x = swap_y(first), swap_x(second)
+        near, away, ctxt, lse = attend(b, idx_col, qkvs[b], seg_col, seg_row)
+        kept.append((qkvs[b], ctxt, lse))
         ctxs.append((near, swap_cores(away)))
-    if not staged:
-        u_near = lax.all_gather(u_shard, "fsdp", axis=0, tiled=True)
-        d_near = lax.all_gather(d_shard, "fsdp", axis=0, tiled=True)
+    if staged:
+        first_y, second_x = tie((first_y, second_x), ctxs[1][0])
+        u_near, d_near = joined((first, first_y, second_x, second), 4, width)
     u_away, d_away = swap_cores(u_near), swap_cores(d_near)
     near, away = (jnp.concatenate([item[i] for item in ctxs], axis=0) for i in range(2))
-    (outputs, grad_one, low_mine, low_theirs, act_mine, act_theirs, dup, dlow, da, cnear, caway, sums, bsum) = feed(
+    (outputs, grad_one, low, act, dup, dlow, da, cnear, caway, sums, bsum) = feed(
         part, tokens.reshape(batches * half, width), near, away,
         cotangent.reshape(batches * half, width), thin_rows, b_up, u_near, u_away, d_near, d_away,
     )
     caway = swap_cores(caway)
 
-    d_theirs = swap_cores(dot_lt(act_theirs, dlow).astype(BF))
+    d_theirs = swap_cores(dot_lt(act[1], dlow).astype(BF))
     uo_theirs = swap_cores(
-        jnp.concatenate([dot_lt(low_theirs, dup).astype(BF), dot_lt(away, da).astype(BF)], axis=1)
+        jnp.concatenate([dot_lt(low[1], dup).astype(BF), dot_lt(away, da).astype(BF)], axis=1)
     )
-    d_sum = (dot_lt(act_mine, dlow) + d_theirs.astype(F32)).astype(BF)
+    d_sum = (dot_lt(act[0], dlow) + d_theirs.astype(F32)).astype(BF)
     uo_sum = jnp.concatenate([
-        (dot_lt(low_mine, dup) + uo_theirs[:, :4 * width].astype(F32)).astype(BF),
+        (dot_lt(low[0], dup) + uo_theirs[:, :4 * width].astype(F32)).astype(BF),
         (dot_lt(near, da) + uo_theirs[:, 4 * width:].astype(F32)).astype(BF),
     ], axis=1)
 
     def back(b, given):
-        idx_col, idx_row, col, row, cosine, sine, xw, q, k, v, ctxt, lse = kept[b]
-        return attend_back(
-            idx_col, q, k, v, col, row, lse, ctxt, *given, cosine, sine
-        )
+        qkv, ctxt, lse = kept[b]
+        return attend_back(b, idx_col, qkv, seg_col, seg_row, lse, ctxt, *given, cosine, sine)
 
     givens = [(cnear[b * half:(b + 1) * half], caway[b * half:(b + 1) * half]) for b in range(batches)]
     if staged:
@@ -814,7 +859,6 @@
         grads, du_step = tie((grads, du_step))
     else:
         grads = [back(b, givens[b]) for b in range(batches)]
-    xws = [item[6] for item in kept]
     gw_own, gb_own = weight_back(xws, grads)
 
     def halves(value):
@@ -838,17 +882,17 @@
         mine[:, :3 * share], theirs[:, :3 * share],
         (mine[:, 3 * share:].astype(F32) + theirs[:, 3 * share:].astype(F32)).astype(BF),
     ], axis=1)
-    backs = [project_back(part, grads[0], kept[0][1], q_near, q_away)]
+    backs = [project_back(0, part, grads[0], idx_row, q_near, q_away)]
     if staged:
         last, q_step, backs = tie((grads[1], fold_one(q_sum), backs))
-        backs.append(project_back(part, last, kept[1][1], q_near, q_away))
+        backs.append(project_back(1, part, last, idx_row, q_near, q_away))
         q_step = fold_two(*q_step, backs[1])
         q_last = fold_three(fold_cross(*q_step))
         g_uo = fold_end(*du_step, q_last)
         g_qkv = fold_end(*q_last, g_uo)
         g_down = jnp.concatenate([g_uo[:, (5 + i) * width:(6 + i) * width] for i in range(4)], axis=0)
     else:
-        backs.append(project_back(part, grads[1], kept[1][1], q_near, q_away))
+        backs.append(project_back(1, part, grads[1], idx_row, q_near, q_away))
         summed = lambda value: lax.psum_scatter(
             value.astype(BF), "fsdp", scatter_dimension=0, tiled=True
         ).astype(F32)

time: 477 us -> 422 us (0.88)
  other arithmetic: 40.6 us -> 23 us
  local copies, waits for them, and re-layouts: 67.4 us -> 53.6 us
  starting transfers between devices: 60.5 us -> 51.7 us
  Pallas kernels: 227 us -> 221 us
    ppermute x15 -> x12, waiting for transfers between devices: 15.8 us -> 7.11 us  [shift_z(): lax.ppermute(value, 'fsdp', [(i, (i + 4 * k) % 16) for i in range(16)])]
    another operation x14 -> x8, local copies, waits for them, and re-layouts: 8.79 us -> 1.3 us  [on_device(): spread.append(vectors[:, i, :size].reshape(1, owners * size))]
    pallas_call x1, Pallas kernels: 62 us -> 54.8 us  [feed(): pl.pallas_call(functools.partial(feed_body, chunk), grid=(rows // block,)...]
    unnamed x101 -> x109, local copies, waits for them, and re-layouts: 16.6 us -> 22.3 us
    ppermute x12, waiting for transfers between devices: 2.54 us -> 7.86 us  [swap_cores(): return lax.ppermute(value, 'seq', [(0, 1), (1, 0)])]
    pad x0 -> x8, local copies, waits for them, and re-layouts: none -> 5.29 us  [on_device(): jnp.pad(shards[i][None], ((0, 0), (0, 128 - size)))]
    ppermute x12 -> x10, waiting for transfers between devices: 8.57 us -> 13.4 us  [swap_y(): return lax.ppermute(value, 'fsdp', [(i, i ^ 2) for i in range(16)])]
    ppermute x12 -> x10, waiting for transfers between devices: 15 us -> 11.1 us  [swap_x(): return lax.ppermute(value, 'fsdp', [(i, i ^ 1) for i in range(16)])]
  transfers between devices with their start and end apart: 51 -> 44, of which waited for: 13 -> 14; matrix products, arithmetic and copies ran while one was open for 17% -> 12% of each run, Pallas kernels for 31% -> 36%
where the time goes in v4:
time: 422 us; the launch traced here: 416 us
  Pallas kernels  221 us (52%)
  local copies, waits for them, and re-layouts  53.6 us (13%)
  starting transfers between devices  51.7 us (12%)
  waiting for transfers between devices  39.5 us (9%)
  matrix products  25.5 us (6%)
  other arithmetic  23 us (5%)
    pallas_call x2, Pallas kernels, attend_back(): pl.pallas_call(functools.partial(attend_back_body, block), grid=(pairs,),...  57.6 us
    pallas_call x1, Pallas kernels, feed(): pl.pallas_call(functools.partial(feed_body, chunk), grid=(rows // block,)...  54.8 us
    pallas_call x2, Pallas kernels, attend(): pl.pallas_call(functools.partial(attend_body, block), grid=(pairs,), in_s...  52 us
    ppermute x12, starting transfers between devices, shift_z(): lax.ppermute(value, 'fsdp', [(i, (i + 4 * k) % 16) for i in range(16)])  28 us
    dot_general x6, matrix products, dot_lt(): lax.dot_general(left, right, (((0,), (0,)), ((), ())), preferred_element_...  25.5 us
    unnamed x109, local copies, waits for them, and re-layouts  22.3 us
    pallas_call x2, Pallas kernels, project_back(): pl.pallas_call(functools.partial(project_back_body, block), grid=(1,), in...  17.2 us
    ppermute x10, waiting for transfers between devices, swap_y(): return lax.ppermute(value, 'fsdp', [(i, i ^ 2) for i in range(16)])  13.4 us
  transfers between devices with their start and end apart: 44, of which 14 were waited for; matrix products, arithmetic and copies ran while one was open for 12% of the time, Pallas kernels for 36%

profile of v4, /device:TPU:0, one launch (start us, length us, event | category | flops | bytes accessed | tf_op | source)
XLA Modules:
  0.0 416.1 jit_solution(7125470204380284148)
XLA Ops:
  6.9 4.1 collective-permute-start.7
  13.8 3.6 ready.1
  18.4 3.6 collective-permute-start.9
  23.6 2.5 collective-permute-done.9
  28.2 2.4 collective-permute-done.1
  30.7 9.7 %arrange.1.xw_ref.refs_0_ = bf16[2,1280,768]{2,1,0:T(8,128)(2,1)S(1)} custom-call(s32[2,1280,1]{2,1,0:T(8,128)S(1)} %get-tuple-element.109.idx_ref, bf16[2,640,768]{2,1,0:T(8,128)(2,1)S(1)} %bitcast.186, bf16[2,640,768]{2,1,0:T(8,128)(2,1)} %collective-permute-done.5.other_ref), custom_call_target="tpu_custom_call" | custom-call | flops 5033164800 | bytes 7864320 | tf_op jit(solution)/shard_map/arrange/pallas_call | solution.py:122
  48.4 2.4 collective-permute-start.3
  50.8 3.4 collective-permute-start.4
  58.8 5.3 %project.3.qkv_ref = bf16[3,1280,384]{2,1,0:T(8,128)(2,1)S(1)} custom-call(s32[1]{0:T(128)} %bitcast.part_ref, bf16[2,1280,768]{2,1,0:T(8,128)(2,1)S(1)} %copy-done.1, bf16[384,2432]{1,0:T(8,128)(2,1)S(1)} %bitcast.180, bf16[384,2432]{1,0:T(8,128)(2,1)} %collective-permute-done.11.away_ref.waway_ref, f32[1,1152]{1,0:T(1,128)S(1)} %pad_maximum_fusion.16.bias_ref, ...), custom_call_target="tpu_custom_call" | custom-call | flops 2264924160 | bytes 6684672 | tf_op jit(solution)/shard_map/project/pallas_call | solution.py:184
  65.8 5.3 %project.2.qkv_ref = bf16[3,1280,384]{2,1,0:T(8,128)(2,1)S(1)} custom-call(s32[1]{0:T(128)} %bitcast.part_ref, bf16[2,1280,768]{2,1,0:T(8,128)(2,1)S(1)} %copy-done.1, bf16[384,2432]{1,0:T(8,128)(2,1)S(1)} %bitcast.181, bf16[384,2432]{1,0:T(8,128)(2,1)} %collective-permute-done.11.away_ref.waway_ref, f32[1,1152]{1,0:T(1,128)S(1)} %pad_maximum_fusion.16.bias_ref, ...), custom_call_target="tpu_custom_call" | custom-call | flops 2264924160 | bytes 6684672 | tf_op jit(solution)/shard_map/project/pallas_call | solution.py:184
  78.9 26.0 %attend.2 = (bf16[640,384]{1,0:T(8,128)(2,1)}, bf16[640,384]{1,0:T(8,128)(2,1)}, bf16[384,1280]{1,0:T(8,128)(2,1)}, f32[3,8,1280]{2,1,0:T(8,128)}) custom-call(s32[2,1280,1]{2,1,0:T(8,128)} %copy-done.8, bf16[3,1280,384]{2,1,0:T(8,128)(2,1)} %copy-done.6, s32[2,1280,1]{2,1,0:T(8,128)} %copy-done.9, s32[2,1,1280]{2,1,0:T(1,128)} %copy-done.12), custom_call_target="tpu_custom_call" | custom-call | flops 7549747200 | bytes 5898240 | tf_op jit(solution)/shard_map/attend/pallas_call | solution.py:259
  108.8 26.0 %attend.3 = (bf16[640,384]{1,0:T(8,128)(2,1)}, bf16[640,384]{1,0:T(8,128)(2,1)}, bf16[384,1280]{1,0:T(8,128)(2,1)}, f32[3,8,1280]{2,1,0:T(8,128)}) custom-call(s32[2,1280,1]{2,1,0:T(8,128)} %copy-done.8, bf16[3,1280,384]{2,1,0:T(8,128)(2,1)} %copy-done.5, s32[2,1280,1]{2,1,0:T(8,128)} %copy-done.9, s32[2,1,1280]{2,1,0:T(1,128)} %copy-done.12), custom_call_target="tpu_custom_call" | custom-call | flops 7549747200 | bytes 5898240 | tf_op jit(solution)/shard_map/attend/pallas_call | solution.py:259
  134.8 2.4 collective-permute-done.16.ay_ref
  138.5 4.9 %assemble.3 = (bf16[16,24,3840]{2,1,0:T(8,128)(2,1)}, bf16[16,96,768]{2,1,0:T(8,128)(2,1)}) custom-call(s32[1]{0:T(128)} %bitcast.13.place_ref, bf16[4,24,6912]{2,1,0:T(8,128)(2,1)} %pad_maximum_fusion.3.ax_ref, bf16[4,24,6912]{2,1,0:T(8,128)(2,1)} %collective-permute-done.16.ay_ref, bf16[4,24,6912]{2,1,0:T(8,128)(2,1)} %collective-permute-done.17.bx_ref, ...), custom_call_target="tpu_custom_call" | custom-call | bytes 10616832 | tf_op jit(solution)/shard_map/assemble/pallas_call | solution.py:671
  147.4 5.8 %collective-permute-done.14 = bf16[640,384]{1,0:T(8,128)(2,1)} collective-permute-done((bf16[640,384]{1,0:T(8,128)(2,1)}, bf16[640,384]{1,0:T(8,128)(2,1)}, u32[]{:S(2)}, u32[]{:S(2)}) %collective-permute-start.14) | collective-permute-done | bytes 491552 | tf_op jit(solution)/shard_map/ppermute | solution.py:629
  157.8 54.8 %feed.1 = (bf16[1280,768]{1,0:T(8,128)(2,1)}, f32[1280,768]{1,0:T(8,128)}, bf16[2,1280,384]{2,1,0:T(8,128)(2,1)}, bf16[2,1280,1536]{2,1,0:T(8,128)(2,1)}, bf16[1...) custom-call(s32[1]{0:T(128)} %bitcast.part_ref, ...), custom_call_target="tpu_custom_call" | custom-call | flops 27179089920 | bytes 41287680 | tf_op jit(solution)/shard_map/feed/pallas_call | solution.py:604
  212.6 7.5 %fusion.6 = bf16[1536,768]{1,0:T(8,128)(2,1)} fusion(bf16[1280,768]{1,0:T(8,128)(2,1)} %get-tuple-element.147, bf16[2,1280,1536]{2,1,0:T(8,128)(2,1)} %get-tuple-element.146), kind=kOutput, calls=%fused_computation.12 | convolution fusion | flops 3021078528 | bytes 8257536 | tf_op jit(solution)/shard_map/dot_general | solution.py:31
  220.3 3.7 convolution_convert_fusion
  233.9 2.4 fusion.67
  236.4 6.3 %add_convert_fusion.1 = bf16[1536,768]{1,0:T(8,128)(2,1)S(1)} fusion(bf16[1536,768]{1,0:T(8,128)(2,1)} %collective-permute-done.21, bf16[1280,768]{1,0:T(8,128)(2,1)S(1)} %copy-done.45, bf16[2,1280,1536]{2,1,0:T(8,128)(2,1)} %get-tuple-element.146), kind=kOutput, calls=%fused_computation.1 | convolution fusion | flops 3023437824 | bytes 10616832 | tf_op jit(solution)/shard_map/dot_general | solution.py:31
  245.9 4.9 %add_convert_fusion = bf16[384,3072]{1,0:T(8,128)(2,1)S(1)} fusion(bf16[1280,3072]{1,0:T(8,128)(2,1)S(1)} %bitcast.218, bf16[384,3840]{1,0:T(8,128)(2,1)} %collective-permute-done.22, bf16[2,1280,384]{2,1,0:T(8,128)(2,1)S(1)} %copy-done.44), kind=kOutput, calls=%fused_computation | convolution fusion | flops 3023437824 | bytes 13565952 | tf_op jit(solution)/shard_map/dot_general | solution.py:31
  259.2 29.0 %attend_back.2.refs_1_.g_ref = bf16[3,1280,384]{2,1,0:T(8,128)(2,1)} custom-call(s32[2,1280,1]{2,1,0:T(8,128)} %copy-done.8, bf16[3,1280,384]{2,1,0:T(8,128)(2,1)} %copy-done.6, s32[2,1280,1]{2,1,0:T(8,128)} %copy-done.9, s32[2,1,1280]{2,1,0:T(1,128)} %copy-done.12, f32[3,8,1280]{2,1,0:T(8,128)} %get-tuple-element.142.lse_ref, ...), custom_call_target="tpu_custom_call" | custom-call | flops 17616076800 | bytes 8847360 | tf_op jit(solution)/shard_map/attend_back/pallas_call | solution.py:372
  288.2 2.2 fusion.62
  303.1 28.6 %attend_back.3.refs_2_.g_ref = bf16[3,1280,384]{2,1,0:T(8,128)(2,1)} custom-call(s32[2,1280,1]{2,1,0:T(8,128)} %copy-done.8, bf16[3,1280,384]{2,1,0:T(8,128)(2,1)} %copy-done.5, s32[2,1280,1]{2,1,0:T(8,128)} %copy-done.9, s32[2,1,1280]{2,1,0:T(1,128)} %copy-done.12, f32[3,8,1280]{2,1,0:T(8,128)} %get-tuple-element.153.lse_ref, ...), custom_call_target="tpu_custom_call" | custom-call | flops 17616076800 | bytes 8847360 | tf_op jit(solution)/shard_map/attend_back/pallas_call | solution.py:372
  336.8 10.3 %weight_back.1 = (bf16[768,1152]{1,0:T(8,128)(2,1)}, f32[8,1152]{1,0:T(8,128)}) custom-call(bf16[2,1280,768]{2,1,0:T(8,128)(2,1)} %copy-done, bf16[3,1280,384]{2,1,0:T(8,128)(2,1)} %attend_back.2.refs_1_.g_ref, bf16[3,1280,384]{2,1,0:T(8,128)(2,1)} %attend_back.3.refs_2_.g_ref), custom_call_target="tpu_custom_call" | custom-call | flops 4529848320 | bytes 11599872 | tf_op jit(solution)/shard_map/weight_back/pallas_call | solution.py:464
  351.7 7.7 %collective-permute-start.41 = (bf16[24,6912]{1,0:T(8,128)(2,1)S(1)}, bf16[24,6912]{1,0:T(8,128)(2,1)S(1)}, u32[]{:S(2)}, u32[]{:S(2)}) collective-permute-start(bf16[24,6912]{1,0:T(8,128)(2,1)S(1)} %copy-done.32), channel_id=1, source_target_pairs={{0,4},{1,5},{2,6},{3,7},{4,8},{5,9},{6,10},{7,11},{8,12},{9,13},{1... | collective-permute-start | bytes 995336 | tf_op jit(solution)/shard_map/ppermute | solution.py:641
  359.5 2.2 collective-permute-start.42
  361.9 8.6 %project_back.2 = (bf16[640,768]{1,0:T(8,128)(2,1)S(1)}, bf16[640,768]{1,0:T(8,128)(2,1)S(1)}) custom-call(s32[1]{0:T(128)} %bitcast.part_ref, bf16[3,1280,384]{2,1,0:T(8,128)(2,1)S(1)} %copy-done.10, s32[2,1,1280]{2,1,0:T(1,128)S(1)} %get-tuple-element.181.row_ref, bf16[384,2432]{1,0:T(8,128)(2,1)S(1)} %bitcast.182, ...), custom_call_target="tpu_custom_call" | custom-call | flops 4781506560 | bytes 6684672 | tf_op jit(solution)/shard_map/project_back/pallas_call | solution.py:430
  372.9 8.6 %project_back.3 = (bf16[640,768]{1,0:T(8,128)(2,1)S(1)}, bf16[640,768]{1,0:T(8,128)(2,1)S(1)}) custom-call(s32[1]{0:T(128)} %bitcast.part_ref, bf16[3,1280,384]{2,1,0:T(8,128)(2,1)S(1)} %copy-done.11, s32[2,1,1280]{2,1,0:T(1,128)S(1)} %get-tuple-element.181.row_ref, bf16[384,2432]{1,0:T(8,128)(2,1)S(1)} %bitcast.183, ...), custom_call_target="tpu_custom_call" | custom-call | flops 4781506560 | bytes 6684672 | tf_op jit(solution)/shard_map/project_back/pallas_call | solution.py:430
  384.8 7.2 %collective-permute-done.36 = bf16[2,24,2432]{2,1,0:T(8,128)(2,1)S(1)} collective-permute-done((bf16[2,24,2432]{2,1,0:T(8,128)(2,1)S(1)}, bf16[2,24,2432]{2,1,0:T(8,128)(2,1)S(1)}, u32[]{:S(2)}, u32[]{:S(2)}) %collective-permute-start.36) | collective-permute-done | bytes 233504 | tf_op jit(solution)/shard_map/ppermute | solution.py:633
  392.5 6.5 %collective-permute-done.37 = bf16[2,24,2432]{2,1,0:T(8,128)(2,1)S(1)} collective-permute-done((bf16[2,24,2432]{2,1,0:T(8,128)(2,1)S(1)}, bf16[2,24,2432]{2,1,0:T(8,128)(2,1)S(1)}, u32[]{:S(2)}, u32[]{:S(2)}) %collective-permute-start.37) | collective-permute-done | bytes 233504 | tf_op jit(solution)/shard_map/ppermute | solution.py:637
  407.3 4.5 %collective-permute-done.39 = bf16[24,2432]{1,0:T(8,128)(2,1)S(1)} collective-permute-done((bf16[24,2432]{1,0:T(8,128)(2,1)S(1)}, bf16[24,2432]{1,0:T(8,128)(2,1)S(1)}, u32[]{:S(2)}, u32[]{:S(2)}) %collective-permute-start.39) | collective-permute-done | bytes 116768 | tf_op jit(solution)/shard_map/ppermute | solution.py:641
  (310 shorter events, 111.7 us)
Async XLA Ops:
  6.9 11.5 %collective-permute-start.7 = (bf16[24,2432]{1,0:T(8,128)(2,1)S(1)}, bf16[24,2432]{1,0:T(8,128)(2,1)S(1)}, u32[]{:S(2)}, u32[]{:S(2)}) collective-permute-start(bf16[24,2432]{1,0:T(8,128)(2,1)S(1)} %get-tuple-element.284), channel_id=1, source_target_pairs={{0,8},{1,9},{2,10},{3,11},{4,12},{5,13},{6,14},{7,15},{8,0},{9,1},... | collective-permute-start | bytes 350216 | tf_op jit(solution)/shard_map/ppermute | solution.py:641
  13.1 17.7 %collective-permute-start.5 = (bf16[2,640,768]{2,1,0:T(8,128)(2,1)}, bf16[2,640,768]{2,1,0:T(8,128)(2,1)}, u32[]{:S(2)}, u32[]{:S(2)}) collective-permute-start(bf16[2,640,768]{2,1,0:T(8,128)(2,1)} %bitcast.184), channel_id=1, source_target_pairs={{0,16},{16,0},{1,17},{17,1},{2,18},{18,2},{3,19},{19,3},{4,20},{20... | collective-permute-start | bytes 5898248 | tf_op jit(solution)/shard_map/ppermute | solution.py:629
  26.1 16.2 %collective-permute-start.10 = (bf16[4,24,2432]{2,1,0:T(8,128)(2,1)S(1)}, bf16[4,24,2432]{2,1,0:T(8,128)(2,1)S(1)}, u32[]{:S(2)}, u32[]{:S(2)}) collective-permute-start(bf16[4,24,2432]{2,1,0:T(8,128)(2,1)S(1)} %pad_maximum_fusion.9.by_ref), channel_id=1, source_target_pairs={{0,1},{1,0},{2,3},{3,2},{4,5},{5,4},{6,7},{7,6},{8,9},{9,8},{10,11... | collective-permute-start | bytes 1400840 | tf_op jit(solution)/shard_map/ppermute | solution.py:633
  30.6 11.7 %collective-permute-start.6 = (bf16[4,24,2432]{2,1,0:T(8,128)(2,1)S(1)}, bf16[4,24,2432]{2,1,0:T(8,128)(2,1)S(1)}, u32[]{:S(2)}, u32[]{:S(2)}) collective-permute-start(bf16[4,24,2432]{2,1,0:T(8,128)(2,1)S(1)} %pad_maximum_fusion.8.ax_ref), channel_id=1, source_target_pairs={{0,2},{1,3},{2,0},{3,1},{4,6},{5,7},{6,4},{7,5},{8,10},{9,11},{10,... | collective-permute-start | bytes 1400840 | tf_op jit(solution)/shard_map/ppermute | solution.py:637
  42.5 11.8 %collective-permute-start.11 = (bf16[384,2432]{1,0:T(8,128)(2,1)S(1)}, bf16[384,2432]{1,0:T(8,128)(2,1)}, u32[]{:S(2)}, u32[]{:S(2)}) collective-permute-start(bf16[384,2432]{1,0:T(8,128)(2,1)S(1)} %bitcast.178), channel_id=1, source_target_pairs={{0,16},{16,0},{1,17},{17,1},{2,18},{18,2},{3,19},{19,3},{4,20},{20... | collective-permute-start | bytes 5603336 | tf_op jit(solution)/shard_map/ppermute | solution.py:629
  46.8 26.0 %collective-permute-start.2 = (bf16[24,6912]{1,0:T(8,128)(2,1)}, bf16[24,6912]{1,0:T(8,128)(2,1)}, u32[]{:S(2)}, u32[]{:S(2)}) collective-permute-start(bf16[24,6912]{1,0:T(8,128)(2,1)} %constant_dynamic-update-slice_fusion), channel_id=1, source_target_pairs={{0,4},{1,5},{2,6},{3,7},{4,8},{5,9},{6,10},{7,11},{8,12},{9,13},{1... | collective-permute-start | bytes 995336 | tf_op jit(solution)/shard_map/ppermute | solution.py:641
  48.4 24.6 %collective-permute-start.3 = (bf16[24,6912]{1,0:T(8,128)(2,1)}, bf16[24,6912]{1,0:T(8,128)(2,1)}, u32[]{:S(2)}, u32[]{:S(2)}) collective-permute-start(bf16[24,6912]{1,0:T(8,128)(2,1)} %constant_dynamic-update-slice_fusion), channel_id=1, source_target_pairs={{0,8},{1,9},{2,10},{3,11},{4,12},{5,13},{6,14},{7,15},{8,0},{9,1},... | collective-permute-start | bytes 995336 | tf_op jit(solution)/shard_map/ppermute | solution.py:641
  50.8 22.2 %collective-permute-start.4 = (bf16[24,6912]{1,0:T(8,128)(2,1)}, bf16[24,6912]{1,0:T(8,128)(2,1)}, u32[]{:S(2)}, u32[]{:S(2)}) collective-permute-start(bf16[24,6912]{1,0:T(8,128)(2,1)} %constant_dynamic-update-slice_fusion), channel_id=1, source_target_pairs={{0,12},{1,13},{2,14},{3,15},{4,0},{5,1},{6,2},{7,3},{8,4},{9,5},{1... | collective-permute-start | bytes 995336 | tf_op jit(solution)/shard_map/ppermute | solution.py:641
  75.3 29.6 %collective-permute-start.12 = (bf16[2,24,6912]{2,1,0:T(8,128)(2,1)S(1)}, bf16[2,24,6912]{2,1,0:T(8,128)(2,1)S(1)}, u32[]{:S(2)}, u32[]{:S(2)}) collective-permute-start(bf16[2,24,6912]{2,1,0:T(8,128)(2,1)S(1)} %pad_maximum_fusion.6), channel_id=1, source_target_pairs={{0,1},{1,0},{2,3},{3,2},{4,5},{5,4},{6,7},{7,6},{8,9},{9,8},{10,11... | collective-permute-start | bytes 1990664 | tf_op jit(solution)/shard_map/ppermute | solution.py:633
  76.9 28.1 %collective-permute-start.13 = (bf16[2,24,6912]{2,1,0:T(8,128)(2,1)S(1)}, bf16[2,24,6912]{2,1,0:T(8,128)(2,1)}, u32[]{:S(2)}, u32[]{:S(2)}) collective-permute-start(bf16[2,24,6912]{2,1,0:T(8,128)(2,1)S(1)} %pad_maximum_fusion.7), channel_id=1, source_target_pairs={{0,2},{1,3},{2,0},{3,1},{4,6},{5,7},{6,4},{7,5},{8,10},{9,11},{10,... | collective-permute-start | bytes 1990664 | tf_op jit(solution)/shard_map/ppermute | solution.py:637
  108.3 29.0 %collective-permute-start.16 = (bf16[4,24,6912]{2,1,0:T(8,128)(2,1)}, bf16[4,24,6912]{2,1,0:T(8,128)(2,1)}, u32[]{:S(2)}, u32[]{:S(2)}) collective-permute-start(bf16[4,24,6912]{2,1,0:T(8,128)(2,1)} %pad_maximum_fusion.3.ax_ref), channel_id=1, source_target_pairs={{0,2},{1,3},{2,0},{3,1},{4,6},{5,7},{6,4},{7,5},{8,10},{9,11},{10,... | collective-permute-start | bytes 3981320 | tf_op jit(solution)/shard_map/ppermute | solution.py:637
  108.3 30.2 %collective-permute-start.17 = (bf16[4,24,6912]{2,1,0:T(8,128)(2,1)S(1)}, bf16[4,24,6912]{2,1,0:T(8,128)(2,1)}, u32[]{:S(2)}, u32[]{:S(2)}) collective-permute-start(bf16[4,24,6912]{2,1,0:T(8,128)(2,1)S(1)} %pad_maximum_fusion.4.by_ref), channel_id=1, source_target_pairs={{0,1},{1,0},{2,3},{3,2},{4,5},{5,4},{6,7},{7,6},{8,9},{9,8},{10,11... | collective-permute-start | bytes 3981320 | tf_op jit(solution)/shard_map/ppermute | solution.py:633
  143.4 13.5 %collective-permute-start.18 = (bf16[384,3840]{1,0:T(8,128)(2,1)}, bf16[384,3840]{1,0:T(8,128)(2,1)}, u32[]{:S(2)}, u32[]{:S(2)}) collective-permute-start(bf16[384,3840]{1,0:T(8,128)(2,1)} %bitcast.24.unear_ref), channel_id=1, source_target_pairs={{0,16},{16,0},{1,17},{17,1},{2,18},{18,2},{3,19},{19,3},{4,20},{20... | collective-permute-start | bytes 8847368 | tf_op jit(solution)/shard_map/ppermute | solution.py:629
  143.4 13.5 %collective-permute-start.19 = (bf16[1536,768]{1,0:T(8,128)(2,1)}, bf16[1536,768]{1,0:T(8,128)(2,1)}, u32[]{:S(2)}, u32[]{:S(2)}) collective-permute-start(bf16[1536,768]{1,0:T(8,128)(2,1)} %bitcast.25.dnear_ref), channel_id=1, source_target_pairs={{0,16},{16,0},{1,17},{17,1},{2,18},{18,2},{3,19},{19,3},{4,20},{20... | collective-permute-start | bytes 7077896 | tf_op jit(solution)/shard_map/ppermute | solution.py:629
  220.2 16.2 %collective-permute-start.21 = (bf16[1536,768]{1,0:T(8,128)(2,1)}, bf16[1536,768]{1,0:T(8,128)(2,1)}, u32[]{:S(2)}, u32[]{:S(2)}) collective-permute-start(bf16[1536,768]{1,0:T(8,128)(2,1)} %fusion.6), channel_id=1, source_target_pairs={{0,16},{16,0},{1,17},{17,1},{2,18},{18,2},{3,19},{19,3},{4,20},{20... | collective-permute-start | bytes 7077896 | tf_op jit(solution)/shard_map/ppermute | solution.py:629
  226.8 19.1 %collective-permute-start.22 = (bf16[384,3840]{1,0:T(8,128)(2,1)}, bf16[384,3840]{1,0:T(8,128)(2,1)}, u32[]{:S(2)}, u32[]{:S(2)}) collective-permute-start(bf16[384,3840]{1,0:T(8,128)(2,1)} %pad_maximum_fusion.1), channel_id=1, source_target_pairs={{0,16},{16,0},{1,17},{17,1},{2,18},{18,2},{3,19},{19,3},{4,20},{20... | collective-permute-start | bytes 8847368 | tf_op jit(solution)/shard_map/ppermute | solution.py:629
  255.1 40.2 %collective-permute-start.25 = (bf16[2,2,24,3840]{3,2,0,1:T(8,128)(2,1)S(1)}, bf16[2,2,24,3840]{3,2,0,1:T(8,128)(2,1)S(1)}, u32[]{:S(2)}, u32[]{:S(2)}) collective-permute-start(bf16[2,2,24,3840]{3,2,0,1:T(8,128)(2,1)S(1)} %copy_bitcast_fusion.3), channel_id=1, source_target_pairs={{0,2},{1,3},{2,0},{3,1},{4,6},{5,7},{6,4},{7,5},{8,10},{9,11},{10,... | collective-permute-start | bytes 2211848 | tf_op jit(solution)/shard_map/ppermute | solution.py:637
  255.6 39.7 %collective-permute-start.26 = (bf16[2,2,24,3840]{3,2,0,1:T(8,128)(2,1)S(1)}, bf16[2,2,24,3840]{3,2,0,1:T(8,128)(2,1)}, u32[]{:S(2)}, u32[]{:S(2)}) collective-permute-start(bf16[2,2,24,3840]{3,2,0,1:T(8,128)(2,1)S(1)} %copy_bitcast_fusion.2), channel_id=1, source_target_pairs={{0,1},{1,0},{2,3},{3,2},{4,5},{5,4},{6,7},{7,6},{8,9},{9,8},{10,11... | collective-permute-start | bytes 2211848 | tf_op jit(solution)/shard_map/ppermute | solution.py:633
  256.2 34.7 %collective-permute-start.23 = (bf16[2,2,96,768]{3,2,0,1:T(8,128)(2,1)}, bf16[2,2,96,768]{3,2,0,1:T(8,128)(2,1)}, u32[]{:S(2)}, u32[]{:S(2)}) collective-permute-start(bf16[2,2,96,768]{3,2,0,1:T(8,128)(2,1)} %copy_bitcast_fusion.7), channel_id=1, source_target_pairs={{0,2},{1,3},{2,0},{3,1},{4,6},{5,7},{6,4},{7,5},{8,10},{9,11},{10,... | collective-permute-start | bytes 1769480 | tf_op jit(solution)/shard_map/ppermute | solution.py:637
  257.7 33.2 %collective-permute-start.24 = (bf16[2,2,96,768]{3,2,0,1:T(8,128)(2,1)}, bf16[2,2,96,768]{3,2,0,1:T(8,128)(2,1)}, u32[]{:S(2)}, u32[]{:S(2)}) collective-permute-start(bf16[2,2,96,768]{3,2,0,1:T(8,128)(2,1)} %copy_bitcast_fusion.6), channel_id=1, source_target_pairs={{0,1},{1,0},{2,3},{3,2},{4,5},{5,4},{6,7},{7,6},{8,9},{9,8},{10,11... | collective-permute-start | bytes 1769480 | tf_op jit(solution)/shard_map/ppermute | solution.py:633
  299.0 32.7 %collective-permute-start.30 = (bf16[2,96,768]{2,1,0:T(8,128)(2,1)}, bf16[2,96,768]{2,1,0:T(8,128)(2,1)}, u32[]{:S(2)}, u32[]{:S(2)}) collective-permute-start(bf16[2,96,768]{2,1,0:T(8,128)(2,1)} %fusion.26), channel_id=1, source_target_pairs={{0,2},{1,3},{2,0},{3,1},{4,6},{5,7},{6,4},{7,5},{8,10},{9,11},{10,... | collective-permute-start | bytes 884744 | tf_op jit(solution)/shard_map/ppermute | solution.py:637
  299.6 33.5 %collective-permute-start.29 = (bf16[2,96,768]{2,1,0:T(8,128)(2,1)}, bf16[2,96,768]{2,1,0:T(8,128)(2,1)}, u32[]{:S(2)}, u32[]{:S(2)}) collective-permute-start(bf16[2,96,768]{2,1,0:T(8,128)(2,1)} %fusion.25), channel_id=1, source_target_pairs={{0,1},{1,0},{2,3},{3,2},{4,5},{5,4},{6,7},{7,6},{8,9},{9,8},{10,11... | collective-permute-start | bytes 884744 | tf_op jit(solution)/shard_map/ppermute | solution.py:633
  300.1 34.1 %collective-permute-start.27 = (bf16[2,24,3840]{2,1,0:T(8,128)(2,1)S(1)}, bf16[2,24,3840]{2,1,0:T(8,128)(2,1)}, u32[]{:S(2)}, u32[]{:S(2)}) collective-permute-start(bf16[2,24,3840]{2,1,0:T(8,128)(2,1)S(1)} %fusion.20), channel_id=1, source_target_pairs={{0,1},{1,0},{2,3},{3,2},{4,5},{5,4},{6,7},{7,6},{8,9},{9,8},{10,11... | collective-permute-start | bytes 1105928 | tf_op jit(solution)/shard_map/ppermute | solution.py:633
  301.6 33.8 %collective-permute-start.28 = (bf16[2,24,3840]{2,1,0:T(8,128)(2,1)}, bf16[2,24,3840]{2,1,0:T(8,128)(2,1)S(1)}, u32[]{:S(2)}, u32[]{:S(2)}) collective-permute-start(bf16[2,24,3840]{2,1,0:T(8,128)(2,1)} %fusion.21), channel_id=1, source_target_pairs={{0,2},{1,3},{2,0},{3,1},{4,6},{5,7},{6,4},{7,5},{8,10},{9,11},{10,... | collective-permute-start | bytes 1105928 | tf_op jit(solution)/shard_map/ppermute | solution.py:637
  351.7 18.9 %collective-permute-start.31 = (bf16[384,1280]{1,0:T(8,128)(2,1)S(1)}, bf16[384,1280]{1,0:T(8,128)(2,1)S(1)}, u32[]{:S(2)}, u32[]{:S(2)}) collective-permute-start(bf16[384,1280]{1,0:T(8,128)(2,1)S(1)} %pad_maximum_fusion.5), channel_id=1, source_target_pairs={{0,16},{16,0},{1,17},{17,1},{2,18},{18,2},{3,19},{19,3},{4,20},{20... | collective-permute-start | bytes 2949128 | tf_op jit(solution)/shard_map/ppermute | solution.py:629
  351.7 47.5 %collective-permute-start.41 = (bf16[24,6912]{1,0:T(8,128)(2,1)S(1)}, bf16[24,6912]{1,0:T(8,128)(2,1)S(1)}, u32[]{:S(2)}, u32[]{:S(2)}) collective-permute-start(bf16[24,6912]{1,0:T(8,128)(2,1)S(1)} %copy-done.32), channel_id=1, source_target_pairs={{0,4},{1,5},{2,6},{3,7},{4,8},{5,9},{6,10},{7,11},{8,12},{9,13},{1... | collective-permute-start | bytes 995336 | tf_op jit(solution)/shard_map/ppermute | solution.py:641
  359.5 41.3 %collective-permute-start.42 = (bf16[24,6912]{1,0:T(8,128)(2,1)S(1)}, bf16[24,6912]{1,0:T(8,128)(2,1)S(1)}, u32[]{:S(2)}, u32[]{:S(2)}) collective-permute-start(bf16[24,6912]{1,0:T(8,128)(2,1)S(1)} %copy-done.31), channel_id=1, source_target_pairs={{0,8},{1,9},{2,10},{3,11},{4,12},{5,13},{6,14},{7,15},{8,0},{9,1},... | collective-permute-start | bytes 995336 | tf_op jit(solution)/shard_map/ppermute | solution.py:641
  361.7 39.9 %collective-permute-start.43 = (bf16[24,6912]{1,0:T(8,128)(2,1)S(1)}, bf16[24,6912]{1,0:T(8,128)(2,1)S(1)}, u32[]{:S(2)}, u32[]{:S(2)}) collective-permute-start(bf16[24,6912]{1,0:T(8,128)(2,1)S(1)} %get-tuple-element.197), channel_id=1, source_target_pairs={{0,12},{1,13},{2,14},{3,15},{4,0},{5,1},{6,2},{7,3},{8,4},{9,5},{1... | collective-permute-start | bytes 995336 | tf_op jit(solution)/shard_map/ppermute | solution.py:641
  371.1 12.5 %collective-permute-start.34 = (bf16[2,2,24,2432]{3,2,0,1:T(8,128)(2,1)S(1)}, bf16[2,2,24,2432]{3,2,0,1:T(8,128)(2,1)S(1)}, u32[]{:S(2)}, u32[]{:S(2)}) collective-permute-start(bf16[2,2,24,2432]{3,2,0,1:T(8,128)(2,1)S(1)} %copy_bitcast_fusion.11), channel_id=1, source_target_pairs={{0,2},{1,3},{2,0},{3,1},{4,6},{5,7},{6,4},{7,5},{8,10},{9,11},{10,... | collective-permute-start | bytes 1400840 | tf_op jit(solution)/shard_map/ppermute | solution.py:637
  371.7 12.2 %collective-permute-start.35 = (bf16[2,2,24,2432]{3,2,0,1:T(8,128)(2,1)S(1)}, bf16[2,2,24,2432]{3,2,0,1:T(8,128)(2,1)S(1)}, u32[]{:S(2)}, u32[]{:S(2)}) collective-permute-start(bf16[2,2,24,2432]{3,2,0,1:T(8,128)(2,1)S(1)} %copy_bitcast_fusion.10), channel_id=1, source_target_pairs={{0,1},{1,0},{2,3},{3,2},{4,5},{5,4},{6,7},{7,6},{8,9},{9,8},{10,11... | collective-permute-start | bytes 1400840 | tf_op jit(solution)/shard_map/ppermute | solution.py:633
  383.6 30.0 %collective-permute-start.33 = (bf16[640,768]{1,0:T(8,128)(2,1)S(1)}, bf16[640,768]{1,0:T(8,128)(2,1)S(1)}, u32[]{:S(2)}, u32[]{:S(2)}) collective-permute-start(bf16[640,768]{1,0:T(8,128)(2,1)S(1)} %get-tuple-element.188), channel_id=1, source_target_pairs={{0,16},{16,0},{1,17},{17,1},{2,18},{18,2},{3,19},{19,3},{4,20},{20... | collective-permute-start | bytes 2949128 | tf_op jit(solution)/shard_map/ppermute | solution.py:629
  399.0 14.7 %collective-permute-start.32 = (bf16[640,768]{1,0:T(8,128)(2,1)S(1)}, bf16[640,768]{1,0:T(8,128)(2,1)S(1)}, u32[]{:S(2)}, u32[]{:S(2)}) collective-permute-start(bf16[640,768]{1,0:T(8,128)(2,1)S(1)} %get-tuple-element.185), channel_id=1, source_target_pairs={{0,16},{16,0},{1,17},{17,1},{2,18},{18,2},{3,19},{19,3},{4,20},{20... | collective-permute-start | bytes 2949128 | tf_op jit(solution)/shard_map/ppermute | solution.py:629
  (60 other events, 461.7 us)

commit v5 on v4

--- a/solution.py
+++ b/solution.py
@@ -100,6 +100,32 @@
     )(part, order, segments, freqs)
 
 
+def pack_body(thin, w_qkv, w_out, w_up, w_down, *refs):
+    q_ref, ud_ref = refs[thin:]
+    n, width = w_out.shape
+    wide = w_qkv.shape[1]
+    q_ref[:, :wide] = w_qkv[...]
+    q_ref[:, wide:] = jnp.zeros((n, q_ref.shape[1] - wide), BF)
+    for i, ref in enumerate(refs[:thin]):
+        q_ref[i:i + 1, wide:wide + ref.shape[1]] = ref[...]
+    ud_ref[:, :width] = w_out[...]
+    ud_ref[:, width:width + w_up.shape[1]] = w_up[...]
+    at = width + w_up.shape[1]
+    for c in range(w_down.shape[0] // n):
+        ud_ref[:, at + c * width:at + (c + 1) * width] = w_down[c * n:(c + 1) * n, :]
+
+
+def pack(w_qkv, w_out, w_up, w_down, thin):
+    n, width = w_out.shape
+    wide = width + w_up.shape[1] + w_down.shape[0] // n * width
+    return pl.pallas_call(
+        functools.partial(pack_body, len(thin)),
+        out_shape=[jax.ShapeDtypeStruct((n, w_qkv.shape[1] + 128), BF), jax.ShapeDtypeStruct((n, wide), BF)],
+        cost_estimate=pl.CostEstimate(flops=0, bytes_accessed=4 * n * (w_qkv.shape[1] + wide), transcendentals=0),
+        name="pack",
+    )(w_qkv, w_out, w_up, w_down, *[value[None] for value in thin])
+
+
 def arrange_body(block, idx_ref, own_ref, other_ref, xw_ref):
     half = own_ref.shape[1]
 
@@ -368,6 +394,7 @@
     half = rows // 2
     whole = lambda shape: pl.BlockSpec((1,) + shape, lambda j: (b, 0, 0))
     three = pl.BlockSpec((3, rows, PAIR), lambda j: (0, 0, j))
+    given = pl.BlockSpec((half, PAIR), lambda j: (b, j))
     column = lambda n: pl.BlockSpec((n, PAIR), lambda j: (0, j))
     return pl.pallas_call(
         functools.partial(attend_back_body, block),
@@ -375,7 +402,7 @@
         in_specs=[whole((rows, 1)), three, whole((rows, 1)), whole((1, rows)),
                   pl.BlockSpec((1, 8, rows), lambda j: (j, 0, 0)),
                   pl.BlockSpec((PAIR, rows), lambda j: (j, 0)),
-                  column(half), column(half), whole((rows, PAIR)), whole((rows, PAIR))],
+                  given, given, whole((rows, PAIR)), whole((rows, PAIR))],
         out_specs=pl.BlockSpec((3, rows, PAIR), lambda j: (0, 0, j)),
         out_shape=jax.ShapeDtypeStruct((3, rows, share), BF),
         scratch_shapes=[pltpu.VMEM((rows, rows), BF), pltpu.VMEM((rows, 2 * PAIR), BF),
@@ -510,15 +537,15 @@
 
 def feed_body(chunk, part_ref, x_ref, near_ref, away_ref, dy_ref, thin_ref, bup_ref,
               unear_ref, uaway_ref, dnear_ref, daway_ref,
-              out_ref, dh_ref, low_ref, act_ref, dup_ref, dlow_ref, da_ref, cnear_ref, caway_ref,
-              sums_ref, bsum_ref, wo_near, wo_away, wup, wdown, slopes, sems):
-    first_step = pl.program_id(0) == 0
+              out_ref, dh_ref, cnear_ref, caway_ref, sums_ref, bsum_ref,
+              dmine_ref, dtheirs_ref, omine_ref, otheirs_ref,
+              wo_near, wo_away, wup, wdown, slopes, acts, gup, gdown, go_near, go_away, sems, out_sems):
     core = part_ref[0]
     width, wide = wup.shape
-    share = near_ref.shape[1]
     half_w, half_f = width // 2, wide // 2
 
-    def loads():
+    @pl.when(pl.program_id(0) == 0)
+    def _():
         copies = []
         for t, (u_ref, d_ref) in enumerate(((unear_ref, dnear_ref), (uaway_ref, daway_ref))):
             side = core if t == 0 else 1 - core
@@ -531,15 +558,10 @@
                 pltpu.make_async_copy(
                     d_ref, wdown.at[pl.ds(pl.multiple_of(side * half_f, 128), half_f), :], sems.at[4 + t]),
             ]
-        return copies
-
-    @pl.when(first_step)
-    def _():
-        copies = loads()
         for copy in copies:
             copy.start()
-        sums_ref[...] = jnp.zeros_like(sums_ref)
-        bsum_ref[...] = jnp.zeros_like(bsum_ref)
+        for ref in (sums_ref, bsum_ref, gup, gdown, go_near, go_away):
+            ref[...] = jnp.zeros_like(ref)
         for copy in copies:
             copy.wait()
 
@@ -552,16 +574,12 @@
     norm_one, root_one = standard(x_ref[...].astype(F32) + attended)
     first = norm_one * gain_one + shift_one
     low = first.astype(BF)
-
-    low_ref[core] = low[:, :half_w]
-    low_ref[1 - core] = low[:, half_w:]
     lowered = None
     for c in range(wide // chunk):
         cols = slice(c * chunk, (c + 1) * chunk)
         act, slope = gauss_parts(dot(low, wup[:, cols]) + bup_ref[:, cols])
         act = act.astype(BF)
-        side = core if c * chunk < half_f else 1 - core
-        act_ref[side, :, c * chunk % half_f:c * chunk % half_f + chunk] = act
+        acts[:, cols] = act
         slopes[:, cols] = slope.astype(BF)
         term = dot(act, wdown[cols, :])
         lowered = term if lowered is None else lowered + term
@@ -572,13 +590,14 @@
     tally(5, dy)
     grad_two = standard_back(dy * gain_two, norm_two, root_two)
     dlow = grad_two.astype(BF)
-    dlow_ref[...] = dlow
     tally(3, dlow.astype(F32))
     total = grad_two
+    low_t, dlow_t = low.T, dlow.T
     for c in range(wide // chunk):
         cols = slice(c * chunk, (c + 1) * chunk)
         dup = (dot_rt(dlow, wdown[cols, :]) * slopes[:, cols].astype(F32)).astype(BF)
-        dup_ref[:, cols] = dup
+        gdown[:, cols] += dot(dlow_t, acts[:, cols])
+        gup[:, cols] += dot(low_t, dup)
         bsum_ref[0:1, cols] += jnp.sum(dup.astype(F32), axis=0, keepdims=True)
         total = total + dot_rt(dup, wup[:, cols])
     tally(1, total * norm_one)
@@ -586,10 +605,37 @@
     grad_one = standard_back(total * gain_one, norm_one, root_one)
     dh_ref[...] = grad_one
     da = grad_one.astype(BF)
-    da_ref[...] = da
     tally(0, da.astype(F32))
+    go_near[...] += dot(near_ref[...].T, da)
+    go_away[...] += dot(away_ref[...].T, da)
     cnear_ref[...] = dot_rt(da, wo_near[...]).astype(BF)
     caway_ref[...] = dot_rt(da, wo_away[...]).astype(BF)
+
+    @pl.when(pl.program_id(0) == pl.num_programs(0) - 1)
+    def _():
+        rows_d = [pl.ds(pl.multiple_of(side * half_f, 128), half_f) for side in (core, 1 - core)]
+        rows_u = [pl.ds(pl.multiple_of(side * half_w, 128), half_w) for side in (core, 1 - core)]
+        copies = []
+        for t, (d_ref, o_ref, hold) in enumerate(((dmine_ref, omine_ref, wo_near), (dtheirs_ref, otheirs_ref, wo_away))):
+            copies += [
+                pltpu.make_async_copy(wdown.at[rows_d[t], :], d_ref, out_sems.at[3 * t]),
+                pltpu.make_async_copy(wup.at[rows_u[t], :], o_ref.at[:, :wide], out_sems.at[3 * t + 1]),
+                pltpu.make_async_copy(hold, o_ref.at[:, wide:], out_sems.at[3 * t + 2]),
+            ]
+        for c in range(wide // width):
+            cols = slice(c * width, (c + 1) * width)
+            wdown[cols, :] = gdown[:, cols].T.astype(BF)
+        copies[0].start()
+        copies[3].start()
+        for c in range(wide // width):
+            cols = slice(c * width, (c + 1) * width)
+            wup[:, cols] = gup[:, cols].astype(BF)
+        wo_near[...] = go_near[...].astype(BF)
+        wo_away[...] = go_away[...].astype(BF)
+        for k in (1, 2, 4, 5):
+            copies[k].start()
+        for copy in copies:
+            copy.wait()
 
 
 def feed(part, x, near, away, dy, thin, bup, unear, uaway, dnear, daway, block=256, chunk=768):
@@ -597,28 +643,30 @@
     share = near.shape[1]
     wide = bup.shape[1]
     line = lambda n: pl.BlockSpec((block, n), lambda i: (i, 0))
-    pair = lambda n: pl.BlockSpec((2, block, n), lambda i: (0, i, 0))
     fixed = lambda shape: pl.BlockSpec(shape, lambda i: (0, 0))
     anywhere = pl.BlockSpec(memory_space=pl.ANY)
     shape = lambda n, dt: jax.ShapeDtypeStruct((rows, n), dt)
+    half = lambda n, m: jax.ShapeDtypeStruct((n // 2, m), BF)
     return pl.pallas_call(
         functools.partial(feed_body, chunk),
         grid=(rows // block,),
         in_specs=[pl.BlockSpec(memory_space=pltpu.SMEM), line(width), line(share), line(share), line(width),
                   fixed(thin.shape), fixed(bup.shape), anywhere, anywhere, anywhere, anywhere],
-        out_specs=[line(width), line(width), pair(width // 2), pair(wide // 2), line(wide), line(width), line(width),
-                   line(share), line(share), fixed((8, width)), fixed((8, wide))],
-        out_shape=[shape(width, BF), shape(width, F32),
-                   jax.ShapeDtypeStruct((2, rows, width // 2), BF), jax.ShapeDtypeStruct((2, rows, wide // 2), BF),
-                   shape(wide, BF), shape(width, BF), shape(width, BF), shape(share, BF), shape(share, BF),
-                   jax.ShapeDtypeStruct((8, width), F32), jax.ShapeDtypeStruct((8, wide), F32)],
+        out_specs=[line(width), line(width), line(share), line(share), fixed((8, width)), fixed((8, wide))]
+        + [anywhere] * 4,
+        out_shape=[shape(width, BF), shape(width, F32), shape(share, BF), shape(share, BF),
+                   jax.ShapeDtypeStruct((8, width), F32), jax.ShapeDtypeStruct((8, wide), F32),
+                   half(wide, width), half(wide, width), half(width, wide + width), half(width, wide + width)],
         scratch_shapes=[pltpu.VMEM((share, width), BF), pltpu.VMEM((share, width), BF),
                         pltpu.VMEM((width, wide), BF), pltpu.VMEM((wide, width), BF),
-                        pltpu.VMEM((block, wide), BF), pltpu.SemaphoreType.DMA((6,))],
+                        pltpu.VMEM((block, wide), BF), pltpu.VMEM((block, wide), BF),
+                        pltpu.VMEM((width, wide), F32), pltpu.VMEM((width, wide), F32),
+                        pltpu.VMEM((share, width), F32), pltpu.VMEM((share, width), F32),
+                        pltpu.SemaphoreType.DMA((6,)), pltpu.SemaphoreType.DMA((6,))],
         compiler_params=pltpu.CompilerParams(vmem_limit_bytes=60 << 20),
         cost_estimate=pl.CostEstimate(
-            flops=2 * rows * width * (2 * width + 4 * wide),
-            bytes_accessed=2 * rows * (7 * width + 2 * wide) + 4 * width * (wide + width),
+            flops=2 * rows * width * (3 * width + 6 * wide),
+            bytes_accessed=2 * rows * 7 * width + 8 * width * (wide + width),
             transcendentals=2 * rows * wide,
         ),
         name="feed",
@@ -635,6 +683,10 @@
 
 def swap_y(value):
     return lax.ppermute(value, "fsdp", [(i, i ^ 2) for i in range(16)])
+
+
+def flip_z(value, k):
+    return lax.ppermute(value, "fsdp", [(i, i ^ (4 * k)) for i in range(16)])
 
 
 def shift_z(value, k):
@@ -727,23 +779,30 @@
     return (first, second), (pick(first, 1 - x, 1).astype(BF), pick(second, 1 - y, 1).astype(BF))
 
 
-def fold_cross(stay, sends):
+def fold_cross(stay, sends, after=()):
     z, y, x = corner()
-    first = pick(stay[0], x, 1) + swap_x(sends[0]).astype(F32)
-    second = pick(stay[1], y, 1) + swap_y(sends[1]).astype(F32)
+    came = tie((swap_x(sends[0]), swap_y(sends[1])), after)
+    first = pick(stay[0], x, 1) + came[0].astype(F32)
+    second = pick(stay[1], y, 1) + came[1].astype(F32)
     return jnp.concatenate([first, second], axis=0)
 
 
 def fold_three(stack):
+    near = corner()[0] % 2
+    cube = stack.reshape((2, 2) + stack.shape[1:])
+    return (cube,), (pick(cube, 1 - near, 1).astype(BF),)
+
+
+def fold_four(stay, sends, after=()):
     z = corner()[0]
-    return (pick(stack, z, 0),), tuple(pick(stack, lax.rem(z + k, 4), 0).astype(BF) for k in (1, 2, 3))
+    near, far = z % 2, z // 2
+    came = tie(flip_z(sends[0], 1), after)
+    total = pick(stay[0], near, 1) + came.astype(F32)
+    return (pick(total, far, 0),), (pick(total, 1 - far, 0).astype(BF),)
 
 
 def fold_end(stay, sends, after=()):
-    total = stay[0]
-    for came in tie([shift_z(send, k) for k, send in zip((1, 2, 3), sends)], after):
-        total = total + came.astype(F32)
-    return total
+    return stay[0] + tie(flip_z(sends[0], 2), after).astype(F32)
 
 
 def on_device(tokens, permutation, segment_ids, cotangent, *shards):
@@ -763,22 +822,19 @@
 
     away_tokens = swap_cores(tokens)
     idx_col, idx_row, seg_col, seg_row, cosine, sine = ready(part, permutation[:, 0], segment_ids[:, 0])
-    xws = arrange(idx_col, tokens, away_tokens)
     if staged:
-        lanes = jnp.concatenate(
-            [jnp.pad(shards[i][None], ((0, 0), (0, 128 - size))) for i, size in zip(thin, sizes)]
-            + [jnp.zeros((n_qkv - len(thin), 128), BF)], axis=0)
-        q_shard = jnp.concatenate([shards[0], lanes], axis=1)
-        ud_shard = jnp.concatenate(
-            [shards[2], shards[6]] + [shards[8][i * n_qkv:(i + 1) * n_qkv] for i in range(4)], axis=1)
+        q_shard, ud_shard = pack(shards[0], shards[2], shards[6], shards[8], [shards[i] for i in thin])
         first, second = reach_z(q_shard)
+        first, second, idx_col = tie((first, second, idx_col))
         first_x, second_y = swap_x(first), swap_y(second)
         ud_shard = tie(ud_shard, first_x)
         q_parts = reach_two(jnp.concatenate([first, first_x], axis=0), jnp.concatenate([second, second_y], axis=0))
         ud_z = tuple(shift_z(ud_shard, k) for k in (1, 2, 3))
-        q_parts = tie(q_parts, (xws, cosine))
+        xws = arrange(idx_col, tokens, away_tokens)
+        q_parts = tie(q_parts, xws)
         (q_near,) = joined(q_parts)
     else:
+        xws = arrange(idx_col, tokens, away_tokens)
         packed = jnp.concatenate([shards[i] for i in thin] + [jnp.zeros((room - count,), BF)])
         q_shard = jnp.concatenate([shards[0], packed.reshape(n_qkv, 128)], axis=1)
         q_near = lax.all_gather(q_shard, "fsdp", axis=0, tiled=True)
@@ -827,38 +883,30 @@
         u_near, d_near = joined((first, first_y, second_x, second), 4, width)
     u_away, d_away = swap_cores(u_near), swap_cores(d_near)
     near, away = (jnp.concatenate([item[i] for item in ctxs], axis=0) for i in range(2))
-    (outputs, grad_one, low, act, dup, dlow, da, cnear, caway, sums, bsum) = feed(
+    (outputs, grad_one, cnear, caway, sums, bsum, d_mine, d_theirs, uo_mine, uo_theirs) = feed(
         part, tokens.reshape(batches * half, width), near, away,
         cotangent.reshape(batches * half, width), thin_rows, b_up, u_near, u_away, d_near, d_away,
     )
     caway = swap_cores(caway)
-
-    d_theirs = swap_cores(dot_lt(act[1], dlow).astype(BF))
-    uo_theirs = swap_cores(
-        jnp.concatenate([dot_lt(low[1], dup).astype(BF), dot_lt(away, da).astype(BF)], axis=1)
-    )
-    d_sum = (dot_lt(act[0], dlow) + d_theirs.astype(F32)).astype(BF)
-    uo_sum = jnp.concatenate([
-        (dot_lt(low[0], dup) + uo_theirs[:, :4 * width].astype(F32)).astype(BF),
-        (dot_lt(near, da) + uo_theirs[:, 4 * width:].astype(F32)).astype(BF),
-    ], axis=1)
+    d_theirs, uo_theirs = swap_cores(d_theirs), swap_cores(uo_theirs)
+    plus = lambda mine, theirs: (mine.astype(F32) + theirs.astype(F32)).astype(BF)
 
     def back(b, given):
         qkv, ctxt, lse = kept[b]
         return attend_back(b, idx_col, qkv, seg_col, seg_row, lse, ctxt, *given, cosine, sine)
 
-    givens = [(cnear[b * half:(b + 1) * half], caway[b * half:(b + 1) * half]) for b in range(batches)]
+    givens = [(cnear, caway)] * batches
     if staged:
-        given, d_step, uo_step = tie((givens[0], fold_one(d_sum), fold_one(uo_sum)))
-        first_back = back(0, given)
-        given, d_step, uo_step = tie((givens[1], fold_two(*d_step), fold_two(*uo_step)), first_back)
+        first_back = back(0, givens[0])
+        d_theirs, uo_theirs = tie((d_theirs, uo_theirs), first_back)
+        d_step, uo_step = fold_one(plus(d_mine, d_theirs)), fold_one(plus(uo_mine, uo_theirs))
+        given, d_step, uo_step = tie((givens[1], d_step, uo_step))
         grads = [first_back, back(1, given)]
-        wide, lines = fold_cross(*uo_step), fold_cross(*d_step)
-        lines = [lines[:, i * n_qkv:(i + 1) * n_qkv] for i in range(4)]
-        du_step = fold_three(jnp.concatenate([wide] + lines, axis=2))
-        grads, du_step = tie((grads, du_step))
+        d_step, uo_step = fold_two(*d_step, grads[1]), fold_two(*uo_step, grads[1])
+        grads, d_step, uo_step = tie((grads, d_step, uo_step))
     else:
         grads = [back(b, givens[b]) for b in range(batches)]
+        d_sum, uo_sum = plus(d_mine, d_theirs), plus(uo_mine, uo_theirs)
     gw_own, gb_own = weight_back(xws, grads)
 
     def halves(value):
@@ -872,9 +920,10 @@
         span = slice(s * share, (s + 1) * share)
         thin_columns += [jnp.where(core == 0, gb_own[0, span], blank),
                          jnp.where(core == 0, blank, gb_own[0, span])]
-    thin_grads = [jnp.concatenate(thin_columns), sums[0], sums[1], sums[2], bsum[0], sums[3], sums[4], sums[5]]
+    six = sums[:6].reshape(6, owners, -1).transpose(1, 0, 2).reshape(owners, -1)
     slab = jnp.concatenate(
-        [value.reshape(owners, -1) for value in thin_grads] + [jnp.zeros((owners, room - count), F32)], axis=1
+        [jnp.concatenate(thin_columns).reshape(owners, -1), bsum[0].reshape(owners, -1), six,
+         jnp.zeros((owners, room - count), F32)], axis=1
     ).astype(BF).reshape(owners * n_qkv, 128)
     mine, theirs = (jnp.concatenate(pair, axis=1) for pair in zip(halves(gw_own), halves(slab)))
     theirs = swap_cores(theirs)
@@ -884,12 +933,16 @@
     ], axis=1)
     backs = [project_back(0, part, grads[0], idx_row, q_near, q_away)]
     if staged:
-        last, q_step, backs = tie((grads[1], fold_one(q_sum), backs))
+        wide, lines = fold_cross(*uo_step, backs[0]), fold_cross(*d_step, backs[0])
+        lines = [lines[:, i * n_qkv:(i + 1) * n_qkv] for i in range(4)]
+        du_step = fold_three(jnp.concatenate([wide] + lines, axis=2))
+        last, q_step, du_step = tie((grads[1], fold_one(q_sum), du_step), backs)
         backs.append(project_back(1, part, last, idx_row, q_near, q_away))
-        q_step = fold_two(*q_step, backs[1])
-        q_last = fold_three(fold_cross(*q_step))
-        g_uo = fold_end(*du_step, q_last)
-        g_qkv = fold_end(*q_last, g_uo)
+        q_step = tie(fold_two(*q_step, backs[1]))
+        du_step = tie(fold_four(*du_step, q_step))
+        q_step = tie(fold_three(fold_cross(*q_step, du_step)))
+        q_step = fold_four(*q_step)
+        g_uo = fold_end(*du_step, q_step)
         g_down = jnp.concatenate([g_uo[:, (5 + i) * width:(6 + i) * width] for i in range(4)], axis=0)
     else:
         backs.append(project_back(1, part, grads[1], idx_row, q_near, q_away))
@@ -897,6 +950,13 @@
             value.astype(BF), "fsdp", scatter_dimension=0, tiled=True
         ).astype(F32)
         g_qkv, g_down, g_uo = summed(q_sum), summed(d_sum), summed(uo_sum)
+    grad_one = grad_one.reshape(batches, half, width)
+    token_grad = jnp.stack([
+        (grad_one[b] + backs[b][0].astype(F32) + swap_cores(backs[b][1]).astype(F32)).astype(BF)
+        for b in range(batches)
+    ])
+    if staged:
+        g_qkv = fold_end(*q_step, (g_uo, token_grad))
     own, other = g_qkv[:, :3 * share], g_qkv[:, 3 * share:6 * share]
     columns = []
     for s in range(3):
@@ -904,17 +964,12 @@
         columns += [jnp.where(core == 0, own[:, span], other[:, span]),
                     jnp.where(core == 0, other[:, span], own[:, span])]
     g_out, g_up = g_uo[:, 4 * width:5 * width], g_uo[:, :4 * width]
-    grad_one = grad_one.reshape(batches, half, width)
-    token_grad = jnp.stack([
-        (grad_one[b] + backs[b][0].astype(F32) + swap_cores(backs[b][1]).astype(F32)).astype(BF)
-        for b in range(batches)
-    ])
     flat = g_qkv[:, 3 * width:].reshape(room)
     thin_out, at = [], 0
-    for size in sizes:
+    for size in [sizes[0], sizes[4]] + [n_qkv] * 6:
         thin_out.append(flat[at:at + size])
         at += size
-    g_bqkv, g_bout, g_g1, g_s1, g_bup, g_bdown, g_g2, g_s2 = thin_out
+    g_bqkv, g_bup, g_bout, g_g1, g_s1, g_bdown, g_g2, g_s2 = thin_out
     return (
         outputs.reshape(batches, 1, half, width), token_grad[:, None],
         jnp.concatenate(columns, axis=1), g_bqkv, g_out, g_bout, g_g1, g_s1, g_up, g_bup, g_down, g_bdown, g_g2, g_s2,

time: 422 us -> 408 us (0.967)
  matrix products: 25.5 us -> 0 us
  Pallas kernels: 221 us -> 240 us
  local copies, waits for them, and re-layouts: 53.6 us -> 41 us
  starting transfers between devices: 51.7 us -> 58.9 us
  waiting for transfers between devices: 39.5 us -> 33.1 us
  other arithmetic: 23 us -> 27.8 us
    dot_general x6 -> x0, matrix products: 25.5 us -> none  [dot_lt(): lax.dot_general(left, right, (((0,), (0,)), ((), ())), preferred_element_...]
    ppermute x0 -> x4, starting transfers between devices: none -> 19.3 us  [flip_z(): return lax.ppermute(value, 'fsdp', [(i, i ^ 4 * k) for i in range(16)])]
    pallas_call x1, Pallas kernels: 54.8 us -> 72.1 us  [feed(): pl.pallas_call(functools.partial(feed_body, chunk), grid=(rows // block,)...]
    ppermute x12 -> x6, starting transfers between devices: 28 us -> 14.6 us  [shift_z(): lax.ppermute(value, 'fsdp', [(i, (i + 4 * k) % 16) for i in range(16)])]
    ppermute x0 -> x4, waiting for transfers between devices: none -> 13.1 us  [flip_z(): return lax.ppermute(value, 'fsdp', [(i, i ^ 4 * k) for i in range(16)])]
    ppermute x10, waiting for transfers between devices: 13.4 us -> 3.63 us  [swap_y(): return lax.ppermute(value, 'fsdp', [(i, i ^ 2) for i in range(16)])]
    ppermute x10, waiting for transfers between devices: 11.1 us -> 4.5 us  [swap_x(): return lax.ppermute(value, 'fsdp', [(i, i ^ 1) for i in range(16)])]
    convert_element_type x1 -> x2, other arithmetic: 0.14 us -> 5.69 us  [on_device(): (mine.astype(F32) + theirs.astype(F32)).astype(BF)]
  transfers between devices with their start and end apart: 44 -> 42, of which waited for: 14 -> 12; matrix products, arithmetic and copies ran while one was open for 12% -> 8% of each run, Pallas kernels for 36% -> 40%
where the time goes in v5:
time: 408 us; the launch traced here: 402 us
  Pallas kernels  240 us (59%)
  starting transfers between devices  58.9 us (14%)
  local copies, waits for them, and re-layouts  41 us (10%)
  waiting for transfers between devices  33.1 us (8%)
  other arithmetic  27.8 us (7%)
    pallas_call x1, Pallas kernels, feed(): pl.pallas_call(functools.partial(feed_body, chunk), grid=(rows // block,)...  72.1 us
    pallas_call x2, Pallas kernels, attend_back(): pl.pallas_call(functools.partial(attend_back_body, block), grid=(pairs,),...  57.1 us
    pallas_call x2, Pallas kernels, attend(): pl.pallas_call(functools.partial(attend_body, block), grid=(pairs,), in_s...  52 us
    unnamed x74, local copies, waits for them, and re-layouts  19.5 us
    ppermute x4, starting transfers between devices, flip_z(): return lax.ppermute(value, 'fsdp', [(i, i ^ 4 * k) for i in range(16)])  19.3 us
    pallas_call x2, Pallas kernels, project_back(): pl.pallas_call(functools.partial(project_back_body, block), grid=(1,), in...  17.3 us
    ppermute x6, starting transfers between devices, shift_z(): lax.ppermute(value, 'fsdp', [(i, (i + 4 * k) % 16) for i in range(16)])  14.6 us
    ppermute x4, waiting for transfers between devices, flip_z(): return lax.ppermute(value, 'fsdp', [(i, i ^ 4 * k) for i in range(16)])  13.1 us
  transfers between devices with their start and end apart: 42, of which 12 were waited for; matrix products, arithmetic and copies ran while one was open for 8% of the time, Pallas kernels for 40%

profile of v5, /device:TPU:0, one launch (start us, length us, event | category | flops | bytes accessed | tf_op | source)
XLA Modules:
  0.0 402.4 jit_solution(11852692502426261676)
XLA Ops:
  2.6 4.1 %collective-permute-start.1 = (bf16[24,2432]{1,0:T(8,128)(2,1)}, bf16[24,2432]{1,0:T(8,128)(2,1)S(1)}, u32[]{:S(2)}, u32[]{:S(2)}) collective-permute-start(bf16[24,2432]{1,0:T(8,128)(2,1)} %get-tuple-element.120), channel_id=1, source_target_pairs={{0,8},{1,9},{2,10},{3,11},{4,12},{5,13},{6,14},{7,15},{8,0},{9,1},... | collective-permute-start | bytes 350216 | tf_op jit(solution)/shard_map/ppermute | solution.py:693
  9.4 3.6 ready.1
  19.4 3.5 collective-permute-done.3
  26.1 9.7 %arrange.1.xw_ref.refs_0_ = bf16[2,1280,768]{2,1,0:T(8,128)(2,1)S(1)} custom-call(s32[2,1280,1]{2,1,0:T(8,128)S(1)} %get-tuple-element.122.idx_ref, bf16[2,640,768]{2,1,0:T(8,128)(2,1)S(1)} %bitcast.167, bf16[2,640,768]{2,1,0:T(8,128)(2,1)} %collective-permute-done.7.other_ref), custom_call_target="tpu_custom_call" | custom-call | flops 5033164800 | bytes 7864320 | tf_op jit(solution)/shard_map/arrange/pallas_call | solution.py:148
  35.8 1.9 copy-done
  37.9 3.3 collective-permute-start.4
  43.1 3.3 collective-permute-start.6
  47.6 2.1 copy-done.1
  51.0 5.3 %project.3.qkv_ref = bf16[3,1280,384]{2,1,0:T(8,128)(2,1)S(1)} custom-call(s32[1]{0:T(128)} %bitcast.part_ref, bf16[2,1280,768]{2,1,0:T(8,128)(2,1)S(1)} %copy-done.1, bf16[384,2432]{1,0:T(8,128)(2,1)S(1)} %bitcast.161, bf16[384,2432]{1,0:T(8,128)(2,1)} %collective-permute-done.11.away_ref.waway_ref, f32[1,1152]{1,0:T(1,128)S(1)} %pad_maximum_fusion.15.bias_ref, ...), custom_call_target="tpu_custom_call" | custom-call | flops 2264924160 | bytes 6684672 | tf_op jit(solution)/shard_map/project/pallas_call | solution.py:210
  57.9 5.3 %project.2.qkv_ref = bf16[3,1280,384]{2,1,0:T(8,128)(2,1)S(1)} custom-call(s32[1]{0:T(128)} %bitcast.part_ref, bf16[2,1280,768]{2,1,0:T(8,128)(2,1)S(1)} %copy-done.1, bf16[384,2432]{1,0:T(8,128)(2,1)S(1)} %bitcast.162, bf16[384,2432]{1,0:T(8,128)(2,1)} %collective-permute-done.11.away_ref.waway_ref, f32[1,1152]{1,0:T(1,128)S(1)} %pad_maximum_fusion.15.bias_ref, ...), custom_call_target="tpu_custom_call" | custom-call | flops 2264924160 | bytes 6684672 | tf_op jit(solution)/shard_map/project/pallas_call | solution.py:210
  69.1 26.0 %attend.2 = (bf16[640,384]{1,0:T(8,128)(2,1)}, bf16[640,384]{1,0:T(8,128)(2,1)}, bf16[384,1280]{1,0:T(8,128)(2,1)}, f32[3,8,1280]{2,1,0:T(8,128)}) custom-call(s32[2,1280,1]{2,1,0:T(8,128)} %copy-done.8, bf16[3,1280,384]{2,1,0:T(8,128)(2,1)} %copy-done.6, s32[2,1280,1]{2,1,0:T(8,128)} %copy-done.9, s32[2,1,1280]{2,1,0:T(1,128)} %copy-done.12), custom_call_target="tpu_custom_call" | custom-call | flops 7549747200 | bytes 5898240 | tf_op jit(solution)/shard_map/attend/pallas_call | solution.py:285
  100.6 26.0 %attend.3 = (bf16[640,384]{1,0:T(8,128)(2,1)}, bf16[640,384]{1,0:T(8,128)(2,1)}, bf16[384,1280]{1,0:T(8,128)(2,1)}, f32[3,8,1280]{2,1,0:T(8,128)}) custom-call(s32[2,1280,1]{2,1,0:T(8,128)} %copy-done.8, bf16[3,1280,384]{2,1,0:T(8,128)(2,1)} %copy-done.5, s32[2,1280,1]{2,1,0:T(8,128)} %copy-done.9, s32[2,1,1280]{2,1,0:T(1,128)} %copy-done.12), custom_call_target="tpu_custom_call" | custom-call | flops 7549747200 | bytes 5898240 | tf_op jit(solution)/shard_map/attend/pallas_call | solution.py:285
  126.6 2.6 collective-permute-done.16.ay_ref
  129.2 4.8 %assemble.3 = (bf16[16,24,3840]{2,1,0:T(8,128)(2,1)}, bf16[16,96,768]{2,1,0:T(8,128)(2,1)}) custom-call(s32[1]{0:T(128)} %bitcast.15.place_ref, bf16[4,24,6912]{2,1,0:T(8,128)(2,1)} %pad_maximum_fusion.2.ax_ref, bf16[4,24,6912]{2,1,0:T(8,128)(2,1)} %collective-permute-done.16.ay_ref, bf16[4,24,6912]{2,1,0:T(8,128)(2,1)} %collective-permute-done.17.bx_ref, ...), custom_call_target="tpu_custom_call" | custom-call | bytes 10616832 | tf_op jit(solution)/shard_map/assemble/pallas_call | solution.py:723
  136.9 2.2 pad_maximum_fusion.4.near_ref
  139.1 4.5 %collective-permute-done.14 = bf16[640,384]{1,0:T(8,128)(2,1)S(1)} collective-permute-done((bf16[640,384]{1,0:T(8,128)(2,1)}, bf16[640,384]{1,0:T(8,128)(2,1)S(1)}, u32[]{:S(2)}, u32[]{:S(2)}) %collective-permute-start.14) | collective-permute-done | bytes 491552 | tf_op jit(solution)/shard_map/ppermute | solution.py:677
  145.5 72.1 %feed.1 = (bf16[1280,768]{1,0:T(8,128)(2,1)}, f32[1280,768]{1,0:T(8,128)}, bf16[1280,384]{1,0:T(8,128)(2,1)}, bf16[1280,384]{1,0:T(8,128)(2,1)}, f32[8,768]{1,0:...) custom-call(s32[1]{0:T(128)} %bitcast.part_ref, ...), custom_call_target="tpu_custom_call" | custom-call | flops 40768634880 | bytes 37355520 | tf_op jit(solution)/shard_map/feed/pallas_call | solution.py:650
  220.9 3.7 collective-permute-done.20.gaway_ref
  225.6 28.6 %attend_back.2.g_ref.refs_1_ = bf16[3,1280,384]{2,1,0:T(8,128)(2,1)} custom-call(s32[2,1280,1]{2,1,0:T(8,128)} %copy-done.8, bf16[3,1280,384]{2,1,0:T(8,128)(2,1)} %copy-done.6, s32[2,1280,1]{2,1,0:T(8,128)} %copy-done.9, s32[2,1,1280]{2,1,0:T(1,128)} %copy-done.12, f32[3,8,1280]{2,1,0:T(8,128)} %get-tuple-element.158.lse_ref, ...), custom_call_target="tpu_custom_call" | custom-call | flops 17616076800 | bytes 8847360 | tf_op jit(solution)/shard_map/attend_back/pallas_call | solution.py:399
  254.2 3.4 add_convert_fusion
  260.3 2.3 add_convert_fusion.1
  269.9 28.6 %attend_back.3.refs_2_.g_ref = bf16[3,1280,384]{2,1,0:T(8,128)(2,1)} custom-call(s32[2,1280,1]{2,1,0:T(8,128)} %copy-done.8, bf16[3,1280,384]{2,1,0:T(8,128)(2,1)} %copy-done.5, s32[2,1280,1]{2,1,0:T(8,128)} %copy-done.9, s32[2,1,1280]{2,1,0:T(1,128)} %copy-done.12, f32[3,8,1280]{2,1,0:T(8,128)} %get-tuple-element.162.lse_ref, ...), custom_call_target="tpu_custom_call" | custom-call | flops 17616076800 | bytes 8847360 | tf_op jit(solution)/shard_map/attend_back/pallas_call | solution.py:399
  298.5 2.2 fusion.34
  314.4 10.4 %weight_back.1 = (bf16[768,1152]{1,0:T(8,128)(2,1)}, f32[8,1152]{1,0:T(8,128)}) custom-call(bf16[2,1280,768]{2,1,0:T(8,128)(2,1)} %copy-done, bf16[3,1280,384]{2,1,0:T(8,128)(2,1)} %attend_back.2.g_ref.refs_1_, bf16[3,1280,384]{2,1,0:T(8,128)(2,1)} %attend_back.3.refs_2_.g_ref), custom_call_target="tpu_custom_call" | custom-call | flops 4529848320 | bytes 11599872 | tf_op jit(solution)/shard_map/weight_back/pallas_call | solution.py:491
  332.6 8.7 %project_back.2 = (bf16[640,768]{1,0:T(8,128)(2,1)S(1)}, bf16[640,768]{1,0:T(8,128)(2,1)S(1)}) custom-call(s32[1]{0:T(128)} %bitcast.part_ref, bf16[3,1280,384]{2,1,0:T(8,128)(2,1)S(1)} %copy-done.11, s32[2,1,1280]{2,1,0:T(1,128)S(1)} %get-tuple-element.183.row_ref, bf16[384,2432]{1,0:T(8,128)(2,1)S(1)} %bitcast.163, ...), custom_call_target="tpu_custom_call" | custom-call | flops 4781506560 | bytes 6684672 | tf_op jit(solution)/shard_map/project_back/pallas_call | solution.py:457
  348.8 8.0 %collective-permute-start.38 = (bf16[2,24,6912]{2,1,0:T(8,128)(2,1)S(1)}, bf16[2,24,6912]{2,1,0:T(8,128)(2,1)S(1)}, u32[]{:S(2)}, u32[]{:S(2)}) collective-permute-start(bf16[2,24,6912]{2,1,0:T(8,128)(2,1)S(1)} %fusion.2), channel_id=1, source_target_pairs={{0,4},{1,5},{2,6},{3,7},{4,0},{5,1},{6,2},{7,3},{8,12},{9,13},{10,... | collective-permute-start | bytes 1990664 | tf_op jit(solution)/shard_map/ppermute | solution.py:689
  356.8 8.6 %project_back.3 = (bf16[640,768]{1,0:T(8,128)(2,1)S(1)}, bf16[640,768]{1,0:T(8,128)(2,1)S(1)}) custom-call(s32[1]{0:T(128)} %bitcast.part_ref, bf16[3,1280,384]{2,1,0:T(8,128)(2,1)S(1)} %copy-done.10, s32[2,1,1280]{2,1,0:T(1,128)S(1)} %get-tuple-element.183.row_ref, bf16[384,2432]{1,0:T(8,128)(2,1)S(1)} %bitcast.164, ...), custom_call_target="tpu_custom_call" | custom-call | flops 4781506560 | bytes 6684672 | tf_op jit(solution)/shard_map/project_back/pallas_call | solution.py:457
  367.8 3.5 collective-permute-done.38
  373.9 2.0 collective-permute-start.39
  376.4 3.4 collective-permute-start.41
  380.1 5.9 %collective-permute-start.40 = (bf16[24,2432]{1,0:T(8,128)(2,1)S(1)}, bf16[24,2432]{1,0:T(8,128)(2,1)S(1)}, u32[]{:S(2)}, u32[]{:S(2)}) collective-permute-start(bf16[24,2432]{1,0:T(8,128)(2,1)S(1)} %fusion.18), channel_id=1, source_target_pairs={{0,8},{1,9},{2,10},{3,11},{4,12},{5,13},{6,14},{7,15},{8,0},{9,1},... | collective-permute-start | bytes 350216 | tf_op jit(solution)/shard_map/ppermute | solution.py:689
  388.2 9.3 %collective-permute-done.41 = bf16[24,6912]{1,0:T(8,128)(2,1)S(1)} collective-permute-done((bf16[24,6912]{1,0:T(8,128)(2,1)S(1)}, bf16[24,6912]{1,0:T(8,128)(2,1)S(1)}, u32[]{:S(2)}, u32[]{:S(2)}) %collective-permute-start.41) | collective-permute-done | bytes 331808 | tf_op jit(solution)/shard_map/ppermute | solution.py:689
  (251 shorter events, 91.8 us)
Async XLA Ops:
  2.6 11.6 %collective-permute-start.1 = (bf16[24,2432]{1,0:T(8,128)(2,1)}, bf16[24,2432]{1,0:T(8,128)(2,1)S(1)}, u32[]{:S(2)}, u32[]{:S(2)}) collective-permute-start(bf16[24,2432]{1,0:T(8,128)(2,1)} %get-tuple-element.120), channel_id=1, source_target_pairs={{0,8},{1,9},{2,10},{3,11},{4,12},{5,13},{6,14},{7,15},{8,0},{9,1},... | collective-permute-start | bytes 350216 | tf_op jit(solution)/shard_map/ppermute | solution.py:693
  8.7 17.4 %collective-permute-start.7 = (bf16[2,640,768]{2,1,0:T(8,128)(2,1)}, bf16[2,640,768]{2,1,0:T(8,128)(2,1)}, u32[]{:S(2)}, u32[]{:S(2)}) collective-permute-start(bf16[2,640,768]{2,1,0:T(8,128)(2,1)} %bitcast.165), channel_id=1, source_target_pairs={{0,16},{16,0},{1,17},{17,1},{2,18},{18,2},{3,19},{19,3},{4,20},{20... | collective-permute-start | bytes 5898248 | tf_op jit(solution)/shard_map/ppermute | solution.py:677
  22.9 14.8 %collective-permute-start.8 = (bf16[4,24,2432]{2,1,0:T(8,128)(2,1)S(1)}, bf16[4,24,2432]{2,1,0:T(8,128)(2,1)S(1)}, u32[]{:S(2)}, u32[]{:S(2)}) collective-permute-start(bf16[4,24,2432]{2,1,0:T(8,128)(2,1)S(1)} %constant_dynamic-update-slice_fusion.ax_ref), channel_id=1, source_target_pairs={{0,2},{1,3},{2,0},{3,1},{4,6},{5,7},{6,4},{7,5},{8,10},{9,11},{10,... | collective-permute-start | bytes 1400840 | tf_op jit(solution)/shard_map/ppermute | solution.py:685
  24.5 13.2 %collective-permute-start.10 = (bf16[4,24,2432]{2,1,0:T(8,128)(2,1)S(1)}, bf16[4,24,2432]{2,1,0:T(8,128)(2,1)S(1)}, u32[]{:S(2)}, u32[]{:S(2)}) collective-permute-start(bf16[4,24,2432]{2,1,0:T(8,128)(2,1)S(1)} %constant_dynamic-update-slice_fusion.2.by_ref), channel_id=1, source_target_pairs={{0,1},{1,0},{2,3},{3,2},{4,5},{5,4},{6,7},{7,6},{8,9},{9,8},{10,11... | collective-permute-start | bytes 1400840 | tf_op jit(solution)/shard_map/ppermute | solution.py:681
  37.9 26.9 %collective-permute-start.4 = (bf16[24,6912]{1,0:T(8,128)(2,1)}, bf16[24,6912]{1,0:T(8,128)(2,1)}, u32[]{:S(2)}, u32[]{:S(2)}) collective-permute-start(bf16[24,6912]{1,0:T(8,128)(2,1)} %get-tuple-element.125), channel_id=1, source_target_pairs={{0,4},{1,5},{2,6},{3,7},{4,8},{5,9},{6,10},{7,11},{8,12},{9,13},{1... | collective-permute-start | bytes 995336 | tf_op jit(solution)/shard_map/ppermute | solution.py:693
  41.2 23.6 %collective-permute-start.5 = (bf16[24,6912]{1,0:T(8,128)(2,1)}, bf16[24,6912]{1,0:T(8,128)(2,1)}, u32[]{:S(2)}, u32[]{:S(2)}) collective-permute-start(bf16[24,6912]{1,0:T(8,128)(2,1)} %get-tuple-element.125), channel_id=1, source_target_pairs={{0,8},{1,9},{2,10},{3,11},{4,12},{5,13},{6,14},{7,15},{8,0},{9,1},... | collective-permute-start | bytes 995336 | tf_op jit(solution)/shard_map/ppermute | solution.py:693
  43.1 21.7 %collective-permute-start.6 = (bf16[24,6912]{1,0:T(8,128)(2,1)}, bf16[24,6912]{1,0:T(8,128)(2,1)}, u32[]{:S(2)}, u32[]{:S(2)}) collective-permute-start(bf16[24,6912]{1,0:T(8,128)(2,1)} %get-tuple-element.125), channel_id=1, source_target_pairs={{0,12},{1,13},{2,14},{3,15},{4,0},{5,1},{6,2},{7,3},{8,4},{9,5},{1... | collective-permute-start | bytes 995336 | tf_op jit(solution)/shard_map/ppermute | solution.py:693
  67.1 28.0 %collective-permute-start.12 = (bf16[2,24,6912]{2,1,0:T(8,128)(2,1)S(1)}, bf16[2,24,6912]{2,1,0:T(8,128)(2,1)S(1)}, u32[]{:S(2)}, u32[]{:S(2)}) collective-permute-start(bf16[2,24,6912]{2,1,0:T(8,128)(2,1)S(1)} %pad_maximum_fusion.8), channel_id=1, source_target_pairs={{0,1},{1,0},{2,3},{3,2},{4,5},{5,4},{6,7},{7,6},{8,9},{9,8},{10,11... | collective-permute-start | bytes 1990664 | tf_op jit(solution)/shard_map/ppermute | solution.py:681
  67.7 27.4 %collective-permute-start.13 = (bf16[2,24,6912]{2,1,0:T(8,128)(2,1)S(1)}, bf16[2,24,6912]{2,1,0:T(8,128)(2,1)}, u32[]{:S(2)}, u32[]{:S(2)}) collective-permute-start(bf16[2,24,6912]{2,1,0:T(8,128)(2,1)S(1)} %pad_maximum_fusion.9), channel_id=1, source_target_pairs={{0,2},{1,3},{2,0},{3,1},{4,6},{5,7},{6,4},{7,5},{8,10},{9,11},{10,... | collective-permute-start | bytes 1990664 | tf_op jit(solution)/shard_map/ppermute | solution.py:685
  98.4 30.8 %collective-permute-start.16 = (bf16[4,24,6912]{2,1,0:T(8,128)(2,1)}, bf16[4,24,6912]{2,1,0:T(8,128)(2,1)}, u32[]{:S(2)}, u32[]{:S(2)}) collective-permute-start(bf16[4,24,6912]{2,1,0:T(8,128)(2,1)} %pad_maximum_fusion.2.ax_ref), channel_id=1, source_target_pairs={{0,2},{1,3},{2,0},{3,1},{4,6},{5,7},{6,4},{7,5},{8,10},{9,11},{10,... | collective-permute-start | bytes 3981320 | tf_op jit(solution)/shard_map/ppermute | solution.py:685
  99.1 30.1 %collective-permute-start.17 = (bf16[4,24,6912]{2,1,0:T(8,128)(2,1)S(1)}, bf16[4,24,6912]{2,1,0:T(8,128)(2,1)}, u32[]{:S(2)}, u32[]{:S(2)}) collective-permute-start(bf16[4,24,6912]{2,1,0:T(8,128)(2,1)S(1)} %pad_maximum_fusion.3.by_ref), channel_id=1, source_target_pairs={{0,1},{1,0},{2,3},{3,2},{4,5},{5,4},{6,7},{7,6},{8,9},{9,8},{10,11... | collective-permute-start | bytes 3981320 | tf_op jit(solution)/shard_map/ppermute | solution.py:681
  134.0 11.5 %collective-permute-start.18 = (bf16[384,3840]{1,0:T(8,128)(2,1)}, bf16[384,3840]{1,0:T(8,128)(2,1)}, u32[]{:S(2)}, u32[]{:S(2)}) collective-permute-start(bf16[384,3840]{1,0:T(8,128)(2,1)} %bitcast.24.unear_ref), channel_id=1, source_target_pairs={{0,16},{16,0},{1,17},{17,1},{2,18},{18,2},{3,19},{19,3},{4,20},{20... | collective-permute-start | bytes 8847368 | tf_op jit(solution)/shard_map/ppermute | solution.py:677
  134.0 11.5 %collective-permute-start.19 = (bf16[1536,768]{1,0:T(8,128)(2,1)}, bf16[1536,768]{1,0:T(8,128)(2,1)}, u32[]{:S(2)}, u32[]{:S(2)}) collective-permute-start(bf16[1536,768]{1,0:T(8,128)(2,1)} %bitcast.25.dnear_ref), channel_id=1, source_target_pairs={{0,16},{16,0},{1,17},{17,1},{2,18},{18,2},{3,19},{19,3},{4,20},{20... | collective-permute-start | bytes 7077896 | tf_op jit(solution)/shard_map/ppermute | solution.py:677
  134.5 9.9 %collective-permute-start.15 = (bf16[640,384]{1,0:T(8,128)(2,1)}, bf16[640,384]{1,0:T(8,128)(2,1)S(1)}, u32[]{:S(2)}, u32[]{:S(2)}) collective-permute-start(bf16[640,384]{1,0:T(8,128)(2,1)} %get-tuple-element.149), channel_id=1, source_target_pairs={{0,16},{16,0},{1,17},{17,1},{2,18},{18,2},{3,19},{19,3},{4,20},{20... | collective-permute-start | bytes 1474568 | tf_op jit(solution)/shard_map/ppermute | solution.py:677
  217.6 36.6 %collective-permute-start.22 = (bf16[384,3840]{1,0:T(8,128)(2,1)}, bf16[384,3840]{1,0:T(8,128)(2,1)}, u32[]{:S(2)}, u32[]{:S(2)}) collective-permute-start(bf16[384,3840]{1,0:T(8,128)(2,1)} %get-tuple-element.166), channel_id=1, source_target_pairs={{0,16},{16,0},{1,17},{17,1},{2,18},{18,2},{3,19},{19,3},{4,20},{20... | collective-permute-start | bytes 8847368 | tf_op jit(solution)/shard_map/ppermute | solution.py:677
  218.1 36.0 %collective-permute-start.21 = (bf16[1536,768]{1,0:T(8,128)(2,1)}, bf16[1536,768]{1,0:T(8,128)(2,1)}, u32[]{:S(2)}, u32[]{:S(2)}) collective-permute-start(bf16[1536,768]{1,0:T(8,128)(2,1)} %get-tuple-element.165), channel_id=1, source_target_pairs={{0,16},{16,0},{1,17},{17,1},{2,18},{18,2},{3,19},{19,3},{4,20},{20... | collective-permute-start | bytes 7077896 | tf_op jit(solution)/shard_map/ppermute | solution.py:677
  265.9 39.4 %collective-permute-start.25 = (bf16[2,2,24,3840]{3,2,0,1:T(8,128)(2,1)S(1)}, bf16[2,2,24,3840]{3,2,0,1:T(8,128)(2,1)S(1)}, u32[]{:S(2)}, u32[]{:S(2)}) collective-permute-start(bf16[2,2,24,3840]{3,2,0,1:T(8,128)(2,1)S(1)} %copy_bitcast_fusion.3), channel_id=1, source_target_pairs={{0,2},{1,3},{2,0},{3,1},{4,6},{5,7},{6,4},{7,5},{8,10},{9,11},{10,... | collective-permute-start | bytes 2211848 | tf_op jit(solution)/shard_map/ppermute | solution.py:685
  267.4 37.9 %collective-permute-start.26 = (bf16[2,2,24,3840]{3,2,0,1:T(8,128)(2,1)S(1)}, bf16[2,2,24,3840]{3,2,0,1:T(8,128)(2,1)}, u32[]{:S(2)}, u32[]{:S(2)}) collective-permute-start(bf16[2,2,24,3840]{3,2,0,1:T(8,128)(2,1)S(1)} %copy_bitcast_fusion.2), channel_id=1, source_target_pairs={{0,1},{1,0},{2,3},{3,2},{4,5},{5,4},{6,7},{7,6},{8,9},{9,8},{10,11... | collective-permute-start | bytes 2211848 | tf_op jit(solution)/shard_map/ppermute | solution.py:681
  267.8 33.4 %collective-permute-start.23 = (bf16[2,2,96,768]{3,2,0,1:T(8,128)(2,1)}, bf16[2,2,96,768]{3,2,0,1:T(8,128)(2,1)}, u32[]{:S(2)}, u32[]{:S(2)}) collective-permute-start(bf16[2,2,96,768]{3,2,0,1:T(8,128)(2,1)} %copy_bitcast_fusion.7), channel_id=1, source_target_pairs={{0,2},{1,3},{2,0},{3,1},{4,6},{5,7},{6,4},{7,5},{8,10},{9,11},{10,... | collective-permute-start | bytes 1769480 | tf_op jit(solution)/shard_map/ppermute | solution.py:685
  269.3 31.9 %collective-permute-start.24 = (bf16[2,2,96,768]{3,2,0,1:T(8,128)(2,1)}, bf16[2,2,96,768]{3,2,0,1:T(8,128)(2,1)}, u32[]{:S(2)}, u32[]{:S(2)}) collective-permute-start(bf16[2,2,96,768]{3,2,0,1:T(8,128)(2,1)} %copy_bitcast_fusion.6), channel_id=1, source_target_pairs={{0,1},{1,0},{2,3},{3,2},{4,5},{5,4},{6,7},{7,6},{8,9},{9,8},{10,11... | collective-permute-start | bytes 1769480 | tf_op jit(solution)/shard_map/ppermute | solution.py:681
  310.3 31.0 %collective-permute-start.31 = (bf16[2,96,768]{2,1,0:T(8,128)(2,1)}, bf16[2,96,768]{2,1,0:T(8,128)(2,1)}, u32[]{:S(2)}, u32[]{:S(2)}) collective-permute-start(bf16[2,96,768]{2,1,0:T(8,128)(2,1)} %fusion.6), channel_id=1, source_target_pairs={{0,1},{1,0},{2,3},{3,2},{4,5},{5,4},{6,7},{7,6},{8,9},{9,8},{10,11... | collective-permute-start | bytes 884744 | tf_op jit(solution)/shard_map/ppermute | solution.py:681
  311.8 29.6 %collective-permute-start.32 = (bf16[2,96,768]{2,1,0:T(8,128)(2,1)}, bf16[2,96,768]{2,1,0:T(8,128)(2,1)}, u32[]{:S(2)}, u32[]{:S(2)}) collective-permute-start(bf16[2,96,768]{2,1,0:T(8,128)(2,1)} %fusion.7), channel_id=1, source_target_pairs={{0,2},{1,3},{2,0},{3,1},{4,6},{5,7},{6,4},{7,5},{8,10},{9,11},{10,... | collective-permute-start | bytes 884744 | tf_op jit(solution)/shard_map/ppermute | solution.py:685
  312.3 31.3 %collective-permute-start.29 = (bf16[2,24,3840]{2,1,0:T(8,128)(2,1)}, bf16[2,24,3840]{2,1,0:T(8,128)(2,1)}, u32[]{:S(2)}, u32[]{:S(2)}) collective-permute-start(bf16[2,24,3840]{2,1,0:T(8,128)(2,1)} %fusion.3), channel_id=1, source_target_pairs={{0,1},{1,0},{2,3},{3,2},{4,5},{5,4},{6,7},{7,6},{8,9},{9,8},{10,11... | collective-permute-start | bytes 1105928 | tf_op jit(solution)/shard_map/ppermute | solution.py:681
  313.9 29.7 %collective-permute-start.30 = (bf16[2,24,3840]{2,1,0:T(8,128)(2,1)}, bf16[2,24,3840]{2,1,0:T(8,128)(2,1)}, u32[]{:S(2)}, u32[]{:S(2)}) collective-permute-start(bf16[2,24,3840]{2,1,0:T(8,128)(2,1)} %fusion.4), channel_id=1, source_target_pairs={{0,2},{1,3},{2,0},{3,1},{4,6},{5,7},{6,4},{7,5},{8,10},{9,11},{10,... | collective-permute-start | bytes 1105928 | tf_op jit(solution)/shard_map/ppermute | solution.py:685
  332.1 14.0 %collective-permute-start.28 = (bf16[384,1280]{1,0:T(8,128)(2,1)S(1)}, bf16[384,1280]{1,0:T(8,128)(2,1)S(1)}, u32[]{:S(2)}, u32[]{:S(2)}) collective-permute-start(bf16[384,1280]{1,0:T(8,128)(2,1)S(1)} %pad_maximum_fusion.6), channel_id=1, source_target_pairs={{0,16},{16,0},{1,17},{17,1},{2,18},{18,2},{3,19},{19,3},{4,20},{20... | collective-permute-start | bytes 2949128 | tf_op jit(solution)/shard_map/ppermute | solution.py:677
  346.6 18.8 %collective-permute-start.34 = (bf16[2,2,24,2432]{3,2,0,1:T(8,128)(2,1)S(1)}, bf16[2,2,24,2432]{3,2,0,1:T(8,128)(2,1)S(1)}, u32[]{:S(2)}, u32[]{:S(2)}) collective-permute-start(bf16[2,2,24,2432]{3,2,0,1:T(8,128)(2,1)S(1)} %copy_bitcast_fusion.11), channel_id=1, source_target_pairs={{0,2},{1,3},{2,0},{3,1},{4,6},{5,7},{6,4},{7,5},{8,10},{9,11},{10,... | collective-permute-start | bytes 1400840 | tf_op jit(solution)/shard_map/ppermute | solution.py:685
  348.2 17.2 %collective-permute-start.35 = (bf16[2,2,24,2432]{3,2,0,1:T(8,128)(2,1)S(1)}, bf16[2,2,24,2432]{3,2,0,1:T(8,128)(2,1)S(1)}, u32[]{:S(2)}, u32[]{:S(2)}) collective-permute-start(bf16[2,2,24,2432]{3,2,0,1:T(8,128)(2,1)S(1)} %copy_bitcast_fusion.10), channel_id=1, source_target_pairs={{0,1},{1,0},{2,3},{3,2},{4,5},{5,4},{6,7},{7,6},{8,9},{9,8},{10,11... | collective-permute-start | bytes 1400840 | tf_op jit(solution)/shard_map/ppermute | solution.py:681
  348.8 22.6 %collective-permute-start.38 = (bf16[2,24,6912]{2,1,0:T(8,128)(2,1)S(1)}, bf16[2,24,6912]{2,1,0:T(8,128)(2,1)S(1)}, u32[]{:S(2)}, u32[]{:S(2)}) collective-permute-start(bf16[2,24,6912]{2,1,0:T(8,128)(2,1)S(1)} %fusion.2), channel_id=1, source_target_pairs={{0,4},{1,5},{2,6},{3,7},{4,0},{5,1},{6,2},{7,3},{8,12},{9,13},{10,... | collective-permute-start | bytes 1990664 | tf_op jit(solution)/shard_map/ppermute | solution.py:689
  375.9 10.1 %collective-permute-start.27 = (bf16[640,768]{1,0:T(8,128)(2,1)S(1)}, bf16[640,768]{1,0:T(8,128)(2,1)S(1)}, u32[]{:S(2)}, u32[]{:S(2)}) collective-permute-start(bf16[640,768]{1,0:T(8,128)(2,1)S(1)} %get-tuple-element.185), channel_id=1, source_target_pairs={{0,16},{16,0},{1,17},{17,1},{2,18},{18,2},{3,19},{19,3},{4,20},{20... | collective-permute-start | bytes 2949128 | tf_op jit(solution)/shard_map/ppermute | solution.py:677
  375.9 10.1 %collective-permute-start.33 = (bf16[640,768]{1,0:T(8,128)(2,1)S(1)}, bf16[640,768]{1,0:T(8,128)(2,1)S(1)}, u32[]{:S(2)}, u32[]{:S(2)}) collective-permute-start(bf16[640,768]{1,0:T(8,128)(2,1)S(1)} %get-tuple-element.205), channel_id=1, source_target_pairs={{0,16},{16,0},{1,17},{17,1},{2,18},{18,2},{3,19},{19,3},{4,20},{20... | collective-permute-start | bytes 2949128 | tf_op jit(solution)/shard_map/ppermute | solution.py:677
  376.4 21.1 %collective-permute-start.41 = (bf16[24,6912]{1,0:T(8,128)(2,1)S(1)}, bf16[24,6912]{1,0:T(8,128)(2,1)S(1)}, u32[]{:S(2)}, u32[]{:S(2)}) collective-permute-start(bf16[24,6912]{1,0:T(8,128)(2,1)S(1)} %fusion.5), channel_id=1, source_target_pairs={{0,8},{1,9},{2,10},{3,11},{4,12},{5,13},{6,14},{7,15},{8,0},{9,1},... | collective-permute-start | bytes 995336 | tf_op jit(solution)/shard_map/ppermute | solution.py:689
  380.1 19.6 %collective-permute-start.40 = (bf16[24,2432]{1,0:T(8,128)(2,1)S(1)}, bf16[24,2432]{1,0:T(8,128)(2,1)S(1)}, u32[]{:S(2)}, u32[]{:S(2)}) collective-permute-start(bf16[24,2432]{1,0:T(8,128)(2,1)S(1)} %fusion.18), channel_id=1, source_target_pairs={{0,8},{1,9},{2,10},{3,11},{4,12},{5,13},{6,14},{7,15},{8,0},{9,1},... | collective-permute-start | bytes 350216 | tf_op jit(solution)/shard_map/ppermute | solution.py:689
  (43 other events, 321.9 us)

commit v6 on v5

--- a/solution.py
+++ b/solution.py
@@ -762,6 +762,92 @@
     return place // 4, (place // 2) % 2, place % 2
 
 
+def fold_call(body, name, grid, place, operands, in_specs, out_specs, out_shape):
+    size = sum(math.prod(item.shape) for item in out_shape)
+    return pl.pallas_call(
+        body,
+        grid_spec=pltpu.PrefetchScalarGridSpec(
+            num_scalar_prefetch=1, grid=grid, in_specs=in_specs, out_specs=out_specs),
+        out_shape=out_shape,
+        compiler_params=pltpu.CompilerParams(vmem_limit_bytes=40 << 20),
+        cost_estimate=pl.CostEstimate(flops=0, bytes_accessed=8 * size, transcendentals=0),
+        name=name,
+    )(place, *operands)
+
+
+def merge_one_body(place_ref, *refs):
+    count = len(refs) // 3
+    for mine, theirs, out in zip(refs[:count], refs[count:2 * count], refs[2 * count:]):
+        out[0, 0] = (mine[0, 0, 0, 0].astype(F32) + theirs[0, 0, 0, 0].astype(F32)).astype(BF)
+
+
+def merge_one(place, mines, theirs):
+    cubes = lambda values: [v.reshape(2, 2, 2, 2, v.shape[0] // 16, v.shape[1]) for v in values for _ in range(2)]
+    specs, outs, shapes = [], [], []
+    for value in mines:
+        n, width = value.shape[0] // 16, value.shape[1]
+        specs += [pl.BlockSpec((1, 1, 1, 1, n, width), lambda k, j, p: (0, k, 1 - p[1], j, 0, 0)),
+                  pl.BlockSpec((1, 1, 1, 1, n, width), lambda k, j, p: (1, k, j, 1 - p[2], 0, 0))]
+        outs += [pl.BlockSpec((1, 1, n, width), lambda k, j, p: (k, j, 0, 0))] * 2
+        shapes += [jax.ShapeDtypeStruct((2, 2, n, width), BF)] * 2
+    return fold_call(merge_one_body, "merge_one", (2, 2), place, cubes(mines) + cubes(theirs), specs * 2, outs, shapes)
+
+
+def merge_two_body(place_ref, *refs):
+    count = len(refs) // 5
+    y, x = place_ref[1], place_ref[2]
+    groups = [refs[i * count:(i + 1) * count] for i in range(5)]
+    for i, (mine, theirs, came, stay, send) in enumerate(zip(*groups)):
+        if i % 2 == 0:
+            part = lambda at: mine[0, 0, 0, at].astype(F32) + theirs[0, 0, 0, at].astype(F32) + came[0, at].astype(F32)
+            own = x
+        else:
+            part = lambda at: mine[0, 0, at, 0].astype(F32) + theirs[0, 0, at, 0].astype(F32) + came[0, at].astype(F32)
+            own = y
+        stay[0] = part(own)
+        send[0] = part(1 - own).astype(BF)
+
+
+def merge_two(place, mines, theirs, came):
+    cubes = lambda values: [v.reshape(2, 2, 2, 2, v.shape[0] // 16, v.shape[1]) for v in values for _ in range(2)]
+    specs, came_specs, outs, stays, sends = [], [], [], [], []
+    for value in mines:
+        n, width = value.shape[0] // 16, value.shape[1]
+        specs += [pl.BlockSpec((1, 1, 1, 2, n, width), lambda k, p: (0, k, p[1], 0, 0, 0)),
+                  pl.BlockSpec((1, 1, 2, 1, n, width), lambda k, p: (1, k, 0, p[2], 0, 0))]
+        came_specs += [pl.BlockSpec((1, 2, n, width), lambda k, p: (k, 0, 0, 0))] * 2
+        outs += [pl.BlockSpec((1, n, width), lambda k, p: (k, 0, 0))] * 2
+        stays += [jax.ShapeDtypeStruct((2, n, width), F32)] * 2
+        sends += [jax.ShapeDtypeStruct((2, n, width), BF)] * 2
+    both = fold_call(merge_two_body, "merge_two", (2,), place, cubes(mines) + cubes(theirs) + list(came),
+                     specs * 2 + came_specs, outs * 2, stays + sends)
+    return both[:len(stays)], both[len(stays):]
+
+
+def merge_three_body(place_ref, *refs):
+    stays, came, (stay_ref, send_ref) = refs[:4], refs[4:8], refs[8:]
+    near = lax.rem(place_ref[0], 2)
+    n = stay_ref.shape[1]
+    for half in range(2):
+        for at, out in ((near, stay_ref), (1 - near, send_ref)):
+            lines = stays[half][at] + came[half][at].astype(F32)
+            wide = stays[2 + half][at] + came[2 + half][at].astype(F32)
+            out[half, :, :wide.shape[1]] = wide.astype(out.dtype)
+            for c in range(lines.shape[0] // n):
+                to = wide.shape[1] + c * lines.shape[1]
+                out[half, :, to:to + lines.shape[1]] = lines[c * n:(c + 1) * n].astype(out.dtype)
+
+
+def merge_three(place, stays, came):
+    rows, line = stays[0].shape[1:]
+    n, wide = stays[2].shape[1:]
+    total = wide + rows // n * line
+    whole = lambda shape: pl.BlockSpec(shape, lambda p: (0,) * len(shape))
+    shapes = [jax.ShapeDtypeStruct((2, n, total), F32), jax.ShapeDtypeStruct((2, n, total), BF)]
+    return fold_call(merge_three_body, "merge_three", (), place, list(stays) + list(came),
+                     [whole(v.shape) for v in list(stays) + list(came)], [whole(v.shape) for v in shapes], shapes)
+
+
 def fold_one(value):
     z, y, x = corner()
     rows, width = value.shape
@@ -790,14 +876,14 @@
 def fold_three(stack):
     near = corner()[0] % 2
     cube = stack.reshape((2, 2) + stack.shape[1:])
-    return (cube,), (pick(cube, 1 - near, 1).astype(BF),)
+    return (pick(cube, near, 1),), (pick(cube, 1 - near, 1).astype(BF),)
 
 
 def fold_four(stay, sends, after=()):
     z = corner()[0]
-    near, far = z % 2, z // 2
+    far = z // 2
     came = tie(flip_z(sends[0], 1), after)
-    total = pick(stay[0], near, 1) + came.astype(F32)
+    total = stay[0] + came.astype(F32)
     return (pick(total, far, 0),), (pick(total, 1 - far, 0).astype(BF),)
 
 
@@ -898,16 +984,24 @@
     givens = [(cnear, caway)] * batches
     if staged:
         first_back = back(0, givens[0])
-        d_theirs, uo_theirs = tie((d_theirs, uo_theirs), first_back)
-        d_step, uo_step = fold_one(plus(d_mine, d_theirs)), fold_one(plus(uo_mine, uo_theirs))
-        given, d_step, uo_step = tie((givens[1], d_step, uo_step))
+        place = jnp.stack(corner()).astype(jnp.int32)
+        mines, theirs = (d_mine, uo_mine), tie((d_theirs, uo_theirs), first_back)
+        sends = merge_one(place, mines, theirs)
+        given, sends = tie((givens[1], sends))
         grads = [first_back, back(1, given)]
-        d_step, uo_step = fold_two(*d_step, grads[1]), fold_two(*uo_step, grads[1])
-        grads, d_step, uo_step = tie((grads, d_step, uo_step))
+        swaps = (swap_y, swap_x)
+        came = tie([swaps[i % 2](send) for i, send in enumerate(sends)], grads[1])
+        stays, sends = merge_two(place, mines, theirs, came)
+        grads, sends = tie((grads, sends))
     else:
         grads = [back(b, givens[b]) for b in range(batches)]
         d_sum, uo_sum = plus(d_mine, d_theirs), plus(uo_mine, uo_theirs)
     gw_own, gb_own = weight_back(xws, grads)
+    if staged:
+        came = tie([swaps[1 - i % 2](send) for i, send in enumerate(sends)], gw_own)
+        stay, send = merge_three(place, stays, came)
+        grads, gw_own, gb_own, send = tie((grads, gw_own, gb_own, send))
+        du_step = ((stay,), (send,))
 
     def halves(value):
         size = value.shape[0] // 2
@@ -933,16 +1027,13 @@
     ], axis=1)
     backs = [project_back(0, part, grads[0], idx_row, q_near, q_away)]
     if staged:
-        wide, lines = fold_cross(*uo_step, backs[0]), fold_cross(*d_step, backs[0])
-        lines = [lines[:, i * n_qkv:(i + 1) * n_qkv] for i in range(4)]
-        du_step = fold_three(jnp.concatenate([wide] + lines, axis=2))
+        du_step = fold_four(*du_step, backs[0])
         last, q_step, du_step = tie((grads[1], fold_one(q_sum), du_step), backs)
         backs.append(project_back(1, part, last, idx_row, q_near, q_away))
         q_step = tie(fold_two(*q_step, backs[1]))
-        du_step = tie(fold_four(*du_step, q_step))
-        q_step = tie(fold_three(fold_cross(*q_step, du_step)))
+        g_uo = fold_end(*du_step, q_step)
+        q_step = tie(fold_three(fold_cross(*q_step, g_uo)))
         q_step = fold_four(*q_step)
-        g_uo = fold_end(*du_step, q_step)
         g_down = jnp.concatenate([g_uo[:, (5 + i) * width:(6 + i) * width] for i in range(4)], axis=0)
     else:
         backs.append(project_back(1, part, grads[1], idx_row, q_near, q_away))

time: 408 us -> 393 us (0.963)
  other arithmetic: 27.8 us -> 12.1 us
  Pallas kernels: 240 us -> 250 us
  starting transfers between devices: 58.9 us -> 52.5 us
    pallas_call x0 -> x3, Pallas kernels: none -> 10.4 us  [fold_call(): pl.pallas_call(body, grid_spec=pltpu.PrefetchScalarGridSpec(num_scalar_pr...]
    unnamed x74 -> x90, local copies, waits for them, and re-layouts: 19.5 us -> 26.7 us
    ppermute x4, starting transfers between devices: 19.3 us -> 13.2 us  [flip_z(): return lax.ppermute(value, 'fsdp', [(i, i ^ 4 * k) for i in range(16)])]
    convert_element_type x2 -> x0, other arithmetic: 5.69 us -> none  [on_device(): (mine.astype(F32) + theirs.astype(F32)).astype(BF)]
  transfers between devices with their start and end apart: 42 -> 42, of which waited for: 12 -> 17; matrix products, arithmetic and copies ran while one was open for 8% -> 5% of each run, Pallas kernels for 40% -> 42%
where the time goes in v6:
time: 393 us; the launch traced here: 387 us
  Pallas kernels  250 us (64%)
  starting transfers between devices  52.5 us (13%)
  local copies, waits for them, and re-layouts  37 us (9%)
  waiting for transfers between devices  34.1 us (9%)
  other arithmetic  12.1 us (3%)
    pallas_call x1, Pallas kernels, feed(): pl.pallas_call(functools.partial(feed_body, chunk), grid=(rows // block,)...  72.1 us
    pallas_call x2, Pallas kernels, attend_back(): pl.pallas_call(functools.partial(attend_back_body, block), grid=(pairs,),...  57.3 us
    pallas_call x2, Pallas kernels, attend(): pl.pallas_call(functools.partial(attend_body, block), grid=(pairs,), in_s...  52.1 us
    unnamed x90, local copies, waits for them, and re-layouts  26.7 us
    pallas_call x2, Pallas kernels, project_back(): pl.pallas_call(functools.partial(project_back_body, block), grid=(1,), in...  17.2 us
    ppermute x6, starting transfers between devices, shift_z(): lax.ppermute(value, 'fsdp', [(i, (i + 4 * k) % 16) for i in range(16)])  14.3 us
    ppermute x4, starting transfers between devices, flip_z(): return lax.ppermute(value, 'fsdp', [(i, i ^ 4 * k) for i in range(16)])  13.2 us
    ppermute x10, starting transfers between devices, swap_y(): return lax.ppermute(value, 'fsdp', [(i, i ^ 2) for i in range(16)])  11.7 us
  transfers between devices with their start and end apart: 42, of which 17 were waited for; matrix products, arithmetic and copies ran while one was open for 5% of the time, Pallas kernels for 42%

profile of v6, /device:TPU:0, one launch (start us, length us, event | category | flops | bytes accessed | tf_op | source)
XLA Modules:
  0.0 387.1 jit_solution(3466924775661537586)
XLA Ops:
  0.7 1.9 pack.1
  2.6 4.1 %collective-permute-start.1 = (bf16[24,2432]{1,0:T(8,128)(2,1)}, bf16[24,2432]{1,0:T(8,128)(2,1)S(1)}, u32[]{:S(2)}, u32[]{:S(2)}) collective-permute-start(bf16[24,2432]{1,0:T(8,128)(2,1)} %get-tuple-element.131), channel_id=1, source_target_pairs={{0,8},{1,9},{2,10},{3,11},{4,12},{5,13},{6,14},{7,15},{8,0},{9,1},... | collective-permute-start | bytes 350216 | tf_op jit(solution)/shard_map/ppermute | solution.py:693
  9.4 3.6 ready.1
  14.2 1.9 collective-permute-done
  19.4 3.5 collective-permute-done.3
  26.1 9.6 %arrange.1.xw_ref.refs_0_ = bf16[2,1280,768]{2,1,0:T(8,128)(2,1)S(1)} custom-call(s32[2,1280,1]{2,1,0:T(8,128)S(1)} %get-tuple-element.133.idx_ref, bf16[2,640,768]{2,1,0:T(8,128)(2,1)S(1)} %bitcast.123, bf16[2,640,768]{2,1,0:T(8,128)(2,1)} %collective-permute-done.7.other_ref), custom_call_target="tpu_custom_call" | custom-call | flops 5033164800 | bytes 7864320 | tf_op jit(solution)/shard_map/arrange/pallas_call | solution.py:148
  37.9 3.3 collective-permute-start.4
  43.1 3.0 collective-permute-start.6
  47.3 2.1 copy-done.6
  50.7 5.3 %project.3.qkv_ref = bf16[3,1280,384]{2,1,0:T(8,128)(2,1)S(1)} custom-call(s32[1]{0:T(128)} %bitcast.part_ref, bf16[2,1280,768]{2,1,0:T(8,128)(2,1)S(1)} %copy-done.6, bf16[384,2432]{1,0:T(8,128)(2,1)S(1)} %bitcast.117, bf16[384,2432]{1,0:T(8,128)(2,1)} %collective-permute-done.11.away_ref.waway_ref, f32[1,1152]{1,0:T(1,128)S(1)} %pad_maximum_fusion.14.bias_ref, ...), custom_call_target="tpu_custom_call" | custom-call | flops 2264924160 | bytes 6684672 | tf_op jit(solution)/shard_map/project/pallas_call | solution.py:210
  57.6 5.3 %project.2.qkv_ref = bf16[3,1280,384]{2,1,0:T(8,128)(2,1)S(1)} custom-call(s32[1]{0:T(128)} %bitcast.part_ref, bf16[2,1280,768]{2,1,0:T(8,128)(2,1)S(1)} %copy-done.6, bf16[384,2432]{1,0:T(8,128)(2,1)S(1)} %bitcast.118, bf16[384,2432]{1,0:T(8,128)(2,1)} %collective-permute-done.11.away_ref.waway_ref, f32[1,1152]{1,0:T(1,128)S(1)} %pad_maximum_fusion.14.bias_ref, ...), custom_call_target="tpu_custom_call" | custom-call | flops 2264924160 | bytes 6684672 | tf_op jit(solution)/shard_map/project/pallas_call | solution.py:210
  68.9 26.0 %attend.2 = (bf16[640,384]{1,0:T(8,128)(2,1)}, bf16[640,384]{1,0:T(8,128)(2,1)}, bf16[384,1280]{1,0:T(8,128)(2,1)}, f32[3,8,1280]{2,1,0:T(8,128)}) custom-call(s32[2,1280,1]{2,1,0:T(8,128)} %copy-done.27, bf16[3,1280,384]{2,1,0:T(8,128)(2,1)} %copy-done.11, s32[2,1280,1]{2,1,0:T(8,128)} %copy-done.28, s32[2,1,1280]{2,1,0:T(1,128)} %copy-done.31), custom_call_target="tpu_custom_call" | custom-call | flops 7549747200 | bytes 5898240 | tf_op jit(solution)/shard_map/attend/pallas_call | solution.py:285
  97.2 26.0 %attend.3 = (bf16[640,384]{1,0:T(8,128)(2,1)}, bf16[640,384]{1,0:T(8,128)(2,1)}, bf16[384,1280]{1,0:T(8,128)(2,1)}, f32[3,8,1280]{2,1,0:T(8,128)}) custom-call(s32[2,1280,1]{2,1,0:T(8,128)} %copy-done.27, bf16[3,1280,384]{2,1,0:T(8,128)(2,1)} %copy-done.10, s32[2,1280,1]{2,1,0:T(8,128)} %copy-done.28, s32[2,1,1280]{2,1,0:T(1,128)} %copy-done.31), custom_call_target="tpu_custom_call" | custom-call | flops 7549747200 | bytes 5898240 | tf_op jit(solution)/shard_map/attend/pallas_call | solution.py:285
  123.2 2.5 collective-permute-done.16.ay_ref
  126.0 4.2 %assemble.3 = (bf16[16,24,3840]{2,1,0:T(8,128)(2,1)}, bf16[16,96,768]{2,1,0:T(8,128)(2,1)}) custom-call(s32[1]{0:T(128)} %bitcast.15.place_ref, bf16[4,24,6912]{2,1,0:T(8,128)(2,1)S(1)} %pad_maximum_fusion.2.ax_ref, bf16[4,24,6912]{2,1,0:T(8,128)(2,1)S(1)} %collective-permute-done.16.ay_ref, bf16[4,24,6912]{2,1,0:T(8,128)(2,1)} %collective-permute-done.17.bx_ref, ...), custom_call_target="tpu_custom_call" | custom-call | bytes 10616832 | tf_op jit(solution)/shard_map/assemble/pallas_call | solution.py:723
  133.8 2.3 pad_maximum_fusion.4.near_ref
  136.1 3.7 collective-permute-done.14
  141.6 72.1 %feed.1 = (bf16[1280,768]{1,0:T(8,128)(2,1)}, f32[1280,768]{1,0:T(8,128)}, bf16[1280,384]{1,0:T(8,128)(2,1)}, bf16[1280,384]{1,0:T(8,128)(2,1)}, f32[8,768]{1,0:...) custom-call(s32[1]{0:T(128)} %bitcast.part_ref, ...), custom_call_target="tpu_custom_call" | custom-call | flops 40768634880 | bytes 37355520 | tf_op jit(solution)/shard_map/feed/pallas_call | solution.py:650
  216.6 4.2 %collective-permute-done.20.gaway_ref = bf16[1280,384]{1,0:T(8,128)(2,1)S(1)} collective-permute-done((bf16[1280,384]{1,0:T(8,128)(2,1)}, bf16[1280,384]{1,0:T(8,128)(2,1)S(1)}, u32[]{:S(2)}, u32[]{:S(2)}) %collective-permute-start.20) | collective-permute-done | bytes 983072 | tf_op jit(solution)/shard_map/ppermute | solution.py:677
  221.8 28.8 %attend_back.2.refs_1_.g_ref = bf16[3,1280,384]{2,1,0:T(8,128)(2,1)} custom-call(s32[2,1280,1]{2,1,0:T(8,128)} %copy-done.27, bf16[3,1280,384]{2,1,0:T(8,128)(2,1)} %copy-done.11, s32[2,1280,1]{2,1,0:T(8,128)} %copy-done.28, s32[2,1,1280]{2,1,0:T(1,128)} %copy-done.31, f32[3,8,1280]{2,1,0:T(8,128)} %get-tuple-element.169.lse_ref, ...), custom_call_target="tpu_custom_call" | custom-call | flops 17616076800 | bytes 8847360 | tf_op jit(solution)/shard_map/attend_back/pallas_call | solution.py:399
  252.2 4.7 %merge_one.1 = (bf16[2,2,96,768]{3,2,1,0:T(8,128)(2,1)}, bf16[2,2,96,768]{3,2,1,0:T(8,128)(2,1)}, bf16[2,2,24,3840]{3,2,1,0:T(8,128)(2,1)}, bf16[2,2,24,3840]{3,2,1,0:T(8,128)(2,1)}) custom-call(s32[3]{0:T(128)S(1)} %pad_add_fusion.place_ref, bf16[2,2,2,2,96,768]{5,4,3,2,1,0:T(8,128)(2,1)S(1)} %bitcast.111, bf16[2,2,2,2,96,768]{5,4,3,2,1,0:T(8,128)(2,1)S(1)} %bitcast.112, ...), custom_call_target="tpu_custom_call" | custom-call | bytes 10616832 | tf_op jit(solution)/shard_map/merge_one/pallas_call | solution.py:767
  261.0 28.6 %attend_back.3.refs_2_.g_ref = bf16[3,1280,384]{2,1,0:T(8,128)(2,1)} custom-call(s32[2,1280,1]{2,1,0:T(8,128)} %copy-done.27, bf16[3,1280,384]{2,1,0:T(8,128)(2,1)} %copy-done.10, s32[2,1280,1]{2,1,0:T(8,128)} %copy-done.28, s32[2,1,1280]{2,1,0:T(1,128)} %copy-done.31, f32[3,8,1280]{2,1,0:T(8,128)} %get-tuple-element.173.lse_ref, ...), custom_call_target="tpu_custom_call" | custom-call | flops 17616076800 | bytes 8847360 | tf_op jit(solution)/shard_map/attend_back/pallas_call | solution.py:399
  291.4 4.1 %merge_two.1 = (f32[2,96,768]{2,1,0:T(8,128)S(1)}, f32[2,96,768]{2,1,0:T(8,128)S(1)}, f32[2,24,3840]{2,1,0:T(8,128)S(1)}, f32[2,24,3840]{2,1,0:T(8,128)S(1)}, bf...) custom-call(s32[3]{0:T(128)S(1)} %pad_add_fusion.place_ref, ...), custom_call_target="tpu_custom_call" | custom-call | bytes 10616832 | tf_op jit(solution)/shard_map/merge_two/pallas_call | solution.py:767
  303.0 10.5 %weight_back.1 = (bf16[768,1152]{1,0:T(8,128)(2,1)}, f32[8,1152]{1,0:T(8,128)}) custom-call(bf16[2,1280,768]{2,1,0:T(8,128)(2,1)} %copy-done.5, bf16[3,1280,384]{2,1,0:T(8,128)(2,1)} %attend_back.2.refs_1_.g_ref, bf16[3,1280,384]{2,1,0:T(8,128)(2,1)} %attend_back.3.refs_2_.g_ref), custom_call_target="tpu_custom_call" | custom-call | flops 4529848320 | bytes 11599872 | tf_op jit(solution)/shard_map/weight_back/pallas_call | solution.py:491
  323.1 8.0 %collective-permute-start.33 = (bf16[2,24,6912]{2,1,0:T(8,128)(2,1)}, bf16[2,24,6912]{2,1,0:T(8,128)(2,1)S(1)}, u32[]{:S(2)}, u32[]{:S(2)}) collective-permute-start(bf16[2,24,6912]{2,1,0:T(8,128)(2,1)} %get-tuple-element.226), channel_id=1, source_target_pairs={{0,4},{1,5},{2,6},{3,7},{4,0},{5,1},{6,2},{7,3},{8,12},{9,13},{10,... | collective-permute-start | bytes 1990664 | tf_op jit(solution)/shard_map/ppermute | solution.py:689
  336.6 8.6 %project_back.2 = (bf16[640,768]{1,0:T(8,128)(2,1)S(1)}, bf16[640,768]{1,0:T(8,128)(2,1)S(1)}) custom-call(s32[1]{0:T(128)} %bitcast.part_ref, bf16[3,1280,384]{2,1,0:T(8,128)(2,1)S(1)} %copy-done.30, s32[2,1,1280]{2,1,0:T(1,128)S(1)} %get-tuple-element.217.row_ref, bf16[384,2432]{1,0:T(8,128)(2,1)S(1)} %bitcast.119, ...), custom_call_target="tpu_custom_call" | custom-call | flops 4781506560 | bytes 6684672 | tf_op jit(solution)/shard_map/project_back/pallas_call | solution.py:457
  348.7 3.2 collective-permute-start.39
  351.9 8.6 %project_back.3 = (bf16[640,768]{1,0:T(8,128)(2,1)S(1)}, bf16[640,768]{1,0:T(8,128)(2,1)S(1)}) custom-call(s32[1]{0:T(128)} %bitcast.part_ref, bf16[3,1280,384]{2,1,0:T(8,128)(2,1)S(1)} %copy-done.29, s32[2,1,1280]{2,1,0:T(1,128)S(1)} %get-tuple-element.217.row_ref, bf16[384,2432]{1,0:T(8,128)(2,1)S(1)} %bitcast.120, ...), custom_call_target="tpu_custom_call" | custom-call | flops 4781506560 | bytes 6684672 | tf_op jit(solution)/shard_map/project_back/pallas_call | solution.py:457
  363.5 2.8 collective-permute-done.39
  366.4 2.8 collective-permute-done.37
  373.4 3.8 collective-permute-done.40
  380.4 3.9 %collective-permute-done.41 = bf16[24,2432]{1,0:T(8,128)(2,1)S(1)} collective-permute-done((bf16[24,2432]{1,0:T(8,128)(2,1)S(1)}, bf16[24,2432]{1,0:T(8,128)(2,1)S(1)}, u32[]{:S(2)}, u32[]{:S(2)}) %collective-permute-start.41) | collective-permute-done | bytes 116768 | tf_op jit(solution)/shard_map/ppermute | solution.py:689
  (244 shorter events, 82.3 us)
Async XLA Ops:
  2.6 11.6 %collective-permute-start.1 = (bf16[24,2432]{1,0:T(8,128)(2,1)}, bf16[24,2432]{1,0:T(8,128)(2,1)S(1)}, u32[]{:S(2)}, u32[]{:S(2)}) collective-permute-start(bf16[24,2432]{1,0:T(8,128)(2,1)} %get-tuple-element.131), channel_id=1, source_target_pairs={{0,8},{1,9},{2,10},{3,11},{4,12},{5,13},{6,14},{7,15},{8,0},{9,1},... | collective-permute-start | bytes 350216 | tf_op jit(solution)/shard_map/ppermute | solution.py:693
  8.7 17.4 %collective-permute-start.7 = (bf16[2,640,768]{2,1,0:T(8,128)(2,1)}, bf16[2,640,768]{2,1,0:T(8,128)(2,1)}, u32[]{:S(2)}, u32[]{:S(2)}) collective-permute-start(bf16[2,640,768]{2,1,0:T(8,128)(2,1)} %bitcast.121), channel_id=1, source_target_pairs={{0,16},{16,0},{1,17},{17,1},{2,18},{18,2},{3,19},{19,3},{4,20},{20... | collective-permute-start | bytes 5898248 | tf_op jit(solution)/shard_map/ppermute | solution.py:677
  22.9 14.7 %collective-permute-start.8 = (bf16[4,24,2432]{2,1,0:T(8,128)(2,1)S(1)}, bf16[4,24,2432]{2,1,0:T(8,128)(2,1)S(1)}, u32[]{:S(2)}, u32[]{:S(2)}) collective-permute-start(bf16[4,24,2432]{2,1,0:T(8,128)(2,1)S(1)} %constant_dynamic-update-slice_fusion.ax_ref), channel_id=1, source_target_pairs={{0,2},{1,3},{2,0},{3,1},{4,6},{5,7},{6,4},{7,5},{8,10},{9,11},{10,... | collective-permute-start | bytes 1400840 | tf_op jit(solution)/shard_map/ppermute | solution.py:685
  24.5 13.1 %collective-permute-start.10 = (bf16[4,24,2432]{2,1,0:T(8,128)(2,1)S(1)}, bf16[4,24,2432]{2,1,0:T(8,128)(2,1)S(1)}, u32[]{:S(2)}, u32[]{:S(2)}) collective-permute-start(bf16[4,24,2432]{2,1,0:T(8,128)(2,1)S(1)} %constant_dynamic-update-slice_fusion.2.by_ref), channel_id=1, source_target_pairs={{0,1},{1,0},{2,3},{3,2},{4,5},{5,4},{6,7},{7,6},{8,9},{9,8},{10,11... | collective-permute-start | bytes 1400840 | tf_op jit(solution)/shard_map/ppermute | solution.py:681
  37.9 26.6 %collective-permute-start.4 = (bf16[24,6912]{1,0:T(8,128)(2,1)}, bf16[24,6912]{1,0:T(8,128)(2,1)}, u32[]{:S(2)}, u32[]{:S(2)}) collective-permute-start(bf16[24,6912]{1,0:T(8,128)(2,1)} %get-tuple-element.136), channel_id=1, source_target_pairs={{0,4},{1,5},{2,6},{3,7},{4,8},{5,9},{6,10},{7,11},{8,12},{9,13},{1... | collective-permute-start | bytes 995336 | tf_op jit(solution)/shard_map/ppermute | solution.py:693
  41.2 23.3 %collective-permute-start.5 = (bf16[24,6912]{1,0:T(8,128)(2,1)}, bf16[24,6912]{1,0:T(8,128)(2,1)}, u32[]{:S(2)}, u32[]{:S(2)}) collective-permute-start(bf16[24,6912]{1,0:T(8,128)(2,1)} %get-tuple-element.136), channel_id=1, source_target_pairs={{0,8},{1,9},{2,10},{3,11},{4,12},{5,13},{6,14},{7,15},{8,0},{9,1},... | collective-permute-start | bytes 995336 | tf_op jit(solution)/shard_map/ppermute | solution.py:693
  43.1 21.4 %collective-permute-start.6 = (bf16[24,6912]{1,0:T(8,128)(2,1)}, bf16[24,6912]{1,0:T(8,128)(2,1)}, u32[]{:S(2)}, u32[]{:S(2)}) collective-permute-start(bf16[24,6912]{1,0:T(8,128)(2,1)} %get-tuple-element.136), channel_id=1, source_target_pairs={{0,12},{1,13},{2,14},{3,15},{4,0},{5,1},{6,2},{7,3},{8,4},{9,5},{1... | collective-permute-start | bytes 995336 | tf_op jit(solution)/shard_map/ppermute | solution.py:693
  66.7 28.2 %collective-permute-start.12 = (bf16[2,24,6912]{2,1,0:T(8,128)(2,1)S(1)}, bf16[2,24,6912]{2,1,0:T(8,128)(2,1)S(1)}, u32[]{:S(2)}, u32[]{:S(2)}) collective-permute-start(bf16[2,24,6912]{2,1,0:T(8,128)(2,1)S(1)} %pad_maximum_fusion.8), channel_id=1, source_target_pairs={{0,1},{1,0},{2,3},{3,2},{4,5},{5,4},{6,7},{7,6},{8,9},{9,8},{10,11... | collective-permute-start | bytes 1990664 | tf_op jit(solution)/shard_map/ppermute | solution.py:681
  67.3 27.6 %collective-permute-start.13 = (bf16[2,24,6912]{2,1,0:T(8,128)(2,1)S(1)}, bf16[2,24,6912]{2,1,0:T(8,128)(2,1)S(1)}, u32[]{:S(2)}, u32[]{:S(2)}) collective-permute-start(bf16[2,24,6912]{2,1,0:T(8,128)(2,1)S(1)} %pad_maximum_fusion.9), channel_id=1, source_target_pairs={{0,2},{1,3},{2,0},{3,1},{4,6},{5,7},{6,4},{7,5},{8,10},{9,11},{10,... | collective-permute-start | bytes 1990664 | tf_op jit(solution)/shard_map/ppermute | solution.py:685
  95.2 30.5 %collective-permute-start.16 = (bf16[4,24,6912]{2,1,0:T(8,128)(2,1)S(1)}, bf16[4,24,6912]{2,1,0:T(8,128)(2,1)S(1)}, u32[]{:S(2)}, u32[]{:S(2)}) collective-permute-start(bf16[4,24,6912]{2,1,0:T(8,128)(2,1)S(1)} %pad_maximum_fusion.2.ax_ref), channel_id=1, source_target_pairs={{0,2},{1,3},{2,0},{3,1},{4,6},{5,7},{6,4},{7,5},{8,10},{9,11},{10,... | collective-permute-start | bytes 3981320 | tf_op jit(solution)/shard_map/ppermute | solution.py:685
  95.7 30.3 %collective-permute-start.17 = (bf16[4,24,6912]{2,1,0:T(8,128)(2,1)S(1)}, bf16[4,24,6912]{2,1,0:T(8,128)(2,1)}, u32[]{:S(2)}, u32[]{:S(2)}) collective-permute-start(bf16[4,24,6912]{2,1,0:T(8,128)(2,1)S(1)} %pad_maximum_fusion.3.by_ref), channel_id=1, source_target_pairs={{0,1},{1,0},{2,3},{3,2},{4,5},{5,4},{6,7},{7,6},{8,9},{9,8},{10,11... | collective-permute-start | bytes 3981320 | tf_op jit(solution)/shard_map/ppermute | solution.py:681
  130.1 11.5 %collective-permute-start.18 = (bf16[384,3840]{1,0:T(8,128)(2,1)}, bf16[384,3840]{1,0:T(8,128)(2,1)}, u32[]{:S(2)}, u32[]{:S(2)}) collective-permute-start(bf16[384,3840]{1,0:T(8,128)(2,1)} %bitcast.24.unear_ref), channel_id=1, source_target_pairs={{0,16},{16,0},{1,17},{17,1},{2,18},{18,2},{3,19},{19,3},{4,20},{20... | collective-permute-start | bytes 8847368 | tf_op jit(solution)/shard_map/ppermute | solution.py:677
  130.1 11.5 %collective-permute-start.19 = (bf16[1536,768]{1,0:T(8,128)(2,1)}, bf16[1536,768]{1,0:T(8,128)(2,1)}, u32[]{:S(2)}, u32[]{:S(2)}) collective-permute-start(bf16[1536,768]{1,0:T(8,128)(2,1)} %bitcast.25.dnear_ref), channel_id=1, source_target_pairs={{0,16},{16,0},{1,17},{17,1},{2,18},{18,2},{3,19},{19,3},{4,20},{20... | collective-permute-start | bytes 7077896 | tf_op jit(solution)/shard_map/ppermute | solution.py:677
  130.7 9.2 %collective-permute-start.14 = (bf16[640,384]{1,0:T(8,128)(2,1)}, bf16[640,384]{1,0:T(8,128)(2,1)S(1)}, u32[]{:S(2)}, u32[]{:S(2)}) collective-permute-start(bf16[640,384]{1,0:T(8,128)(2,1)} %get-tuple-element.159), channel_id=1, source_target_pairs={{0,16},{16,0},{1,17},{17,1},{2,18},{18,2},{3,19},{19,3},{4,20},{20... | collective-permute-start | bytes 1474568 | tf_op jit(solution)/shard_map/ppermute | solution.py:677
  130.7 9.9 %collective-permute-start.15 = (bf16[640,384]{1,0:T(8,128)(2,1)}, bf16[640,384]{1,0:T(8,128)(2,1)S(1)}, u32[]{:S(2)}, u32[]{:S(2)}) collective-permute-start(bf16[640,384]{1,0:T(8,128)(2,1)} %get-tuple-element.160), channel_id=1, source_target_pairs={{0,16},{16,0},{1,17},{17,1},{2,18},{18,2},{3,19},{19,3},{4,20},{20... | collective-permute-start | bytes 1474568 | tf_op jit(solution)/shard_map/ppermute | solution.py:677
  213.7 36.8 %collective-permute-start.22 = (bf16[384,3840]{1,0:T(8,128)(2,1)}, bf16[384,3840]{1,0:T(8,128)(2,1)}, u32[]{:S(2)}, u32[]{:S(2)}) collective-permute-start(bf16[384,3840]{1,0:T(8,128)(2,1)} %get-tuple-element.178), channel_id=1, source_target_pairs={{0,16},{16,0},{1,17},{17,1},{2,18},{18,2},{3,19},{19,3},{4,20},{20... | collective-permute-start | bytes 8847368 | tf_op jit(solution)/shard_map/ppermute | solution.py:677
  214.3 36.2 %collective-permute-start.21 = (bf16[1536,768]{1,0:T(8,128)(2,1)}, bf16[1536,768]{1,0:T(8,128)(2,1)}, u32[]{:S(2)}, u32[]{:S(2)}) collective-permute-start(bf16[1536,768]{1,0:T(8,128)(2,1)} %get-tuple-element.177), channel_id=1, source_target_pairs={{0,16},{16,0},{1,17},{17,1},{2,18},{18,2},{3,19},{19,3},{4,20},{20... | collective-permute-start | bytes 7077896 | tf_op jit(solution)/shard_map/ppermute | solution.py:677
  256.9 32.8 %collective-permute-start.25 = (bf16[2,2,24,3840]{3,2,1,0:T(8,128)(2,1)}, bf16[2,2,24,3840]{3,2,1,0:T(8,128)(2,1)S(1)}, u32[]{:S(2)}, u32[]{:S(2)}) collective-permute-start(bf16[2,2,24,3840]{3,2,1,0:T(8,128)(2,1)} %get-tuple-element.189), channel_id=1, source_target_pairs={{0,2},{1,3},{2,0},{3,1},{4,6},{5,7},{6,4},{7,5},{8,10},{9,11},{10,... | collective-permute-start | bytes 2211848 | tf_op jit(solution)/shard_map/ppermute | solution.py:685
  258.5 31.2 %collective-permute-start.26 = (bf16[2,2,24,3840]{3,2,1,0:T(8,128)(2,1)}, bf16[2,2,24,3840]{3,2,1,0:T(8,128)(2,1)}, u32[]{:S(2)}, u32[]{:S(2)}) collective-permute-start(bf16[2,2,24,3840]{3,2,1,0:T(8,128)(2,1)} %get-tuple-element.190), channel_id=1, source_target_pairs={{0,1},{1,0},{2,3},{3,2},{4,5},{5,4},{6,7},{7,6},{8,9},{9,8},{10,11... | collective-permute-start | bytes 2211848 | tf_op jit(solution)/shard_map/ppermute | solution.py:681
  258.9 30.6 %collective-permute-start.23 = (bf16[2,2,96,768]{3,2,1,0:T(8,128)(2,1)}, bf16[2,2,96,768]{3,2,1,0:T(8,128)(2,1)}, u32[]{:S(2)}, u32[]{:S(2)}) collective-permute-start(bf16[2,2,96,768]{3,2,1,0:T(8,128)(2,1)} %get-tuple-element.187), channel_id=1, source_target_pairs={{0,2},{1,3},{2,0},{3,1},{4,6},{5,7},{6,4},{7,5},{8,10},{9,11},{10,... | collective-permute-start | bytes 1769480 | tf_op jit(solution)/shard_map/ppermute | solution.py:685
  260.4 29.3 %collective-permute-start.24 = (bf16[2,2,96,768]{3,2,1,0:T(8,128)(2,1)}, bf16[2,2,96,768]{3,2,1,0:T(8,128)(2,1)}, u32[]{:S(2)}, u32[]{:S(2)}) collective-permute-start(bf16[2,2,96,768]{3,2,1,0:T(8,128)(2,1)} %get-tuple-element.188), channel_id=1, source_target_pairs={{0,1},{1,0},{2,3},{3,2},{4,5},{5,4},{6,7},{7,6},{8,9},{9,8},{10,11... | collective-permute-start | bytes 1769480 | tf_op jit(solution)/shard_map/ppermute | solution.py:681
  299.0 17.8 %collective-permute-start.29 = (bf16[2,24,3840]{2,1,0:T(8,128)(2,1)}, bf16[2,24,3840]{2,1,0:T(8,128)(2,1)S(1)}, u32[]{:S(2)}, u32[]{:S(2)}) collective-permute-start(bf16[2,24,3840]{2,1,0:T(8,128)(2,1)} %get-tuple-element.209), channel_id=1, source_target_pairs={{0,1},{1,0},{2,3},{3,2},{4,5},{5,4},{6,7},{7,6},{8,9},{9,8},{10,11... | collective-permute-start | bytes 1105928 | tf_op jit(solution)/shard_map/ppermute | solution.py:681
  300.3 16.5 %collective-permute-start.30 = (bf16[2,24,3840]{2,1,0:T(8,128)(2,1)}, bf16[2,24,3840]{2,1,0:T(8,128)(2,1)S(1)}, u32[]{:S(2)}, u32[]{:S(2)}) collective-permute-start(bf16[2,24,3840]{2,1,0:T(8,128)(2,1)} %get-tuple-element.210), channel_id=1, source_target_pairs={{0,2},{1,3},{2,0},{3,1},{4,6},{5,7},{6,4},{7,5},{8,10},{9,11},{10,... | collective-permute-start | bytes 1105928 | tf_op jit(solution)/shard_map/ppermute | solution.py:685
  300.9 14.1 %collective-permute-start.27 = (bf16[2,96,768]{2,1,0:T(8,128)(2,1)}, bf16[2,96,768]{2,1,0:T(8,128)(2,1)S(1)}, u32[]{:S(2)}, u32[]{:S(2)}) collective-permute-start(bf16[2,96,768]{2,1,0:T(8,128)(2,1)} %get-tuple-element.207), channel_id=1, source_target_pairs={{0,1},{1,0},{2,3},{3,2},{4,5},{5,4},{6,7},{7,6},{8,9},{9,8},{10,11... | collective-permute-start | bytes 884744 | tf_op jit(solution)/shard_map/ppermute | solution.py:681
  302.4 13.6 %collective-permute-start.28 = (bf16[2,96,768]{2,1,0:T(8,128)(2,1)}, bf16[2,96,768]{2,1,0:T(8,128)(2,1)S(1)}, u32[]{:S(2)}, u32[]{:S(2)}) collective-permute-start(bf16[2,96,768]{2,1,0:T(8,128)(2,1)} %get-tuple-element.208), channel_id=1, source_target_pairs={{0,2},{1,3},{2,0},{3,1},{4,6},{5,7},{6,4},{7,5},{8,10},{9,11},{10,... | collective-permute-start | bytes 884744 | tf_op jit(solution)/shard_map/ppermute | solution.py:685
  323.1 22.2 %collective-permute-start.33 = (bf16[2,24,6912]{2,1,0:T(8,128)(2,1)}, bf16[2,24,6912]{2,1,0:T(8,128)(2,1)S(1)}, u32[]{:S(2)}, u32[]{:S(2)}) collective-permute-start(bf16[2,24,6912]{2,1,0:T(8,128)(2,1)} %get-tuple-element.226), channel_id=1, source_target_pairs={{0,4},{1,5},{2,6},{3,7},{4,0},{5,1},{6,2},{7,3},{8,12},{9,13},{10,... | collective-permute-start | bytes 1990664 | tf_op jit(solution)/shard_map/ppermute | solution.py:689
  335.5 10.1 %collective-permute-start.32 = (bf16[384,1280]{1,0:T(8,128)(2,1)S(1)}, bf16[384,1280]{1,0:T(8,128)(2,1)S(1)}, u32[]{:S(2)}, u32[]{:S(2)}) collective-permute-start(bf16[384,1280]{1,0:T(8,128)(2,1)S(1)} %pad_maximum_fusion.6), channel_id=1, source_target_pairs={{0,16},{16,0},{1,17},{17,1},{2,18},{18,2},{3,19},{19,3},{4,20},{20... | collective-permute-start | bytes 2949128 | tf_op jit(solution)/shard_map/ppermute | solution.py:677
  345.2 33.1 %collective-permute-start.31 = (bf16[640,768]{1,0:T(8,128)(2,1)S(1)}, bf16[640,768]{1,0:T(8,128)(2,1)S(1)}, u32[]{:S(2)}, u32[]{:S(2)}) collective-permute-start(bf16[640,768]{1,0:T(8,128)(2,1)S(1)} %get-tuple-element.219), channel_id=1, source_target_pairs={{0,16},{16,0},{1,17},{17,1},{2,18},{18,2},{3,19},{19,3},{4,20},{20... | collective-permute-start | bytes 2949128 | tf_op jit(solution)/shard_map/ppermute | solution.py:677
  346.8 13.9 %collective-permute-start.35 = (bf16[2,2,24,2432]{3,2,0,1:T(8,128)(2,1)S(1)}, bf16[2,2,24,2432]{3,2,0,1:T(8,128)(2,1)S(1)}, u32[]{:S(2)}, u32[]{:S(2)}) collective-permute-start(bf16[2,2,24,2432]{3,2,0,1:T(8,128)(2,1)S(1)} %copy_bitcast_fusion.3), channel_id=1, source_target_pairs={{0,2},{1,3},{2,0},{3,1},{4,6},{5,7},{6,4},{7,5},{8,10},{9,11},{10,... | collective-permute-start | bytes 1400840 | tf_op jit(solution)/shard_map/ppermute | solution.py:685
  347.6 13.1 %collective-permute-start.36 = (bf16[2,2,24,2432]{3,2,0,1:T(8,128)(2,1)S(1)}, bf16[2,2,24,2432]{3,2,0,1:T(8,128)(2,1)S(1)}, u32[]{:S(2)}, u32[]{:S(2)}) collective-permute-start(bf16[2,2,24,2432]{3,2,0,1:T(8,128)(2,1)S(1)} %copy_bitcast_fusion.2), channel_id=1, source_target_pairs={{0,1},{1,0},{2,3},{3,2},{4,5},{5,4},{6,7},{7,6},{8,9},{9,8},{10,11... | collective-permute-start | bytes 1400840 | tf_op jit(solution)/shard_map/ppermute | solution.py:681
  348.7 17.7 %collective-permute-start.39 = (bf16[24,6912]{1,0:T(8,128)(2,1)S(1)}, bf16[24,6912]{1,0:T(8,128)(2,1)S(1)}, u32[]{:S(2)}, u32[]{:S(2)}) collective-permute-start(bf16[24,6912]{1,0:T(8,128)(2,1)S(1)} %fusion.2), channel_id=1, source_target_pairs={{0,8},{1,9},{2,10},{3,11},{4,12},{5,13},{6,14},{7,15},{8,0},{9,1},... | collective-permute-start | bytes 995336 | tf_op jit(solution)/shard_map/ppermute | solution.py:689
  360.5 17.8 %collective-permute-start.34 = (bf16[640,768]{1,0:T(8,128)(2,1)S(1)}, bf16[640,768]{1,0:T(8,128)(2,1)S(1)}, u32[]{:S(2)}, u32[]{:S(2)}) collective-permute-start(bf16[640,768]{1,0:T(8,128)(2,1)S(1)} %get-tuple-element.230), channel_id=1, source_target_pairs={{0,16},{16,0},{1,17},{17,1},{2,18},{18,2},{3,19},{19,3},{4,20},{20... | collective-permute-start | bytes 2949128 | tf_op jit(solution)/shard_map/ppermute | solution.py:677
  (51 other events, 387.2 us)

commit v7 on v6

--- a/solution.py
+++ b/solution.py
@@ -150,7 +150,7 @@
         grid=(batches,),
         in_specs=[each(rows, 1), each(half, width), each(half, width)],
         out_specs=each(rows, width),
-        out_shape=jax.ShapeDtypeStruct((batches, rows, width), BF),
+        out_shape=pltpu.HBM((batches, rows, width), BF),
         compiler_params=pltpu.CompilerParams(vmem_limit_bytes=40 << 20),
         cost_estimate=pl.CostEstimate(
             flops=2 * batches * rows * rows * width, bytes_accessed=4 * batches * rows * width, transcendentals=0
@@ -212,7 +212,7 @@
         grid=(1,),
         in_specs=[smem, each(width), anywhere, anywhere, vmem, each(PAIR), each(PAIR)],
         out_specs=pl.BlockSpec((3, rows, share), lambda i: (0, 0, 0)),
-        out_shape=jax.ShapeDtypeStruct((3, rows, share), BF),
+        out_shape=pltpu.HBM((3, rows, share), BF),
         scratch_shapes=[pltpu.VMEM((width, 3 * share), BF), pltpu.SemaphoreType.DMA((6,))],
         compiler_params=pltpu.CompilerParams(vmem_limit_bytes=40 << 20),
         cost_estimate=pl.CostEstimate(
@@ -404,7 +404,7 @@
                   pl.BlockSpec((PAIR, rows), lambda j: (j, 0)),
                   given, given, whole((rows, PAIR)), whole((rows, PAIR))],
         out_specs=pl.BlockSpec((3, rows, PAIR), lambda j: (0, 0, j)),
-        out_shape=jax.ShapeDtypeStruct((3, rows, share), BF),
+        out_shape=pltpu.HBM((3, rows, share), BF),
         scratch_shapes=[pltpu.VMEM((rows, rows), BF), pltpu.VMEM((rows, 2 * PAIR), BF),
                         pltpu.VMEM((rows, 2 * PAIR), BF), pltpu.VMEM((PAIR, rows), BF),
                         pltpu.VMEM((PAIR, rows), BF), pltpu.VMEM((PAIR, rows), BF),
@@ -817,8 +817,8 @@
                   pl.BlockSpec((1, 1, 2, 1, n, width), lambda k, p: (1, k, 0, p[2], 0, 0))]
         came_specs += [pl.BlockSpec((1, 2, n, width), lambda k, p: (k, 0, 0, 0))] * 2
         outs += [pl.BlockSpec((1, n, width), lambda k, p: (k, 0, 0))] * 2
-        stays += [jax.ShapeDtypeStruct((2, n, width), F32)] * 2
-        sends += [jax.ShapeDtypeStruct((2, n, width), BF)] * 2
+        stays += [pltpu.HBM((2, n, width), F32)] * 2
+        sends += [pltpu.HBM((2, n, width), BF)] * 2
     both = fold_call(merge_two_body, "merge_two", (2,), place, cubes(mines) + cubes(theirs) + list(came),
                      specs * 2 + came_specs, outs * 2, stays + sends)
     return both[:len(stays)], both[len(stays):]
@@ -966,7 +966,8 @@
         ctxs.append((near, swap_cores(away)))
     if staged:
         first_y, second_x = tie((first_y, second_x), ctxs[1][0])
-        u_near, d_near = joined((first, first_y, second_x, second), 4, width)
+        ctxs[0] = (ctxs[0][0], tie(ctxs[0][1], ctxs[1][0]))
+        u_near, d_near = tie(joined((first, first_y, second_x, second), 4, width), [pair[1] for pair in ctxs])
     u_away, d_away = swap_cores(u_near), swap_cores(d_near)
     near, away = (jnp.concatenate([item[i] for item in ctxs], axis=0) for i in range(2))
     (outputs, grad_one, cnear, caway, sums, bsum, d_mine, d_theirs, uo_mine, uo_theirs) = feed(
@@ -974,7 +975,7 @@
         cotangent.reshape(batches * half, width), thin_rows, b_up, u_near, u_away, d_near, d_away,
     )
     caway = swap_cores(caway)
-    d_theirs, uo_theirs = swap_cores(d_theirs), swap_cores(uo_theirs)
+    d_theirs, uo_theirs = (swap_cores(value) for value in tie((d_theirs, uo_theirs), caway))
     plus = lambda mine, theirs: (mine.astype(F32) + theirs.astype(F32)).astype(BF)
 
     def back(b, given):

time: 393 us -> 386 us (0.982)
  waiting for transfers between devices: 34.1 us -> 28.2 us
  local copies, waits for them, and re-layouts: 37 us -> 32 us
  Pallas kernels: 250 us -> 254 us
    unnamed x90 -> x78, local copies, waits for them, and re-layouts: 26.7 us -> 21.8 us
    ppermute x12, waiting for transfers between devices: 8.63 us -> 4.08 us  [swap_cores(): return lax.ppermute(value, 'seq', [(0, 1), (1, 0)])]
  transfers between devices with their start and end apart: 42 -> 42, of which waited for: 17 -> 16; matrix products, arithmetic and copies ran while one was open for 5% -> 6% of each run, Pallas kernels for 42% -> 45%
where the time goes in v7:
time: 386 us; the launch traced here: 380 us
  Pallas kernels  254 us (66%)
  starting transfers between devices  50.4 us (13%)
  local copies, waits for them, and re-layouts  32 us (8%)
  waiting for transfers between devices  28.2 us (7%)
  other arithmetic  13.3 us (3%)
    pallas_call x1, Pallas kernels, feed(): pl.pallas_call(functools.partial(feed_body, chunk), grid=(rows // block,)...  72.1 us
    pallas_call x2, Pallas kernels, attend_back(): pl.pallas_call(functools.partial(attend_back_body, block), grid=(pairs,),...  57.4 us
    pallas_call x2, Pallas kernels, attend(): pl.pallas_call(functools.partial(attend_body, block), grid=(pairs,), in_s...  52 us
    unnamed x78, local copies, waits for them, and re-layouts  21.8 us
    pallas_call x2, Pallas kernels, project_back(): pl.pallas_call(functools.partial(project_back_body, block), grid=(1,), in...  17.2 us
    pallas_call x2, Pallas kernels, project(): pl.pallas_call(functools.partial(project_body, block), grid=(1,), in_spec...  13.7 us
    ppermute x6, starting transfers between devices, shift_z(): lax.ppermute(value, 'fsdp', [(i, (i + 4 * k) % 16) for i in range(16)])  13.1 us
    ppermute x4, starting transfers between devices, flip_z(): return lax.ppermute(value, 'fsdp', [(i, i ^ 4 * k) for i in range(16)])  12.4 us
  transfers between devices with their start and end apart: 42, of which 16 were waited for; matrix products, arithmetic and copies ran while one was open for 6% of the time, Pallas kernels for 45%

profile of v7, /device:TPU:0, one launch (start us, length us, event | category | flops | bytes accessed | tf_op | source)
XLA Modules:
  0.0 379.9 jit_solution(15118862830155198953)
XLA Ops:
  0.7 1.9 pack.1
  2.6 4.1 %collective-permute-start.1 = (bf16[24,2432]{1,0:T(8,128)(2,1)}, bf16[24,2432]{1,0:T(8,128)(2,1)S(1)}, u32[]{:S(2)}, u32[]{:S(2)}) collective-permute-start(bf16[24,2432]{1,0:T(8,128)(2,1)} %get-tuple-element.136), channel_id=1, source_target_pairs={{0,8},{1,9},{2,10},{3,11},{4,12},{5,13},{6,14},{7,15},{8,0},{9,1},... | collective-permute-start | bytes 350216 | tf_op jit(solution)/shard_map/ppermute | solution.py:693
  9.4 3.6 ready.1
  19.4 4.7 %collective-permute-done.3 = bf16[2,24,2432]{2,1,0:T(8,128)(2,1)S(1)} collective-permute-done((bf16[2,24,2432]{2,1,0:T(8,128)(2,1)S(1)}, bf16[2,24,2432]{2,1,0:T(8,128)(2,1)S(1)}, u32[]{:S(2)}, u32[]{:S(2)}) %collective-permute-start.3) | collective-permute-done | bytes 233504 | tf_op jit(solution)/shard_map/ppermute | solution.py:681
  27.3 11.0 %arrange.1.xw_ref.refs_0_ = bf16[2,1280,768]{2,1,0:T(8,128)(2,1)} custom-call(s32[2,1280,1]{2,1,0:T(8,128)S(1)} %get-tuple-element.138.idx_ref, bf16[2,640,768]{2,1,0:T(8,128)(2,1)S(1)} %bitcast.123, bf16[2,640,768]{2,1,0:T(8,128)(2,1)} %collective-permute-done.7.other_ref), custom_call_target="tpu_custom_call" | custom-call | flops 5033164800 | bytes 7864320 | tf_op jit(solution)/shard_map/arrange/pallas_call | solution.py:148
  38.5 2.1 collective-permute-start.4
  40.6 1.9 collective-permute-start.5
  42.5 3.0 collective-permute-start.6
  46.7 2.1 copy-done.5
  50.1 6.8 %project.3.qkv_ref = bf16[3,1280,384]{2,1,0:T(8,128)(2,1)} custom-call(s32[1]{0:T(128)} %bitcast.part_ref, bf16[2,1280,768]{2,1,0:T(8,128)(2,1)S(1)} %copy-done.5, bf16[384,2432]{1,0:T(8,128)(2,1)S(1)} %bitcast.117, bf16[384,2432]{1,0:T(8,128)(2,1)} %collective-permute-done.11.away_ref.waway_ref, f32[1,1152]{1,0:T(1,128)S(1)} %pad_maximum_fusion.14.bias_ref, ...), custom_call_target="tpu_custom_call" | custom-call | flops 2264924160 | bytes 6684672 | tf_op jit(solution)/shard_map/project/pallas_call | solution.py:210
  57.0 6.9 %project.2.qkv_ref = bf16[3,1280,384]{2,1,0:T(8,128)(2,1)} custom-call(s32[1]{0:T(128)} %bitcast.part_ref, bf16[2,1280,768]{2,1,0:T(8,128)(2,1)S(1)} %copy-done.5, bf16[384,2432]{1,0:T(8,128)(2,1)S(1)} %bitcast.118, bf16[384,2432]{1,0:T(8,128)(2,1)} %collective-permute-done.11.away_ref.waway_ref, f32[1,1152]{1,0:T(1,128)S(1)} %pad_maximum_fusion.14.bias_ref, ...), custom_call_target="tpu_custom_call" | custom-call | flops 2264924160 | bytes 6684672 | tf_op jit(solution)/shard_map/project/pallas_call | solution.py:210
  69.1 26.0 %attend.2 = (bf16[640,384]{1,0:T(8,128)(2,1)}, bf16[640,384]{1,0:T(8,128)(2,1)}, bf16[384,1280]{1,0:T(8,128)(2,1)}, f32[3,8,1280]{2,1,0:T(8,128)}) custom-call(s32[2,1280,1]{2,1,0:T(8,128)} %copy-done.20, bf16[3,1280,384]{2,1,0:T(8,128)(2,1)} %project.2.qkv_ref, s32[2,1280,1]{2,1,0:T(8,128)} %copy-done.21, s32[2,1,1280]{2,1,0:T(1,128)} %copy-done.24), custom_call_target="tpu_custom_call" | custom-call | flops 7549747200 | bytes 5898240 | tf_op jit(solution)/shard_map/attend/pallas_call | solution.py:285
  97.8 26.0 %attend.3 = (bf16[640,384]{1,0:T(8,128)(2,1)}, bf16[640,384]{1,0:T(8,128)(2,1)}, bf16[384,1280]{1,0:T(8,128)(2,1)}, f32[3,8,1280]{2,1,0:T(8,128)}) custom-call(s32[2,1280,1]{2,1,0:T(8,128)} %copy-done.20, bf16[3,1280,384]{2,1,0:T(8,128)(2,1)} %project.3.qkv_ref, s32[2,1280,1]{2,1,0:T(8,128)} %copy-done.21, s32[2,1,1280]{2,1,0:T(1,128)} %copy-done.24), custom_call_target="tpu_custom_call" | custom-call | flops 7549747200 | bytes 5898240 | tf_op jit(solution)/shard_map/attend/pallas_call | solution.py:285
  126.7 4.2 %assemble.3 = (bf16[16,24,3840]{2,1,0:T(8,128)(2,1)}, bf16[16,96,768]{2,1,0:T(8,128)(2,1)}) custom-call(s32[1]{0:T(128)} %bitcast.15.place_ref, bf16[4,24,6912]{2,1,0:T(8,128)(2,1)S(1)} %pad_maximum_fusion.2.ax_ref, bf16[4,24,6912]{2,1,0:T(8,128)(2,1)S(1)} %collective-permute-done.16.ay_ref, bf16[4,24,6912]{2,1,0:T(8,128)(2,1)} %collective-permute-done.17.bx_ref, ...), custom_call_target="tpu_custom_call" | custom-call | bytes 10616832 | tf_op jit(solution)/shard_map/assemble/pallas_call | solution.py:723
  134.1 2.2 pad_maximum_fusion.4.near_ref
  136.3 2.3 pad_maximum_fusion.5.away_ref
  141.5 72.1 %feed.1 = (bf16[1280,768]{1,0:T(8,128)(2,1)}, f32[1280,768]{1,0:T(8,128)}, bf16[1280,384]{1,0:T(8,128)(2,1)}, bf16[1280,384]{1,0:T(8,128)(2,1)}, f32[8,768]{1,0:...) custom-call(s32[1]{0:T(128)} %bitcast.part_ref, ...), custom_call_target="tpu_custom_call" | custom-call | flops 40768634880 | bytes 37355520 | tf_op jit(solution)/shard_map/feed/pallas_call | solution.py:650
  213.8 2.6 collective-permute-done.20.gaway_ref
  219.1 28.8 %attend_back.2.refs_1_.g_ref = bf16[3,1280,384]{2,1,0:T(8,128)(2,1)} custom-call(s32[2,1280,1]{2,1,0:T(8,128)} %copy-done.20, bf16[3,1280,384]{2,1,0:T(8,128)(2,1)} %project.2.qkv_ref, s32[2,1280,1]{2,1,0:T(8,128)} %copy-done.21, s32[2,1,1280]{2,1,0:T(1,128)} %copy-done.24, f32[3,8,1280]{2,1,0:T(8,128)} %get-tuple-element.177.lse_ref, ...), custom_call_target="tpu_custom_call" | custom-call | flops 17616076800 | bytes 8847360 | tf_op jit(solution)/shard_map/attend_back/pallas_call | solution.py:399
  249.6 4.7 %merge_one.1 = (bf16[2,2,96,768]{3,2,1,0:T(8,128)(2,1)}, bf16[2,2,96,768]{3,2,1,0:T(8,128)(2,1)}, bf16[2,2,24,3840]{3,2,1,0:T(8,128)(2,1)}, bf16[2,2,24,3840]{3,2,1,0:T(8,128)(2,1)}) custom-call(s32[3]{0:T(128)S(1)} %pad_add_fusion.place_ref, bf16[2,2,2,2,96,768]{5,4,3,2,1,0:T(8,128)(2,1)S(1)} %bitcast.111, bf16[2,2,2,2,96,768]{5,4,3,2,1,0:T(8,128)(2,1)S(1)} %bitcast.112, ...), custom_call_target="tpu_custom_call" | custom-call | bytes 10616832 | tf_op jit(solution)/shard_map/merge_one/pallas_call | solution.py:767
  258.4 28.6 %attend_back.3.refs_2_.g_ref = bf16[3,1280,384]{2,1,0:T(8,128)(2,1)} custom-call(s32[2,1280,1]{2,1,0:T(8,128)} %copy-done.20, bf16[3,1280,384]{2,1,0:T(8,128)(2,1)} %project.3.qkv_ref, s32[2,1280,1]{2,1,0:T(8,128)} %copy-done.21, s32[2,1,1280]{2,1,0:T(1,128)} %copy-done.24, f32[3,8,1280]{2,1,0:T(8,128)} %get-tuple-element.181.lse_ref, ...), custom_call_target="tpu_custom_call" | custom-call | flops 17616076800 | bytes 8847360 | tf_op jit(solution)/shard_map/attend_back/pallas_call | solution.py:399
  288.7 4.5 %merge_two.1 = (f32[2,96,768]{2,1,0:T(8,128)}, f32[2,96,768]{2,1,0:T(8,128)}, f32[2,24,3840]{2,1,0:T(8,128)}, f32[2,24,3840]{2,1,0:T(8,128)}, bf16[2,96,768]{2,1...) custom-call(s32[3]{0:T(128)S(1)} %pad_add_fusion.place_ref, ...), custom_call_target="tpu_custom_call" | custom-call | bytes 10616832 | tf_op jit(solution)/shard_map/merge_two/pallas_call | solution.py:767
  297.3 10.3 %weight_back.1 = (bf16[768,1152]{1,0:T(8,128)(2,1)}, f32[8,1152]{1,0:T(8,128)}) custom-call(bf16[2,1280,768]{2,1,0:T(8,128)(2,1)} %arrange.1.xw_ref.refs_0_, bf16[3,1280,384]{2,1,0:T(8,128)(2,1)} %attend_back.2.refs_1_.g_ref, bf16[3,1280,384]{2,1,0:T(8,128)(2,1)} %attend_back.3.refs_2_.g_ref), custom_call_target="tpu_custom_call" | custom-call | flops 4529848320 | bytes 11599872 | tf_op jit(solution)/shard_map/weight_back/pallas_call | solution.py:491
  317.5 7.7 %collective-permute-start.33 = (bf16[2,24,6912]{2,1,0:T(8,128)(2,1)}, bf16[2,24,6912]{2,1,0:T(8,128)(2,1)S(1)}, u32[]{:S(2)}, u32[]{:S(2)}) collective-permute-start(bf16[2,24,6912]{2,1,0:T(8,128)(2,1)} %get-tuple-element.236), channel_id=1, source_target_pairs={{0,4},{1,5},{2,6},{3,7},{4,0},{5,1},{6,2},{7,3},{8,12},{9,13},{10,... | collective-permute-start | bytes 1990664 | tf_op jit(solution)/shard_map/ppermute | solution.py:689
  327.9 1.7 constant_dynamic-slice_fusion.6
  330.9 8.6 %project_back.2 = (bf16[640,768]{1,0:T(8,128)(2,1)S(1)}, bf16[640,768]{1,0:T(8,128)(2,1)S(1)}) custom-call(s32[1]{0:T(128)} %bitcast.part_ref, bf16[3,1280,384]{2,1,0:T(8,128)(2,1)S(1)} %copy-done.23, s32[2,1,1280]{2,1,0:T(1,128)S(1)} %get-tuple-element.227.row_ref, bf16[384,2432]{1,0:T(8,128)(2,1)S(1)} %bitcast.119, ...), custom_call_target="tpu_custom_call" | custom-call | flops 4781506560 | bytes 6684672 | tf_op jit(solution)/shard_map/project_back/pallas_call | solution.py:457
  342.8 2.4 collective-permute-start.39
  345.3 8.6 %project_back.3 = (bf16[640,768]{1,0:T(8,128)(2,1)S(1)}, bf16[640,768]{1,0:T(8,128)(2,1)S(1)}) custom-call(s32[1]{0:T(128)} %bitcast.part_ref, bf16[3,1280,384]{2,1,0:T(8,128)(2,1)S(1)} %copy-done.22, s32[2,1,1280]{2,1,0:T(1,128)S(1)} %get-tuple-element.227.row_ref, bf16[384,2432]{1,0:T(8,128)(2,1)S(1)} %bitcast.120, ...), custom_call_target="tpu_custom_call" | custom-call | flops 4781506560 | bytes 6684672 | tf_op jit(solution)/shard_map/project_back/pallas_call | solution.py:457
  357.4 2.5 collective-permute-done.39
  360.0 2.6 collective-permute-done.37
  366.5 3.6 collective-permute-done.40
  373.8 3.4 collective-permute-done.41
  (232 shorter events, 76.7 us)
Async XLA Ops:
  2.6 13.2 %collective-permute-start.1 = (bf16[24,2432]{1,0:T(8,128)(2,1)}, bf16[24,2432]{1,0:T(8,128)(2,1)S(1)}, u32[]{:S(2)}, u32[]{:S(2)}) collective-permute-start(bf16[24,2432]{1,0:T(8,128)(2,1)} %get-tuple-element.136), channel_id=1, source_target_pairs={{0,8},{1,9},{2,10},{3,11},{4,12},{5,13},{6,14},{7,15},{8,0},{9,1},... | collective-permute-start | bytes 350216 | tf_op jit(solution)/shard_map/ppermute | solution.py:693
  6.6 9.2 %collective-permute-start.2 = (bf16[24,2432]{1,0:T(8,128)(2,1)}, bf16[24,2432]{1,0:T(8,128)(2,1)S(1)}, u32[]{:S(2)}, u32[]{:S(2)}) collective-permute-start(bf16[24,2432]{1,0:T(8,128)(2,1)} %get-tuple-element.136), channel_id=1, source_target_pairs={{0,12},{1,13},{2,14},{3,15},{4,0},{5,1},{6,2},{7,3},{8,4},{9,5},{1... | collective-permute-start | bytes 350216 | tf_op jit(solution)/shard_map/ppermute | solution.py:693
  8.7 18.6 %collective-permute-start.7 = (bf16[2,640,768]{2,1,0:T(8,128)(2,1)}, bf16[2,640,768]{2,1,0:T(8,128)(2,1)}, u32[]{:S(2)}, u32[]{:S(2)}) collective-permute-start(bf16[2,640,768]{2,1,0:T(8,128)(2,1)} %bitcast.121), channel_id=1, source_target_pairs={{0,16},{16,0},{1,17},{17,1},{2,18},{18,2},{3,19},{19,3},{4,20},{20... | collective-permute-start | bytes 5898248 | tf_op jit(solution)/shard_map/ppermute | solution.py:677
  24.1 14.1 %collective-permute-start.8 = (bf16[4,24,2432]{2,1,0:T(8,128)(2,1)S(1)}, bf16[4,24,2432]{2,1,0:T(8,128)(2,1)S(1)}, u32[]{:S(2)}, u32[]{:S(2)}) collective-permute-start(bf16[4,24,2432]{2,1,0:T(8,128)(2,1)S(1)} %constant_dynamic-update-slice_fusion.ax_ref), channel_id=1, source_target_pairs={{0,2},{1,3},{2,0},{3,1},{4,6},{5,7},{6,4},{7,5},{8,10},{9,11},{10,... | collective-permute-start | bytes 1400840 | tf_op jit(solution)/shard_map/ppermute | solution.py:685
  25.7 12.5 %collective-permute-start.10 = (bf16[4,24,2432]{2,1,0:T(8,128)(2,1)S(1)}, bf16[4,24,2432]{2,1,0:T(8,128)(2,1)S(1)}, u32[]{:S(2)}, u32[]{:S(2)}) collective-permute-start(bf16[4,24,2432]{2,1,0:T(8,128)(2,1)S(1)} %constant_dynamic-update-slice_fusion.2.by_ref), channel_id=1, source_target_pairs={{0,1},{1,0},{2,3},{3,2},{4,5},{5,4},{6,7},{7,6},{8,9},{9,8},{10,11... | collective-permute-start | bytes 1400840 | tf_op jit(solution)/shard_map/ppermute | solution.py:681
  38.5 25.3 %collective-permute-start.4 = (bf16[24,6912]{1,0:T(8,128)(2,1)}, bf16[24,6912]{1,0:T(8,128)(2,1)}, u32[]{:S(2)}, u32[]{:S(2)}) collective-permute-start(bf16[24,6912]{1,0:T(8,128)(2,1)} %get-tuple-element.141), channel_id=1, source_target_pairs={{0,4},{1,5},{2,6},{3,7},{4,8},{5,9},{6,10},{7,11},{8,12},{9,13},{1... | collective-permute-start | bytes 995336 | tf_op jit(solution)/shard_map/ppermute | solution.py:693
  40.6 24.5 %collective-permute-start.5 = (bf16[24,6912]{1,0:T(8,128)(2,1)}, bf16[24,6912]{1,0:T(8,128)(2,1)}, u32[]{:S(2)}, u32[]{:S(2)}) collective-permute-start(bf16[24,6912]{1,0:T(8,128)(2,1)} %get-tuple-element.141), channel_id=1, source_target_pairs={{0,8},{1,9},{2,10},{3,11},{4,12},{5,13},{6,14},{7,15},{8,0},{9,1},... | collective-permute-start | bytes 995336 | tf_op jit(solution)/shard_map/ppermute | solution.py:693
  42.5 22.7 %collective-permute-start.6 = (bf16[24,6912]{1,0:T(8,128)(2,1)}, bf16[24,6912]{1,0:T(8,128)(2,1)}, u32[]{:S(2)}, u32[]{:S(2)}) collective-permute-start(bf16[24,6912]{1,0:T(8,128)(2,1)} %get-tuple-element.141), channel_id=1, source_target_pairs={{0,12},{1,13},{2,14},{3,15},{4,0},{5,1},{6,2},{7,3},{8,4},{9,5},{1... | collective-permute-start | bytes 995336 | tf_op jit(solution)/shard_map/ppermute | solution.py:693
  67.3 27.7 %collective-permute-start.12 = (bf16[2,24,6912]{2,1,0:T(8,128)(2,1)S(1)}, bf16[2,24,6912]{2,1,0:T(8,128)(2,1)S(1)}, u32[]{:S(2)}, u32[]{:S(2)}) collective-permute-start(bf16[2,24,6912]{2,1,0:T(8,128)(2,1)S(1)} %pad_maximum_fusion.8), channel_id=1, source_target_pairs={{0,1},{1,0},{2,3},{3,2},{4,5},{5,4},{6,7},{7,6},{8,9},{9,8},{10,11... | collective-permute-start | bytes 1990664 | tf_op jit(solution)/shard_map/ppermute | solution.py:681
  68.0 27.1 %collective-permute-start.13 = (bf16[2,24,6912]{2,1,0:T(8,128)(2,1)S(1)}, bf16[2,24,6912]{2,1,0:T(8,128)(2,1)S(1)}, u32[]{:S(2)}, u32[]{:S(2)}) collective-permute-start(bf16[2,24,6912]{2,1,0:T(8,128)(2,1)S(1)} %pad_maximum_fusion.9), channel_id=1, source_target_pairs={{0,2},{1,3},{2,0},{3,1},{4,6},{5,7},{6,4},{7,5},{8,10},{9,11},{10,... | collective-permute-start | bytes 1990664 | tf_op jit(solution)/shard_map/ppermute | solution.py:685
  95.4 30.5 %collective-permute-start.16 = (bf16[4,24,6912]{2,1,0:T(8,128)(2,1)S(1)}, bf16[4,24,6912]{2,1,0:T(8,128)(2,1)S(1)}, u32[]{:S(2)}, u32[]{:S(2)}) collective-permute-start(bf16[4,24,6912]{2,1,0:T(8,128)(2,1)S(1)} %pad_maximum_fusion.2.ax_ref), channel_id=1, source_target_pairs={{0,2},{1,3},{2,0},{3,1},{4,6},{5,7},{6,4},{7,5},{8,10},{9,11},{10,... | collective-permute-start | bytes 3981320 | tf_op jit(solution)/shard_map/ppermute | solution.py:685
  96.4 30.3 %collective-permute-start.17 = (bf16[4,24,6912]{2,1,0:T(8,128)(2,1)S(1)}, bf16[4,24,6912]{2,1,0:T(8,128)(2,1)}, u32[]{:S(2)}, u32[]{:S(2)}) collective-permute-start(bf16[4,24,6912]{2,1,0:T(8,128)(2,1)S(1)} %pad_maximum_fusion.3.by_ref), channel_id=1, source_target_pairs={{0,1},{1,0},{2,3},{3,2},{4,5},{5,4},{6,7},{7,6},{8,9},{9,8},{10,11... | collective-permute-start | bytes 3981320 | tf_op jit(solution)/shard_map/ppermute | solution.py:681
  97.8 26.5 %collective-permute-start.14 = (bf16[640,384]{1,0:T(8,128)(2,1)}, bf16[640,384]{1,0:T(8,128)(2,1)}, u32[]{:S(2)}, u32[]{:S(2)}) collective-permute-start(bf16[640,384]{1,0:T(8,128)(2,1)} %get-tuple-element.164), channel_id=1, source_target_pairs={{0,16},{16,0},{1,17},{17,1},{2,18},{18,2},{3,19},{19,3},{4,20},{20... | collective-permute-start | bytes 1474568 | tf_op jit(solution)/shard_map/ppermute | solution.py:677
  130.9 9.1 %collective-permute-start.18 = (bf16[384,3840]{1,0:T(8,128)(2,1)}, bf16[384,3840]{1,0:T(8,128)(2,1)S(1)}, u32[]{:S(2)}, u32[]{:S(2)}) collective-permute-start(bf16[384,3840]{1,0:T(8,128)(2,1)} %bitcast.24.unear_ref), channel_id=1, source_target_pairs={{0,16},{16,0},{1,17},{17,1},{2,18},{18,2},{3,19},{19,3},{4,20},{20... | collective-permute-start | bytes 8847368 | tf_op jit(solution)/shard_map/ppermute | solution.py:677
  130.9 9.1 %collective-permute-start.19 = (bf16[1536,768]{1,0:T(8,128)(2,1)}, bf16[1536,768]{1,0:T(8,128)(2,1)}, u32[]{:S(2)}, u32[]{:S(2)}) collective-permute-start(bf16[1536,768]{1,0:T(8,128)(2,1)} %bitcast.25.dnear_ref), channel_id=1, source_target_pairs={{0,16},{16,0},{1,17},{17,1},{2,18},{18,2},{3,19},{19,3},{4,20},{20... | collective-permute-start | bytes 7077896 | tf_op jit(solution)/shard_map/ppermute | solution.py:677
  216.5 31.5 %collective-permute-start.22 = (bf16[384,3840]{1,0:T(8,128)(2,1)}, bf16[384,3840]{1,0:T(8,128)(2,1)}, u32[]{:S(2)}, u32[]{:S(2)}) collective-permute-start(bf16[384,3840]{1,0:T(8,128)(2,1)} %get-tuple-element.188), channel_id=1, source_target_pairs={{0,16},{16,0},{1,17},{17,1},{2,18},{18,2},{3,19},{19,3},{4,20},{20... | collective-permute-start | bytes 8847368 | tf_op jit(solution)/shard_map/ppermute | solution.py:677
  216.6 31.3 %collective-permute-start.21 = (bf16[1536,768]{1,0:T(8,128)(2,1)}, bf16[1536,768]{1,0:T(8,128)(2,1)}, u32[]{:S(2)}, u32[]{:S(2)}) collective-permute-start(bf16[1536,768]{1,0:T(8,128)(2,1)} %get-tuple-element.187), channel_id=1, source_target_pairs={{0,16},{16,0},{1,17},{17,1},{2,18},{18,2},{3,19},{19,3},{4,20},{20... | collective-permute-start | bytes 7077896 | tf_op jit(solution)/shard_map/ppermute | solution.py:677
  254.3 32.6 %collective-permute-start.25 = (bf16[2,2,24,3840]{3,2,1,0:T(8,128)(2,1)}, bf16[2,2,24,3840]{3,2,1,0:T(8,128)(2,1)S(1)}, u32[]{:S(2)}, u32[]{:S(2)}) collective-permute-start(bf16[2,2,24,3840]{3,2,1,0:T(8,128)(2,1)} %get-tuple-element.199), channel_id=1, source_target_pairs={{0,2},{1,3},{2,0},{3,1},{4,6},{5,7},{6,4},{7,5},{8,10},{9,11},{10,... | collective-permute-start | bytes 2211848 | tf_op jit(solution)/shard_map/ppermute | solution.py:685
  255.4 31.6 %collective-permute-start.26 = (bf16[2,2,24,3840]{3,2,1,0:T(8,128)(2,1)}, bf16[2,2,24,3840]{3,2,1,0:T(8,128)(2,1)}, u32[]{:S(2)}, u32[]{:S(2)}) collective-permute-start(bf16[2,2,24,3840]{3,2,1,0:T(8,128)(2,1)} %get-tuple-element.200), channel_id=1, source_target_pairs={{0,1},{1,0},{2,3},{3,2},{4,5},{5,4},{6,7},{7,6},{8,9},{9,8},{10,11... | collective-permute-start | bytes 2211848 | tf_op jit(solution)/shard_map/ppermute | solution.py:681
  256.3 30.7 %collective-permute-start.23 = (bf16[2,2,96,768]{3,2,1,0:T(8,128)(2,1)}, bf16[2,2,96,768]{3,2,1,0:T(8,128)(2,1)}, u32[]{:S(2)}, u32[]{:S(2)}) collective-permute-start(bf16[2,2,96,768]{3,2,1,0:T(8,128)(2,1)} %get-tuple-element.197), channel_id=1, source_target_pairs={{0,2},{1,3},{2,0},{3,1},{4,6},{5,7},{6,4},{7,5},{8,10},{9,11},{10,... | collective-permute-start | bytes 1769480 | tf_op jit(solution)/shard_map/ppermute | solution.py:685
  257.8 29.2 %collective-permute-start.24 = (bf16[2,2,96,768]{3,2,1,0:T(8,128)(2,1)}, bf16[2,2,96,768]{3,2,1,0:T(8,128)(2,1)}, u32[]{:S(2)}, u32[]{:S(2)}) collective-permute-start(bf16[2,2,96,768]{3,2,1,0:T(8,128)(2,1)} %get-tuple-element.198), channel_id=1, source_target_pairs={{0,1},{1,0},{2,3},{3,2},{4,5},{5,4},{6,7},{7,6},{8,9},{9,8},{10,11... | collective-permute-start | bytes 1769480 | tf_op jit(solution)/shard_map/ppermute | solution.py:681
  293.2 18.0 %collective-permute-start.29 = (bf16[2,24,3840]{2,1,0:T(8,128)(2,1)}, bf16[2,24,3840]{2,1,0:T(8,128)(2,1)S(1)}, u32[]{:S(2)}, u32[]{:S(2)}) collective-permute-start(bf16[2,24,3840]{2,1,0:T(8,128)(2,1)} %get-tuple-element.219), channel_id=1, source_target_pairs={{0,1},{1,0},{2,3},{3,2},{4,5},{5,4},{6,7},{7,6},{8,9},{9,8},{10,11... | collective-permute-start | bytes 1105928 | tf_op jit(solution)/shard_map/ppermute | solution.py:681
  294.7 16.5 %collective-permute-start.30 = (bf16[2,24,3840]{2,1,0:T(8,128)(2,1)}, bf16[2,24,3840]{2,1,0:T(8,128)(2,1)S(1)}, u32[]{:S(2)}, u32[]{:S(2)}) collective-permute-start(bf16[2,24,3840]{2,1,0:T(8,128)(2,1)} %get-tuple-element.220), channel_id=1, source_target_pairs={{0,2},{1,3},{2,0},{3,1},{4,6},{5,7},{6,4},{7,5},{8,10},{9,11},{10,... | collective-permute-start | bytes 1105928 | tf_op jit(solution)/shard_map/ppermute | solution.py:685
  295.3 14.0 %collective-permute-start.27 = (bf16[2,96,768]{2,1,0:T(8,128)(2,1)}, bf16[2,96,768]{2,1,0:T(8,128)(2,1)S(1)}, u32[]{:S(2)}, u32[]{:S(2)}) collective-permute-start(bf16[2,96,768]{2,1,0:T(8,128)(2,1)} %get-tuple-element.217), channel_id=1, source_target_pairs={{0,1},{1,0},{2,3},{3,2},{4,5},{5,4},{6,7},{7,6},{8,9},{9,8},{10,11... | collective-permute-start | bytes 884744 | tf_op jit(solution)/shard_map/ppermute | solution.py:681
  296.4 14.1 %collective-permute-start.28 = (bf16[2,96,768]{2,1,0:T(8,128)(2,1)}, bf16[2,96,768]{2,1,0:T(8,128)(2,1)S(1)}, u32[]{:S(2)}, u32[]{:S(2)}) collective-permute-start(bf16[2,96,768]{2,1,0:T(8,128)(2,1)} %get-tuple-element.218), channel_id=1, source_target_pairs={{0,2},{1,3},{2,0},{3,1},{4,6},{5,7},{6,4},{7,5},{8,10},{9,11},{10,... | collective-permute-start | bytes 884744 | tf_op jit(solution)/shard_map/ppermute | solution.py:685
  317.5 22.1 %collective-permute-start.33 = (bf16[2,24,6912]{2,1,0:T(8,128)(2,1)}, bf16[2,24,6912]{2,1,0:T(8,128)(2,1)S(1)}, u32[]{:S(2)}, u32[]{:S(2)}) collective-permute-start(bf16[2,24,6912]{2,1,0:T(8,128)(2,1)} %get-tuple-element.236), channel_id=1, source_target_pairs={{0,4},{1,5},{2,6},{3,7},{4,0},{5,1},{6,2},{7,3},{8,12},{9,13},{10,... | collective-permute-start | bytes 1990664 | tf_op jit(solution)/shard_map/ppermute | solution.py:689
  329.8 10.1 %collective-permute-start.32 = (bf16[384,1280]{1,0:T(8,128)(2,1)S(1)}, bf16[384,1280]{1,0:T(8,128)(2,1)S(1)}, u32[]{:S(2)}, u32[]{:S(2)}) collective-permute-start(bf16[384,1280]{1,0:T(8,128)(2,1)S(1)} %pad_maximum_fusion.6), channel_id=1, source_target_pairs={{0,16},{16,0},{1,17},{17,1},{2,18},{18,2},{3,19},{19,3},{4,20},{20... | collective-permute-start | bytes 2949128 | tf_op jit(solution)/shard_map/ppermute | solution.py:677
  339.5 32.1 %collective-permute-start.31 = (bf16[640,768]{1,0:T(8,128)(2,1)S(1)}, bf16[640,768]{1,0:T(8,128)(2,1)S(1)}, u32[]{:S(2)}, u32[]{:S(2)}) collective-permute-start(bf16[640,768]{1,0:T(8,128)(2,1)S(1)} %get-tuple-element.229), channel_id=1, source_target_pairs={{0,16},{16,0},{1,17},{17,1},{2,18},{18,2},{3,19},{19,3},{4,20},{20... | collective-permute-start | bytes 2949128 | tf_op jit(solution)/shard_map/ppermute | solution.py:677
  341.1 13.1 %collective-permute-start.35 = (bf16[2,2,24,2432]{3,2,0,1:T(8,128)(2,1)S(1)}, bf16[2,2,24,2432]{3,2,0,1:T(8,128)(2,1)S(1)}, u32[]{:S(2)}, u32[]{:S(2)}) collective-permute-start(bf16[2,2,24,2432]{3,2,0,1:T(8,128)(2,1)S(1)} %copy_bitcast_fusion.3), channel_id=1, source_target_pairs={{0,2},{1,3},{2,0},{3,1},{4,6},{5,7},{6,4},{7,5},{8,10},{9,11},{10,... | collective-permute-start | bytes 1400840 | tf_op jit(solution)/shard_map/ppermute | solution.py:685
  341.8 12.8 %collective-permute-start.36 = (bf16[2,2,24,2432]{3,2,0,1:T(8,128)(2,1)S(1)}, bf16[2,2,24,2432]{3,2,0,1:T(8,128)(2,1)S(1)}, u32[]{:S(2)}, u32[]{:S(2)}) collective-permute-start(bf16[2,2,24,2432]{3,2,0,1:T(8,128)(2,1)S(1)} %copy_bitcast_fusion.2), channel_id=1, source_target_pairs={{0,1},{1,0},{2,3},{3,2},{4,5},{5,4},{6,7},{7,6},{8,9},{9,8},{10,11... | collective-permute-start | bytes 1400840 | tf_op jit(solution)/shard_map/ppermute | solution.py:681
  342.8 17.1 %collective-permute-start.39 = (bf16[24,6912]{1,0:T(8,128)(2,1)S(1)}, bf16[24,6912]{1,0:T(8,128)(2,1)S(1)}, u32[]{:S(2)}, u32[]{:S(2)}) collective-permute-start(bf16[24,6912]{1,0:T(8,128)(2,1)S(1)} %fusion.2), channel_id=1, source_target_pairs={{0,8},{1,9},{2,10},{3,11},{4,12},{5,13},{6,14},{7,15},{8,0},{9,1},... | collective-permute-start | bytes 995336 | tf_op jit(solution)/shard_map/ppermute | solution.py:689
  353.9 17.8 %collective-permute-start.34 = (bf16[640,768]{1,0:T(8,128)(2,1)S(1)}, bf16[640,768]{1,0:T(8,128)(2,1)S(1)}, u32[]{:S(2)}, u32[]{:S(2)}) collective-permute-start(bf16[640,768]{1,0:T(8,128)(2,1)S(1)} %get-tuple-element.240), channel_id=1, source_target_pairs={{0,16},{16,0},{1,17},{17,1},{2,18},{18,2},{3,19},{19,3},{4,20},{20... | collective-permute-start | bytes 2949128 | tf_op jit(solution)/shard_map/ppermute | solution.py:677
  (45 other events, 322.6 us)
